TPU v7x, 32 devices: a whole 2x2x4 slice. The times are simulated.
32 devices in a mesh: dp: 8 (over z, x), tensor: 4 (over y, core).
Axes of the slice: x: 2, y: 2, z: 4, core: 2. Of those that a mesh axis runs over, the one named last changes fastest.
Arguments:
- query_states: bfloat16 [1, 8192, 1024], P(None, 'dp', 'tensor'), may hold values from -6 to 6
- key_states: bfloat16 [1, 8192, 1024], P(None, 'dp', 'tensor'), may hold values from -6 to 6
- value_states: bfloat16 [1, 8192, 1024], P(None, 'dp', 'tensor'), may hold values from -6 to 6
- joining_weight: bfloat16 [1, 1024, 2048], P(None, 'tensor'), may hold values from -0.1875 to 0.1875
- norm_gain: float32 [2048], replicated, may hold values from 0.1 to 1.9
- next_hidden: bfloat16 [8192, 2048], P(('dp', 'tensor')), may hold values from -6 to 6
- lengths: int32 [8], P('dp'), may hold values from 256 to 1024
- vote_counts: int32 [8], P('dp'), may hold values from 1 to 8
Outputs:
- draft_hidden: bfloat16 [8192, 2048], P(('dp', 'tensor'))
- weight_grad: bfloat16 [1, 1024, 2048], P(None, 'tensor', 'dp')
- gain_grad: float32 [2048], replicated
- draft_loss: float32 [], replicated
All inputs are finite; a program needn't handle non-finite values.
Results may differ from a plain program's by a relative error of at most 0.014.
Values may be sent and summed in bfloat16 or wider, within the bound.
No kernel may reach another device: no remote copies, remote signals or barrier semaphores. Data moves between devices by JAX's collectives and lax.ppermute only.
A program may use at most 64 MiB of HBM per device.

v0:
```python
import math

import jax
import jax.numpy as jnp
from jax import lax
from jax.sharding import PartitionSpec as P

HD = 128


loss_scale = 65536.0
neg_large = -1e30


def on_device(
    query_states,
    key_states,
    value_states,
    joining_weight,
    norm_gain,
    next_hidden,
    lengths,
    vote_counts,
):
    n_layers, tok_group, col_width = query_states.shape
    chains = lengths.shape[0]
    seq_len = tok_group // chains
    heads_here = col_width // HD
    shaped = (n_layers, chains, seq_len, heads_here, HD)
    scores = jnp.einsum(
        "lcqhd,lckhd->lchqk",
        query_states.reshape(shaped),
        key_states.reshape(shaped),
        preferred_element_type=jnp.float32,
    ) / math.sqrt(HD)
    positions = jnp.arange(seq_len)
    causal = positions[None, :] <= positions[:, None]
    key_valid = positions[None, :] < lengths[:, None]
    visible = causal[None, None, None, :, :] & key_valid[None, :, None, None, :]
    scores = jnp.where(visible, scores, neg_large)
    row_peak = jnp.max(scores, axis=-1, keepdims=True)
    exponent = jnp.exp(scores - row_peak)
    attn_probs = (exponent / jnp.sum(exponent, axis=-1, keepdims=True)).astype(jnp.bfloat16)
    context = jnp.einsum(
        "lchqk,lckhd->lcqhd",
        attn_probs,
        value_states.reshape(shaped),
        preferred_element_type=jnp.float32,
    )
    context = context.astype(jnp.bfloat16).reshape(n_layers, tok_group, col_width)
    own_rows = next_hidden.shape[0]
    offset = lax.axis_index("tensor") * own_rows
    partial_sum = jnp.einsum(
        "ltc,lcd->td", context, joining_weight, preferred_element_type=jnp.float32
    )
    summed = lax.psum(partial_sum.astype(jnp.bfloat16), "tensor").astype(jnp.float32)
    joined_rows = lax.dynamic_slice_in_dim(summed, offset, own_rows, 0)
    token_pos = offset + jnp.arange(own_rows, dtype=jnp.int32)
    chain_of = token_pos // seq_len
    in_chain = token_pos % seq_len
    onehot = (chain_of[:, None] == jnp.arange(chains)[None, :]).astype(jnp.float32)
    tok_votes = jnp.dot(onehot, vote_counts.astype(jnp.float32), precision=lax.Precision.HIGHEST)
    tok_length = jnp.dot(onehot, lengths.astype(jnp.float32), precision=lax.Precision.HIGHEST)
    token_weight = jnp.where(in_chain.astype(jnp.float32) < tok_length - 1.0, tok_votes, 0.0)
    inv_rms = lax.rsqrt(jnp.mean(joined_rows * joined_rows, axis=-1, keepdims=True) + 1e-06)
    normed = joined_rows * inv_rms
    predicted = normed * norm_gain
    draft_hidden = predicted.astype(jnp.bfloat16)
    misfit = predicted - next_hidden.astype(jnp.float32)
    local_loss = jnp.sum(token_weight * jnp.mean(misfit * misfit, axis=-1))
    grad_pred = loss_scale * 2.0 / joined_rows.shape[1] * token_weight[:, None] * misfit
    local_gain = jnp.sum(grad_pred * normed, axis=0)
    grad_normed = grad_pred * norm_gain
    grad_joined = (
        inv_rms * (grad_normed - normed * jnp.mean(grad_normed * normed, axis=-1, keepdims=True))
    ).astype(jnp.bfloat16)
    gain_sum, loss_sum, weight_total = lax.psum(
        (local_gain, local_loss, jnp.sum(token_weight)), ("dp", "tensor")
    )
    grad_total = jnp.einsum(
        "ltc,td->lcd",
        context,
        lax.all_gather(grad_joined, "tensor", axis=0, tiled=True),
        preferred_element_type=jnp.float32,
    )
    grad_cols = lax.psum_scatter(
        grad_total.astype(jnp.bfloat16), "dp", scatter_dimension=2, tiled=True
    ).astype(jnp.float32)
    weight_grad = (grad_cols / weight_total).astype(jnp.bfloat16)
    return (draft_hidden, weight_grad, gain_sum / weight_total, loss_sum / weight_total)


def solution(mesh):
    return jax.shard_map(
        on_device,
        mesh=mesh,
        in_specs=(
            P(None, "dp", "tensor"),
            P(None, "dp", "tensor"),
            P(None, "dp", "tensor"),
            P(None, "tensor", None),
            P(),
            P(("dp", "tensor"), None),
            P("dp"),
            P("dp"),
        ),
        out_specs=(P(("dp", "tensor"), None), P(None, "tensor", "dp"), P(), P()),
        check_vma=False,
    )
```

profile of v0, /device:TPU:0, one launch (start us, length us, event | category | flops | bytes accessed | tf_op | source)
XLA Modules:
  0.0 236.3 jit_solution(4800602347688197091)
XLA Ops:
  7.2 0.0 all-reduce.3.cloned.1.call-start
  8.0 0.4 fusion.4
  8.4 2.0 reshape.122
  10.4 1.0 reshape.123
  11.4 1.0 copy.17
  12.4 7.7 %fusion.39 = (f32[2,1024]{1,0:T(2,128)S(1)}, f32[2,1024,1024]{1,2,0:T(8,128)}) fusion(pred[1024,1024]{0,1:T(8,128)(4,1)S(1)} %fusion.4, bf16[1024,2,128]{2,1,0:T(2,128)(2,1)} %reshape.123, bf16[1024,2,128]{2,1,0:T(2,128)(2,1)} %reshape.122), kind=kOutput, calls=%fused_computation.54 | convolution fusion | flops 545260544 | bytes 10493952 | tf_op jit(solution)/shard_map/sub | solution.py:42
  20.1 4.1 %fusion.20 = bf16[2,1024,128]{1,2,0:T(8,128)(2,1)S(1)} fusion(bf16[1024,2,128]{0,2,1:T(8,128)(2,1)S(1)} %bitcast.23, f32[2,1024,1024]{1,2,0:T(8,128)} %get-tuple-element.13, f32[2,1024]{1,0:T(2,128)S(1)} %get-tuple-element.12), kind=kOutput, calls=%fused_computation.29 | convolution fusion | flops 541327360 | bytes 9445376 | tf_op jit(solution)/shard_map/lchqk,lckhd->lcqhd/dot_general | solution.py:44
  24.3 3.3 %convolution_convert_fusion = bf16[1024,2048]{1,0:T(8,128)(2,1)} fusion(bf16[1024,256]{0,1:T(8,128)(2,1)S(1)} %bitcast.21, bf16[1,256,2048]{2,1,0:T(8,128)(2,1)S(1)} %copy-done), kind=kOutput, calls=%fused_computation.11 | convolution fusion | flops 1075838976 | bytes 5767168 | tf_op jit(solution)/shard_map/ltc,lcd->td/dot_general | solution.py:53
  27.5 0.0 all-reduce.3.cloned.1.call-update
  27.6 0.0 all-gather.2.cloned.1.call-start
  28.3 0.6 broadcast_multiply_fusion
  29.0 86.9 %all-reduce.3.cloned.1.call-done = bf16[1024,2048]{1,0:T(8,128)(2,1)} async-done(((bf16[1024,2048]{1,0:T(8,128)(2,1)}), bf16[1024,2048]{1,0:T(8,128)(2,1)}) %all-reduce.3.cloned.1.call-update) | async-done | bytes 4194320 | tf_op jit(solution)/shard_map/psum | solution.py:56
  115.9 1.5 fusion.19
  117.4 2.3 fusion.18
  119.8 3.4 %fusion.17 = (bf16[256,2048]{1,0:T(8,128)(2,1)}, bf16[256,2048]{1,0:T(8,128)(2,1)}) fusion(bf16[256,2048]{1,0:T(8,128)(2,1)S(1)} %copy-done.1, f32[256]{0:T(256)S(1)} %broadcast_multiply_fusion.1, f32[256]{0:T(256)S(1)} %get-tuple-element.14, f32[2048]{0:T(1024)S(1)} %copy-done.5, f32[256]{0:T(256)S(1)} %add_rsqrt_fusion, ...), kind=kLoop, calls=%fused_computation.25 | loop fusion | flops 6291456 | bytes 4205572 | tf_op jit(solution)/shard_map/convert_element_type | solution.py:76
  123.2 0.0 all-gather.2.cloned.1.call-update
  123.2 0.0 reduce-scatter.2.cloned.1.call-start
  123.3 34.7 %all-gather.2.cloned.1.call-done = bf16[1024,2048]{1,0:T(8,128)(2,1)} async-done(((bf16[256,2048]{1,0:T(8,128)(2,1)}), bf16[1024,2048]{1,0:T(8,128)(2,1)}) %all-gather.2.cloned.1.call-update) | async-done | bytes 4194320 | tf_op jit(solution)/shard_map/all_gather | solution.py:83
  158.0 4.4 %fusion.11 = bf16[1,256,2048]{2,1,0:T(8,128)(2,1)} fusion(bf16[1024,256]{0,1:T(8,128)(2,1)S(1)} %bitcast.22, bf16[1024,2048]{1,0:T(8,128)(2,1)} %all-gather.2.cloned.1.call-done), kind=kOutput, calls=%fused_computation.19 | convolution fusion | flops 1074266112 | bytes 5767168 | tf_op jit(solution)/shard_map/ltc,td->lcd/dot_general | solution.py:80
  162.4 0.7 multiply_reduce_fusion.1
  163.1 39.7 %all-reduce = (f32[]{:T(128)}, f32[2048]{0:T(1024)S(1)}, f32[]{:T(128)}) all-reduce(f32[]{:T(128)} %get-tuple-element.15, f32[2048]{0:T(1024)S(1)} %get-tuple-element.4, f32[]{:T(128)} %multiply_reduce_fusion.1), channel_id=1, replica_groups=mesh['dp'=8,'tensor'=4] {'dp','tensor'}, use_global_device_ids=true, to_apply=%region_7.8 | all-reduce | flops 2050 | bytes 16400 | tf_op jit(solution)/shard_map/psum | solution.py:77
  204.1 1.2 broadcast_divide_fusion
  205.2 21.3 %reduce-scatter.2.cloned.1.call-done = bf16[1,256,256]{2,1,0:T(8,128)(2,1)} async-done(((bf16[1,256,2048]{2,1,0:T(8,128)(2,1)}), bf16[1,256,256]{2,1,0:T(8,128)(2,1)}) %reduce-scatter.2.cloned.1.call-update) | async-done | bytes 131088 | tf_op jit(solution)/shard_map/reduce_scatter | solution.py:86
  226.5 2.1 divide_convert_fusion.4
  (16 shorter events, 0.1 us)
Async XLA Ops:
  7.2 17.1 %copy-start = (bf16[1,256,2048]{2,1,0:T(8,128)(2,1)S(1)}, bf16[1,256,2048]{2,1,0:T(8,128)(2,1)}, u32[]{:S(2)}) copy-start(bf16[1,256,2048]{2,1,0:T(8,128)(2,1)} %param.11) | copy-start | bytes 3145732
  7.2 3.3 %copy-start.2 = (bf16[1,1024,256]{2,1,0:T(8,128)(2,1)S(1)}, bf16[1,1024,256]{2,1,0:T(8,128)(2,1)}, u32[]{:S(2)}) copy-start(bf16[1,1024,256]{2,1,0:T(8,128)(2,1)} %param.9) | copy-start | bytes 1572868
  7.2 4.2 %copy-start.3 = (bf16[1,1024,256]{2,1,0:T(8,128)(2,1)S(1)}, bf16[1,1024,256]{2,1,0:T(8,128)(2,1)}, u32[]{:S(2)}) copy-start(bf16[1,1024,256]{2,1,0:T(8,128)(2,1)} %param.10) | copy-start | bytes 1572868
  7.2 108.7 %all-reduce.3.cloned.1.call-start = ((), (), s32[]{:S(2)}) async-start(), calls=%async_computation.1 | async-start | bytes 8388608 | tf_op jit(solution)/shard_map/psum | solution.py:56
  12.4 7.7 %copy-start.4 = (bf16[1,1024,256]{1,2,0:T(8,128)(2,1)S(1)}, bf16[1,1024,256]{1,2,0:T(8,128)(2,1)}, u32[]{:S(2)}) copy-start(bf16[1,1024,256]{1,2,0:T(8,128)(2,1)} %copy.17) | copy-start | bytes 1572868
  27.5 89.9 %copy-start.1 = (bf16[256,2048]{1,0:T(8,128)(2,1)S(1)}, bf16[256,2048]{1,0:T(8,128)(2,1)}, u32[]{:S(2)}) copy-start(bf16[256,2048]{1,0:T(8,128)(2,1)} %param.13) | copy-start | bytes 3145732
  27.5 89.9 %copy-start.5 = (f32[2048]{0:T(1024)S(1)}, f32[2048]{0:T(1024)}, u32[]{:S(2)}) copy-start(f32[2048]{0:T(1024)} %param.12) | copy-start | bytes 24580
  27.6 130.4 %all-gather.2.cloned.1.call-start = ((), (), s32[]{:S(2)}) async-start(), calls=%async_computation.2 | async-start | bytes 5242880 | tf_op jit(solution)/shard_map/all_gather | solution.py:83
  123.2 103.3 %reduce-scatter.2.cloned.1.call-start = ((), (), s32[]{:S(2)}) async-start(), calls=%async_computation.3 | async-start | bytes 1179648 | tf_op jit(solution)/shard_map/reduce_scatter | solution.py:86
Sparse Core Ops, SparseCore 0:
  27.7 88.1 all-reduce.2
  123.3 34.6 all-gather.1
  162.5 63.9 reduce-scatter.1
where the time goes:
time: 237 us; the launch traced here: 236 us
  waiting for transfers between devices  143 us (60%)
  blocking collectives  39.7 us (17%)
  matrix products  19.5 us (8%)
  between operations  17.7 us (7%)
  other arithmetic  12.2 us (5%)
  local copies, waits for them, and re-layouts  4.04 us (2%)
    psum x1, waiting for transfers between devices, on_device(): lax.psum(partial_sum.astype(jnp.bfloat16), 'tensor').astype(jnp.float32)  86.9 us
    psum x1, blocking collectives, on_device(): lax.psum((local_gain, local_loss, jnp.sum(token_weight)), ('dp', 'tensor'))  39.7 us
    all_gather x1, waiting for transfers between devices, on_device(): lax.all_gather(grad_joined, 'tensor', axis=0, tiled=True)  34.7 us
    reduce_scatter x1, waiting for transfers between devices, on_device(): lax.psum_scatter(grad_total.astype(jnp.bfloat16), 'dp', scatter_dimension...  21.3 us
    sub x1, matrix products, on_device(): exponent = jnp.exp(scores - row_peak)  7.73 us
  transfers between devices with their start and end apart: 3, of which 3 were waited for; matrix products, arithmetic and copies ran while one was open for 1% of the time, Pallas kernels for 0%

commit v1 on v0

v1 whole, which is shorter than its diff:
```python
import functools
import math

import jax
import jax.numpy as jnp
from jax import lax
from jax.experimental import pallas as pl
from jax.experimental.pallas import tpu as pltpu
from jax.sharding import PartitionSpec as P

HD = 128
QB = 256
ROWS = 16
COLS = 512

loss_scale = 65536.0
neg_large = -1e30
MIB = 1 << 20


def dot(a, b, dims):
    return lax.dot_general(a, b, (dims, ((), ())), preferred_element_type=jnp.float32)


def attend(len_ref, q_ref, k_ref, v_ref, o_ref):
    seq = q_ref.shape[0]
    rate = math.log2(math.e) / math.sqrt(HD)
    length = len_ref[0]
    for i in range(seq // QB):
        rows = slice(i * QB, (i + 1) * QB)
        keys = (i + 1) * QB
        scores = dot(q_ref[rows, :], k_ref[:keys, :], ((1,), (1,)))
        col = lax.broadcasted_iota(jnp.int32, (1, keys), 1)
        scores = scores + jnp.where(col < length, 0.0, neg_large)
        r = lax.broadcasted_iota(jnp.int32, (QB, QB), 0)
        c = lax.broadcasted_iota(jnp.int32, (QB, QB), 1)
        last = jnp.where(c <= r, scores[:, keys - QB :], neg_large)
        scores = last if i == 0 else jnp.concatenate([scores[:, : keys - QB], last], 1)
        peak = jnp.max(scores, axis=1, keepdims=True)
        e = jnp.exp2((scores - peak) * rate)
        total = jnp.sum(e, axis=1, keepdims=True)
        out = dot(e.astype(jnp.bfloat16), v_ref[:keys, :], ((1,), (0,)))
        o_ref[rows, :] = (out / total).astype(jnp.bfloat16)


def attention(q, k, v, lengths):
    seq, width = q.shape
    heads = width // HD
    block = pl.BlockSpec((seq, HD), lambda h: (0, h))
    return pl.pallas_call(
        attend,
        grid=(heads,),
        in_specs=[pl.BlockSpec(memory_space=pltpu.SMEM), block, block, block],
        out_specs=block,
        out_shape=jax.ShapeDtypeStruct((seq, width), jnp.bfloat16),
        compiler_params=pltpu.CompilerParams(vmem_limit_bytes=32 * MIB),
        cost_estimate=pl.CostEstimate(
            flops=4 * seq * seq * width, bytes_accessed=8 * seq * width, transcendentals=heads * seq * seq
        ),
        name="attend",
    )(lengths, q, k, v)


def join_body(n_tensor, n_dp, chunks, seq, info_ref, ctx_ref, gain_ref, next_ref, *refs):
    w_refs = refs[:n_tensor]
    hidden_ref = refs[n_tensor]
    grad_refs = refs[n_tensor + 1 : n_tensor + 1 + chunks]
    stat_ref, joined_ref, square_ref, acc_ref = refs[n_tensor + 1 + chunks :]
    rows, dout = joined_ref.shape
    me, length, votes = info_ref[0], info_ref[1], info_ref[2]
    for c in range(0, dout, COLS):
        total = None
        for m in range(n_tensor):
            part = dot(ctx_ref[me ^ m], w_refs[m][:, c : c + COLS], ((1,), (0,)))
            part = part.astype(jnp.bfloat16).astype(jnp.float32)
            total = part if total is None else total + part
        joined_ref[:, c : c + COLS] = total
        sq = total * total
        lanes = sum(sq[:, i : i + 128] for i in range(0, COLS, 128))
        square_ref[...] = lanes if c == 0 else square_ref[...] + lanes
    acc_ref[...] = jnp.zeros_like(acc_ref)
    slice_w = dout // n_dp
    cw = slice_w // chunks

    def body(r, carry):
        loss, weights = carry
        at = pl.ds(pl.multiple_of(r * ROWS, ROWS), ROWS)
        inv = lax.rsqrt(jnp.sum(square_ref[at, :], axis=1, keepdims=True) * (1.0 / dout) + 1e-06)
        pos = (me * rows + r * ROWS) % seq + lax.broadcasted_iota(jnp.int32, (ROWS, 1), 0)
        weight = jnp.where(pos < length - 1, votes.astype(jnp.float32), 0.0)
        scaled = weight * (loss_scale * 2.0 / dout)
        miss = jnp.zeros((ROWS, 128), jnp.float32)
        lean = jnp.zeros((ROWS, 128), jnp.float32)
        for c in range(0, dout, COLS):
            cs = slice(c, c + COLS)
            normed = joined_ref[at, cs] * inv
            gain = gain_ref[:, cs]
            predicted = normed * gain
            hidden_ref[at, cs] = predicted.astype(jnp.bfloat16)
            misfit = predicted - next_ref[at, cs].astype(jnp.float32)
            grad = scaled * misfit
            both = grad * normed
            acc_ref[:, cs] += both
            sq = misfit * misfit
            ln = both * gain
            miss += sum(sq[:, i : i + 128] for i in range(0, COLS, 128))
            lean += sum(ln[:, i : i + 128] for i in range(0, COLS, 128))
            joined_ref[at, cs] = normed
        lean = jnp.sum(lean, axis=1, keepdims=True) * (1.0 / dout)
        for d in range(n_dp):
            for j in range(chunks):
                at0 = d * slice_w + j * cw
                cs = slice(at0, at0 + cw)
                normed = joined_ref[at, cs]
                gain = gain_ref[:, cs]
                misfit = normed * gain - next_ref[at, cs].astype(jnp.float32)
                g = inv * (scaled * misfit * gain - normed * lean)
                grad_refs[j][at, d * cw : (d + 1) * cw] = g.astype(jnp.bfloat16)
        loss = loss + weight * (jnp.sum(miss, axis=1, keepdims=True) * (1.0 / dout))
        return loss, weights + weight

    zero = jnp.zeros((ROWS, 1), jnp.float32)
    loss, weights = lax.fori_loop(0, rows // ROWS, body, (zero, zero))
    stat_ref[:, :dout] = jnp.sum(acc_ref[...], axis=0, keepdims=True)
    lane = lax.broadcasted_iota(jnp.int32, (1, 128), 1)
    loss = jnp.sum(loss, axis=0, keepdims=True)
    weights = jnp.sum(weights, axis=0, keepdims=True)
    stat_ref[:, dout:] = jnp.where(lane == 0, loss, jnp.where(lane == 1, weights, 0.0))


def join(info, ctx, gain, next_hidden, weights, n_dp, chunks, seq):
    n_tensor, rows, _ = ctx.shape
    dout = gain.shape[1]
    vmem = pl.BlockSpec(memory_space=pltpu.VMEM)
    out = pl.pallas_call(
        functools.partial(join_body, n_tensor, n_dp, chunks, seq),
        in_specs=[pl.BlockSpec(memory_space=pltpu.SMEM)] + [vmem] * (3 + n_tensor),
        out_specs=[vmem] * (2 + chunks),
        out_shape=[jax.ShapeDtypeStruct((rows, dout), jnp.bfloat16)]
        + [jax.ShapeDtypeStruct((rows, dout // chunks), jnp.bfloat16)] * chunks
        + [jax.ShapeDtypeStruct((1, dout + 128), jnp.float32)],
        scratch_shapes=[
            pltpu.VMEM((rows, dout), jnp.float32),
            pltpu.VMEM((rows, 128), jnp.float32),
            pltpu.VMEM((ROWS, dout), jnp.float32),
        ],
        compiler_params=pltpu.CompilerParams(vmem_limit_bytes=48 * MIB),
        cost_estimate=pl.CostEstimate(
            flops=2 * rows * dout * ctx.shape[2] * n_tensor,
            bytes_accessed=2 * dout * (ctx.shape[2] * n_tensor + 3 * rows),
            transcendentals=rows,
        ),
        name="join",
    )(info, ctx, gain, next_hidden, *weights)
    return out[0], out[1 : 1 + chunks], out[1 + chunks]


def grad_body(n_tensor, info_ref, ctx_ref, *refs):
    g_refs, out_ref = refs[:n_tensor], refs[n_tensor]
    n_dp, _, cw = out_ref.shape
    me = info_ref[0]
    step = max(1, 256 // cw)
    for d in range(0, n_dp, step):
        total = None
        for m in range(n_tensor):
            part = dot(ctx_ref[me ^ m], g_refs[m][:, d * cw : (d + step) * cw], ((0,), (0,)))
            total = part if total is None else total + part
        total = total.astype(jnp.bfloat16)
        for i in range(step):
            out_ref[d + i] = total[:, i * cw : (i + 1) * cw]


def gradient(info, ctx, grads, n_dp):
    n_tensor, rows, feats = ctx.shape
    cols = grads[0].shape[1]
    vmem = pl.BlockSpec(memory_space=pltpu.VMEM)
    return pl.pallas_call(
        functools.partial(grad_body, n_tensor),
        in_specs=[pl.BlockSpec(memory_space=pltpu.SMEM)] + [vmem] * (1 + n_tensor),
        out_specs=vmem,
        out_shape=jax.ShapeDtypeStruct((n_dp, feats, cols // n_dp), jnp.bfloat16),
        compiler_params=pltpu.CompilerParams(vmem_limit_bytes=48 * MIB),
        cost_estimate=pl.CostEstimate(
            flops=2 * n_tensor * rows * feats * cols,
            bytes_accessed=2 * (n_tensor * rows * (feats + cols) + feats * cols),
            transcendentals=0,
        ),
        name="gradient",
    )(info, ctx, *grads)


def swap(x, axis, n, mask):
    return lax.ppermute(x, axis, [(i, i ^ mask) for i in range(n)])


def gather_xor(x, axis, n):
    held = {0: x}
    bit = n // 2
    while bit:
        held.update({m | bit: swap(p, axis, n, bit) for m, p in list(held.items())})
        bit //= 2
    return [held[m] for m in range(n)]


def on_device(
    n_dp,
    n_tensor,
    query_states,
    key_states,
    value_states,
    joining_weight,
    norm_gain,
    next_hidden,
    lengths,
    vote_counts,
):
    _, tokens, width = query_states.shape
    seq = tokens // lengths.shape[0]
    dout = norm_gain.shape[0]
    rows = next_hidden.shape[0]
    chunks = 2 if dout // n_dp >= 256 else 1
    me = lax.axis_index("tensor").astype(jnp.int32)
    info = jnp.stack([me, lengths[0], vote_counts[0]])
    weights = gather_xor(joining_weight[0], "tensor", n_tensor)
    context = attention(query_states[0], key_states[0], value_states[0], lengths)
    context = context.reshape(n_tensor, rows, width)
    ctx = lax.all_to_all(context, "tensor", 0, 0, tiled=True)
    hidden, grads, stats = join(info, ctx, norm_gain[None, :], next_hidden, weights, n_dp, chunks, seq)
    parts = []
    for j in range(chunks):
        every = gather_xor(grads[j], "tensor", n_tensor)
        slabs = gradient(info, context, every, n_dp)
        parts.append(lax.all_to_all(slabs, "dp", 0, 0, tiled=True))
    for axis, n in (("tensor", n_tensor), ("dp", n_dp)):
        bit = 1
        while bit < n:
            stats = stats + swap(stats, axis, n, bit)
            bit *= 2
    stats = stats[0]
    weight_total = stats[dout + 1]
    cols = [jnp.sum(p.astype(jnp.float32), axis=0) for p in parts]
    weight_grad = (jnp.concatenate(cols, axis=1) / weight_total).astype(jnp.bfloat16)
    return (hidden, weight_grad[None], stats[:dout] / weight_total, stats[dout] / weight_total)


def solution(mesh):
    return jax.shard_map(
        functools.partial(on_device, mesh.shape["dp"], mesh.shape["tensor"]),
        mesh=mesh,
        in_specs=(
            P(None, "dp", "tensor"),
            P(None, "dp", "tensor"),
            P(None, "dp", "tensor"),
            P(None, "tensor", None),
            P(),
            P(("dp", "tensor"), None),
            P("dp"),
            P("dp"),
        ),
        out_specs=(P(("dp", "tensor"), None), P(None, "tensor", "dp"), P(), P()),
        check_vma=False,
    )
```

time: 237 us -> 122 us (0.51)
  waiting for transfers between devices: 143 us -> 67.8 us
  blocking collectives: 39.7 us -> 0 us
  starting transfers between devices: 0.12 us -> 24.7 us
  matrix products: 19.5 us -> 0 us
  Pallas kernels: 0 us -> 17.3 us
  between operations: 17.7 us -> 4.55 us
  other arithmetic: 12.2 us -> 2.9 us
    psum x1 -> x0, waiting for transfers between devices: 86.9 us -> none  [on_device(): lax.psum(partial_sum.astype(jnp.bfloat16), 'tensor').astype(jnp.float32)]
    ppermute x0 -> x14, waiting for transfers between devices: none -> 53.3 us  [swap(): return lax.ppermute(x, axis, [(i, i ^ mask) for i in range(n)])]
    psum x1 -> x0, blocking collectives: 39.7 us -> none  [on_device(): lax.psum((local_gain, local_loss, jnp.sum(token_weight)), ('dp', 'tensor'))]
    all_gather x1 -> x0, waiting for transfers between devices: 34.7 us -> none  [on_device(): lax.all_gather(grad_joined, 'tensor', axis=0, tiled=True)]
    reduce_scatter x1 -> x0, waiting for transfers between devices: 21.3 us -> none  [on_device(): lax.psum_scatter(grad_total.astype(jnp.bfloat16), 'dp', scatter_dimension...]
    pallas_call x0 -> x4, Pallas kernels: none -> 17.3 us  [the longest x1 7.68 us: join(): pl.pallas_call(functools.partial(join_body, n_tensor, n_dp, chunks, seq),...]
    all_to_all x0 -> x3, waiting for transfers between devices: none -> 14.4 us  [the longest x1 8.14 us: on_device(): ctx = lax.all_to_all(context, 'tensor', 0, 0, tiled=True)]
    all_to_all x0 -> x3, starting transfers between devices: none -> 13.1 us  [the longest x2 9.5 us: on_device(): parts.append(lax.all_to_all(slabs, 'dp', 0, 0, tiled=True))]
  transfers between devices with their start and end apart: 3 -> 17, of which waited for: 3 -> 12; matrix products, arithmetic and copies ran while one was open for 1% -> 2% of each run, Pallas kernels for 0% -> 8%
where the time goes in v1:
time: 122 us; the launch traced here: 121 us
  waiting for transfers between devices  67.8 us (56%)
  starting transfers between devices  24.7 us (20%)
  Pallas kernels  17.3 us (14%)
  between operations  4.55 us (4%)
  local copies, waits for them, and re-layouts  3.78 us (3%)
  other arithmetic  2.9 us (2%)
    ppermute x14, waiting for transfers between devices, swap(): return lax.ppermute(x, axis, [(i, i ^ mask) for i in range(n)])  53.3 us
    ppermute x14, starting transfers between devices, swap(): return lax.ppermute(x, axis, [(i, i ^ mask) for i in range(n)])  11.6 us
    all_to_all x2, starting transfers between devices, on_device(): parts.append(lax.all_to_all(slabs, 'dp', 0, 0, tiled=True))  9.5 us
    all_to_all x1, waiting for transfers between devices, on_device(): ctx = lax.all_to_all(context, 'tensor', 0, 0, tiled=True)  8.14 us
    pallas_call x1, Pallas kernels, join(): pl.pallas_call(functools.partial(join_body, n_tensor, n_dp, chunks, seq),...  7.68 us
    all_to_all x2, waiting for transfers between devices, on_device(): parts.append(lax.all_to_all(slabs, 'dp', 0, 0, tiled=True))  6.31 us
    pallas_call x2, Pallas kernels, gradient(): pl.pallas_call(functools.partial(grad_body, n_tensor), in_specs=[pl.Block...  5.25 us
    pallas_call x1, Pallas kernels, attention(): pl.pallas_call(attend, grid=(heads,), in_specs=[pl.BlockSpec(memory_space...  4.42 us
  transfers between devices with their start and end apart: 17, of which 12 were waited for; matrix products, arithmetic and copies ran while one was open for 2% of the time, Pallas kernels for 8%

profile of v1, /device:TPU:0, one launch (start us, length us, event | category | flops | bytes accessed | tf_op | source)
XLA Modules:
  0.0 121.0 jit_solution(8906646285255852649)
XLA Ops:
  0.6 3.0 %collective-permute-start.1 = (bf16[256,2048]{1,0:T(8,128)(2,1)}, bf16[256,2048]{1,0:T(8,128)(2,1)}, u32[]{:S(2)}, u32[]{:S(2)}) collective-permute-start(bf16[256,2048]{1,0:T(8,128)(2,1)} %bitcast.12), channel_id=1, source_target_pairs={{0,2},{1,3},{2,0},{3,1},{4,6},{5,7},{6,4},{7,5},{8,10},{9,11},{10,... | collective-permute-start | bytes 3145736 | tf_op jit(solution)/shard_map/ppermute | solution.py:193
  3.7 23.5 %collective-permute-done.1.refs_2_ = bf16[256,2048]{1,0:T(8,128)(2,1)} collective-permute-done((bf16[256,2048]{1,0:T(8,128)(2,1)}, bf16[256,2048]{1,0:T(8,128)(2,1)}, u32[]{:S(2)}, u32[]{:S(2)}) %collective-permute-start.1) | collective-permute-done | bytes 1048608 | tf_op jit(solution)/shard_map/ppermute | solution.py:193
  30.9 4.4 %attend.1 = bf16[1024,256]{1,0:T(8,128)(2,1)} custom-call(s32[1]{0:T(128)S(6)} %copy.12.len_ref, bf16[1024,256]{1,0:T(8,128)(2,1)S(1)} %bitcast.16, bf16[1024,256]{1,0:T(8,128)(2,1)S(1)} %bitcast.17, bf16[1024,256]{1,0:T(8,128)(2,1)S(1)} %bitcast.18), custom_call_target="tpu_custom_call" | custom-call | flops 1073741824 | bytes 2097152 | tf_op jit(solution)/shard_map/attend/pallas_call | solution.py:50
  35.3 3.6 %all-to-all-start = ((bf16[4,256,256]{2,1,0:T(8,128)(2,1)}), bf16[4,256,256]{2,1,0:T(8,128)(2,1)S(1)}, u32[]{:S(2)}, u32[]{:S(2)}) async-start(bf16[4,256,256]{2,1,0:T(8,128)(2,1)} %bitcast.4.ctx_ref), calls=%async_computation | async-start | bytes 1048576 | tf_op jit(solution)/shard_map/all_to_all | solution.py:227
  39.7 8.1 %all-to-all-done.ctx_ref = bf16[4,256,256]{2,1,0:T(8,128)(2,1)S(1)} async-done(((bf16[4,256,256]{2,1,0:T(8,128)(2,1)}), bf16[4,256,256]{2,1,0:T(8,128)(2,1)S(1)}, u32[]{:S(2)}, u32[]{:S(2)}) %all-to-all-start) | async-done | bytes 524320 | tf_op jit(solution)/shard_map/all_to_all | solution.py:227
  47.9 7.7 %join.1 = (bf16[256,2048]{1,0:T(8,128)(2,1)}, bf16[256,1024]{1,0:T(8,128)(2,1)S(1)}, bf16[256,1024]{1,0:T(8,128)(2,1)S(1)}, f32[1,2176]{1,0:T(1,128)S(1)}) custom-call(s32[3]{0:T(128)S(1)} %pad_add_fusion.info_ref, bf16[4,256,256]{2,1,0:T(8,128)(2,1)S(1)} %all-to-all-done.ctx_ref, f32[1,2048]{1,0:T(1,128)S(1)} %bitcast.15, bf16[256,2048]{1,0:T(8,128)(2,1)S(1)} %copy-done, ...), custom_call_target="tpu_custom_call" | custom-call | flops 1073741824 | bytes 7340032 | tf_op jit(solution)/shard_map/join/pallas_call | solution.py:135
  55.8 13.3 %collective-permute-done.4.refs_2_ = bf16[256,1024]{1,0:T(8,128)(2,1)S(1)} collective-permute-done((bf16[256,1024]{1,0:T(8,128)(2,1)S(1)}, bf16[256,1024]{1,0:T(8,128)(2,1)S(1)}, u32[]{:S(2)}, u32[]{:S(2)}) %collective-permute-start.4) | collective-permute-done | bytes 524320 | tf_op jit(solution)/shard_map/ppermute | solution.py:193
  69.6 1.4 %collective-permute-done.5.refs_3_ = bf16[256,1024]{1,0:T(8,128)(2,1)S(1)} collective-permute-done((bf16[256,1024]{1,0:T(8,128)(2,1)S(1)}, bf16[256,1024]{1,0:T(8,128)(2,1)S(1)}, u32[]{:S(2)}, u32[]{:S(2)}) %collective-permute-start.5) | collective-permute-done | bytes 524320 | tf_op jit(solution)/shard_map/ppermute | solution.py:193
  71.0 2.6 %gradient.2 = bf16[8,256,128]{2,1,0:T(8,128)(2,1)} custom-call(s32[3]{0:T(128)S(1)} %pad_add_fusion.info_ref, bf16[4,256,256]{2,1,0:T(8,128)(2,1)} %bitcast.4.ctx_ref, bf16[256,1024]{1,0:T(8,128)(2,1)S(1)} %get-tuple-element.9.refs_0_, bf16[256,1024]{1,0:T(8,128)(2,1)S(1)} %collective-permute-done.3.refs_1_, ...), custom_call_target="tpu_custom_call" | custom-call | flops 536870912 | bytes 3145728 | tf_op jit(solution)/shard_map/gradient/pallas_call | solution.py:177
  73.6 5.9 %all-to-all-start.1 = ((bf16[8,256,128]{2,1,0:T(8,128)(2,1)}), bf16[8,256,128]{2,1,0:T(8,128)(2,1)S(1)}, u32[]{:S(2)}, u32[]{:S(2)}) async-start(bf16[8,256,128]{2,1,0:T(8,128)(2,1)} %gradient.2), calls=%async_computation.1 | async-start | bytes 1048576 | tf_op jit(solution)/shard_map/all_to_all | solution.py:233
  79.5 3.9 %collective-permute-done.7.refs_2_ = bf16[256,1024]{1,0:T(8,128)(2,1)S(1)} collective-permute-done((bf16[256,1024]{1,0:T(8,128)(2,1)S(1)}, bf16[256,1024]{1,0:T(8,128)(2,1)S(1)}, u32[]{:S(2)}, u32[]{:S(2)}) %collective-permute-start.7) | collective-permute-done | bytes 524320 | tf_op jit(solution)/shard_map/ppermute | solution.py:193
  83.4 1.9 %collective-permute-done.8.refs_3_ = bf16[256,1024]{1,0:T(8,128)(2,1)S(1)} collective-permute-done((bf16[256,1024]{1,0:T(8,128)(2,1)S(1)}, bf16[256,1024]{1,0:T(8,128)(2,1)S(1)}, u32[]{:S(2)}, u32[]{:S(2)}) %collective-permute-start.8) | collective-permute-done | bytes 524320 | tf_op jit(solution)/shard_map/ppermute | solution.py:193
  85.4 2.6 %gradient.3 = bf16[8,256,128]{2,1,0:T(8,128)(2,1)} custom-call(s32[3]{0:T(128)S(1)} %pad_add_fusion.info_ref, bf16[4,256,256]{2,1,0:T(8,128)(2,1)} %bitcast.4.ctx_ref, bf16[256,1024]{1,0:T(8,128)(2,1)S(1)} %get-tuple-element.10.refs_0_, bf16[256,1024]{1,0:T(8,128)(2,1)S(1)} %collective-permute-done.6.refs_1_, ...), custom_call_target="tpu_custom_call" | custom-call | flops 536870912 | bytes 3145728 | tf_op jit(solution)/shard_map/gradient/pallas_call | solution.py:177
  88.0 6.3 %all-to-all-done.1 = bf16[8,256,128]{2,1,0:T(8,128)(2,1)S(1)} async-done(((bf16[8,256,128]{2,1,0:T(8,128)(2,1)}), bf16[8,256,128]{2,1,0:T(8,128)(2,1)S(1)}, u32[]{:S(2)}, u32[]{:S(2)}) %all-to-all-start.1) | async-done | bytes 524320 | tf_op jit(solution)/shard_map/all_to_all | solution.py:233
  94.3 3.6 %all-to-all-start.2 = ((bf16[8,256,128]{2,1,0:T(8,128)(2,1)}), bf16[8,256,128]{2,1,0:T(8,128)(2,1)S(1)}, u32[]{:S(2)}, u32[]{:S(2)}) async-start(bf16[8,256,128]{2,1,0:T(8,128)(2,1)} %gradient.3), calls=%async_computation.2 | async-start | bytes 1048576 | tf_op jit(solution)/shard_map/all_to_all | solution.py:233
  99.8 3.0 %collective-permute-done.10 = f32[1,2176]{1,0:T(1,128)S(1)} collective-permute-done((f32[1,2176]{1,0:T(1,128)S(1)}, f32[1,2176]{1,0:T(1,128)S(1)}, u32[]{:S(2)}, u32[]{:S(2)}) %collective-permute-start.10) | collective-permute-done | bytes 8736 | tf_op jit(solution)/shard_map/ppermute | solution.py:193
  102.8 2.1 %collective-permute-start.11 = (f32[1,2176]{1,0:T(1,128)S(1)}, f32[1,2176]{1,0:T(1,128)S(1)}, u32[]{:S(2)}, u32[]{:S(2)}) collective-permute-start(f32[1,2176]{1,0:T(1,128)S(1)} %add.16), channel_id=1, source_target_pairs={{0,4},{4,0},{8,12},{12,8},{16,20},{20,16},{24,28},{28,24},{1,5},{5... | collective-permute-start | bytes 26120 | tf_op jit(solution)/shard_map/ppermute | solution.py:193
  104.9 1.7 %collective-permute-done.11 = f32[1,2176]{1,0:T(1,128)S(1)} collective-permute-done((f32[1,2176]{1,0:T(1,128)S(1)}, f32[1,2176]{1,0:T(1,128)S(1)}, u32[]{:S(2)}, u32[]{:S(2)}) %collective-permute-start.11) | collective-permute-done | bytes 8736 | tf_op jit(solution)/shard_map/ppermute | solution.py:193
  106.7 2.0 %collective-permute-start.12 = (f32[1,2176]{1,0:T(1,128)S(1)}, f32[1,2176]{1,0:T(1,128)S(1)}, u32[]{:S(2)}, u32[]{:S(2)}) collective-permute-start(f32[1,2176]{1,0:T(1,128)S(1)} %add.17), channel_id=1, source_target_pairs={{0,8},{4,12},{8,0},{12,4},{16,24},{20,28},{24,16},{28,20},{1,9},{5... | collective-permute-start | bytes 26120 | tf_op jit(solution)/shard_map/ppermute | solution.py:193
  108.7 1.7 %collective-permute-done.12 = f32[1,2176]{1,0:T(1,128)S(1)} collective-permute-done((f32[1,2176]{1,0:T(1,128)S(1)}, f32[1,2176]{1,0:T(1,128)S(1)}, u32[]{:S(2)}, u32[]{:S(2)}) %collective-permute-start.12) | collective-permute-done | bytes 8736 | tf_op jit(solution)/shard_map/ppermute | solution.py:193
  110.4 3.0 %collective-permute-start.13 = (f32[1,2176]{1,0:T(1,128)S(1)}, f32[1,2176]{1,0:T(1,128)S(1)}, u32[]{:S(2)}, u32[]{:S(2)}) collective-permute-start(f32[1,2176]{1,0:T(1,128)S(1)} %add.18), channel_id=1, source_target_pairs={{0,16},{4,20},{8,24},{12,28},{16,0},{20,4},{24,8},{28,12},{1,17},{... | collective-permute-start | bytes 26120 | tf_op jit(solution)/shard_map/ppermute | solution.py:193
  113.4 1.7 %collective-permute-done.13 = f32[1,2176]{1,0:T(1,128)S(1)} collective-permute-done((f32[1,2176]{1,0:T(1,128)S(1)}, f32[1,2176]{1,0:T(1,128)S(1)}, u32[]{:S(2)}, u32[]{:S(2)}) %collective-permute-start.13) | collective-permute-done | bytes 8736 | tf_op jit(solution)/shard_map/ppermute | solution.py:193
  117.1 1.3 %slice_divide_fusion = f32[1,2048]{1,0:T(1,128)} fusion(f32[1,2176]{1,0:T(1,128)S(1)} %add.19, f32[]{:T(128)} %bitcast.9), kind=kLoop, calls=%fused_computation.4 | loop fusion | flops 2048 | bytes 16388 | tf_op jit(solution)/shard_map/div | solution.py:243
  118.5 1.3 %fusion = bf16[1,256,256]{2,1,0:T(8,128)(2,1)} fusion(f32[1,256,128]{2,1,0:T(8,128)S(1)} %bitcast.20, f32[1,256,128]{2,1,0:T(8,128)S(1)} %bitcast.19, f32[]{:T(128)} %bitcast.9), kind=kLoop, calls=%fused_computation.3 | loop fusion | flops 196608 | bytes 393220 | tf_op jit(solution)/shard_map/convert_element_type | solution.py:242
  (37 shorter events, 6.7 us)
Async XLA Ops:
  0.6 26.5 %collective-permute-start.1 = (bf16[256,2048]{1,0:T(8,128)(2,1)}, bf16[256,2048]{1,0:T(8,128)(2,1)}, u32[]{:S(2)}, u32[]{:S(2)}) collective-permute-start(bf16[256,2048]{1,0:T(8,128)(2,1)} %bitcast.12), channel_id=1, source_target_pairs={{0,2},{1,3},{2,0},{3,1},{4,6},{5,7},{6,4},{7,5},{8,10},{9,11},{10,... | collective-permute-start | bytes 3145736 | tf_op jit(solution)/shard_map/ppermute | solution.py:193
  3.7 44.2 %collective-permute-start = (bf16[256,2048]{1,0:T(8,128)(2,1)}, bf16[256,2048]{1,0:T(8,128)(2,1)}, u32[]{:S(2)}, u32[]{:S(2)}) collective-permute-start(bf16[256,2048]{1,0:T(8,128)(2,1)} %bitcast.13), channel_id=1, source_target_pairs={{0,1},{1,0},{2,3},{3,2},{4,5},{5,4},{6,7},{7,6},{8,9},{9,8},{10,11... | collective-permute-start | bytes 3145736 | tf_op jit(solution)/shard_map/ppermute | solution.py:193
  27.1 20.7 %collective-permute-start.2 = (bf16[256,2048]{1,0:T(8,128)(2,1)}, bf16[256,2048]{1,0:T(8,128)(2,1)}, u32[]{:S(2)}, u32[]{:S(2)}) collective-permute-start(bf16[256,2048]{1,0:T(8,128)(2,1)} %collective-permute-done.1.refs_2_), channel_id=1, source_target_pairs={{0,1},{1,0},{2,3},{3,2},{4,5},{5,4},{6,7},{7,6},{8,9},{9,8},{10,11... | collective-permute-start | bytes 3145736 | tf_op jit(solution)/shard_map/ppermute | solution.py:193
  27.8 1.0 copy-start.3
  28.8 1.0 copy-start.4
  29.9 1.0 copy-start.5
  30.9 16.9 %copy-start.1 = (bf16[1,256,2048]{2,1,0:T(8,128)(2,1)S(1)}, bf16[1,256,2048]{2,1,0:T(8,128)(2,1)}, u32[]{:S(2)}) copy-start(bf16[1,256,2048]{2,1,0:T(8,128)(2,1)} %param.11) | copy-start | bytes 3145732
  35.3 12.5 %copy-start = (bf16[256,2048]{1,0:T(8,128)(2,1)S(1)}, bf16[256,2048]{1,0:T(8,128)(2,1)}, u32[]{:S(2)}) copy-start(bf16[256,2048]{1,0:T(8,128)(2,1)} %next_ref.1) | copy-start | bytes 3145732
  35.3 12.5 %all-to-all-start = ((bf16[4,256,256]{2,1,0:T(8,128)(2,1)}), bf16[4,256,256]{2,1,0:T(8,128)(2,1)S(1)}, u32[]{:S(2)}, u32[]{:S(2)}) async-start(bf16[4,256,256]{2,1,0:T(8,128)(2,1)} %bitcast.4.ctx_ref), calls=%async_computation | async-start | bytes 1048576 | tf_op jit(solution)/shard_map/all_to_all | solution.py:227
  39.0 8.9 %copy-start.2 = (f32[2048]{0:T(1024)S(1)}, f32[2048]{0:T(1024)}, u32[]{:S(2)}) copy-start(f32[2048]{0:T(1024)} %param.12) | copy-start | bytes 24580
  55.5 13.6 %collective-permute-start.4 = (bf16[256,1024]{1,0:T(8,128)(2,1)S(1)}, bf16[256,1024]{1,0:T(8,128)(2,1)S(1)}, u32[]{:S(2)}, u32[]{:S(2)}) collective-permute-start(bf16[256,1024]{1,0:T(8,128)(2,1)S(1)} %get-tuple-element.9.refs_0_), channel_id=1, source_target_pairs={{0,2},{1,3},{2,0},{3,1},{4,6},{5,7},{6,4},{7,5},{8,10},{9,11},{10,... | collective-permute-start | bytes 1572872 | tf_op jit(solution)/shard_map/ppermute | solution.py:193
  55.8 13.7 %collective-permute-start.3 = (bf16[256,1024]{1,0:T(8,128)(2,1)S(1)}, bf16[256,1024]{1,0:T(8,128)(2,1)S(1)}, u32[]{:S(2)}, u32[]{:S(2)}) collective-permute-start(bf16[256,1024]{1,0:T(8,128)(2,1)S(1)} %get-tuple-element.9.refs_0_), channel_id=1, source_target_pairs={{0,1},{1,0},{2,3},{3,2},{4,5},{5,4},{6,7},{7,6},{8,9},{9,8},{10,11... | collective-permute-start | bytes 1572872 | tf_op jit(solution)/shard_map/ppermute | solution.py:193
  69.1 1.9 %collective-permute-start.5 = (bf16[256,1024]{1,0:T(8,128)(2,1)S(1)}, bf16[256,1024]{1,0:T(8,128)(2,1)S(1)}, u32[]{:S(2)}, u32[]{:S(2)}) collective-permute-start(bf16[256,1024]{1,0:T(8,128)(2,1)S(1)} %collective-permute-done.4.refs_2_), channel_id=1, source_target_pairs={{0,1},{1,0},{2,3},{3,2},{4,5},{5,4},{6,7},{7,6},{8,9},{9,8},{10,11... | collective-permute-start | bytes 1572872 | tf_op jit(solution)/shard_map/ppermute | solution.py:193
  69.1 14.3 %collective-permute-start.7 = (bf16[256,1024]{1,0:T(8,128)(2,1)S(1)}, bf16[256,1024]{1,0:T(8,128)(2,1)S(1)}, u32[]{:S(2)}, u32[]{:S(2)}) collective-permute-start(bf16[256,1024]{1,0:T(8,128)(2,1)S(1)} %get-tuple-element.10.refs_0_), channel_id=1, source_target_pairs={{0,2},{1,3},{2,0},{3,1},{4,6},{5,7},{6,4},{7,5},{8,10},{9,11},{10,... | collective-permute-start | bytes 1572872 | tf_op jit(solution)/shard_map/ppermute | solution.py:193
  73.6 20.7 %all-to-all-start.1 = ((bf16[8,256,128]{2,1,0:T(8,128)(2,1)}), bf16[8,256,128]{2,1,0:T(8,128)(2,1)S(1)}, u32[]{:S(2)}, u32[]{:S(2)}) async-start(bf16[8,256,128]{2,1,0:T(8,128)(2,1)} %gradient.2), calls=%async_computation.1 | async-start | bytes 1048576 | tf_op jit(solution)/shard_map/all_to_all | solution.py:233
  79.5 3.9 %collective-permute-start.6 = (bf16[256,1024]{1,0:T(8,128)(2,1)S(1)}, bf16[256,1024]{1,0:T(8,128)(2,1)S(1)}, u32[]{:S(2)}, u32[]{:S(2)}) collective-permute-start(bf16[256,1024]{1,0:T(8,128)(2,1)S(1)} %get-tuple-element.10.refs_0_), channel_id=1, source_target_pairs={{0,1},{1,0},{2,3},{3,2},{4,5},{5,4},{6,7},{7,6},{8,9},{9,8},{10,11... | collective-permute-start | bytes 1572872 | tf_op jit(solution)/shard_map/ppermute | solution.py:193
  83.4 1.9 %collective-permute-start.8 = (bf16[256,1024]{1,0:T(8,128)(2,1)S(1)}, bf16[256,1024]{1,0:T(8,128)(2,1)S(1)}, u32[]{:S(2)}, u32[]{:S(2)}) collective-permute-start(bf16[256,1024]{1,0:T(8,128)(2,1)S(1)} %collective-permute-done.7.refs_2_), channel_id=1, source_target_pairs={{0,1},{1,0},{2,3},{3,2},{4,5},{5,4},{6,7},{7,6},{8,9},{9,8},{10,11... | collective-permute-start | bytes 1572872 | tf_op jit(solution)/shard_map/ppermute | solution.py:193
  94.3 24.1 %all-to-all-start.2 = ((bf16[8,256,128]{2,1,0:T(8,128)(2,1)}), bf16[8,256,128]{2,1,0:T(8,128)(2,1)S(1)}, u32[]{:S(2)}, u32[]{:S(2)}) async-start(bf16[8,256,128]{2,1,0:T(8,128)(2,1)} %gradient.3), calls=%async_computation.2 | async-start | bytes 1048576 | tf_op jit(solution)/shard_map/all_to_all | solution.py:233
  97.9 1.2 collective-permute-start.9
  99.1 3.7 %collective-permute-start.10 = (f32[1,2176]{1,0:T(1,128)S(1)}, f32[1,2176]{1,0:T(1,128)S(1)}, u32[]{:S(2)}, u32[]{:S(2)}) collective-permute-start(f32[1,2176]{1,0:T(1,128)S(1)} %add.15), channel_id=1, source_target_pairs={{0,2},{1,3},{2,0},{3,1},{4,6},{5,7},{6,4},{7,5},{8,10},{9,11},{10,... | collective-permute-start | bytes 26120 | tf_op jit(solution)/shard_map/ppermute | solution.py:193
  102.8 3.8 %collective-permute-start.11 = (f32[1,2176]{1,0:T(1,128)S(1)}, f32[1,2176]{1,0:T(1,128)S(1)}, u32[]{:S(2)}, u32[]{:S(2)}) collective-permute-start(f32[1,2176]{1,0:T(1,128)S(1)} %add.16), channel_id=1, source_target_pairs={{0,4},{4,0},{8,12},{12,8},{16,20},{20,16},{24,28},{28,24},{1,5},{5... | collective-permute-start | bytes 26120 | tf_op jit(solution)/shard_map/ppermute | solution.py:193
  106.7 3.7 %collective-permute-start.12 = (f32[1,2176]{1,0:T(1,128)S(1)}, f32[1,2176]{1,0:T(1,128)S(1)}, u32[]{:S(2)}, u32[]{:S(2)}) collective-permute-start(f32[1,2176]{1,0:T(1,128)S(1)} %add.17), channel_id=1, source_target_pairs={{0,8},{4,12},{8,0},{12,4},{16,24},{20,28},{24,16},{28,20},{1,9},{5... | collective-permute-start | bytes 26120 | tf_op jit(solution)/shard_map/ppermute | solution.py:193
  110.4 4.6 %collective-permute-start.13 = (f32[1,2176]{1,0:T(1,128)S(1)}, f32[1,2176]{1,0:T(1,128)S(1)}, u32[]{:S(2)}, u32[]{:S(2)}) collective-permute-start(f32[1,2176]{1,0:T(1,128)S(1)} %add.18), channel_id=1, source_target_pairs={{0,16},{4,20},{8,24},{12,28},{16,0},{20,4},{24,8},{28,12},{1,17},{... | collective-permute-start | bytes 26120 | tf_op jit(solution)/shard_map/ppermute | solution.py:193

commit v2 on v1

--- a/solution.py
+++ b/solution.py
@@ -193,9 +193,8 @@
     return lax.ppermute(x, axis, [(i, i ^ mask) for i in range(n)])
 
 
-def gather_xor(x, axis, n):
-    held = {0: x}
-    bit = n // 2
+def gather_xor(held, axis, n, bit):
+    held = dict(held)
     while bit:
         held.update({m | bit: swap(p, axis, n, bit) for m, p in list(held.items())})
         bit //= 2
@@ -221,21 +220,28 @@
     chunks = 2 if dout // n_dp >= 256 else 1
     me = lax.axis_index("tensor").astype(jnp.int32)
     info = jnp.stack([me, lengths[0], vote_counts[0]])
-    weights = gather_xor(joining_weight[0], "tensor", n_tensor)
+    held = {0: joining_weight[0]}
+    held[n_tensor // 2] = swap(held[0], "tensor", n_tensor, n_tensor // 2)
     context = attention(query_states[0], key_states[0], value_states[0], lengths)
     context = context.reshape(n_tensor, rows, width)
     ctx = lax.all_to_all(context, "tensor", 0, 0, tiled=True)
+    held[n_tensor // 2], ctx = lax.optimization_barrier((held[n_tensor // 2], ctx))
+    weights = gather_xor(held, "tensor", n_tensor, n_tensor // 4)
     hidden, grads, stats = join(info, ctx, norm_gain[None, :], next_hidden, weights, n_dp, chunks, seq)
+    half = n_tensor // 2
+    far = [swap(g, "tensor", n_tensor, half) for g in grads]
+    steps = [("dp", n_dp, 1 << i) for i in reversed(range(n_dp.bit_length() - 1))]
+    steps += [("tensor", n_tensor, 1 << i) for i in range(n_tensor.bit_length() - 1)]
     parts = []
     for j in range(chunks):
-        every = gather_xor(grads[j], "tensor", n_tensor)
+        take = 3 if j + 1 < chunks else len(steps)
+        for axis, n, bit in steps[:take]:
+            stats = stats + swap(stats, axis, n, bit)
+        steps = steps[take:]
+        far[j], stats = lax.optimization_barrier((far[j], stats))
+        every = gather_xor({0: grads[j], half: far[j]}, "tensor", n_tensor, half // 2)
         slabs = gradient(info, context, every, n_dp)
         parts.append(lax.all_to_all(slabs, "dp", 0, 0, tiled=True))
-    for axis, n in (("tensor", n_tensor), ("dp", n_dp)):
-        bit = 1
-        while bit < n:
-            stats = stats + swap(stats, axis, n, bit)
-            bit *= 2
     stats = stats[0]
     weight_total = stats[dout + 1]
     cols = [jnp.sum(p.astype(jnp.float32), axis=0) for p in parts]

time: 122 us -> 104 us (0.85)
  waiting for transfers between devices: 67.8 us -> 47.3 us
  starting transfers between devices: 24.7 us -> 27.7 us
    ppermute x14, waiting for transfers between devices: 53.3 us -> 14 us  [swap(): return lax.ppermute(x, axis, [(i, i ^ mask) for i in range(n)])]
    all_to_all x2, waiting for transfers between devices: 6.31 us -> 16.6 us  [on_device(): parts.append(lax.all_to_all(slabs, 'dp', 0, 0, tiled=True))]
    all_to_all x1, waiting for transfers between devices: 8.14 us -> 16.7 us  [on_device(): ctx = lax.all_to_all(context, 'tensor', 0, 0, tiled=True)]
    ppermute x14, starting transfers between devices: 11.6 us -> 14.4 us  [swap(): return lax.ppermute(x, axis, [(i, i ^ mask) for i in range(n)])]
  transfers between devices with their start and end apart: 17 -> 17, of which waited for: 12 -> 12; matrix products, arithmetic and copies ran while one was open for 2% -> 2% of each run, Pallas kernels for 8% -> 9%
where the time goes in v2:
time: 104 us
  waiting for transfers between devices  47.3 us (45%)
  starting transfers between devices  27.7 us (27%)
  Pallas kernels  17.3 us (17%)
  between operations  4.54 us (4%)
  local copies, waits for them, and re-layouts  3.78 us (4%)
  other arithmetic  2.9 us (3%)
    all_to_all x1, waiting for transfers between devices, on_device(): ctx = lax.all_to_all(context, 'tensor', 0, 0, tiled=True)  16.7 us
    all_to_all x2, waiting for transfers between devices, on_device(): parts.append(lax.all_to_all(slabs, 'dp', 0, 0, tiled=True))  16.6 us
    ppermute x14, starting transfers between devices, swap(): return lax.ppermute(x, axis, [(i, i ^ mask) for i in range(n)])  14.4 us
    ppermute x14, waiting for transfers between devices, swap(): return lax.ppermute(x, axis, [(i, i ^ mask) for i in range(n)])  14 us
    all_to_all x2, starting transfers between devices, on_device(): parts.append(lax.all_to_all(slabs, 'dp', 0, 0, tiled=True))  9.66 us
    pallas_call x1, Pallas kernels, join(): pl.pallas_call(functools.partial(join_body, n_tensor, n_dp, chunks, seq),...  7.67 us
    pallas_call x2, Pallas kernels, gradient(): pl.pallas_call(functools.partial(grad_body, n_tensor), in_specs=[pl.Block...  5.25 us
    pallas_call x1, Pallas kernels, attention(): pl.pallas_call(attend, grid=(heads,), in_specs=[pl.BlockSpec(memory_space...  4.42 us
  transfers between devices with their start and end apart: 17, of which 12 were waited for; matrix products, arithmetic and copies ran while one was open for 2% of the time, Pallas kernels for 9%

profile of v2, /device:TPU:0, one launch (start us, length us, event | category | flops | bytes accessed | tf_op | source)
XLA Modules:
  0.0 103.5 jit_solution(4920567133242940167)
XLA Ops:
  0.6 3.0 %collective-permute-start = (bf16[256,2048]{1,0:T(8,128)(2,1)}, bf16[256,2048]{1,0:T(8,128)(2,1)}, u32[]{:S(2)}, u32[]{:S(2)}) collective-permute-start(bf16[256,2048]{1,0:T(8,128)(2,1)} %bitcast.12), channel_id=1, source_target_pairs={{0,2},{1,3},{2,0},{3,1},{4,6},{5,7},{6,4},{7,5},{8,10},{9,11},{10,... | collective-permute-start | bytes 3145736 | tf_op jit(solution)/shard_map/ppermute | solution.py:193
  7.4 4.4 %attend.1 = bf16[1024,256]{1,0:T(8,128)(2,1)} custom-call(s32[1]{0:T(128)S(6)} %copy.12.len_ref, bf16[1024,256]{1,0:T(8,128)(2,1)S(1)} %bitcast.16, bf16[1024,256]{1,0:T(8,128)(2,1)S(1)} %bitcast.17, bf16[1024,256]{1,0:T(8,128)(2,1)S(1)} %bitcast.18), custom_call_target="tpu_custom_call" | custom-call | flops 1073741824 | bytes 2097152 | tf_op jit(solution)/shard_map/attend/pallas_call | solution.py:50
  11.9 3.6 %all-to-all-start = ((bf16[4,256,256]{2,1,0:T(8,128)(2,1)}), bf16[4,256,256]{2,1,0:T(8,128)(2,1)S(1)}, u32[]{:S(2)}, u32[]{:S(2)}) async-start(bf16[4,256,256]{2,1,0:T(8,128)(2,1)} %bitcast.5.ctx_ref), calls=%async_computation | async-start | bytes 1048576 | tf_op jit(solution)/shard_map/all_to_all | solution.py:227
  15.9 16.7 %all-to-all-done.ctx_ref = bf16[4,256,256]{2,1,0:T(8,128)(2,1)S(1)} async-done(((bf16[4,256,256]{2,1,0:T(8,128)(2,1)}), bf16[4,256,256]{2,1,0:T(8,128)(2,1)S(1)}, u32[]{:S(2)}, u32[]{:S(2)}) %all-to-all-start) | async-done | bytes 524320 | tf_op jit(solution)/shard_map/all_to_all | solution.py:227
  33.4 2.3 %collective-permute-done.2.refs_3_ = bf16[256,2048]{1,0:T(8,128)(2,1)} collective-permute-done((bf16[256,2048]{1,0:T(8,128)(2,1)}, bf16[256,2048]{1,0:T(8,128)(2,1)}, u32[]{:S(2)}, u32[]{:S(2)}) %collective-permute-start.2) | collective-permute-done | bytes 1048608 | tf_op jit(solution)/shard_map/ppermute | solution.py:193
  35.7 7.7 %join.1 = (bf16[256,2048]{1,0:T(8,128)(2,1)}, bf16[256,1024]{1,0:T(8,128)(2,1)S(1)}, bf16[256,1024]{1,0:T(8,128)(2,1)S(1)}, f32[1,2176]{1,0:T(1,128)S(1)}) custom-call(s32[3]{0:T(128)S(1)} %pad_add_fusion.info_ref, bf16[4,256,256]{2,1,0:T(8,128)(2,1)S(1)} %all-to-all-done.ctx_ref, f32[1,2048]{1,0:T(1,128)S(1)} %bitcast.15, bf16[256,2048]{1,0:T(8,128)(2,1)S(1)} %copy-done, ...), custom_call_target="tpu_custom_call" | custom-call | flops 1073741824 | bytes 7340032 | tf_op jit(solution)/shard_map/join/pallas_call | solution.py:135
  43.3 1.7 %collective-permute-start.4 = (bf16[256,1024]{1,0:T(8,128)(2,1)S(1)}, bf16[256,1024]{1,0:T(8,128)(2,1)S(1)}, u32[]{:S(2)}, u32[]{:S(2)}) collective-permute-start(bf16[256,1024]{1,0:T(8,128)(2,1)S(1)} %get-tuple-element.17.refs_0_), channel_id=1, source_target_pairs={{0,2},{1,3},{2,0},{3,1},{4,6},{5,7},{6,4},{7,5},{8,10},{9,11},{10,... | collective-permute-start | bytes 1572872 | tf_op jit(solution)/shard_map/ppermute | solution.py:193
  45.1 2.6 %collective-permute-start.5 = (f32[1,2176]{1,0:T(1,128)S(1)}, f32[1,2176]{1,0:T(1,128)S(1)}, u32[]{:S(2)}, u32[]{:S(2)}) collective-permute-start(f32[1,2176]{1,0:T(1,128)S(1)} %get-tuple-element.18), channel_id=1, source_target_pairs={{0,16},{4,20},{8,24},{12,28},{16,0},{20,4},{24,8},{28,12},{1,17},{... | collective-permute-start | bytes 26120 | tf_op jit(solution)/shard_map/ppermute | solution.py:193
  47.7 2.0 %collective-permute-done.5 = f32[1,2176]{1,0:T(1,128)S(1)} collective-permute-done((f32[1,2176]{1,0:T(1,128)S(1)}, f32[1,2176]{1,0:T(1,128)S(1)}, u32[]{:S(2)}, u32[]{:S(2)}) %collective-permute-start.5) | collective-permute-done | bytes 8736 | tf_op jit(solution)/shard_map/ppermute | solution.py:193
  49.6 1.6 %collective-permute-start.6 = (f32[1,2176]{1,0:T(1,128)S(1)}, f32[1,2176]{1,0:T(1,128)S(1)}, u32[]{:S(2)}, u32[]{:S(2)}) collective-permute-start(f32[1,2176]{1,0:T(1,128)S(1)} %add.15), channel_id=1, source_target_pairs={{0,8},{4,12},{8,0},{12,4},{16,24},{20,28},{24,16},{28,20},{1,9},{5... | collective-permute-start | bytes 26120 | tf_op jit(solution)/shard_map/ppermute | solution.py:193
  51.3 2.1 %collective-permute-done.6 = f32[1,2176]{1,0:T(1,128)S(1)} collective-permute-done((f32[1,2176]{1,0:T(1,128)S(1)}, f32[1,2176]{1,0:T(1,128)S(1)}, u32[]{:S(2)}, u32[]{:S(2)}) %collective-permute-start.6) | collective-permute-done | bytes 8736 | tf_op jit(solution)/shard_map/ppermute | solution.py:193
  53.4 1.6 %collective-permute-start.7 = (f32[1,2176]{1,0:T(1,128)S(1)}, f32[1,2176]{1,0:T(1,128)S(1)}, u32[]{:S(2)}, u32[]{:S(2)}) collective-permute-start(f32[1,2176]{1,0:T(1,128)S(1)} %add.16), channel_id=1, source_target_pairs={{0,4},{4,0},{8,12},{12,8},{16,20},{20,16},{24,28},{28,24},{1,5},{5... | collective-permute-start | bytes 26120 | tf_op jit(solution)/shard_map/ppermute | solution.py:193
  54.9 2.2 %collective-permute-done.7 = f32[1,2176]{1,0:T(1,128)S(1)} collective-permute-done((f32[1,2176]{1,0:T(1,128)S(1)}, f32[1,2176]{1,0:T(1,128)S(1)}, u32[]{:S(2)}, u32[]{:S(2)}) %collective-permute-start.7) | collective-permute-done | bytes 8736 | tf_op jit(solution)/shard_map/ppermute | solution.py:193
  57.3 1.7 %collective-permute-start.10 = (bf16[256,1024]{1,0:T(8,128)(2,1)S(1)}, bf16[256,1024]{1,0:T(8,128)(2,1)S(1)}, u32[]{:S(2)}, u32[]{:S(2)}) collective-permute-start(bf16[256,1024]{1,0:T(8,128)(2,1)S(1)} %get-tuple-element.20.refs_0_), channel_id=1, source_target_pairs={{0,2},{1,3},{2,0},{3,1},{4,6},{5,7},{6,4},{7,5},{8,10},{9,11},{10,... | collective-permute-start | bytes 1572872 | tf_op jit(solution)/shard_map/ppermute | solution.py:193
  59.2 2.6 %gradient.2 = bf16[8,256,128]{2,1,0:T(8,128)(2,1)} custom-call(s32[3]{0:T(128)S(1)} %pad_add_fusion.info_ref, bf16[4,256,256]{2,1,0:T(8,128)(2,1)} %bitcast.5.ctx_ref, bf16[256,1024]{1,0:T(8,128)(2,1)S(1)} %get-tuple-element.17.refs_0_, bf16[256,1024]{1,0:T(8,128)(2,1)S(1)} %collective-permute-done.3.refs_1_, ...), custom_call_target="tpu_custom_call" | custom-call | flops 536870912 | bytes 3145728 | tf_op jit(solution)/shard_map/gradient/pallas_call | solution.py:177
  61.8 6.0 %all-to-all-start.1 = ((bf16[8,256,128]{2,1,0:T(8,128)(2,1)}), bf16[8,256,128]{2,1,0:T(8,128)(2,1)S(1)}, u32[]{:S(2)}, u32[]{:S(2)}) async-start(bf16[8,256,128]{2,1,0:T(8,128)(2,1)} %gradient.2), calls=%async_computation.1 | async-start | bytes 1048576 | tf_op jit(solution)/shard_map/all_to_all | solution.py:244
  69.0 1.6 %collective-permute-start.12 = (f32[1,2176]{1,0:T(1,128)S(1)}, f32[1,2176]{1,0:T(1,128)S(1)}, u32[]{:S(2)}, u32[]{:S(2)}) collective-permute-start(f32[1,2176]{1,0:T(1,128)S(1)} %add.18), channel_id=1, source_target_pairs={{0,2},{1,3},{2,0},{3,1},{4,6},{5,7},{6,4},{7,5},{8,10},{9,11},{10,... | collective-permute-start | bytes 26120 | tf_op jit(solution)/shard_map/ppermute | solution.py:193
  70.6 2.1 %collective-permute-done.12 = f32[1,2176]{1,0:T(1,128)S(1)} collective-permute-done((f32[1,2176]{1,0:T(1,128)S(1)}, f32[1,2176]{1,0:T(1,128)S(1)}, u32[]{:S(2)}, u32[]{:S(2)}) %collective-permute-start.12) | collective-permute-done | bytes 8736 | tf_op jit(solution)/shard_map/ppermute | solution.py:193
  72.9 1.9 %collective-permute-done.13.refs_3_ = bf16[256,1024]{1,0:T(8,128)(2,1)S(1)} collective-permute-done((bf16[256,1024]{1,0:T(8,128)(2,1)S(1)}, bf16[256,1024]{1,0:T(8,128)(2,1)S(1)}, u32[]{:S(2)}, u32[]{:S(2)}) %collective-permute-start.13) | collective-permute-done | bytes 524320 | tf_op jit(solution)/shard_map/ppermute | solution.py:193
  74.8 2.6 %gradient.3 = bf16[8,256,128]{2,1,0:T(8,128)(2,1)} custom-call(s32[3]{0:T(128)S(1)} %pad_add_fusion.info_ref, bf16[4,256,256]{2,1,0:T(8,128)(2,1)} %bitcast.5.ctx_ref, bf16[256,1024]{1,0:T(8,128)(2,1)S(1)} %get-tuple-element.20.refs_0_, bf16[256,1024]{1,0:T(8,128)(2,1)S(1)} %collective-permute-done.9.refs_1_, ...), custom_call_target="tpu_custom_call" | custom-call | flops 536870912 | bytes 3145728 | tf_op jit(solution)/shard_map/gradient/pallas_call | solution.py:177
  77.4 5.2 %all-to-all-done.1 = bf16[8,256,128]{2,1,0:T(8,128)(2,1)S(1)} async-done(((bf16[8,256,128]{2,1,0:T(8,128)(2,1)}), bf16[8,256,128]{2,1,0:T(8,128)(2,1)S(1)}, u32[]{:S(2)}, u32[]{:S(2)}) %all-to-all-start.1) | async-done | bytes 524320 | tf_op jit(solution)/shard_map/all_to_all | solution.py:244
  82.6 3.6 %all-to-all-start.2 = ((bf16[8,256,128]{2,1,0:T(8,128)(2,1)}), bf16[8,256,128]{2,1,0:T(8,128)(2,1)S(1)}, u32[]{:S(2)}, u32[]{:S(2)}) async-start(bf16[8,256,128]{2,1,0:T(8,128)(2,1)} %gradient.3), calls=%async_computation.2 | async-start | bytes 1048576 | tf_op jit(solution)/shard_map/all_to_all | solution.py:244
  89.6 11.3 %all-to-all-done.2 = bf16[8,256,128]{2,1,0:T(8,128)(2,1)S(1)} async-done(((bf16[8,256,128]{2,1,0:T(8,128)(2,1)}), bf16[8,256,128]{2,1,0:T(8,128)(2,1)S(1)}, u32[]{:S(2)}, u32[]{:S(2)}) %all-to-all-start.2) | async-done | bytes 524320 | tf_op jit(solution)/shard_map/all_to_all | solution.py:244
  101.0 1.3 %fusion = bf16[1,256,256]{2,1,0:T(8,128)(2,1)} fusion(f32[1,256,128]{2,1,0:T(8,128)S(1)} %bitcast.20, f32[1,256,128]{2,1,0:T(8,128)S(1)} %bitcast.19, f32[]{:T(128)} %bitcast.9), kind=kLoop, calls=%fused_computation.3 | loop fusion | flops 196608 | bytes 393220 | tf_op jit(solution)/shard_map/convert_element_type | solution.py:248
  (37 shorter events, 7.4 us)
Async XLA Ops:
  0.6 32.0 %collective-permute-start = (bf16[256,2048]{1,0:T(8,128)(2,1)}, bf16[256,2048]{1,0:T(8,128)(2,1)}, u32[]{:S(2)}, u32[]{:S(2)}) collective-permute-start(bf16[256,2048]{1,0:T(8,128)(2,1)} %bitcast.12), channel_id=1, source_target_pairs={{0,2},{1,3},{2,0},{3,1},{4,6},{5,7},{6,4},{7,5},{8,10},{9,11},{10,... | collective-permute-start | bytes 3145736 | tf_op jit(solution)/shard_map/ppermute | solution.py:193
  4.3 1.0 %copy-start.3 = (bf16[1,1024,256]{2,1,0:T(8,128)(2,1)S(1)}, bf16[1,1024,256]{2,1,0:T(8,128)(2,1)}, u32[]{:S(2)}) copy-start(bf16[1,1024,256]{2,1,0:T(8,128)(2,1)} %param.8) | copy-start | bytes 1572868
  5.4 1.0 %copy-start.4 = (bf16[1,1024,256]{2,1,0:T(8,128)(2,1)S(1)}, bf16[1,1024,256]{2,1,0:T(8,128)(2,1)}, u32[]{:S(2)}) copy-start(bf16[1,1024,256]{2,1,0:T(8,128)(2,1)} %param.9) | copy-start | bytes 1572868
  6.4 1.0 %copy-start.5 = (bf16[1,1024,256]{2,1,0:T(8,128)(2,1)S(1)}, bf16[1,1024,256]{2,1,0:T(8,128)(2,1)}, u32[]{:S(2)}) copy-start(bf16[1,1024,256]{2,1,0:T(8,128)(2,1)} %param.10) | copy-start | bytes 1572868
  7.4 8.0 %copy-start.1 = (bf16[1,256,2048]{2,1,0:T(8,128)(2,1)S(1)}, bf16[1,256,2048]{2,1,0:T(8,128)(2,1)}, u32[]{:S(2)}) copy-start(bf16[1,256,2048]{2,1,0:T(8,128)(2,1)} %param.11) | copy-start | bytes 3145732
  11.9 23.8 %copy-start = (bf16[256,2048]{1,0:T(8,128)(2,1)S(1)}, bf16[256,2048]{1,0:T(8,128)(2,1)}, u32[]{:S(2)}) copy-start(bf16[256,2048]{1,0:T(8,128)(2,1)} %next_ref.1) | copy-start | bytes 3145732
  11.9 20.8 %all-to-all-start = ((bf16[4,256,256]{2,1,0:T(8,128)(2,1)}), bf16[4,256,256]{2,1,0:T(8,128)(2,1)S(1)}, u32[]{:S(2)}, u32[]{:S(2)}) async-start(bf16[4,256,256]{2,1,0:T(8,128)(2,1)} %bitcast.5.ctx_ref), calls=%async_computation | async-start | bytes 1048576 | tf_op jit(solution)/shard_map/all_to_all | solution.py:227
  15.5 20.2 %copy-start.2 = (f32[2048]{0:T(1024)S(1)}, f32[2048]{0:T(1024)}, u32[]{:S(2)}) copy-start(f32[2048]{0:T(1024)} %param.12) | copy-start | bytes 24580
  15.5 17.9 %collective-permute-start.1 = (bf16[256,2048]{1,0:T(8,128)(2,1)S(1)}, bf16[256,2048]{1,0:T(8,128)(2,1)}, u32[]{:S(2)}, u32[]{:S(2)}) collective-permute-start(bf16[256,2048]{1,0:T(8,128)(2,1)S(1)} %bitcast.13), channel_id=1, source_target_pairs={{0,1},{1,0},{2,3},{3,2},{4,5},{5,4},{6,7},{7,6},{8,9},{9,8},{10,11... | collective-permute-start | bytes 3145736 | tf_op jit(solution)/shard_map/ppermute | solution.py:193
  32.7 3.0 %collective-permute-start.2 = (bf16[256,2048]{1,0:T(8,128)(2,1)}, bf16[256,2048]{1,0:T(8,128)(2,1)}, u32[]{:S(2)}, u32[]{:S(2)}) collective-permute-start(bf16[256,2048]{1,0:T(8,128)(2,1)} %collective-permute-done.refs_2_), channel_id=1, source_target_pairs={{0,1},{1,0},{2,3},{3,2},{4,5},{5,4},{6,7},{7,6},{8,9},{9,8},{10,11... | collective-permute-start | bytes 3145736 | tf_op jit(solution)/shard_map/ppermute | solution.py:193
  43.3 14.0 %collective-permute-start.4 = (bf16[256,1024]{1,0:T(8,128)(2,1)S(1)}, bf16[256,1024]{1,0:T(8,128)(2,1)S(1)}, u32[]{:S(2)}, u32[]{:S(2)}) collective-permute-start(bf16[256,1024]{1,0:T(8,128)(2,1)S(1)} %get-tuple-element.17.refs_0_), channel_id=1, source_target_pairs={{0,2},{1,3},{2,0},{3,1},{4,6},{5,7},{6,4},{7,5},{8,10},{9,11},{10,... | collective-permute-start | bytes 1572872 | tf_op jit(solution)/shard_map/ppermute | solution.py:193
  45.1 4.6 %collective-permute-start.5 = (f32[1,2176]{1,0:T(1,128)S(1)}, f32[1,2176]{1,0:T(1,128)S(1)}, u32[]{:S(2)}, u32[]{:S(2)}) collective-permute-start(f32[1,2176]{1,0:T(1,128)S(1)} %get-tuple-element.18), channel_id=1, source_target_pairs={{0,16},{4,20},{8,24},{12,28},{16,0},{20,4},{24,8},{28,12},{1,17},{... | collective-permute-start | bytes 26120 | tf_op jit(solution)/shard_map/ppermute | solution.py:193
  49.6 3.7 %collective-permute-start.6 = (f32[1,2176]{1,0:T(1,128)S(1)}, f32[1,2176]{1,0:T(1,128)S(1)}, u32[]{:S(2)}, u32[]{:S(2)}) collective-permute-start(f32[1,2176]{1,0:T(1,128)S(1)} %add.15), channel_id=1, source_target_pairs={{0,8},{4,12},{8,0},{12,4},{16,24},{20,28},{24,16},{28,20},{1,9},{5... | collective-permute-start | bytes 26120 | tf_op jit(solution)/shard_map/ppermute | solution.py:193
  53.4 3.7 %collective-permute-start.7 = (f32[1,2176]{1,0:T(1,128)S(1)}, f32[1,2176]{1,0:T(1,128)S(1)}, u32[]{:S(2)}, u32[]{:S(2)}) collective-permute-start(f32[1,2176]{1,0:T(1,128)S(1)} %add.16), channel_id=1, source_target_pairs={{0,4},{4,0},{8,12},{12,8},{16,20},{20,16},{24,28},{28,24},{1,5},{5... | collective-permute-start | bytes 26120 | tf_op jit(solution)/shard_map/ppermute | solution.py:193
  54.9 4.1 %collective-permute-start.3 = (bf16[256,1024]{1,0:T(8,128)(2,1)S(1)}, bf16[256,1024]{1,0:T(8,128)(2,1)S(1)}, u32[]{:S(2)}, u32[]{:S(2)}) collective-permute-start(bf16[256,1024]{1,0:T(8,128)(2,1)S(1)} %get-tuple-element.17.refs_0_), channel_id=1, source_target_pairs={{0,1},{1,0},{2,3},{3,2},{4,5},{5,4},{6,7},{7,6},{8,9},{9,8},{10,11... | collective-permute-start | bytes 1572872 | tf_op jit(solution)/shard_map/ppermute | solution.py:193
  57.3 1.9 %collective-permute-start.8 = (bf16[256,1024]{1,0:T(8,128)(2,1)S(1)}, bf16[256,1024]{1,0:T(8,128)(2,1)S(1)}, u32[]{:S(2)}, u32[]{:S(2)}) collective-permute-start(bf16[256,1024]{1,0:T(8,128)(2,1)S(1)} %collective-permute-done.4.refs_2_), channel_id=1, source_target_pairs={{0,1},{1,0},{2,3},{3,2},{4,5},{5,4},{6,7},{7,6},{8,9},{9,8},{10,11... | collective-permute-start | bytes 1572872 | tf_op jit(solution)/shard_map/ppermute | solution.py:193
  57.3 15.5 %collective-permute-start.10 = (bf16[256,1024]{1,0:T(8,128)(2,1)S(1)}, bf16[256,1024]{1,0:T(8,128)(2,1)S(1)}, u32[]{:S(2)}, u32[]{:S(2)}) collective-permute-start(bf16[256,1024]{1,0:T(8,128)(2,1)S(1)} %get-tuple-element.20.refs_0_), channel_id=1, source_target_pairs={{0,2},{1,3},{2,0},{3,1},{4,6},{5,7},{6,4},{7,5},{8,10},{9,11},{10,... | collective-permute-start | bytes 1572872 | tf_op jit(solution)/shard_map/ppermute | solution.py:193
  61.8 20.8 %all-to-all-start.1 = ((bf16[8,256,128]{2,1,0:T(8,128)(2,1)}), bf16[8,256,128]{2,1,0:T(8,128)(2,1)S(1)}, u32[]{:S(2)}, u32[]{:S(2)}) async-start(bf16[8,256,128]{2,1,0:T(8,128)(2,1)} %gradient.2), calls=%async_computation.1 | async-start | bytes 1048576 | tf_op jit(solution)/shard_map/all_to_all | solution.py:244
  67.9 1.2 %collective-permute-start.11 = (f32[1,2176]{1,0:T(1,128)S(1)}, f32[1,2176]{1,0:T(1,128)S(1)}, u32[]{:S(2)}, u32[]{:S(2)}) collective-permute-start(f32[1,2176]{1,0:T(1,128)S(1)} %add.17), channel_id=1, source_target_pairs={{0,1},{1,0},{2,3},{3,2},{4,5},{5,4},{6,7},{7,6},{8,9},{9,8},{10,11... | collective-permute-start | bytes 26120 | tf_op jit(solution)/shard_map/ppermute | solution.py:193
  69.0 3.7 %collective-permute-start.12 = (f32[1,2176]{1,0:T(1,128)S(1)}, f32[1,2176]{1,0:T(1,128)S(1)}, u32[]{:S(2)}, u32[]{:S(2)}) collective-permute-start(f32[1,2176]{1,0:T(1,128)S(1)} %add.18), channel_id=1, source_target_pairs={{0,2},{1,3},{2,0},{3,1},{4,6},{5,7},{6,4},{7,5},{8,10},{9,11},{10,... | collective-permute-start | bytes 26120 | tf_op jit(solution)/shard_map/ppermute | solution.py:193
  70.6 2.2 %collective-permute-start.9 = (bf16[256,1024]{1,0:T(8,128)(2,1)S(1)}, bf16[256,1024]{1,0:T(8,128)(2,1)S(1)}, u32[]{:S(2)}, u32[]{:S(2)}) collective-permute-start(bf16[256,1024]{1,0:T(8,128)(2,1)S(1)} %get-tuple-element.20.refs_0_), channel_id=1, source_target_pairs={{0,1},{1,0},{2,3},{3,2},{4,5},{5,4},{6,7},{7,6},{8,9},{9,8},{10,11... | collective-permute-start | bytes 1572872 | tf_op jit(solution)/shard_map/ppermute | solution.py:193
  72.8 2.0 %collective-permute-start.13 = (bf16[256,1024]{1,0:T(8,128)(2,1)S(1)}, bf16[256,1024]{1,0:T(8,128)(2,1)S(1)}, u32[]{:S(2)}, u32[]{:S(2)}) collective-permute-start(bf16[256,1024]{1,0:T(8,128)(2,1)S(1)} %collective-permute-done.10.refs_2_), channel_id=1, source_target_pairs={{0,1},{1,0},{2,3},{3,2},{4,5},{5,4},{6,7},{7,6},{8,9},{9,8},{10,11... | collective-permute-start | bytes 1572872 | tf_op jit(solution)/shard_map/ppermute | solution.py:193
  82.6 18.3 %all-to-all-start.2 = ((bf16[8,256,128]{2,1,0:T(8,128)(2,1)}), bf16[8,256,128]{2,1,0:T(8,128)(2,1)S(1)}, u32[]{:S(2)}, u32[]{:S(2)}) async-start(bf16[8,256,128]{2,1,0:T(8,128)(2,1)} %gradient.3), calls=%async_computation.2 | async-start | bytes 1048576 | tf_op jit(solution)/shard_map/all_to_all | solution.py:244

commit v3 on v1

v3 whole, which is shorter than its diff:
```python
import functools
import math

import jax
import jax.numpy as jnp
from jax import lax
from jax.experimental import pallas as pl
from jax.experimental.pallas import tpu as pltpu
from jax.sharding import PartitionSpec as P

HD = 128
QB = 256
ROWS = 16
COLS = 256
NEAR = 4
STAT_ROWS = 32

loss_scale = 65536.0
neg_large = -1e30
MIB = 1 << 20
BF = jnp.bfloat16
F32 = jnp.float32


def dot(a, b, dims):
    return lax.dot_general(a, b, (dims, ((), ())), preferred_element_type=F32)


def split_words(x):
    high = x.astype(BF).astype(F32)
    return high, (x - high).astype(BF).astype(F32)


def shape(dims, dtype=BF):
    return jax.ShapeDtypeStruct(dims, dtype)


def params():
    return pltpu.CompilerParams(vmem_limit_bytes=48 * MIB)


VM = pl.BlockSpec(memory_space=pltpu.VMEM)
SM = pl.BlockSpec(memory_space=pltpu.SMEM)


def attend_body(info_ref, q_ref, k_ref, v_ref, o_ref):
    seq = q_ref.shape[0]
    rows = o_ref.shape[2]
    rate = math.log2(math.e) / math.sqrt(HD)
    length = info_ref[2]
    for i in range(seq // QB):
        keys = (i + 1) * QB
        scores = dot(q_ref[i * QB : keys, :], k_ref[:keys, :], ((1,), (1,)))
        col = lax.broadcasted_iota(jnp.int32, (1, keys), 1)
        scores = scores + jnp.where(col < length, 0.0, neg_large)
        r = lax.broadcasted_iota(jnp.int32, (QB, QB), 0)
        c = lax.broadcasted_iota(jnp.int32, (QB, QB), 1)
        last = jnp.where(c <= r, scores[:, keys - QB :], neg_large)
        scores = last if i == 0 else jnp.concatenate([scores[:, : keys - QB], last], 1)
        peak = jnp.max(scores, axis=1, keepdims=True)
        e = jnp.exp2((scores - peak) * rate)
        total = jnp.sum(e, axis=1, keepdims=True)
        out = dot(e.astype(BF), v_ref[:keys, :], ((1,), (0,))) / total
        out = out.T.astype(BF)
        for n in range(QB // rows):
            o_ref[i * (QB // rows) + n] = out[:, n * rows : (n + 1) * rows]


def attend(info, q, k, v, rows):
    seq, width = q.shape
    heads = width // HD
    block = pl.BlockSpec((seq, HD), lambda h: (0, h))
    return pl.pallas_call(
        attend_body,
        grid=(heads,),
        in_specs=[SM, block, block, block],
        out_specs=pl.BlockSpec((seq // rows, HD, rows), lambda h: (0, h, 0)),
        out_shape=shape((seq // rows, width, rows)),
        compiler_params=params(),
        cost_estimate=pl.CostEstimate(
            flops=4 * seq * seq * width, bytes_accessed=8 * seq * width, transcendentals=heads * seq * seq
        ),
        name="attend",
    )(info, q, k, v)


def join_body(plan, counts, info_ref, ctx_ref, gain_ref, next_ref, *refs):
    n_dp, n_tensor, chunks, seq, xor_far = plan
    w_refs, at = [], 0
    for n in counts:
        w_refs.append(refs[at : at + n])
        at += n
    hidden_ref, grad_refs = refs[at], refs[at + 1 : -4]
    turned_ref, joined_ref, square_ref, acc_ref = refs[-4:]
    rows, dout = joined_ref.shape
    me, group, length, votes = info_ref[0], info_ref[1], info_ref[2], info_ref[3]
    for m in range(n_tensor):
        turned_ref[m] = ctx_ref[me ^ m].T
    for c in range(0, dout, COLS):
        total = None
        for m in range(n_tensor):
            first = 0
            for ref in w_refs[m]:
                if first <= c < first + ref.shape[1]:
                    w = ref[:, c - first : c - first + COLS]
                first += ref.shape[1]
            part = dot(turned_ref[m], w, ((1,), (0,)))
            part = part.astype(BF).astype(F32)
            total = part if total is None else total + part
        joined_ref[:, c : c + COLS] = total
        sq = total * total
        lanes = sum(sq[:, i : i + 128] for i in range(0, COLS, 128))
        square_ref[...] = lanes if c == 0 else square_ref[...] + lanes
    acc_ref[...] = jnp.zeros_like(acc_ref)
    slice_w = dout // n_dp
    cw = slice_w // chunks
    near, far = group % NEAR, group // NEAR
    n_far = n_dp // NEAR

    def body(r, carry):
        loss, weights = carry
        at = pl.ds(pl.multiple_of(r * ROWS, ROWS), ROWS)
        inv = lax.rsqrt(jnp.sum(square_ref[at, :], axis=1, keepdims=True) * (1.0 / dout) + 1e-06)
        pos = (me * rows + r * ROWS) % seq + lax.broadcasted_iota(jnp.int32, (ROWS, 1), 0)
        weight = jnp.where(pos < length - 1, votes.astype(F32), 0.0)
        scaled = weight * (loss_scale * 2.0 / dout)
        miss = jnp.zeros((ROWS, 128), F32)
        lean = jnp.zeros((ROWS, 128), F32)
        for c in range(0, dout, 512):
            cs = slice(c, c + 512)
            normed = joined_ref[at, cs] * inv
            gain = gain_ref[:, cs]
            predicted = normed * gain
            hidden_ref[at, cs] = predicted.astype(BF)
            misfit = predicted - next_ref[at, cs].astype(F32)
            both = scaled * misfit * normed
            acc_ref[:, cs] += both
            sq = misfit * misfit
            ln = both * gain
            miss += sum(sq[:, i : i + 128] for i in range(0, 512, 128))
            lean += sum(ln[:, i : i + 128] for i in range(0, 512, 128))
            joined_ref[at, cs] = normed
        lean = jnp.sum(lean, axis=1, keepdims=True) * (1.0 / dout)

        def gradient_at(cs):
            normed = joined_ref[at, cs]
            gain = gain_ref[:, cs]
            misfit = normed * gain - next_ref[at, cs].astype(F32)
            return (inv * (scaled * misfit * gain - normed * lean)).astype(BF)

        for j in range(chunks):
            for q in range(NEAR):
                for b in range(n_far):
                    to = slice(b * cw, (b + 1) * cw)
                    if cw % 128 == 0:
                        other = (far ^ b if xor_far else b) * NEAR + (near ^ q)
                        start = pl.multiple_of(other * slice_w + j * cw, 128)
                        grad_refs[j * NEAR + q][at, to] = gradient_at(pl.ds(start, cw))
                    else:
                        start = (b * NEAR + q) * slice_w + j * cw
                        grad_refs[j][near ^ q, at, to] = gradient_at(slice(start, start + cw))
        loss = loss + weight * (jnp.sum(miss, axis=1, keepdims=True) * (1.0 / dout))
        return loss, weights + weight

    zero = jnp.zeros((ROWS, 1), F32)
    loss, weights = lax.fori_loop(0, rows // ROWS, body, (zero, zero))
    wide = n_far * cw
    gain_sum = jnp.sum(acc_ref[...], axis=0, keepdims=True)
    gain_sum = jnp.concatenate([gain_sum[:, i : i + wide] for i in range(0, dout, wide)], 0)
    lane = lax.broadcasted_iota(jnp.int32, (1, wide), 1)
    loss = jnp.sum(loss, axis=0, keepdims=True)
    weights = jnp.sum(weights, axis=0, keepdims=True)
    scalars = jnp.where(lane == 0, loss, jnp.where(lane == 1, weights, 0.0))
    words = [*split_words(gain_sum), *split_words(scalars)]
    left = STAT_ROWS - sum(w.shape[0] for w in words)
    words = jnp.concatenate([*words, jnp.zeros((left, wide), F32)], 0).astype(BF)
    if cw % 128 == 0:
        for q in range(NEAR):
            grad_refs[q][rows:, :] = words
    else:
        for q in range(NEAR):
            grad_refs[0][q, rows:, :] = words


def join(plan, info, ctx, gain, next_hidden, weights):
    n_dp, n_tensor, chunks, _, _ = plan
    _, width, rows = ctx.shape
    dout = gain.shape[1]
    wide = dout // NEAR // chunks
    tall = [rows + STAT_ROWS] + [rows] * (chunks - 1)
    aligned = dout // n_dp // chunks % 128 == 0
    if aligned:
        grads = [shape((n, wide)) for n in tall for _ in range(NEAR)]
    else:
        grads = [shape((NEAR, n, wide)) for n in tall]
    out = pl.pallas_call(
        functools.partial(join_body, plan, [len(w) for w in weights]),
        in_specs=[SM] + [VM] * (3 + sum(len(w) for w in weights)),
        out_specs=[VM] * (1 + len(grads)),
        out_shape=[shape((rows, dout)), *grads],
        scratch_shapes=[
            pltpu.VMEM((n_tensor, rows, width), BF),
            pltpu.VMEM((rows, dout), F32),
            pltpu.VMEM((rows, 128), F32),
            pltpu.VMEM((ROWS, dout), F32),
        ],
        compiler_params=params(),
        cost_estimate=pl.CostEstimate(
            flops=2 * rows * dout * width * n_tensor,
            bytes_accessed=2 * dout * (width * n_tensor + 3 * rows),
            transcendentals=rows,
        ),
        name="join",
    )(info, ctx, gain, next_hidden, *[w for held in weights for w in held])
    if aligned:
        return out[0], [out[1 + j * NEAR : 1 + (j + 1) * NEAR] for j in range(chunks)]
    return out[0], [[g[q] for q in range(NEAR)] for g in out[1:]]


def stat_sizes(dout, wide, cw):
    in_block = dout // cw
    return dout // wide, in_block, -(-(2 * in_block + 2) // 16) * 16


def block_words(gains, scalars, tall, cw):
    words = [*split_words(gains), *split_words(scalars)]
    left = tall - sum(w.shape[0] for w in words)
    return jnp.concatenate([*words, jnp.zeros((left, cw), F32)], 0).astype(BF)


def block_sums(words, n):
    words = words.astype(F32)
    return words[:n] + words[n : 2 * n], words[2 * n : 2 * n + 1] + words[2 * n + 1 : 2 * n + 2]


def grad_body(plan, dout, info_ref, *refs):
    n_dp, n_tensor, _, _, xor_far = plan
    ctx_refs, g_refs, (keep_ref, send_ref) = refs[:NEAR], refs[NEAR : 2 * NEAR], refs[2 * NEAR :]
    n_y, n_far, tall, cw = keep_ref.shape
    feats, rows = ctx_refs[0].shape[1:]
    wide = n_far * cw
    me = info_ref[0]
    core, y = me % 2, me // 2
    if tall > feats:
        in_piece, in_block, stat_rows = stat_sizes(dout, wide, cw)
        sums = sum(ref[rows:, :].astype(F32) for ref in g_refs)
        gains, scalars = block_sums(sums, in_piece)
        gains = jnp.concatenate([gains[:, b * cw : (b + 1) * cw] for b in range(n_far)], 0)
        words = block_words(gains, scalars[:, :cw], stat_rows, cw)
    for s, ref in ((1, send_ref), (0, keep_ref)):
        for a in range(n_y):
            m = (y ^ a if xor_far else a) * 2 + (core ^ s)
            total = sum(dot(c[m], g[:rows, :], ((1,), (0,))) for c, g in zip(ctx_refs, g_refs))
            total = total.astype(BF)
            for b in range(n_far):
                ref[a, b, :feats, :] = total[:, b * cw : (b + 1) * cw]
                if tall > feats:
                    ref[a, b, feats:, :] = words


def gradient(plan, dout, info, ctxs, grads):
    n_dp, n_tensor, chunks, _, _ = plan
    _, feats, rows = ctxs[0].shape
    wide = grads[0].shape[1]
    cw = dout // n_dp // chunks
    tall = feats
    if grads[0].shape[0] > rows:
        tall += stat_sizes(dout, wide, cw)[2]
    block = shape((n_tensor // 2, n_dp // NEAR, tall, cw))
    return pl.pallas_call(
        functools.partial(grad_body, plan, dout),
        in_specs=[SM] + [VM] * (2 * NEAR),
        out_specs=[VM, VM],
        out_shape=[block, block],
        compiler_params=params(),
        cost_estimate=pl.CostEstimate(
            flops=2 * NEAR * n_tensor * rows * feats * wide,
            bytes_accessed=2 * (NEAR * rows * (n_tensor * feats + wide) + n_tensor * feats * wide),
            transcendentals=0,
        ),
        name="gradient",
    )(info, *ctxs, *grads)


def merge_body(in_block, feats, keep_ref, got_ref, *out_refs):
    n_y, n_far, tall, cw = keep_ref.shape
    if tall > feats:
        gains, scalars = block_sums(keep_ref[0, 0, feats:, :], in_block)
        more, others = block_sums(got_ref[0, 0, feats:, :], in_block)
        words = block_words(gains + more, scalars + others, tall - feats, cw)
    for i in range(n_y * n_far):
        a, b = divmod(i, n_far)
        total = keep_ref[a, b, :feats, :].astype(F32) + got_ref[a, b, :feats, :].astype(F32)
        ref, at = (out_refs[0], (a, b)) if len(out_refs) == 1 else (out_refs[i], (0, 0))
        ref[(*at, slice(0, feats), slice(None))] = total.astype(BF)
        if tall > feats:
            ref[(*at, slice(feats, tall), slice(None))] = words


def merge(plan, dout, feats, keep, got):
    n_y, n_far, tall, cw = keep.shape
    if plan[4]:
        outs = [shape((1, 1, tall, cw))] * (n_y * n_far)
    else:
        outs = [shape(keep.shape)]
    return pl.pallas_call(
        functools.partial(merge_body, dout // cw, feats),
        in_specs=[VM, VM],
        out_specs=[VM] * len(outs),
        out_shape=outs,
        compiler_params=params(),
        cost_estimate=pl.CostEstimate(flops=keep.size, bytes_accessed=6 * keep.size, transcendentals=0),
        name="merge",
    )(keep, got)


def finish_body(counts, in_piece, n_far, *refs):
    grad_ref, gain_ref, loss_ref = refs[-3:]
    feats = grad_ref.shape[0]
    chunks, at = [], 0
    for n in counts:
        chunks.append(refs[at : at + n])
        at += n
    tall, cw = chunks[0][0].shape[2:]

    def total(blocks, rows):
        parts = [
            r[a, b, rows, :].astype(F32) for r in blocks for a in range(r.shape[0]) for b in range(r.shape[1])
        ]
        return sum(parts[1:], parts[0])

    gains, scalars = block_sums(total(chunks[0], slice(feats, tall)), in_piece * n_far)
    lane = lax.broadcasted_iota(jnp.int32, (1, cw), 1)
    weight = jnp.sum(jnp.where(lane == 1, scalars, 0.0), axis=1, keepdims=True)
    loss_ref[0, 0] = jnp.sum(jnp.where(lane == 0, scalars / weight, 0.0))
    gains = gains / weight
    for r in range(in_piece):
        for b in range(n_far):
            gain_ref[pl.ds(r * n_far + b, 1), :] = gains[b * in_piece + r : b * in_piece + r + 1, :]
    for j, blocks in enumerate(chunks):
        grad_ref[:, j * cw : (j + 1) * cw] = (total(blocks, slice(0, feats)) / weight).astype(BF)


def finish(plan, dout, feats, chunks):
    n_dp = plan[0]
    cw = chunks[0][0].shape[3]
    n_far = n_dp // NEAR
    return pl.pallas_call(
        functools.partial(finish_body, [len(c) for c in chunks], dout // (n_far * cw), n_far),
        in_specs=[VM] * sum(len(c) for c in chunks),
        out_specs=[VM, VM, SM],
        out_shape=[shape((feats, dout // n_dp)), shape((dout // cw, cw), F32), shape((1, 1), F32)],
        compiler_params=params(),
        name="finish",
    )(*[b for c in chunks for b in c])


def swap(x, axis, n, mask):
    return lax.ppermute(x, axis, [(i, i ^ mask) for i in range(n)])


def swap_far(x, n_dp, n_tensor, a, b):
    mask = b * NEAR * n_tensor + a * 2
    return lax.ppermute(x, ("dp", "tensor"), [(i, i ^ mask) for i in range(n_dp * n_tensor)])


def exchange_far(plan, blocks):
    n_dp, n_tensor, _, _, xor_far = plan
    n_far = n_dp // NEAR
    if xor_far:
        return [blocks[0]] + [
            swap_far(block, n_dp, n_tensor, *divmod(i, n_far)) for i, block in enumerate(blocks) if i
        ]
    cores = [[2 * y + c for y in range(n_tensor // 2)] for c in range(2)]
    nears = [[NEAR * f + q for f in range(n_far)] for q in range(NEAR)]
    x = lax.all_to_all(blocks[0], "tensor", 0, 0, tiled=True, axis_index_groups=cores)
    return [lax.all_to_all(x, "dp", 1, 1, tiled=True, axis_index_groups=nears)]


def on_device(
    n_dp,
    n_tensor,
    query_states,
    key_states,
    value_states,
    joining_weight,
    norm_gain,
    next_hidden,
    lengths,
    vote_counts,
):
    _, tokens, width = query_states.shape
    seq = tokens // lengths.shape[0]
    dout = norm_gain.shape[0]
    rows = next_hidden.shape[0]
    chunks = 2 if dout // n_dp >= 256 else 1
    xor_far = (n_tensor // 2) * (n_dp // NEAR) <= 4
    plan = (n_dp, n_tensor, chunks, seq, xor_far)
    me = lax.axis_index("tensor").astype(jnp.int32)
    group = lax.axis_index("dp").astype(jnp.int32)
    info = jnp.stack([me, group, lengths[0], vote_counts[0]])

    weight = joining_weight[0]
    half = n_tensor // 2
    cut = dout * 3 // 8 // COLS * COLS
    first, second = weight[:, :cut], weight[:, cut:]
    first = swap(first, "tensor", n_tensor, half)
    context = attend(info, query_states[0], key_states[0], value_states[0], rows)
    second, context = lax.optimization_barrier((second, context))
    ctx = lax.all_to_all(context, "tensor", 0, 0, tiled=True)
    second = swap(second, "tensor", n_tensor, half)
    first, ctx = lax.optimization_barrier((first, ctx))
    ctxs = [ctx] + [swap(ctx, "dp", n_dp, q) for q in range(1, NEAR)]
    held = {0: [weight], half: [first, second]}
    bit = half // 2
    while bit:
        held.update({m | bit: [swap(p, "tensor", n_tensor, bit) for p in w] for m, w in list(held.items())})
        bit //= 2
    weights = [held[m] for m in range(n_tensor)]

    hidden, grads = join(plan, info, ctx, norm_gain[None, :], next_hidden, weights)
    parts = []
    for j in range(chunks):
        near = [grads[j][0]] + [swap(grads[j][q], "dp", n_dp, q) for q in range(1, NEAR)]
        keep, send = gradient(plan, dout, info, ctxs, near)
        blocks = merge(plan, dout, width, keep, swap(send, "tensor", n_tensor, 1))
        parts.append(exchange_far(plan, blocks))
    weight_grad, gain_grad, loss = finish(plan, dout, width, parts)
    return (hidden, weight_grad[None], gain_grad.reshape(dout), loss.reshape(()))


def solution(mesh):
    return jax.shard_map(
        functools.partial(on_device, mesh.shape["dp"], mesh.shape["tensor"]),
        mesh=mesh,
        in_specs=(
            P(None, "dp", "tensor"),
            P(None, "dp", "tensor"),
            P(None, "dp", "tensor"),
            P(None, "tensor", None),
            P(),
            P(("dp", "tensor"), None),
            P("dp"),
            P("dp"),
        ),
        out_specs=(P(("dp", "tensor"), None), P(None, "tensor", "dp"), P(), P()),
        check_vma=False,
    )
```

time: 122 us -> 99.8 us (0.82)
  waiting for transfers between devices: 67.8 us -> 44 us
  starting transfers between devices: 24.7 us -> 33.7 us
  other arithmetic: 2.9 us -> 0.08 us
  between operations: 4.55 us -> 2.08 us
  Pallas kernels: 17.3 us -> 15 us
    ppermute x14 -> x16, waiting for transfers between devices: 53.3 us -> 23 us  [swap(): return lax.ppermute(x, axis, [(i, i ^ mask) for i in range(n)])]
    ppermute x0 -> x6, starting transfers between devices: none -> 10 us  [swap_far(): lax.ppermute(x, ('dp', 'tensor'), [(i, i ^ mask) for i in range(n_dp * n_...]
    all_to_all x2 -> x0, starting transfers between devices: 9.5 us -> none  [on_device(): parts.append(lax.all_to_all(slabs, 'dp', 0, 0, tiled=True))]
    ppermute x14 -> x16, starting transfers between devices: 11.6 us -> 20.2 us  [swap(): return lax.ppermute(x, axis, [(i, i ^ mask) for i in range(n)])]
    all_to_all x1, waiting for transfers between devices: 8.14 us -> 15.1 us  [on_device(): ctx = lax.all_to_all(context, 'tensor', 0, 0, tiled=True)]
    all_to_all x2 -> x0, waiting for transfers between devices: 6.31 us -> none  [on_device(): parts.append(lax.all_to_all(slabs, 'dp', 0, 0, tiled=True))]
    ppermute x0 -> x6, waiting for transfers between devices: none -> 5.8 us  [swap_far(): lax.ppermute(x, ('dp', 'tensor'), [(i, i ^ mask) for i in range(n_dp * n_...]
    pallas_call x4 -> x7, Pallas kernels: 17.3 us -> 15 us  [the longest x1 7.16 us: join(): pl.pallas_call(functools.partial(join_body, plan, [len(w) for w in weight...]
  transfers between devices with their start and end apart: 17 -> 23, of which waited for: 12 -> 10; matrix products, arithmetic and copies ran while one was open for 2% -> 1% of each run, Pallas kernels for 8% -> 10%
where the time goes in v3:
time: 99.8 us; the launch traced here: 99.5 us
  waiting for transfers between devices  44 us (44%)
  starting transfers between devices  33.7 us (34%)
  Pallas kernels  15 us (15%)
  local copies, waits for them, and re-layouts  4.67 us (5%)
  between operations  2.08 us (2%)
    ppermute x16, waiting for transfers between devices, swap(): return lax.ppermute(x, axis, [(i, i ^ mask) for i in range(n)])  23 us
    ppermute x16, starting transfers between devices, swap(): return lax.ppermute(x, axis, [(i, i ^ mask) for i in range(n)])  20.2 us
    all_to_all x1, waiting for transfers between devices, on_device(): ctx = lax.all_to_all(context, 'tensor', 0, 0, tiled=True)  15.1 us
    ppermute x6, starting transfers between devices, swap_far(): lax.ppermute(x, ('dp', 'tensor'), [(i, i ^ mask) for i in range(n_dp * n_...  10 us
    pallas_call x1, Pallas kernels, join(): pl.pallas_call(functools.partial(join_body, plan, [len(w) for w in weight...  7.16 us
    ppermute x6, waiting for transfers between devices, swap_far(): lax.ppermute(x, ('dp', 'tensor'), [(i, i ^ mask) for i in range(n_dp * n_...  5.8 us
    pallas_call x1, Pallas kernels, attend(): pl.pallas_call(attend_body, grid=(heads,), in_specs=[SM, block, block, bl...  4.43 us
    all_to_all x1, starting transfers between devices, on_device(): ctx = lax.all_to_all(context, 'tensor', 0, 0, tiled=True)  3.47 us
  transfers between devices with their start and end apart: 23, of which 10 were waited for; matrix products, arithmetic and copies ran while one was open for 1% of the time, Pallas kernels for 10%

profile of v3, /device:TPU:0, one launch (start us, length us, event | category | flops | bytes accessed | tf_op | source)
XLA Modules:
  0.0 99.5 jit_solution(10234853404375950908)
XLA Ops:
  1.9 2.1 %slice.9 = bf16[256,1280]{1,0:T(8,128)(2,1)} slice(bf16[256,2048]{1,0:T(8,128)(2,1)} %bitcast.10), slice={[0:256], [768:2048]} | slice | bytes 1310720 | tf_op jit(solution)/shard_map/slice | solution.py:406
  5.1 4.4 %attend.1 = bf16[4,256,256]{2,1,0:T(8,128)(2,1)S(1)} custom-call(s32[4]{0:T(128)S(1)} %pad_add_fusion.info_ref, bf16[1024,256]{1,0:T(8,128)(2,1)S(1)} %bitcast.15, bf16[1024,256]{1,0:T(8,128)(2,1)S(1)} %bitcast.16, bf16[1024,256]{1,0:T(8,128)(2,1)S(1)} %bitcast.17), custom_call_target="tpu_custom_call" | custom-call | flops 1073741824 | bytes 2097152 | tf_op jit(solution)/shard_map/attend/pallas_call | solution.py:73
  10.4 3.0 %collective-permute-start.2 = (bf16[256,1280]{1,0:T(8,128)(2,1)}, bf16[256,1280]{1,0:T(8,128)(2,1)S(1)}, u32[]{:S(2)}, u32[]{:S(2)}) collective-permute-start(bf16[256,1280]{1,0:T(8,128)(2,1)} %slice.9), channel_id=1, source_target_pairs={{0,2},{1,3},{2,0},{3,1},{4,6},{5,7},{6,4},{7,5},{8,10},{9,11},{10,... | collective-permute-start | bytes 1966088 | tf_op jit(solution)/shard_map/ppermute | solution.py:359
  13.3 3.5 %all-to-all-start = ((bf16[4,256,256]{2,1,0:T(8,128)(2,1)}), bf16[4,256,256]{2,1,0:T(8,128)(2,1)S(1)}, u32[]{:S(2)}, u32[]{:S(2)}) async-start(bf16[4,256,256]{2,1,0:T(8,128)(2,1)} %copy-done.2), calls=%async_computation | async-start | bytes 1048576 | tf_op jit(solution)/shard_map/all_to_all | solution.py:410
  17.6 2.0 %collective-permute-start = (bf16[256,768]{1,0:T(8,128)(2,1)}, bf16[256,768]{1,0:T(8,128)(2,1)}, u32[]{:S(2)}, u32[]{:S(2)}) collective-permute-start(bf16[256,768]{1,0:T(8,128)(2,1)} %slice.8), channel_id=1, source_target_pairs={{0,2},{1,3},{2,0},{3,1},{4,6},{5,7},{6,4},{7,5},{8,10},{9,11},{10,... | collective-permute-start | bytes 1179656 | tf_op jit(solution)/shard_map/ppermute | solution.py:359
  19.6 15.1 %all-to-all-done.ctx_ref.refs_0_ = bf16[4,256,256]{2,1,0:T(8,128)(2,1)S(1)} async-done(((bf16[4,256,256]{2,1,0:T(8,128)(2,1)}), bf16[4,256,256]{2,1,0:T(8,128)(2,1)S(1)}, u32[]{:S(2)}, u32[]{:S(2)}) %all-to-all-start) | async-done | bytes 524320 | tf_op jit(solution)/shard_map/all_to_all | solution.py:410
  34.7 7.7 %collective-permute-done.refs_2_ = bf16[256,768]{1,0:T(8,128)(2,1)} collective-permute-done((bf16[256,768]{1,0:T(8,128)(2,1)}, bf16[256,768]{1,0:T(8,128)(2,1)}, u32[]{:S(2)}, u32[]{:S(2)}) %collective-permute-start) | collective-permute-done | bytes 393248 | tf_op jit(solution)/shard_map/ppermute | solution.py:359
  42.9 1.7 %collective-permute-start.5 = (bf16[4,256,256]{2,1,0:T(8,128)(2,1)S(1)}, bf16[4,256,256]{2,1,0:T(8,128)(2,1)S(1)}, u32[]{:S(2)}, u32[]{:S(2)}) collective-permute-start(bf16[4,256,256]{2,1,0:T(8,128)(2,1)S(1)} %all-to-all-done.ctx_ref.refs_0_), channel_id=1, source_target_pairs={{0,4},{4,0},{8,12},{12,8},{16,20},{20,16},{24,28},{28,24},{1,5},{5... | collective-permute-start | bytes 1572872 | tf_op jit(solution)/shard_map/ppermute | solution.py:359
  44.6 1.6 %collective-permute-start.6 = (bf16[4,256,256]{2,1,0:T(8,128)(2,1)S(1)}, bf16[4,256,256]{2,1,0:T(8,128)(2,1)S(1)}, u32[]{:S(2)}, u32[]{:S(2)}) collective-permute-start(bf16[4,256,256]{2,1,0:T(8,128)(2,1)S(1)} %all-to-all-done.ctx_ref.refs_0_), channel_id=1, source_target_pairs={{0,8},{4,12},{8,0},{12,4},{16,24},{20,28},{24,16},{28,20},{1,9},{5... | collective-permute-start | bytes 1572872 | tf_op jit(solution)/shard_map/ppermute | solution.py:359
  47.6 7.2 %join.1 = (bf16[256,2048]{1,0:T(8,128)(2,1)}, bf16[288,256]{1,0:T(8,128)(2,1)S(1)}, bf16[288,256]{1,0:T(8,128)(2,1)S(1)}, bf16[288,256]{1,0:T(8,128)(2,1)S(1)}, ...) custom-call(s32[4]{0:T(128)S(1)} %pad_add_fusion.info_ref, ...), custom_call_target="tpu_custom_call" | custom-call | flops 1073741824 | bytes 7340032 | tf_op jit(solution)/shard_map/join/pallas_call | solution.py:196
  55.3 1.6 %collective-permute-start.16 = (bf16[256,256]{1,0:T(8,128)(2,1)S(1)}, bf16[256,256]{1,0:T(8,128)(2,1)S(1)}, u32[]{:S(2)}, u32[]{:S(2)}) collective-permute-start(bf16[256,256]{1,0:T(8,128)(2,1)S(1)} %get-tuple-element.49), channel_id=1, source_target_pairs={{0,8},{4,12},{8,0},{12,4},{16,24},{20,28},{24,16},{28,20},{1,9},{5... | collective-permute-start | bytes 393224 | tf_op jit(solution)/shard_map/ppermute | solution.py:359
  57.0 4.5 %collective-permute-start.17 = (bf16[256,256]{1,0:T(8,128)(2,1)S(1)}, bf16[256,256]{1,0:T(8,128)(2,1)S(1)}, u32[]{:S(2)}, u32[]{:S(2)}) collective-permute-start(bf16[256,256]{1,0:T(8,128)(2,1)S(1)} %get-tuple-element.50), channel_id=1, source_target_pairs={{0,12},{4,8},{8,4},{12,0},{16,28},{20,24},{24,20},{28,16},{1,13},{... | collective-permute-start | bytes 393224 | tf_op jit(solution)/shard_map/ppermute | solution.py:359
  61.5 9.0 %collective-permute-done.7.refs_3_ = bf16[4,256,256]{2,1,0:T(8,128)(2,1)S(1)} collective-permute-done((bf16[4,256,256]{2,1,0:T(8,128)(2,1)S(1)}, bf16[4,256,256]{2,1,0:T(8,128)(2,1)S(1)}, u32[]{:S(2)}, u32[]{:S(2)}) %collective-permute-start.7) | collective-permute-done | bytes 524320 | tf_op jit(solution)/shard_map/ppermute | solution.py:359
  70.5 1.7 %collective-permute-start.8 = (bf16[288,256]{1,0:T(8,128)(2,1)S(1)}, bf16[288,256]{1,0:T(8,128)(2,1)S(1)}, u32[]{:S(2)}, u32[]{:S(2)}) collective-permute-start(bf16[288,256]{1,0:T(8,128)(2,1)S(1)} %get-tuple-element.38), channel_id=1, source_target_pairs={{0,4},{4,0},{8,12},{12,8},{16,20},{20,16},{24,28},{28,24},{1,5},{5... | collective-permute-start | bytes 442376 | tf_op jit(solution)/shard_map/ppermute | solution.py:359
  72.2 1.6 %collective-permute-start.9 = (bf16[288,256]{1,0:T(8,128)(2,1)S(1)}, bf16[288,256]{1,0:T(8,128)(2,1)S(1)}, u32[]{:S(2)}, u32[]{:S(2)}) collective-permute-start(bf16[288,256]{1,0:T(8,128)(2,1)S(1)} %get-tuple-element.39), channel_id=1, source_target_pairs={{0,8},{4,12},{8,0},{12,4},{16,24},{20,28},{24,16},{28,20},{1,9},{5... | collective-permute-start | bytes 442376 | tf_op jit(solution)/shard_map/ppermute | solution.py:359
  73.8 2.4 %collective-permute-done.17.refs_7_ = bf16[256,256]{1,0:T(8,128)(2,1)S(1)} collective-permute-done((bf16[256,256]{1,0:T(8,128)(2,1)S(1)}, bf16[256,256]{1,0:T(8,128)(2,1)S(1)}, u32[]{:S(2)}, u32[]{:S(2)}) %collective-permute-start.17) | collective-permute-done | bytes 131104 | tf_op jit(solution)/shard_map/ppermute | solution.py:359
  77.5 1.8 %collective-permute-done.10.refs_7_ = bf16[288,256]{1,0:T(8,128)(2,1)S(1)} collective-permute-done((bf16[288,256]{1,0:T(8,128)(2,1)S(1)}, bf16[288,256]{1,0:T(8,128)(2,1)S(1)}, u32[]{:S(2)}, u32[]{:S(2)}) %collective-permute-start.10) | collective-permute-done | bytes 147488 | tf_op jit(solution)/shard_map/ppermute | solution.py:359
  82.8 2.7 %collective-permute-start.19 = (bf16[1,1,256,128]{3,2,1,0:T(8,128)(2,1)S(1)}, bf16[1,1,256,128]{3,2,1,0:T(8,128)(2,1)S(1)}, u32[]{:S(2)}, u32[]{:S(2)}) collective-permute-start(bf16[1,1,256,128]{3,2,1,0:T(8,128)(2,1)S(1)} %get-tuple-element.54), channel_id=1, source_target_pairs={{0,16},{1,17},{2,18},{3,19},{4,20},{5,21},{6,22},{7,23},{8,24},{9,... | collective-permute-start | bytes 196616 | tf_op jit(solution)/shard_map/ppermute | solution.py:364
  85.5 1.5 %collective-permute-start.12 = (bf16[1,1,304,128]{3,2,1,0:T(8,128)(2,1)S(1)}, bf16[1,1,304,128]{3,2,1,0:T(8,128)(2,1)S(1)}, u32[]{:S(2)}, u32[]{:S(2)}) collective-permute-start(bf16[1,1,304,128]{3,2,1,0:T(8,128)(2,1)S(1)} %get-tuple-element.44), channel_id=1, source_target_pairs={{0,16},{1,17},{2,18},{3,19},{4,20},{5,21},{6,22},{7,23},{8,24},{9,... | collective-permute-start | bytes 233480 | tf_op jit(solution)/shard_map/ppermute | solution.py:364
  87.1 1.5 %collective-permute-start.13 = (bf16[1,1,304,128]{3,2,1,0:T(8,128)(2,1)S(1)}, bf16[1,1,304,128]{3,2,1,0:T(8,128)(2,1)S(1)}, u32[]{:S(2)}, u32[]{:S(2)}) collective-permute-start(bf16[1,1,304,128]{3,2,1,0:T(8,128)(2,1)S(1)} %get-tuple-element.45), channel_id=1, source_target_pairs={{0,2},{1,3},{2,0},{3,1},{4,6},{5,7},{6,4},{7,5},{8,10},{9,11},{10,... | collective-permute-start | bytes 233480 | tf_op jit(solution)/shard_map/ppermute | solution.py:364
  88.6 1.4 %collective-permute-start.14 = (bf16[1,1,304,128]{3,2,1,0:T(8,128)(2,1)S(1)}, bf16[1,1,304,128]{3,2,1,0:T(8,128)(2,1)S(1)}, u32[]{:S(2)}, u32[]{:S(2)}) collective-permute-start(bf16[1,1,304,128]{3,2,1,0:T(8,128)(2,1)S(1)} %get-tuple-element.46), channel_id=1, source_target_pairs={{0,18},{1,19},{2,16},{3,17},{4,22},{5,23},{6,20},{7,21},{8,26},{9,... | collective-permute-start | bytes 233480 | tf_op jit(solution)/shard_map/ppermute | solution.py:364
  90.0 1.5 %collective-permute-start.20 = (bf16[1,1,256,128]{3,2,1,0:T(8,128)(2,1)S(1)}, bf16[1,1,256,128]{3,2,1,0:T(8,128)(2,1)S(1)}, u32[]{:S(2)}, u32[]{:S(2)}) collective-permute-start(bf16[1,1,256,128]{3,2,1,0:T(8,128)(2,1)S(1)} %get-tuple-element.55), channel_id=1, source_target_pairs={{0,2},{1,3},{2,0},{3,1},{4,6},{5,7},{6,4},{7,5},{8,10},{9,11},{10,... | collective-permute-start | bytes 196616 | tf_op jit(solution)/shard_map/ppermute | solution.py:364
  92.9 1.4 %collective-permute-done.20.refs_6_ = bf16[1,1,256,128]{3,2,1,0:T(8,128)(2,1)S(1)} collective-permute-done((bf16[1,1,256,128]{3,2,1,0:T(8,128)(2,1)S(1)}, bf16[1,1,256,128]{3,2,1,0:T(8,128)(2,1)S(1)}, u32[]{:S(2)}, u32[]{:S(2)}) %collective-permute-start.20) | collective-permute-done | bytes 65568 | tf_op jit(solution)/shard_map/ppermute | solution.py:364
  94.3 4.4 %collective-permute-done.21.refs_7_ = bf16[1,1,256,128]{3,2,1,0:T(8,128)(2,1)S(1)} collective-permute-done((bf16[1,1,256,128]{3,2,1,0:T(8,128)(2,1)S(1)}, bf16[1,1,256,128]{3,2,1,0:T(8,128)(2,1)S(1)}, u32[]{:S(2)}, u32[]{:S(2)}) %collective-permute-start.21) | collective-permute-done | bytes 65568 | tf_op jit(solution)/shard_map/ppermute | solution.py:364
  (46 shorter events, 12.3 us)
Async XLA Ops:
  5.1 42.4 %copy-start.1 = (bf16[256,2048]{1,0:T(8,128)(2,1)S(1)}, bf16[256,2048]{1,0:T(8,128)(2,1)}, u32[]{:S(2)}) copy-start(bf16[256,2048]{1,0:T(8,128)(2,1)} %next_ref.1) | copy-start | bytes 3145732
  10.4 32.1 %collective-permute-start.2 = (bf16[256,1280]{1,0:T(8,128)(2,1)}, bf16[256,1280]{1,0:T(8,128)(2,1)S(1)}, u32[]{:S(2)}, u32[]{:S(2)}) collective-permute-start(bf16[256,1280]{1,0:T(8,128)(2,1)} %slice.9), channel_id=1, source_target_pairs={{0,2},{1,3},{2,0},{3,1},{4,6},{5,7},{6,4},{7,5},{8,10},{9,11},{10,... | collective-permute-start | bytes 1966088 | tf_op jit(solution)/shard_map/ppermute | solution.py:359
  13.3 21.4 %all-to-all-start = ((bf16[4,256,256]{2,1,0:T(8,128)(2,1)}), bf16[4,256,256]{2,1,0:T(8,128)(2,1)S(1)}, u32[]{:S(2)}, u32[]{:S(2)}) async-start(bf16[4,256,256]{2,1,0:T(8,128)(2,1)} %copy-done.2), calls=%async_computation | async-start | bytes 1048576 | tf_op jit(solution)/shard_map/all_to_all | solution.py:410
  17.6 24.8 %collective-permute-start = (bf16[256,768]{1,0:T(8,128)(2,1)}, bf16[256,768]{1,0:T(8,128)(2,1)}, u32[]{:S(2)}, u32[]{:S(2)}) collective-permute-start(bf16[256,768]{1,0:T(8,128)(2,1)} %slice.8), channel_id=1, source_target_pairs={{0,2},{1,3},{2,0},{3,1},{4,6},{5,7},{6,4},{7,5},{8,10},{9,11},{10,... | collective-permute-start | bytes 1179656 | tf_op jit(solution)/shard_map/ppermute | solution.py:359
  19.6 28.0 %collective-permute-start.1 = (bf16[256,2048]{1,0:T(8,128)(2,1)S(1)}, bf16[256,2048]{1,0:T(8,128)(2,1)}, u32[]{:S(2)}, u32[]{:S(2)}) collective-permute-start(bf16[256,2048]{1,0:T(8,128)(2,1)S(1)} %bitcast.12), channel_id=1, source_target_pairs={{0,1},{1,0},{2,3},{3,2},{4,5},{5,4},{6,7},{7,6},{8,9},{9,8},{10,11... | collective-permute-start | bytes 3145736 | tf_op jit(solution)/shard_map/ppermute | solution.py:359
  42.4 3.8 %collective-permute-start.3 = (bf16[256,768]{1,0:T(8,128)(2,1)}, bf16[256,768]{1,0:T(8,128)(2,1)S(1)}, u32[]{:S(2)}, u32[]{:S(2)}) collective-permute-start(bf16[256,768]{1,0:T(8,128)(2,1)} %collective-permute-done.refs_2_), channel_id=1, source_target_pairs={{0,1},{1,0},{2,3},{3,2},{4,5},{5,4},{6,7},{7,6},{8,9},{9,8},{10,11... | collective-permute-start | bytes 1179656 | tf_op jit(solution)/shard_map/ppermute | solution.py:359
  42.4 5.1 %collective-permute-start.4 = (bf16[256,1280]{1,0:T(8,128)(2,1)S(1)}, bf16[256,1280]{1,0:T(8,128)(2,1)S(1)}, u32[]{:S(2)}, u32[]{:S(2)}) collective-permute-start(bf16[256,1280]{1,0:T(8,128)(2,1)S(1)} %collective-permute-done.2.refs_3_), channel_id=1, source_target_pairs={{0,1},{1,0},{2,3},{3,2},{4,5},{5,4},{6,7},{7,6},{8,9},{9,8},{10,11... | collective-permute-start | bytes 1966088 | tf_op jit(solution)/shard_map/ppermute | solution.py:359
  42.9 14.0 %collective-permute-start.5 = (bf16[4,256,256]{2,1,0:T(8,128)(2,1)S(1)}, bf16[4,256,256]{2,1,0:T(8,128)(2,1)S(1)}, u32[]{:S(2)}, u32[]{:S(2)}) collective-permute-start(bf16[4,256,256]{2,1,0:T(8,128)(2,1)S(1)} %all-to-all-done.ctx_ref.refs_0_), channel_id=1, source_target_pairs={{0,4},{4,0},{8,12},{12,8},{16,20},{20,16},{24,28},{28,24},{1,5},{5... | collective-permute-start | bytes 1572872 | tf_op jit(solution)/shard_map/ppermute | solution.py:359
  44.6 16.9 %collective-permute-start.6 = (bf16[4,256,256]{2,1,0:T(8,128)(2,1)S(1)}, bf16[4,256,256]{2,1,0:T(8,128)(2,1)S(1)}, u32[]{:S(2)}, u32[]{:S(2)}) collective-permute-start(bf16[4,256,256]{2,1,0:T(8,128)(2,1)S(1)} %all-to-all-done.ctx_ref.refs_0_), channel_id=1, source_target_pairs={{0,8},{4,12},{8,0},{12,4},{16,24},{20,28},{24,16},{28,20},{1,9},{5... | collective-permute-start | bytes 1572872 | tf_op jit(solution)/shard_map/ppermute | solution.py:359
  46.2 24.3 %collective-permute-start.7 = (bf16[4,256,256]{2,1,0:T(8,128)(2,1)S(1)}, bf16[4,256,256]{2,1,0:T(8,128)(2,1)S(1)}, u32[]{:S(2)}, u32[]{:S(2)}) collective-permute-start(bf16[4,256,256]{2,1,0:T(8,128)(2,1)S(1)} %all-to-all-done.ctx_ref.refs_0_), channel_id=1, source_target_pairs={{0,12},{4,8},{8,4},{12,0},{16,28},{20,24},{24,20},{28,16},{1,13},{... | collective-permute-start | bytes 1572872 | tf_op jit(solution)/shard_map/ppermute | solution.py:359
  54.7 17.5 %collective-permute-start.15 = (bf16[256,256]{1,0:T(8,128)(2,1)S(1)}, bf16[256,256]{1,0:T(8,128)(2,1)S(1)}, u32[]{:S(2)}, u32[]{:S(2)}) collective-permute-start(bf16[256,256]{1,0:T(8,128)(2,1)S(1)} %get-tuple-element.48), channel_id=1, source_target_pairs={{0,4},{4,0},{8,12},{12,8},{16,20},{20,16},{24,28},{28,24},{1,5},{5... | collective-permute-start | bytes 393224 | tf_op jit(solution)/shard_map/ppermute | solution.py:359
  55.3 18.5 %collective-permute-start.16 = (bf16[256,256]{1,0:T(8,128)(2,1)S(1)}, bf16[256,256]{1,0:T(8,128)(2,1)S(1)}, u32[]{:S(2)}, u32[]{:S(2)}) collective-permute-start(bf16[256,256]{1,0:T(8,128)(2,1)S(1)} %get-tuple-element.49), channel_id=1, source_target_pairs={{0,8},{4,12},{8,0},{12,4},{16,24},{20,28},{24,16},{28,20},{1,9},{5... | collective-permute-start | bytes 393224 | tf_op jit(solution)/shard_map/ppermute | solution.py:359
  57.0 19.2 %collective-permute-start.17 = (bf16[256,256]{1,0:T(8,128)(2,1)S(1)}, bf16[256,256]{1,0:T(8,128)(2,1)S(1)}, u32[]{:S(2)}, u32[]{:S(2)}) collective-permute-start(bf16[256,256]{1,0:T(8,128)(2,1)S(1)} %get-tuple-element.50), channel_id=1, source_target_pairs={{0,12},{4,8},{8,4},{12,0},{16,28},{20,24},{24,20},{28,16},{1,13},{... | collective-permute-start | bytes 393224 | tf_op jit(solution)/shard_map/ppermute | solution.py:359
  61.5 17.8 %collective-permute-start.10 = (bf16[288,256]{1,0:T(8,128)(2,1)S(1)}, bf16[288,256]{1,0:T(8,128)(2,1)S(1)}, u32[]{:S(2)}, u32[]{:S(2)}) collective-permute-start(bf16[288,256]{1,0:T(8,128)(2,1)S(1)} %get-tuple-element.40), channel_id=1, source_target_pairs={{0,12},{4,8},{8,4},{12,0},{16,28},{20,24},{24,20},{28,16},{1,13},{... | collective-permute-start | bytes 442376 | tf_op jit(solution)/shard_map/ppermute | solution.py:359
  70.5 9.7 %collective-permute-start.8 = (bf16[288,256]{1,0:T(8,128)(2,1)S(1)}, bf16[288,256]{1,0:T(8,128)(2,1)S(1)}, u32[]{:S(2)}, u32[]{:S(2)}) collective-permute-start(bf16[288,256]{1,0:T(8,128)(2,1)S(1)} %get-tuple-element.38), channel_id=1, source_target_pairs={{0,4},{4,0},{8,12},{12,8},{16,20},{20,16},{24,28},{28,24},{1,5},{5... | collective-permute-start | bytes 442376 | tf_op jit(solution)/shard_map/ppermute | solution.py:359
  72.2 9.2 %collective-permute-start.9 = (bf16[288,256]{1,0:T(8,128)(2,1)S(1)}, bf16[288,256]{1,0:T(8,128)(2,1)S(1)}, u32[]{:S(2)}, u32[]{:S(2)}) collective-permute-start(bf16[288,256]{1,0:T(8,128)(2,1)S(1)} %get-tuple-element.39), channel_id=1, source_target_pairs={{0,8},{4,12},{8,0},{12,4},{16,24},{20,28},{24,16},{28,20},{1,9},{5... | collective-permute-start | bytes 442376 | tf_op jit(solution)/shard_map/ppermute | solution.py:359
  77.4 5.3 %collective-permute-start.18 = (bf16[2,2,256,128]{3,2,1,0:T(8,128)(2,1)S(1)}, bf16[2,2,256,128]{3,2,1,0:T(8,128)(2,1)S(1)}, u32[]{:S(2)}, u32[]{:S(2)}) collective-permute-start(bf16[2,2,256,128]{3,2,1,0:T(8,128)(2,1)S(1)} %get-tuple-element.52), channel_id=1, source_target_pairs={{0,1},{1,0},{2,3},{3,2},{4,5},{5,4},{6,7},{7,6},{8,9},{9,8},{10,11... | collective-permute-start | bytes 786440 | tf_op jit(solution)/shard_map/ppermute | solution.py:359
  82.7 2.8 %collective-permute-start.11 = (bf16[2,2,304,128]{3,2,1,0:T(8,128)(2,1)S(1)}, bf16[2,2,304,128]{3,2,1,0:T(8,128)(2,1)S(1)}, u32[]{:S(2)}, u32[]{:S(2)}) collective-permute-start(bf16[2,2,304,128]{3,2,1,0:T(8,128)(2,1)S(1)} %get-tuple-element.42), channel_id=1, source_target_pairs={{0,1},{1,0},{2,3},{3,2},{4,5},{5,4},{6,7},{7,6},{8,9},{9,8},{10,11... | collective-permute-start | bytes 933896 | tf_op jit(solution)/shard_map/ppermute | solution.py:359
  82.8 8.7 %collective-permute-start.19 = (bf16[1,1,256,128]{3,2,1,0:T(8,128)(2,1)S(1)}, bf16[1,1,256,128]{3,2,1,0:T(8,128)(2,1)S(1)}, u32[]{:S(2)}, u32[]{:S(2)}) collective-permute-start(bf16[1,1,256,128]{3,2,1,0:T(8,128)(2,1)S(1)} %get-tuple-element.54), channel_id=1, source_target_pairs={{0,16},{1,17},{2,18},{3,19},{4,20},{5,21},{6,22},{7,23},{8,24},{9,... | collective-permute-start | bytes 196616 | tf_op jit(solution)/shard_map/ppermute | solution.py:364
  85.5 13.2 %collective-permute-start.12 = (bf16[1,1,304,128]{3,2,1,0:T(8,128)(2,1)S(1)}, bf16[1,1,304,128]{3,2,1,0:T(8,128)(2,1)S(1)}, u32[]{:S(2)}, u32[]{:S(2)}) collective-permute-start(bf16[1,1,304,128]{3,2,1,0:T(8,128)(2,1)S(1)} %get-tuple-element.44), channel_id=1, source_target_pairs={{0,16},{1,17},{2,18},{3,19},{4,20},{5,21},{6,22},{7,23},{8,24},{9,... | collective-permute-start | bytes 233480 | tf_op jit(solution)/shard_map/ppermute | solution.py:364
  87.1 11.7 %collective-permute-start.13 = (bf16[1,1,304,128]{3,2,1,0:T(8,128)(2,1)S(1)}, bf16[1,1,304,128]{3,2,1,0:T(8,128)(2,1)S(1)}, u32[]{:S(2)}, u32[]{:S(2)}) collective-permute-start(bf16[1,1,304,128]{3,2,1,0:T(8,128)(2,1)S(1)} %get-tuple-element.45), channel_id=1, source_target_pairs={{0,2},{1,3},{2,0},{3,1},{4,6},{5,7},{6,4},{7,5},{8,10},{9,11},{10,... | collective-permute-start | bytes 233480 | tf_op jit(solution)/shard_map/ppermute | solution.py:364
  88.6 10.1 %collective-permute-start.14 = (bf16[1,1,304,128]{3,2,1,0:T(8,128)(2,1)S(1)}, bf16[1,1,304,128]{3,2,1,0:T(8,128)(2,1)S(1)}, u32[]{:S(2)}, u32[]{:S(2)}) collective-permute-start(bf16[1,1,304,128]{3,2,1,0:T(8,128)(2,1)S(1)} %get-tuple-element.46), channel_id=1, source_target_pairs={{0,18},{1,19},{2,16},{3,17},{4,22},{5,23},{6,20},{7,21},{8,26},{9,... | collective-permute-start | bytes 233480 | tf_op jit(solution)/shard_map/ppermute | solution.py:364
  90.0 4.3 %collective-permute-start.20 = (bf16[1,1,256,128]{3,2,1,0:T(8,128)(2,1)S(1)}, bf16[1,1,256,128]{3,2,1,0:T(8,128)(2,1)S(1)}, u32[]{:S(2)}, u32[]{:S(2)}) collective-permute-start(bf16[1,1,256,128]{3,2,1,0:T(8,128)(2,1)S(1)} %get-tuple-element.55), channel_id=1, source_target_pairs={{0,2},{1,3},{2,0},{3,1},{4,6},{5,7},{6,4},{7,5},{8,10},{9,11},{10,... | collective-permute-start | bytes 196616 | tf_op jit(solution)/shard_map/ppermute | solution.py:364
  91.5 7.2 %collective-permute-start.21 = (bf16[1,1,256,128]{3,2,1,0:T(8,128)(2,1)S(1)}, bf16[1,1,256,128]{3,2,1,0:T(8,128)(2,1)S(1)}, u32[]{:S(2)}, u32[]{:S(2)}) collective-permute-start(bf16[1,1,256,128]{3,2,1,0:T(8,128)(2,1)S(1)} %get-tuple-element.56), channel_id=1, source_target_pairs={{0,18},{1,19},{2,16},{3,17},{4,22},{5,23},{6,20},{7,21},{8,26},{9,... | collective-permute-start | bytes 196616 | tf_op jit(solution)/shard_map/ppermute | solution.py:364
  (6 other events, 43.3 us)

commit v4 on v3

--- a/solution.py
+++ b/solution.py
@@ -405,16 +405,19 @@
     cut = dout * 3 // 8 // COLS * COLS
     first, second = weight[:, :cut], weight[:, cut:]
     first = swap(first, "tensor", n_tensor, half)
+    beside = swap(weight, "tensor", n_tensor, 1)
     context = attend(info, query_states[0], key_states[0], value_states[0], rows)
-    second, context = lax.optimization_barrier((second, context))
+    first, beside, context = lax.optimization_barrier((first, beside, context))
     ctx = lax.all_to_all(context, "tensor", 0, 0, tiled=True)
+    across = swap(first, "tensor", n_tensor, 1)
+    across, second, ctx = lax.optimization_barrier((across, second, ctx))
     second = swap(second, "tensor", n_tensor, half)
-    first, ctx = lax.optimization_barrier((first, ctx))
     ctxs = [ctx] + [swap(ctx, "dp", n_dp, q) for q in range(1, NEAR)]
-    held = {0: [weight], half: [first, second]}
+    held = {0: [weight], 1: [beside], half: [first, second]}
+    held[half + 1] = [across, swap(second, "tensor", n_tensor, 1)]
     bit = half // 2
-    while bit:
-        held.update({m | bit: [swap(p, "tensor", n_tensor, bit) for p in w] for m, w in list(held.items())})
+    while bit > 1:
+        held.update({m ^ bit: [swap(p, "tensor", n_tensor, bit) for p in w] for m, w in list(held.items())})
         bit //= 2
     weights = [held[m] for m in range(n_tensor)]
 

time: 99.8 us -> 100 us (level)
  waiting for transfers between devices: 44 us -> 47.9 us
  starting transfers between devices: 33.7 us -> 29.9 us
    ppermute x16, waiting for transfers between devices: 23 us -> 35 us  [swap(): return lax.ppermute(x, axis, [(i, i ^ mask) for i in range(n)])]
    all_to_all x1, waiting for transfers between devices: 15.1 us -> 7.97 us  [on_device(): ctx = lax.all_to_all(context, 'tensor', 0, 0, tiled=True)]
    ppermute x16, starting transfers between devices: 20.2 us -> 16.5 us  [swap(): return lax.ppermute(x, axis, [(i, i ^ mask) for i in range(n)])]
    unnamed x14 -> x12, local copies, waits for them, and re-layouts: 1.84 us -> 2.1 us
  transfers between devices with their start and end apart: 23 -> 23, of which waited for: 10 -> 11; matrix products, arithmetic and copies ran while one was open for 1% -> 2% of each run, Pallas kernels for 10% -> 15%
where the time goes in v4:
time: 100 us; the launch traced here: 99.6 us
  waiting for transfers between devices  47.9 us (48%)
  starting transfers between devices  29.9 us (30%)
  Pallas kernels  15.6 us (16%)
  local copies, waits for them, and re-layouts  4.02 us (4%)
  between operations  2.05 us (2%)
    ppermute x16, waiting for transfers between devices, swap(): return lax.ppermute(x, axis, [(i, i ^ mask) for i in range(n)])  35 us
    ppermute x16, starting transfers between devices, swap(): return lax.ppermute(x, axis, [(i, i ^ mask) for i in range(n)])  16.5 us
    ppermute x6, starting transfers between devices, swap_far(): lax.ppermute(x, ('dp', 'tensor'), [(i, i ^ mask) for i in range(n_dp * n_...  10 us
    all_to_all x1, waiting for transfers between devices, on_device(): ctx = lax.all_to_all(context, 'tensor', 0, 0, tiled=True)  7.97 us
    pallas_call x1, Pallas kernels, join(): pl.pallas_call(functools.partial(join_body, plan, [len(w) for w in weight...  7.11 us
    pallas_call x1, Pallas kernels, attend(): pl.pallas_call(attend_body, grid=(heads,), in_specs=[SM, block, block, bl...  5.11 us
    ppermute x6, waiting for transfers between devices, swap_far(): lax.ppermute(x, ('dp', 'tensor'), [(i, i ^ mask) for i in range(n_dp * n_...  4.92 us
    all_to_all x1, starting transfers between devices, on_device(): ctx = lax.all_to_all(context, 'tensor', 0, 0, tiled=True)  3.47 us
  transfers between devices with their start and end apart: 23, of which 11 were waited for; matrix products, arithmetic and copies ran while one was open for 2% of the time, Pallas kernels for 15%

profile of v4, /device:TPU:0, one launch (start us, length us, event | category | flops | bytes accessed | tf_op | source)
XLA Modules:
  0.0 99.6 jit_solution(8976255416754275976)
XLA Ops:
  2.2 2.6 %collective-permute-start = (bf16[256,768]{1,0:T(8,128)(2,1)S(1)}, bf16[256,768]{1,0:T(8,128)(2,1)S(1)}, u32[]{:S(2)}, u32[]{:S(2)}) collective-permute-start(bf16[256,768]{1,0:T(8,128)(2,1)S(1)} %slice.8), channel_id=1, source_target_pairs={{0,2},{1,3},{2,0},{3,1},{4,6},{5,7},{6,4},{7,5},{8,10},{9,11},{10,... | collective-permute-start | bytes 1179656 | tf_op jit(solution)/shard_map/ppermute | solution.py:359
  8.3 5.1 %attend.1 = bf16[4,256,256]{2,1,0:T(8,128)(2,1)} custom-call(s32[4]{0:T(128)S(1)} %pad_add_fusion.info_ref, bf16[1024,256]{1,0:T(8,128)(2,1)S(1)} %bitcast.15, bf16[1024,256]{1,0:T(8,128)(2,1)S(1)} %bitcast.16, bf16[1024,256]{1,0:T(8,128)(2,1)S(1)} %bitcast.17), custom_call_target="tpu_custom_call" | custom-call | flops 1073741824 | bytes 2097152 | tf_op jit(solution)/shard_map/attend/pallas_call | solution.py:73
  14.6 3.5 %all-to-all-start = ((bf16[4,256,256]{2,1,0:T(8,128)(2,1)}), bf16[4,256,256]{2,1,0:T(8,128)(2,1)S(1)}, u32[]{:S(2)}, u32[]{:S(2)}) async-start(bf16[4,256,256]{2,1,0:T(8,128)(2,1)} %attend.1), calls=%async_computation | async-start | bytes 1048576 | tf_op jit(solution)/shard_map/all_to_all | solution.py:411
  19.0 8.0 %all-to-all-done.ctx_ref.refs_0_ = bf16[4,256,256]{2,1,0:T(8,128)(2,1)S(1)} async-done(((bf16[4,256,256]{2,1,0:T(8,128)(2,1)}), bf16[4,256,256]{2,1,0:T(8,128)(2,1)S(1)}, u32[]{:S(2)}, u32[]{:S(2)}) %all-to-all-start) | async-done | bytes 524320 | tf_op jit(solution)/shard_map/all_to_all | solution.py:411
  27.2 16.3 %collective-permute-done.3.refs_3_ = bf16[256,1280]{1,0:T(8,128)(2,1)S(1)} collective-permute-done((bf16[256,1280]{1,0:T(8,128)(2,1)}, bf16[256,1280]{1,0:T(8,128)(2,1)S(1)}, u32[]{:S(2)}, u32[]{:S(2)}) %collective-permute-start.3) | collective-permute-done | bytes 655392 | tf_op jit(solution)/shard_map/ppermute | solution.py:359
  43.5 1.5 %collective-permute-start.5 = (bf16[4,256,256]{2,1,0:T(8,128)(2,1)S(1)}, bf16[4,256,256]{2,1,0:T(8,128)(2,1)S(1)}, u32[]{:S(2)}, u32[]{:S(2)}) collective-permute-start(bf16[4,256,256]{2,1,0:T(8,128)(2,1)S(1)} %all-to-all-done.ctx_ref.refs_0_), channel_id=1, source_target_pairs={{0,4},{4,0},{8,12},{12,8},{16,20},{20,16},{24,28},{28,24},{1,5},{5... | collective-permute-start | bytes 1572872 | tf_op jit(solution)/shard_map/ppermute | solution.py:359
  45.1 1.6 %collective-permute-start.6 = (bf16[4,256,256]{2,1,0:T(8,128)(2,1)S(1)}, bf16[4,256,256]{2,1,0:T(8,128)(2,1)S(1)}, u32[]{:S(2)}, u32[]{:S(2)}) collective-permute-start(bf16[4,256,256]{2,1,0:T(8,128)(2,1)S(1)} %all-to-all-done.ctx_ref.refs_0_), channel_id=1, source_target_pairs={{0,8},{4,12},{8,0},{12,4},{16,24},{20,28},{24,16},{28,20},{1,9},{5... | collective-permute-start | bytes 1572872 | tf_op jit(solution)/shard_map/ppermute | solution.py:359
  47.0 7.1 %join.1 = (bf16[256,2048]{1,0:T(8,128)(2,1)}, bf16[288,256]{1,0:T(8,128)(2,1)S(1)}, bf16[288,256]{1,0:T(8,128)(2,1)S(1)}, bf16[288,256]{1,0:T(8,128)(2,1)S(1)}, ...) custom-call(s32[4]{0:T(128)S(1)} %pad_add_fusion.info_ref, ...), custom_call_target="tpu_custom_call" | custom-call | flops 1073741824 | bytes 7340032 | tf_op jit(solution)/shard_map/join/pallas_call | solution.py:196
  54.1 1.5 %collective-permute-start.15 = (bf16[256,256]{1,0:T(8,128)(2,1)S(1)}, bf16[256,256]{1,0:T(8,128)(2,1)S(1)}, u32[]{:S(2)}, u32[]{:S(2)}) collective-permute-start(bf16[256,256]{1,0:T(8,128)(2,1)S(1)} %get-tuple-element.52), channel_id=1, source_target_pairs={{0,4},{4,0},{8,12},{12,8},{16,20},{20,16},{24,28},{28,24},{1,5},{5... | collective-permute-start | bytes 393224 | tf_op jit(solution)/shard_map/ppermute | solution.py:359
  55.7 1.6 %collective-permute-start.16 = (bf16[256,256]{1,0:T(8,128)(2,1)S(1)}, bf16[256,256]{1,0:T(8,128)(2,1)S(1)}, u32[]{:S(2)}, u32[]{:S(2)}) collective-permute-start(bf16[256,256]{1,0:T(8,128)(2,1)S(1)} %get-tuple-element.53), channel_id=1, source_target_pairs={{0,8},{4,12},{8,0},{12,4},{16,24},{20,28},{24,16},{28,20},{1,9},{5... | collective-permute-start | bytes 393224 | tf_op jit(solution)/shard_map/ppermute | solution.py:359
  58.2 2.6 %collective-permute-start.17 = (bf16[256,256]{1,0:T(8,128)(2,1)S(1)}, bf16[256,256]{1,0:T(8,128)(2,1)S(1)}, u32[]{:S(2)}, u32[]{:S(2)}) collective-permute-start(bf16[256,256]{1,0:T(8,128)(2,1)S(1)} %get-tuple-element.54), channel_id=1, source_target_pairs={{0,12},{4,8},{8,4},{12,0},{16,28},{20,24},{24,20},{28,16},{1,13},{... | collective-permute-start | bytes 393224 | tf_op jit(solution)/shard_map/ppermute | solution.py:359
  61.4 9.6 %collective-permute-done.7.refs_3_ = bf16[4,256,256]{2,1,0:T(8,128)(2,1)S(1)} collective-permute-done((bf16[4,256,256]{2,1,0:T(8,128)(2,1)S(1)}, bf16[4,256,256]{2,1,0:T(8,128)(2,1)S(1)}, u32[]{:S(2)}, u32[]{:S(2)}) %collective-permute-start.7) | collective-permute-done | bytes 524320 | tf_op jit(solution)/shard_map/ppermute | solution.py:359
  71.0 1.5 %collective-permute-start.8 = (bf16[288,256]{1,0:T(8,128)(2,1)S(1)}, bf16[288,256]{1,0:T(8,128)(2,1)S(1)}, u32[]{:S(2)}, u32[]{:S(2)}) collective-permute-start(bf16[288,256]{1,0:T(8,128)(2,1)S(1)} %get-tuple-element.42), channel_id=1, source_target_pairs={{0,4},{4,0},{8,12},{12,8},{16,20},{20,16},{24,28},{28,24},{1,5},{5... | collective-permute-start | bytes 442376 | tf_op jit(solution)/shard_map/ppermute | solution.py:359
  72.6 1.6 %collective-permute-start.9 = (bf16[288,256]{1,0:T(8,128)(2,1)S(1)}, bf16[288,256]{1,0:T(8,128)(2,1)S(1)}, u32[]{:S(2)}, u32[]{:S(2)}) collective-permute-start(bf16[288,256]{1,0:T(8,128)(2,1)S(1)} %get-tuple-element.43), channel_id=1, source_target_pairs={{0,8},{4,12},{8,0},{12,4},{16,24},{20,28},{24,16},{28,20},{1,9},{5... | collective-permute-start | bytes 442376 | tf_op jit(solution)/shard_map/ppermute | solution.py:359
  74.1 2.6 %collective-permute-done.17.refs_7_ = bf16[256,256]{1,0:T(8,128)(2,1)S(1)} collective-permute-done((bf16[256,256]{1,0:T(8,128)(2,1)S(1)}, bf16[256,256]{1,0:T(8,128)(2,1)S(1)}, u32[]{:S(2)}, u32[]{:S(2)}) %collective-permute-start.17) | collective-permute-done | bytes 131104 | tf_op jit(solution)/shard_map/ppermute | solution.py:359
  78.1 1.8 %collective-permute-done.10.refs_7_ = bf16[288,256]{1,0:T(8,128)(2,1)S(1)} collective-permute-done((bf16[288,256]{1,0:T(8,128)(2,1)S(1)}, bf16[288,256]{1,0:T(8,128)(2,1)S(1)}, u32[]{:S(2)}, u32[]{:S(2)}) %collective-permute-start.10) | collective-permute-done | bytes 147488 | tf_op jit(solution)/shard_map/ppermute | solution.py:359
  79.8 1.6 %collective-permute-done.8.refs_5_ = bf16[288,256]{1,0:T(8,128)(2,1)S(1)} collective-permute-done((bf16[288,256]{1,0:T(8,128)(2,1)S(1)}, bf16[288,256]{1,0:T(8,128)(2,1)S(1)}, u32[]{:S(2)}, u32[]{:S(2)}) %collective-permute-start.8) | collective-permute-done | bytes 147488 | tf_op jit(solution)/shard_map/ppermute | solution.py:359
  82.4 1.3 %gradient.2 = (bf16[2,2,304,128]{3,2,1,0:T(8,128)(2,1)S(1)}, bf16[2,2,304,128]{3,2,1,0:T(8,128)(2,1)S(1)}) custom-call(s32[4]{0:T(128)S(1)} %pad_add_fusion.info_ref, bf16[4,256,256]{2,1,0:T(8,128)(2,1)S(1)} %all-to-all-done.ctx_ref.refs_0_, bf16[4,256,256]{2,1,0:T(8,128)(2,1)S(1)} %collective-permute-done.5.refs_1_, ...), custom_call_target="tpu_custom_call" | custom-call | flops 536870912 | bytes 3145728 | tf_op jit(solution)/shard_map/gradient/pallas_call | solution.py:270
  83.8 2.7 %collective-permute-start.19 = (bf16[1,1,256,128]{3,2,1,0:T(8,128)(2,1)S(1)}, bf16[1,1,256,128]{3,2,1,0:T(8,128)(2,1)S(1)}, u32[]{:S(2)}, u32[]{:S(2)}) collective-permute-start(bf16[1,1,256,128]{3,2,1,0:T(8,128)(2,1)S(1)} %get-tuple-element.58), channel_id=1, source_target_pairs={{0,16},{1,17},{2,18},{3,19},{4,20},{5,21},{6,22},{7,23},{8,24},{9,... | collective-permute-start | bytes 196616 | tf_op jit(solution)/shard_map/ppermute | solution.py:364
  86.5 1.5 %collective-permute-start.12 = (bf16[1,1,304,128]{3,2,1,0:T(8,128)(2,1)S(1)}, bf16[1,1,304,128]{3,2,1,0:T(8,128)(2,1)S(1)}, u32[]{:S(2)}, u32[]{:S(2)}) collective-permute-start(bf16[1,1,304,128]{3,2,1,0:T(8,128)(2,1)S(1)} %get-tuple-element.48), channel_id=1, source_target_pairs={{0,16},{1,17},{2,18},{3,19},{4,20},{5,21},{6,22},{7,23},{8,24},{9,... | collective-permute-start | bytes 233480 | tf_op jit(solution)/shard_map/ppermute | solution.py:364
  88.7 2.3 %collective-permute-start.14 = (bf16[1,1,304,128]{3,2,1,0:T(8,128)(2,1)S(1)}, bf16[1,1,304,128]{3,2,1,0:T(8,128)(2,1)S(1)}, u32[]{:S(2)}, u32[]{:S(2)}) collective-permute-start(bf16[1,1,304,128]{3,2,1,0:T(8,128)(2,1)S(1)} %get-tuple-element.50), channel_id=1, source_target_pairs={{0,18},{1,19},{2,16},{3,17},{4,22},{5,23},{6,20},{7,21},{8,26},{9,... | collective-permute-start | bytes 233480 | tf_op jit(solution)/shard_map/ppermute | solution.py:364
  91.6 2.3 %collective-permute-start.21 = (bf16[1,1,256,128]{3,2,1,0:T(8,128)(2,1)S(1)}, bf16[1,1,256,128]{3,2,1,0:T(8,128)(2,1)S(1)}, u32[]{:S(2)}, u32[]{:S(2)}) collective-permute-start(bf16[1,1,256,128]{3,2,1,0:T(8,128)(2,1)S(1)} %get-tuple-element.60), channel_id=1, source_target_pairs={{0,18},{1,19},{2,16},{3,17},{4,22},{5,23},{6,20},{7,21},{8,26},{9,... | collective-permute-start | bytes 196616 | tf_op jit(solution)/shard_map/ppermute | solution.py:364
  93.9 1.6 %collective-permute-done.20.refs_6_ = bf16[1,1,256,128]{3,2,1,0:T(8,128)(2,1)S(1)} collective-permute-done((bf16[1,1,256,128]{3,2,1,0:T(8,128)(2,1)S(1)}, bf16[1,1,256,128]{3,2,1,0:T(8,128)(2,1)S(1)}, u32[]{:S(2)}, u32[]{:S(2)}) %collective-permute-start.20) | collective-permute-done | bytes 65568 | tf_op jit(solution)/shard_map/ppermute | solution.py:364
  95.5 3.3 %collective-permute-done.21.refs_7_ = bf16[1,1,256,128]{3,2,1,0:T(8,128)(2,1)S(1)} collective-permute-done((bf16[1,1,256,128]{3,2,1,0:T(8,128)(2,1)S(1)}, bf16[1,1,256,128]{3,2,1,0:T(8,128)(2,1)S(1)}, u32[]{:S(2)}, u32[]{:S(2)}) %collective-permute-start.21) | collective-permute-done | bytes 65568 | tf_op jit(solution)/shard_map/ppermute | solution.py:364
  (44 shorter events, 12.5 us)
Async XLA Ops:
  0.6 13.9 %collective-permute-start.1 = (bf16[256,2048]{1,0:T(8,128)(2,1)}, bf16[256,2048]{1,0:T(8,128)(2,1)}, u32[]{:S(2)}, u32[]{:S(2)}) collective-permute-start(bf16[256,2048]{1,0:T(8,128)(2,1)} %bitcast.10), channel_id=1, source_target_pairs={{0,1},{1,0},{2,3},{3,2},{4,5},{5,4},{6,7},{7,6},{8,9},{9,8},{10,11... | collective-permute-start | bytes 3145736 | tf_op jit(solution)/shard_map/ppermute | solution.py:359
  2.2 12.4 %collective-permute-start = (bf16[256,768]{1,0:T(8,128)(2,1)S(1)}, bf16[256,768]{1,0:T(8,128)(2,1)S(1)}, u32[]{:S(2)}, u32[]{:S(2)}) collective-permute-start(bf16[256,768]{1,0:T(8,128)(2,1)S(1)} %slice.8), channel_id=1, source_target_pairs={{0,2},{1,3},{2,0},{3,1},{4,6},{5,7},{6,4},{7,5},{8,10},{9,11},{10,... | collective-permute-start | bytes 1179656 | tf_op jit(solution)/shard_map/ppermute | solution.py:359
  13.4 33.6 %copy-start.1 = (bf16[256,2048]{1,0:T(8,128)(2,1)S(1)}, bf16[256,2048]{1,0:T(8,128)(2,1)}, u32[]{:S(2)}) copy-start(bf16[256,2048]{1,0:T(8,128)(2,1)} %next_ref.1) | copy-start | bytes 3145732
  14.6 4.4 %collective-permute-start.2 = (bf16[256,768]{1,0:T(8,128)(2,1)S(1)}, bf16[256,768]{1,0:T(8,128)(2,1)S(1)}, u32[]{:S(2)}, u32[]{:S(2)}) collective-permute-start(bf16[256,768]{1,0:T(8,128)(2,1)S(1)} %collective-permute-done.refs_2_), channel_id=1, source_target_pairs={{0,1},{1,0},{2,3},{3,2},{4,5},{5,4},{6,7},{7,6},{8,9},{9,8},{10,11... | collective-permute-start | bytes 1179656 | tf_op jit(solution)/shard_map/ppermute | solution.py:359
  14.6 12.4 %all-to-all-start = ((bf16[4,256,256]{2,1,0:T(8,128)(2,1)}), bf16[4,256,256]{2,1,0:T(8,128)(2,1)S(1)}, u32[]{:S(2)}, u32[]{:S(2)}) async-start(bf16[4,256,256]{2,1,0:T(8,128)(2,1)} %attend.1), calls=%async_computation | async-start | bytes 1048576 | tf_op jit(solution)/shard_map/all_to_all | solution.py:411
  26.9 16.6 %collective-permute-start.3 = (bf16[256,1280]{1,0:T(8,128)(2,1)}, bf16[256,1280]{1,0:T(8,128)(2,1)S(1)}, u32[]{:S(2)}, u32[]{:S(2)}) collective-permute-start(bf16[256,1280]{1,0:T(8,128)(2,1)} %slice.9), channel_id=1, source_target_pairs={{0,2},{1,3},{2,0},{3,1},{4,6},{5,7},{6,4},{7,5},{8,10},{9,11},{10,... | collective-permute-start | bytes 1966088 | tf_op jit(solution)/shard_map/ppermute | solution.py:359
  43.5 3.5 %collective-permute-start.4 = (bf16[256,1280]{1,0:T(8,128)(2,1)S(1)}, bf16[256,1280]{1,0:T(8,128)(2,1)S(1)}, u32[]{:S(2)}, u32[]{:S(2)}) collective-permute-start(bf16[256,1280]{1,0:T(8,128)(2,1)S(1)} %collective-permute-done.3.refs_3_), channel_id=1, source_target_pairs={{0,1},{1,0},{2,3},{3,2},{4,5},{5,4},{6,7},{7,6},{8,9},{9,8},{10,11... | collective-permute-start | bytes 1966088 | tf_op jit(solution)/shard_map/ppermute | solution.py:359
  43.5 14.7 %collective-permute-start.5 = (bf16[4,256,256]{2,1,0:T(8,128)(2,1)S(1)}, bf16[4,256,256]{2,1,0:T(8,128)(2,1)S(1)}, u32[]{:S(2)}, u32[]{:S(2)}) collective-permute-start(bf16[4,256,256]{2,1,0:T(8,128)(2,1)S(1)} %all-to-all-done.ctx_ref.refs_0_), channel_id=1, source_target_pairs={{0,4},{4,0},{8,12},{12,8},{16,20},{20,16},{24,28},{28,24},{1,5},{5... | collective-permute-start | bytes 1572872 | tf_op jit(solution)/shard_map/ppermute | solution.py:359
  45.1 15.7 %collective-permute-start.6 = (bf16[4,256,256]{2,1,0:T(8,128)(2,1)S(1)}, bf16[4,256,256]{2,1,0:T(8,128)(2,1)S(1)}, u32[]{:S(2)}, u32[]{:S(2)}) collective-permute-start(bf16[4,256,256]{2,1,0:T(8,128)(2,1)S(1)} %all-to-all-done.ctx_ref.refs_0_), channel_id=1, source_target_pairs={{0,8},{4,12},{8,0},{12,4},{16,24},{20,28},{24,16},{28,20},{1,9},{5... | collective-permute-start | bytes 1572872 | tf_op jit(solution)/shard_map/ppermute | solution.py:359
  46.6 24.4 %collective-permute-start.7 = (bf16[4,256,256]{2,1,0:T(8,128)(2,1)S(1)}, bf16[4,256,256]{2,1,0:T(8,128)(2,1)S(1)}, u32[]{:S(2)}, u32[]{:S(2)}) collective-permute-start(bf16[4,256,256]{2,1,0:T(8,128)(2,1)S(1)} %all-to-all-done.ctx_ref.refs_0_), channel_id=1, source_target_pairs={{0,12},{4,8},{8,4},{12,0},{16,28},{20,24},{24,20},{28,16},{1,13},{... | collective-permute-start | bytes 1572872 | tf_op jit(solution)/shard_map/ppermute | solution.py:359
  54.1 18.4 %collective-permute-start.15 = (bf16[256,256]{1,0:T(8,128)(2,1)S(1)}, bf16[256,256]{1,0:T(8,128)(2,1)S(1)}, u32[]{:S(2)}, u32[]{:S(2)}) collective-permute-start(bf16[256,256]{1,0:T(8,128)(2,1)S(1)} %get-tuple-element.52), channel_id=1, source_target_pairs={{0,4},{4,0},{8,12},{12,8},{16,20},{20,16},{24,28},{28,24},{1,5},{5... | collective-permute-start | bytes 393224 | tf_op jit(solution)/shard_map/ppermute | solution.py:359
  55.7 18.5 %collective-permute-start.16 = (bf16[256,256]{1,0:T(8,128)(2,1)S(1)}, bf16[256,256]{1,0:T(8,128)(2,1)S(1)}, u32[]{:S(2)}, u32[]{:S(2)}) collective-permute-start(bf16[256,256]{1,0:T(8,128)(2,1)S(1)} %get-tuple-element.53), channel_id=1, source_target_pairs={{0,8},{4,12},{8,0},{12,4},{16,24},{20,28},{24,16},{28,20},{1,9},{5... | collective-permute-start | bytes 393224 | tf_op jit(solution)/shard_map/ppermute | solution.py:359
  58.2 18.5 %collective-permute-start.17 = (bf16[256,256]{1,0:T(8,128)(2,1)S(1)}, bf16[256,256]{1,0:T(8,128)(2,1)S(1)}, u32[]{:S(2)}, u32[]{:S(2)}) collective-permute-start(bf16[256,256]{1,0:T(8,128)(2,1)S(1)} %get-tuple-element.54), channel_id=1, source_target_pairs={{0,12},{4,8},{8,4},{12,0},{16,28},{20,24},{24,20},{28,16},{1,13},{... | collective-permute-start | bytes 393224 | tf_op jit(solution)/shard_map/ppermute | solution.py:359
  60.8 19.0 %collective-permute-start.10 = (bf16[288,256]{1,0:T(8,128)(2,1)S(1)}, bf16[288,256]{1,0:T(8,128)(2,1)S(1)}, u32[]{:S(2)}, u32[]{:S(2)}) collective-permute-start(bf16[288,256]{1,0:T(8,128)(2,1)S(1)} %get-tuple-element.44), channel_id=1, source_target_pairs={{0,12},{4,8},{8,4},{12,0},{16,28},{20,24},{24,20},{28,16},{1,13},{... | collective-permute-start | bytes 442376 | tf_op jit(solution)/shard_map/ppermute | solution.py:359
  71.0 10.4 %collective-permute-start.8 = (bf16[288,256]{1,0:T(8,128)(2,1)S(1)}, bf16[288,256]{1,0:T(8,128)(2,1)S(1)}, u32[]{:S(2)}, u32[]{:S(2)}) collective-permute-start(bf16[288,256]{1,0:T(8,128)(2,1)S(1)} %get-tuple-element.42), channel_id=1, source_target_pairs={{0,4},{4,0},{8,12},{12,8},{16,20},{20,16},{24,28},{28,24},{1,5},{5... | collective-permute-start | bytes 442376 | tf_op jit(solution)/shard_map/ppermute | solution.py:359
  72.6 9.8 %collective-permute-start.9 = (bf16[288,256]{1,0:T(8,128)(2,1)S(1)}, bf16[288,256]{1,0:T(8,128)(2,1)S(1)}, u32[]{:S(2)}, u32[]{:S(2)}) collective-permute-start(bf16[288,256]{1,0:T(8,128)(2,1)S(1)} %get-tuple-element.43), channel_id=1, source_target_pairs={{0,8},{4,12},{8,0},{12,4},{16,24},{20,28},{24,16},{28,20},{1,9},{5... | collective-permute-start | bytes 442376 | tf_op jit(solution)/shard_map/ppermute | solution.py:359
  78.0 5.7 %collective-permute-start.18 = (bf16[2,2,256,128]{3,2,1,0:T(8,128)(2,1)S(1)}, bf16[2,2,256,128]{3,2,1,0:T(8,128)(2,1)S(1)}, u32[]{:S(2)}, u32[]{:S(2)}) collective-permute-start(bf16[2,2,256,128]{3,2,1,0:T(8,128)(2,1)S(1)} %get-tuple-element.56), channel_id=1, source_target_pairs={{0,1},{1,0},{2,3},{3,2},{4,5},{5,4},{6,7},{7,6},{8,9},{9,8},{10,11... | collective-permute-start | bytes 786440 | tf_op jit(solution)/shard_map/ppermute | solution.py:359
  83.6 2.8 %collective-permute-start.11 = (bf16[2,2,304,128]{3,2,1,0:T(8,128)(2,1)S(1)}, bf16[2,2,304,128]{3,2,1,0:T(8,128)(2,1)S(1)}, u32[]{:S(2)}, u32[]{:S(2)}) collective-permute-start(bf16[2,2,304,128]{3,2,1,0:T(8,128)(2,1)S(1)} %get-tuple-element.46), channel_id=1, source_target_pairs={{0,1},{1,0},{2,3},{3,2},{4,5},{5,4},{6,7},{7,6},{8,9},{9,8},{10,11... | collective-permute-start | bytes 933896 | tf_op jit(solution)/shard_map/ppermute | solution.py:359
  83.8 7.8 %collective-permute-start.19 = (bf16[1,1,256,128]{3,2,1,0:T(8,128)(2,1)S(1)}, bf16[1,1,256,128]{3,2,1,0:T(8,128)(2,1)S(1)}, u32[]{:S(2)}, u32[]{:S(2)}) collective-permute-start(bf16[1,1,256,128]{3,2,1,0:T(8,128)(2,1)S(1)} %get-tuple-element.58), channel_id=1, source_target_pairs={{0,16},{1,17},{2,18},{3,19},{4,20},{5,21},{6,22},{7,23},{8,24},{9,... | collective-permute-start | bytes 196616 | tf_op jit(solution)/shard_map/ppermute | solution.py:364
  86.5 12.3 %collective-permute-start.12 = (bf16[1,1,304,128]{3,2,1,0:T(8,128)(2,1)S(1)}, bf16[1,1,304,128]{3,2,1,0:T(8,128)(2,1)S(1)}, u32[]{:S(2)}, u32[]{:S(2)}) collective-permute-start(bf16[1,1,304,128]{3,2,1,0:T(8,128)(2,1)S(1)} %get-tuple-element.48), channel_id=1, source_target_pairs={{0,16},{1,17},{2,18},{3,19},{4,20},{5,21},{6,22},{7,23},{8,24},{9,... | collective-permute-start | bytes 233480 | tf_op jit(solution)/shard_map/ppermute | solution.py:364
  88.0 10.8 %collective-permute-start.13 = (bf16[1,1,304,128]{3,2,1,0:T(8,128)(2,1)S(1)}, bf16[1,1,304,128]{3,2,1,0:T(8,128)(2,1)S(1)}, u32[]{:S(2)}, u32[]{:S(2)}) collective-permute-start(bf16[1,1,304,128]{3,2,1,0:T(8,128)(2,1)S(1)} %get-tuple-element.49), channel_id=1, source_target_pairs={{0,2},{1,3},{2,0},{3,1},{4,6},{5,7},{6,4},{7,5},{8,10},{9,11},{10,... | collective-permute-start | bytes 233480 | tf_op jit(solution)/shard_map/ppermute | solution.py:364
  88.7 10.1 %collective-permute-start.14 = (bf16[1,1,304,128]{3,2,1,0:T(8,128)(2,1)S(1)}, bf16[1,1,304,128]{3,2,1,0:T(8,128)(2,1)S(1)}, u32[]{:S(2)}, u32[]{:S(2)}) collective-permute-start(bf16[1,1,304,128]{3,2,1,0:T(8,128)(2,1)S(1)} %get-tuple-element.50), channel_id=1, source_target_pairs={{0,18},{1,19},{2,16},{3,17},{4,22},{5,23},{6,20},{7,21},{8,26},{9,... | collective-permute-start | bytes 233480 | tf_op jit(solution)/shard_map/ppermute | solution.py:364
  91.0 4.5 %collective-permute-start.20 = (bf16[1,1,256,128]{3,2,1,0:T(8,128)(2,1)S(1)}, bf16[1,1,256,128]{3,2,1,0:T(8,128)(2,1)S(1)}, u32[]{:S(2)}, u32[]{:S(2)}) collective-permute-start(bf16[1,1,256,128]{3,2,1,0:T(8,128)(2,1)S(1)} %get-tuple-element.59), channel_id=1, source_target_pairs={{0,2},{1,3},{2,0},{3,1},{4,6},{5,7},{6,4},{7,5},{8,10},{9,11},{10,... | collective-permute-start | bytes 196616 | tf_op jit(solution)/shard_map/ppermute | solution.py:364
  91.6 7.2 %collective-permute-start.21 = (bf16[1,1,256,128]{3,2,1,0:T(8,128)(2,1)S(1)}, bf16[1,1,256,128]{3,2,1,0:T(8,128)(2,1)S(1)}, u32[]{:S(2)}, u32[]{:S(2)}) collective-permute-start(bf16[1,1,256,128]{3,2,1,0:T(8,128)(2,1)S(1)} %get-tuple-element.60), channel_id=1, source_target_pairs={{0,18},{1,19},{2,16},{3,17},{4,22},{5,23},{6,20},{7,21},{8,26},{9,... | collective-permute-start | bytes 196616 | tf_op jit(solution)/shard_map/ppermute | solution.py:364
  (5 other events, 41.3 us)

commit v5 on v4

--- a/solution.py
+++ b/solution.py
@@ -90,8 +90,8 @@
     for n in counts:
         w_refs.append(refs[at : at + n])
         at += n
-    hidden_ref, grad_refs = refs[at], refs[at + 1 : -4]
-    turned_ref, joined_ref, square_ref, acc_ref = refs[-4:]
+    hidden_ref, grad_refs = refs[at], refs[at + 1 : -5]
+    turned_ref, joined_ref, square_ref, acc_ref, slope_ref = refs[-5:]
     rows, dout = joined_ref.shape
     me, group, length, votes = info_ref[0], info_ref[1], info_ref[2], info_ref[3]
     for m in range(n_tensor):
@@ -105,7 +105,6 @@
                     w = ref[:, c - first : c - first + COLS]
                 first += ref.shape[1]
             part = dot(turned_ref[m], w, ((1,), (0,)))
-            part = part.astype(BF).astype(F32)
             total = part if total is None else total + part
         joined_ref[:, c : c + COLS] = total
         sq = total * total
@@ -133,20 +132,19 @@
             predicted = normed * gain
             hidden_ref[at, cs] = predicted.astype(BF)
             misfit = predicted - next_ref[at, cs].astype(F32)
-            both = scaled * misfit * normed
-            acc_ref[:, cs] += both
+            grad = scaled * misfit
+            slope = grad * gain
+            acc_ref[:, cs] += grad * normed
+            slope_ref[:, cs] = slope
             sq = misfit * misfit
-            ln = both * gain
+            ln = slope * normed
             miss += sum(sq[:, i : i + 128] for i in range(0, 512, 128))
             lean += sum(ln[:, i : i + 128] for i in range(0, 512, 128))
             joined_ref[at, cs] = normed
         lean = jnp.sum(lean, axis=1, keepdims=True) * (1.0 / dout)
 
         def gradient_at(cs):
-            normed = joined_ref[at, cs]
-            gain = gain_ref[:, cs]
-            misfit = normed * gain - next_ref[at, cs].astype(F32)
-            return (inv * (scaled * misfit * gain - normed * lean)).astype(BF)
+            return (inv * (slope_ref[:, cs] - joined_ref[at, cs] * lean)).astype(BF)
 
         for j in range(chunks):
             for q in range(NEAR):
@@ -203,6 +201,7 @@
             pltpu.VMEM((rows, dout), F32),
             pltpu.VMEM((rows, 128), F32),
             pltpu.VMEM((ROWS, dout), F32),
+            pltpu.VMEM((ROWS, dout), F32),
         ],
         compiler_params=params(),
         cost_estimate=pl.CostEstimate(
@@ -235,7 +234,7 @@
 
 def grad_body(plan, dout, info_ref, *refs):
     n_dp, n_tensor, _, _, xor_far = plan
-    ctx_refs, g_refs, (keep_ref, send_ref) = refs[:NEAR], refs[NEAR : 2 * NEAR], refs[2 * NEAR :]
+    ctx_refs, g_refs, (keep_ref, send_ref) = refs[: NEAR + 1], refs[NEAR + 1 : -2], refs[-2:]
     n_y, n_far, tall, cw = keep_ref.shape
     feats, rows = ctx_refs[0].shape[1:]
     wide = n_far * cw
@@ -250,8 +249,9 @@
     for s, ref in ((1, send_ref), (0, keep_ref)):
         for a in range(n_y):
             m = (y ^ a if xor_far else a) * 2 + (core ^ s)
-            total = sum(dot(c[m], g[:rows, :], ((1,), (0,))) for c, g in zip(ctx_refs, g_refs))
-            total = total.astype(BF)
+            total = sum(dot(c[m], g[:rows, :], ((1,), (0,))) for c, g in zip(ctx_refs[:-2], g_refs))
+            last = [dot(c[m], g_refs[-1][:rows, :], ((1,), (0,))) for c in ctx_refs[-2:]]
+            total = (total + jnp.concatenate(last, 0)).astype(BF)
             for b in range(n_far):
                 ref[a, b, :feats, :] = total[:, b * cw : (b + 1) * cw]
                 if tall > feats:
@@ -269,7 +269,7 @@
     block = shape((n_tensor // 2, n_dp // NEAR, tall, cw))
     return pl.pallas_call(
         functools.partial(grad_body, plan, dout),
-        in_specs=[SM] + [VM] * (2 * NEAR),
+        in_specs=[SM] + [VM] * (2 * NEAR + 1),
         out_specs=[VM, VM],
         out_shape=[block, block],
         compiler_params=params(),
@@ -402,7 +402,7 @@
 
     weight = joining_weight[0]
     half = n_tensor // 2
-    cut = dout * 3 // 8 // COLS * COLS
+    cut = dout // 2
     first, second = weight[:, :cut], weight[:, cut:]
     first = swap(first, "tensor", n_tensor, half)
     beside = swap(weight, "tensor", n_tensor, 1)
@@ -412,7 +412,10 @@
     across = swap(first, "tensor", n_tensor, 1)
     across, second, ctx = lax.optimization_barrier((across, second, ctx))
     second = swap(second, "tensor", n_tensor, half)
-    ctxs = [ctx] + [swap(ctx, "dp", n_dp, q) for q in range(1, NEAR)]
+    beside_x, beside_z = (swap(ctx, "dp", n_dp, q) for q in (1, 2))
+    second, beside_x, beside_z = lax.optimization_barrier((second, beside_x, beside_z))
+    diagonal = [swap(beside_x[:, : width // 2], "dp", n_dp, 2), swap(beside_z[:, width // 2 :], "dp", n_dp, 1)]
+    ctxs = [ctx, beside_x, beside_z, *diagonal]
     held = {0: [weight], 1: [beside], half: [first, second]}
     held[half + 1] = [across, swap(second, "tensor", n_tensor, 1)]
     bit = half // 2

time: 100 us -> 90.3 us (0.903)
  waiting for transfers between devices: 47.9 us -> 34.7 us
  blocking collectives: 0 us -> 11.8 us
  starting transfers between devices: 29.9 us -> 24.1 us
  local copies, waits for them, and re-layouts: 4.02 us -> 2.31 us
    all_to_all x0 -> x1, blocking collectives: none -> 11.8 us  [on_device(): ctx = lax.all_to_all(context, 'tensor', 0, 0, tiled=True)]
    all_to_all x1 -> x0, waiting for transfers between devices: 7.97 us -> none  [on_device(): ctx = lax.all_to_all(context, 'tensor', 0, 0, tiled=True)]
    ppermute x16 -> x17, waiting for transfers between devices: 35 us -> 27.5 us  [swap(): return lax.ppermute(x, axis, [(i, i ^ mask) for i in range(n)])]
    all_to_all x1 -> x0, starting transfers between devices: 3.47 us -> none  [on_device(): ctx = lax.all_to_all(context, 'tensor', 0, 0, tiled=True)]
    ppermute x6, waiting for transfers between devices: 4.92 us -> 7.23 us  [swap_far(): lax.ppermute(x, ('dp', 'tensor'), [(i, i ^ mask) for i in range(n_dp * n_...]
    unnamed x12 -> x16, local copies, waits for them, and re-layouts: 2.1 us -> 0.04 us
    ppermute x16 -> x17, starting transfers between devices: 16.5 us -> 14.8 us  [swap(): return lax.ppermute(x, axis, [(i, i ^ mask) for i in range(n)])]
    slice x2 -> x1, local copies, waits for them, and re-layouts: 1.91 us -> 2.23 us  [on_device(): first, second = (weight[:, :cut], weight[:, cut:])]
  transfers between devices with their start and end apart: 23 -> 23, of which waited for: 11 -> 12; matrix products, arithmetic and copies ran while one was open for 2% -> 3% of each run, Pallas kernels for 15% -> 16%
where the time goes in v5:
time: 90.3 us; the launch traced here: 90 us
  waiting for transfers between devices  34.7 us (38%)
  starting transfers between devices  24.1 us (27%)
  Pallas kernels  14.9 us (17%)
  blocking collectives  11.8 us (13%)
  local copies, waits for them, and re-layouts  2.31 us (3%)
  between operations  2.1 us (2%)
    ppermute x17, waiting for transfers between devices, swap(): return lax.ppermute(x, axis, [(i, i ^ mask) for i in range(n)])  27.5 us
    ppermute x17, starting transfers between devices, swap(): return lax.ppermute(x, axis, [(i, i ^ mask) for i in range(n)])  14.8 us
    all_to_all x1, blocking collectives, on_device(): ctx = lax.all_to_all(context, 'tensor', 0, 0, tiled=True)  11.8 us
    ppermute x6, starting transfers between devices, swap_far(): lax.ppermute(x, ('dp', 'tensor'), [(i, i ^ mask) for i in range(n_dp * n_...  9.28 us
    ppermute x6, waiting for transfers between devices, swap_far(): lax.ppermute(x, ('dp', 'tensor'), [(i, i ^ mask) for i in range(n_dp * n_...  7.23 us
    pallas_call x1, Pallas kernels, join(): pl.pallas_call(functools.partial(join_body, plan, [len(w) for w in weight...  7.1 us
    pallas_call x1, Pallas kernels, attend(): pl.pallas_call(attend_body, grid=(heads,), in_specs=[SM, block, block, bl...  4.43 us
    pallas_call x2, Pallas kernels, gradient(): pl.pallas_call(functools.partial(grad_body, plan, dout), in_specs=[SM] +...  2.5 us
  transfers between devices with their start and end apart: 23, of which 12 were waited for; matrix products, arithmetic and copies ran while one was open for 3% of the time, Pallas kernels for 16%

profile of v5, /device:TPU:0, one launch (start us, length us, event | category | flops | bytes accessed | tf_op | source)
XLA Modules:
  0.0 90.0 jit_solution(15481249920336687246)
XLA Ops:
  1.2 2.2 %fusion = (bf16[256,1024]{1,0:T(8,128)(2,1)}, bf16[256,1024]{1,0:T(8,128)(2,1)}) fusion(bf16[256,2048]{1,0:T(8,128)(2,1)} %bitcast.11), kind=kLoop, calls=%fused_computation.1 | loop fusion | bytes 2097152 | tf_op jit(solution)/shard_map/slice | solution.py:406
  3.4 2.6 %collective-permute-start = (bf16[256,1024]{1,0:T(8,128)(2,1)}, bf16[256,1024]{1,0:T(8,128)(2,1)S(1)}, u32[]{:S(2)}, u32[]{:S(2)}) collective-permute-start(bf16[256,1024]{1,0:T(8,128)(2,1)} %get-tuple-element.71), channel_id=1, source_target_pairs={{0,2},{1,3},{2,0},{3,1},{4,6},{5,7},{6,4},{7,5},{8,10},{9,11},{10,... | collective-permute-start | bytes 1572872 | tf_op jit(solution)/shard_map/ppermute | solution.py:359
  7.5 4.4 %attend.1 = bf16[4,256,256]{2,1,0:T(8,128)(2,1)S(1)} custom-call(s32[4]{0:T(128)S(1)} %pad_add_fusion.info_ref, bf16[1024,256]{1,0:T(8,128)(2,1)S(1)} %bitcast.14, bf16[1024,256]{1,0:T(8,128)(2,1)S(1)} %bitcast.15, bf16[1024,256]{1,0:T(8,128)(2,1)S(1)} %bitcast.16), custom_call_target="tpu_custom_call" | custom-call | flops 1073741824 | bytes 2097152 | tf_op jit(solution)/shard_map/attend/pallas_call | solution.py:73
  11.9 6.8 %collective-permute-done.refs_2_ = bf16[256,1024]{1,0:T(8,128)(2,1)S(1)} collective-permute-done((bf16[256,1024]{1,0:T(8,128)(2,1)}, bf16[256,1024]{1,0:T(8,128)(2,1)S(1)}, u32[]{:S(2)}, u32[]{:S(2)}) %collective-permute-start) | collective-permute-done | bytes 524320 | tf_op jit(solution)/shard_map/ppermute | solution.py:359
  18.7 11.8 %all_to_all.5.ctx_ref.refs_0_ = bf16[4,256,256]{2,1,0:T(8,128)(2,1)S(1)} all-to-all(bf16[4,256,256]{2,1,0:T(8,128)(2,1)S(1)} %attend.1), channel_id=1, replica_groups=mesh['dp'=8,'tensor'=4] {'tensor'}, dimensions={0} | all-to-all | bytes 1048576 | tf_op jit(solution)/shard_map/all_to_all | solution.py:411
  30.5 1.5 %collective-permute-start.4 = (bf16[4,256,256]{2,1,0:T(8,128)(2,1)S(1)}, bf16[4,256,256]{2,1,0:T(8,128)(2,1)S(1)}, u32[]{:S(2)}, u32[]{:S(2)}) collective-permute-start(bf16[4,256,256]{2,1,0:T(8,128)(2,1)S(1)} %all_to_all.5.ctx_ref.refs_0_), channel_id=1, source_target_pairs={{0,4},{4,0},{8,12},{12,8},{16,20},{20,16},{24,28},{28,24},{1,5},{5... | collective-permute-start | bytes 1572872 | tf_op jit(solution)/shard_map/ppermute | solution.py:359
  32.0 1.6 %collective-permute-start.5 = (bf16[4,256,256]{2,1,0:T(8,128)(2,1)S(1)}, bf16[4,256,256]{2,1,0:T(8,128)(2,1)S(1)}, u32[]{:S(2)}, u32[]{:S(2)}) collective-permute-start(bf16[4,256,256]{2,1,0:T(8,128)(2,1)S(1)} %all_to_all.5.ctx_ref.refs_0_), channel_id=1, source_target_pairs={{0,8},{4,12},{8,0},{12,4},{16,24},{20,28},{24,16},{28,20},{1,9},{5... | collective-permute-start | bytes 1572872 | tf_op jit(solution)/shard_map/ppermute | solution.py:359
  34.0 9.9 %collective-permute-done.4.refs_1_ = bf16[4,256,256]{2,1,0:T(8,128)(2,1)S(1)} collective-permute-done((bf16[4,256,256]{2,1,0:T(8,128)(2,1)S(1)}, bf16[4,256,256]{2,1,0:T(8,128)(2,1)S(1)}, u32[]{:S(2)}, u32[]{:S(2)}) %collective-permute-start.4) | collective-permute-done | bytes 524320 | tf_op jit(solution)/shard_map/ppermute | solution.py:359
  43.8 1.2 %collective-permute-done.5.refs_2_ = bf16[4,256,256]{2,1,0:T(8,128)(2,1)S(1)} collective-permute-done((bf16[4,256,256]{2,1,0:T(8,128)(2,1)S(1)}, bf16[4,256,256]{2,1,0:T(8,128)(2,1)S(1)}, u32[]{:S(2)}, u32[]{:S(2)}) %collective-permute-start.5) | collective-permute-done | bytes 524320 | tf_op jit(solution)/shard_map/ppermute | solution.py:359
  45.1 1.3 %collective-permute-done.3.refs_3_ = bf16[256,1024]{1,0:T(8,128)(2,1)S(1)} collective-permute-done((bf16[256,1024]{1,0:T(8,128)(2,1)S(1)}, bf16[256,1024]{1,0:T(8,128)(2,1)S(1)}, u32[]{:S(2)}, u32[]{:S(2)}) %collective-permute-start.3) | collective-permute-done | bytes 524320 | tf_op jit(solution)/shard_map/ppermute | solution.py:359
  48.3 7.1 %join.1 = (bf16[256,2048]{1,0:T(8,128)(2,1)}, bf16[288,256]{1,0:T(8,128)(2,1)S(1)}, bf16[288,256]{1,0:T(8,128)(2,1)S(1)}, bf16[288,256]{1,0:T(8,128)(2,1)S(1)}, ...) custom-call(s32[4]{0:T(128)S(1)} %pad_add_fusion.info_ref, ...), custom_call_target="tpu_custom_call" | custom-call | flops 1073741824 | bytes 7340032 | tf_op jit(solution)/shard_map/join/pallas_call | solution.py:194
  56.2 1.6 %collective-permute-start.17 = (bf16[256,256]{1,0:T(8,128)(2,1)S(1)}, bf16[256,256]{1,0:T(8,128)(2,1)S(1)}, u32[]{:S(2)}, u32[]{:S(2)}) collective-permute-start(bf16[256,256]{1,0:T(8,128)(2,1)S(1)} %get-tuple-element.59), channel_id=1, source_target_pairs={{0,8},{4,12},{8,0},{12,4},{16,24},{20,28},{24,16},{28,20},{1,9},{5... | collective-permute-start | bytes 393224 | tf_op jit(solution)/shard_map/ppermute | solution.py:359
  59.7 1.4 %collective-permute-start.11 = (bf16[288,256]{1,0:T(8,128)(2,1)S(1)}, bf16[288,256]{1,0:T(8,128)(2,1)S(1)}, u32[]{:S(2)}, u32[]{:S(2)}) collective-permute-start(bf16[288,256]{1,0:T(8,128)(2,1)S(1)} %get-tuple-element.50), channel_id=1, source_target_pairs={{0,12},{4,8},{8,4},{12,0},{16,28},{20,24},{24,20},{28,16},{1,13},{... | collective-permute-start | bytes 442376 | tf_op jit(solution)/shard_map/ppermute | solution.py:359
  61.1 1.2 %collective-permute-start.9 = (bf16[288,256]{1,0:T(8,128)(2,1)S(1)}, bf16[288,256]{1,0:T(8,128)(2,1)S(1)}, u32[]{:S(2)}, u32[]{:S(2)}) collective-permute-start(bf16[288,256]{1,0:T(8,128)(2,1)S(1)} %get-tuple-element.48), channel_id=1, source_target_pairs={{0,4},{4,0},{8,12},{12,8},{16,20},{20,16},{24,28},{28,24},{1,5},{5... | collective-permute-start | bytes 442376 | tf_op jit(solution)/shard_map/ppermute | solution.py:359
  62.6 3.5 %collective-permute-done.18.refs_8_ = bf16[256,256]{1,0:T(8,128)(2,1)S(1)} collective-permute-done((bf16[256,256]{1,0:T(8,128)(2,1)S(1)}, bf16[256,256]{1,0:T(8,128)(2,1)S(1)}, u32[]{:S(2)}, u32[]{:S(2)}) %collective-permute-start.18) | collective-permute-done | bytes 131104 | tf_op jit(solution)/shard_map/ppermute | solution.py:359
  66.0 1.2 %gradient.3 = (bf16[2,2,256,128]{3,2,1,0:T(8,128)(2,1)S(1)}, bf16[2,2,256,128]{3,2,1,0:T(8,128)(2,1)S(1)}) custom-call(s32[4]{0:T(128)S(1)} %pad_add_fusion.info_ref, bf16[4,256,256]{2,1,0:T(8,128)(2,1)S(1)} %all_to_all.5.ctx_ref.refs_0_, bf16[4,256,256]{2,1,0:T(8,128)(2,1)S(1)} %collective-permute-done.4.refs_1_, ...), custom_call_target="tpu_custom_call" | custom-call | flops 536870912 | bytes 3145728 | tf_op jit(solution)/shard_map/gradient/pallas_call | solution.py:270
  68.5 2.7 %collective-permute-done.11.refs_8_ = bf16[288,256]{1,0:T(8,128)(2,1)S(1)} collective-permute-done((bf16[288,256]{1,0:T(8,128)(2,1)S(1)}, bf16[288,256]{1,0:T(8,128)(2,1)S(1)}, u32[]{:S(2)}, u32[]{:S(2)}) %collective-permute-start.11) | collective-permute-done | bytes 147488 | tf_op jit(solution)/shard_map/ppermute | solution.py:359
  71.2 1.3 %gradient.2 = (bf16[2,2,304,128]{3,2,1,0:T(8,128)(2,1)S(1)}, bf16[2,2,304,128]{3,2,1,0:T(8,128)(2,1)S(1)}) custom-call(s32[4]{0:T(128)S(1)} %pad_add_fusion.info_ref, bf16[4,256,256]{2,1,0:T(8,128)(2,1)S(1)} %all_to_all.5.ctx_ref.refs_0_, bf16[4,256,256]{2,1,0:T(8,128)(2,1)S(1)} %collective-permute-done.4.refs_1_, ...), custom_call_target="tpu_custom_call" | custom-call | flops 536870912 | bytes 3145728 | tf_op jit(solution)/shard_map/gradient/pallas_call | solution.py:270
  72.6 2.6 %collective-permute-start.20 = (bf16[1,1,256,128]{3,2,1,0:T(8,128)(2,1)S(1)}, bf16[1,1,256,128]{3,2,1,0:T(8,128)(2,1)S(1)}, u32[]{:S(2)}, u32[]{:S(2)}) collective-permute-start(bf16[1,1,256,128]{3,2,1,0:T(8,128)(2,1)S(1)} %get-tuple-element.64), channel_id=1, source_target_pairs={{0,16},{1,17},{2,18},{3,19},{4,20},{5,21},{6,22},{7,23},{8,24},{9,... | collective-permute-start | bytes 196616 | tf_op jit(solution)/shard_map/ppermute | solution.py:364
  75.4 1.5 %collective-permute-start.13 = (bf16[1,1,304,128]{3,2,1,0:T(8,128)(2,1)S(1)}, bf16[1,1,304,128]{3,2,1,0:T(8,128)(2,1)S(1)}, u32[]{:S(2)}, u32[]{:S(2)}) collective-permute-start(bf16[1,1,304,128]{3,2,1,0:T(8,128)(2,1)S(1)} %get-tuple-element.54), channel_id=1, source_target_pairs={{0,16},{1,17},{2,18},{3,19},{4,20},{5,21},{6,22},{7,23},{8,24},{9,... | collective-permute-start | bytes 233480 | tf_op jit(solution)/shard_map/ppermute | solution.py:364
  77.7 2.1 %collective-permute-start.15 = (bf16[1,1,304,128]{3,2,1,0:T(8,128)(2,1)S(1)}, bf16[1,1,304,128]{3,2,1,0:T(8,128)(2,1)S(1)}, u32[]{:S(2)}, u32[]{:S(2)}) collective-permute-start(bf16[1,1,304,128]{3,2,1,0:T(8,128)(2,1)S(1)} %get-tuple-element.56), channel_id=1, source_target_pairs={{0,18},{1,19},{2,16},{3,17},{4,22},{5,23},{6,20},{7,21},{8,26},{9,... | collective-permute-start | bytes 233480 | tf_op jit(solution)/shard_map/ppermute | solution.py:364
  81.4 1.4 %collective-permute-start.22 = (bf16[1,1,256,128]{3,2,1,0:T(8,128)(2,1)S(1)}, bf16[1,1,256,128]{3,2,1,0:T(8,128)(2,1)S(1)}, u32[]{:S(2)}, u32[]{:S(2)}) collective-permute-start(bf16[1,1,256,128]{3,2,1,0:T(8,128)(2,1)S(1)} %get-tuple-element.66), channel_id=1, source_target_pairs={{0,18},{1,19},{2,16},{3,17},{4,22},{5,23},{6,20},{7,21},{8,26},{9,... | collective-permute-start | bytes 196616 | tf_op jit(solution)/shard_map/ppermute | solution.py:364
  82.7 1.4 %collective-permute-done.21.refs_6_ = bf16[1,1,256,128]{3,2,1,0:T(8,128)(2,1)S(1)} collective-permute-done((bf16[1,1,256,128]{3,2,1,0:T(8,128)(2,1)S(1)}, bf16[1,1,256,128]{3,2,1,0:T(8,128)(2,1)S(1)}, u32[]{:S(2)}, u32[]{:S(2)}) %collective-permute-start.21) | collective-permute-done | bytes 65568 | tf_op jit(solution)/shard_map/ppermute | solution.py:364
  84.1 5.1 %collective-permute-done.22.refs_7_ = bf16[1,1,256,128]{3,2,1,0:T(8,128)(2,1)S(1)} collective-permute-done((bf16[1,1,256,128]{3,2,1,0:T(8,128)(2,1)S(1)}, bf16[1,1,256,128]{3,2,1,0:T(8,128)(2,1)S(1)}, u32[]{:S(2)}, u32[]{:S(2)}) %collective-permute-start.22) | collective-permute-done | bytes 65568 | tf_op jit(solution)/shard_map/ppermute | solution.py:364
  (50 shorter events, 10.5 us)
Async XLA Ops:
  0.7 18.1 %collective-permute-start.1 = (bf16[256,2048]{1,0:T(8,128)(2,1)}, bf16[256,2048]{1,0:T(8,128)(2,1)S(1)}, u32[]{:S(2)}, u32[]{:S(2)}) collective-permute-start(bf16[256,2048]{1,0:T(8,128)(2,1)} %bitcast.10), channel_id=1, source_target_pairs={{0,1},{1,0},{2,3},{3,2},{4,5},{5,4},{6,7},{7,6},{8,9},{9,8},{10,11... | collective-permute-start | bytes 3145736 | tf_op jit(solution)/shard_map/ppermute | solution.py:359
  3.4 15.3 %collective-permute-start = (bf16[256,1024]{1,0:T(8,128)(2,1)}, bf16[256,1024]{1,0:T(8,128)(2,1)S(1)}, u32[]{:S(2)}, u32[]{:S(2)}) collective-permute-start(bf16[256,1024]{1,0:T(8,128)(2,1)} %get-tuple-element.71), channel_id=1, source_target_pairs={{0,2},{1,3},{2,0},{3,1},{4,6},{5,7},{6,4},{7,5},{8,10},{9,11},{10,... | collective-permute-start | bytes 1572872 | tf_op jit(solution)/shard_map/ppermute | solution.py:359
  7.4 40.8 %copy-start.2 = (f32[2048]{0:T(1024)S(1)}, f32[2048]{0:T(1024)}, u32[]{:S(2)}) copy-start(f32[2048]{0:T(1024)} %param.12) | copy-start | bytes 24580
  18.7 11.8 %collective-permute-start.2 = (bf16[256,1024]{1,0:T(8,128)(2,1)S(1)}, bf16[256,1024]{1,0:T(8,128)(2,1)S(1)}, u32[]{:S(2)}, u32[]{:S(2)}) collective-permute-start(bf16[256,1024]{1,0:T(8,128)(2,1)S(1)} %collective-permute-done.refs_2_), channel_id=1, source_target_pairs={{0,1},{1,0},{2,3},{3,2},{4,5},{5,4},{6,7},{7,6},{8,9},{9,8},{10,11... | collective-permute-start | bytes 1572872 | tf_op jit(solution)/shard_map/ppermute | solution.py:359
  30.5 13.3 %collective-permute-start.4 = (bf16[4,256,256]{2,1,0:T(8,128)(2,1)S(1)}, bf16[4,256,256]{2,1,0:T(8,128)(2,1)S(1)}, u32[]{:S(2)}, u32[]{:S(2)}) collective-permute-start(bf16[4,256,256]{2,1,0:T(8,128)(2,1)S(1)} %all_to_all.5.ctx_ref.refs_0_), channel_id=1, source_target_pairs={{0,4},{4,0},{8,12},{12,8},{16,20},{20,16},{24,28},{28,24},{1,5},{5... | collective-permute-start | bytes 1572872 | tf_op jit(solution)/shard_map/ppermute | solution.py:359
  32.0 13.0 %collective-permute-start.5 = (bf16[4,256,256]{2,1,0:T(8,128)(2,1)S(1)}, bf16[4,256,256]{2,1,0:T(8,128)(2,1)S(1)}, u32[]{:S(2)}, u32[]{:S(2)}) collective-permute-start(bf16[4,256,256]{2,1,0:T(8,128)(2,1)S(1)} %all_to_all.5.ctx_ref.refs_0_), channel_id=1, source_target_pairs={{0,8},{4,12},{8,0},{12,4},{16,24},{20,28},{24,16},{28,20},{1,9},{5... | collective-permute-start | bytes 1572872 | tf_op jit(solution)/shard_map/ppermute | solution.py:359
  33.6 12.7 %collective-permute-start.3 = (bf16[256,1024]{1,0:T(8,128)(2,1)S(1)}, bf16[256,1024]{1,0:T(8,128)(2,1)S(1)}, u32[]{:S(2)}, u32[]{:S(2)}) collective-permute-start(bf16[256,1024]{1,0:T(8,128)(2,1)S(1)} %copy-done.7), channel_id=1, source_target_pairs={{0,2},{1,3},{2,0},{3,1},{4,6},{5,7},{6,4},{7,5},{8,10},{9,11},{10,... | collective-permute-start | bytes 1572872 | tf_op jit(solution)/shard_map/ppermute | solution.py:359
  46.4 1.9 %collective-permute-start.6 = (bf16[256,1024]{1,0:T(8,128)(2,1)S(1)}, bf16[256,1024]{1,0:T(8,128)(2,1)S(1)}, u32[]{:S(2)}, u32[]{:S(2)}) collective-permute-start(bf16[256,1024]{1,0:T(8,128)(2,1)S(1)} %collective-permute-done.3.refs_3_), channel_id=1, source_target_pairs={{0,1},{1,0},{2,3},{3,2},{4,5},{5,4},{6,7},{7,6},{8,9},{9,8},{10,11... | collective-permute-start | bytes 1572872 | tf_op jit(solution)/shard_map/ppermute | solution.py:359
  46.4 12.5 %collective-permute-start.7 = (bf16[4,128,256]{2,1,0:T(8,128)(2,1)S(1)}, bf16[4,128,256]{2,1,0:T(8,128)(2,1)S(1)}, u32[]{:S(2)}, u32[]{:S(2)}) collective-permute-start(bf16[4,128,256]{2,1,0:T(8,128)(2,1)S(1)} %slice.14), channel_id=1, source_target_pairs={{0,8},{4,12},{8,0},{12,4},{16,24},{20,28},{24,16},{28,20},{1,9},{5... | collective-permute-start | bytes 786440 | tf_op jit(solution)/shard_map/ppermute | solution.py:359
  46.9 12.8 %collective-permute-start.8 = (bf16[4,128,256]{2,1,0:T(8,128)(2,1)S(1)}, bf16[4,128,256]{2,1,0:T(8,128)(2,1)S(1)}, u32[]{:S(2)}, u32[]{:S(2)}) collective-permute-start(bf16[4,128,256]{2,1,0:T(8,128)(2,1)S(1)} %slice.15), channel_id=1, source_target_pairs={{0,4},{4,0},{8,12},{12,8},{16,20},{20,16},{24,28},{28,24},{1,5},{5... | collective-permute-start | bytes 786440 | tf_op jit(solution)/shard_map/ppermute | solution.py:359
  55.4 5.7 %collective-permute-start.16 = (bf16[256,256]{1,0:T(8,128)(2,1)S(1)}, bf16[256,256]{1,0:T(8,128)(2,1)S(1)}, u32[]{:S(2)}, u32[]{:S(2)}) collective-permute-start(bf16[256,256]{1,0:T(8,128)(2,1)S(1)} %get-tuple-element.58), channel_id=1, source_target_pairs={{0,4},{4,0},{8,12},{12,8},{16,20},{20,16},{24,28},{28,24},{1,5},{5... | collective-permute-start | bytes 393224 | tf_op jit(solution)/shard_map/ppermute | solution.py:359
  56.2 6.4 %collective-permute-start.17 = (bf16[256,256]{1,0:T(8,128)(2,1)S(1)}, bf16[256,256]{1,0:T(8,128)(2,1)S(1)}, u32[]{:S(2)}, u32[]{:S(2)}) collective-permute-start(bf16[256,256]{1,0:T(8,128)(2,1)S(1)} %get-tuple-element.59), channel_id=1, source_target_pairs={{0,8},{4,12},{8,0},{12,4},{16,24},{20,28},{24,16},{28,20},{1,9},{5... | collective-permute-start | bytes 393224 | tf_op jit(solution)/shard_map/ppermute | solution.py:359
  57.7 8.3 %collective-permute-start.18 = (bf16[256,256]{1,0:T(8,128)(2,1)S(1)}, bf16[256,256]{1,0:T(8,128)(2,1)S(1)}, u32[]{:S(2)}, u32[]{:S(2)}) collective-permute-start(bf16[256,256]{1,0:T(8,128)(2,1)S(1)} %get-tuple-element.60), channel_id=1, source_target_pairs={{0,12},{4,8},{8,4},{12,0},{16,28},{20,24},{24,20},{28,16},{1,13},{... | collective-permute-start | bytes 393224 | tf_op jit(solution)/shard_map/ppermute | solution.py:359
  58.9 9.7 %collective-permute-start.10 = (bf16[288,256]{1,0:T(8,128)(2,1)S(1)}, bf16[288,256]{1,0:T(8,128)(2,1)S(1)}, u32[]{:S(2)}, u32[]{:S(2)}) collective-permute-start(bf16[288,256]{1,0:T(8,128)(2,1)S(1)} %get-tuple-element.49), channel_id=1, source_target_pairs={{0,8},{4,12},{8,0},{12,4},{16,24},{20,28},{24,16},{28,20},{1,9},{5... | collective-permute-start | bytes 442376 | tf_op jit(solution)/shard_map/ppermute | solution.py:359
  59.7 11.5 %collective-permute-start.11 = (bf16[288,256]{1,0:T(8,128)(2,1)S(1)}, bf16[288,256]{1,0:T(8,128)(2,1)S(1)}, u32[]{:S(2)}, u32[]{:S(2)}) collective-permute-start(bf16[288,256]{1,0:T(8,128)(2,1)S(1)} %get-tuple-element.50), channel_id=1, source_target_pairs={{0,12},{4,8},{8,4},{12,0},{16,28},{20,24},{24,20},{28,16},{1,13},{... | collective-permute-start | bytes 442376 | tf_op jit(solution)/shard_map/ppermute | solution.py:359
  61.1 10.1 %collective-permute-start.9 = (bf16[288,256]{1,0:T(8,128)(2,1)S(1)}, bf16[288,256]{1,0:T(8,128)(2,1)S(1)}, u32[]{:S(2)}, u32[]{:S(2)}) collective-permute-start(bf16[288,256]{1,0:T(8,128)(2,1)S(1)} %get-tuple-element.48), channel_id=1, source_target_pairs={{0,4},{4,0},{8,12},{12,8},{16,20},{20,16},{24,28},{28,24},{1,5},{5... | collective-permute-start | bytes 442376 | tf_op jit(solution)/shard_map/ppermute | solution.py:359
  67.3 5.3 %collective-permute-start.19 = (bf16[2,2,256,128]{3,2,1,0:T(8,128)(2,1)S(1)}, bf16[2,2,256,128]{3,2,1,0:T(8,128)(2,1)S(1)}, u32[]{:S(2)}, u32[]{:S(2)}) collective-permute-start(bf16[2,2,256,128]{3,2,1,0:T(8,128)(2,1)S(1)} %get-tuple-element.62), channel_id=1, source_target_pairs={{0,1},{1,0},{2,3},{3,2},{4,5},{5,4},{6,7},{7,6},{8,9},{9,8},{10,11... | collective-permute-start | bytes 786440 | tf_op jit(solution)/shard_map/ppermute | solution.py:359
  72.5 2.8 %collective-permute-start.12 = (bf16[2,2,304,128]{3,2,1,0:T(8,128)(2,1)S(1)}, bf16[2,2,304,128]{3,2,1,0:T(8,128)(2,1)S(1)}, u32[]{:S(2)}, u32[]{:S(2)}) collective-permute-start(bf16[2,2,304,128]{3,2,1,0:T(8,128)(2,1)S(1)} %get-tuple-element.52), channel_id=1, source_target_pairs={{0,1},{1,0},{2,3},{3,2},{4,5},{5,4},{6,7},{7,6},{8,9},{9,8},{10,11... | collective-permute-start | bytes 933896 | tf_op jit(solution)/shard_map/ppermute | solution.py:359
  72.6 8.7 %collective-permute-start.20 = (bf16[1,1,256,128]{3,2,1,0:T(8,128)(2,1)S(1)}, bf16[1,1,256,128]{3,2,1,0:T(8,128)(2,1)S(1)}, u32[]{:S(2)}, u32[]{:S(2)}) collective-permute-start(bf16[1,1,256,128]{3,2,1,0:T(8,128)(2,1)S(1)} %get-tuple-element.64), channel_id=1, source_target_pairs={{0,16},{1,17},{2,18},{3,19},{4,20},{5,21},{6,22},{7,23},{8,24},{9,... | collective-permute-start | bytes 196616 | tf_op jit(solution)/shard_map/ppermute | solution.py:364
  75.4 13.9 %collective-permute-start.13 = (bf16[1,1,304,128]{3,2,1,0:T(8,128)(2,1)S(1)}, bf16[1,1,304,128]{3,2,1,0:T(8,128)(2,1)S(1)}, u32[]{:S(2)}, u32[]{:S(2)}) collective-permute-start(bf16[1,1,304,128]{3,2,1,0:T(8,128)(2,1)S(1)} %get-tuple-element.54), channel_id=1, source_target_pairs={{0,16},{1,17},{2,18},{3,19},{4,20},{5,21},{6,22},{7,23},{8,24},{9,... | collective-permute-start | bytes 233480 | tf_op jit(solution)/shard_map/ppermute | solution.py:364
  76.9 12.4 %collective-permute-start.14 = (bf16[1,1,304,128]{3,2,1,0:T(8,128)(2,1)S(1)}, bf16[1,1,304,128]{3,2,1,0:T(8,128)(2,1)S(1)}, u32[]{:S(2)}, u32[]{:S(2)}) collective-permute-start(bf16[1,1,304,128]{3,2,1,0:T(8,128)(2,1)S(1)} %get-tuple-element.55), channel_id=1, source_target_pairs={{0,2},{1,3},{2,0},{3,1},{4,6},{5,7},{6,4},{7,5},{8,10},{9,11},{10,... | collective-permute-start | bytes 233480 | tf_op jit(solution)/shard_map/ppermute | solution.py:364
  77.7 11.5 %collective-permute-start.15 = (bf16[1,1,304,128]{3,2,1,0:T(8,128)(2,1)S(1)}, bf16[1,1,304,128]{3,2,1,0:T(8,128)(2,1)S(1)}, u32[]{:S(2)}, u32[]{:S(2)}) collective-permute-start(bf16[1,1,304,128]{3,2,1,0:T(8,128)(2,1)S(1)} %get-tuple-element.56), channel_id=1, source_target_pairs={{0,18},{1,19},{2,16},{3,17},{4,22},{5,23},{6,20},{7,21},{8,26},{9,... | collective-permute-start | bytes 233480 | tf_op jit(solution)/shard_map/ppermute | solution.py:364
  79.8 4.3 %collective-permute-start.21 = (bf16[1,1,256,128]{3,2,1,0:T(8,128)(2,1)S(1)}, bf16[1,1,256,128]{3,2,1,0:T(8,128)(2,1)S(1)}, u32[]{:S(2)}, u32[]{:S(2)}) collective-permute-start(bf16[1,1,256,128]{3,2,1,0:T(8,128)(2,1)S(1)} %get-tuple-element.65), channel_id=1, source_target_pairs={{0,2},{1,3},{2,0},{3,1},{4,6},{5,7},{6,4},{7,5},{8,10},{9,11},{10,... | collective-permute-start | bytes 196616 | tf_op jit(solution)/shard_map/ppermute | solution.py:364
  81.4 7.9 %collective-permute-start.22 = (bf16[1,1,256,128]{3,2,1,0:T(8,128)(2,1)S(1)}, bf16[1,1,256,128]{3,2,1,0:T(8,128)(2,1)S(1)}, u32[]{:S(2)}, u32[]{:S(2)}) collective-permute-start(bf16[1,1,256,128]{3,2,1,0:T(8,128)(2,1)S(1)} %get-tuple-element.66), channel_id=1, source_target_pairs={{0,18},{1,19},{2,16},{3,17},{4,22},{5,23},{6,20},{7,21},{8,26},{9,... | collective-permute-start | bytes 196616 | tf_op jit(solution)/shard_map/ppermute | solution.py:364
  (7 other events, 147.4 us)

commit v6 on v5

--- a/solution.py
+++ b/solution.py
@@ -9,8 +9,8 @@
 from jax.sharding import PartitionSpec as P
 
 HD = 128
-QB = 256
-ROWS = 16
+QB = 128
+ROWS = 128
 COLS = 256
 NEAR = 4
 STAT_ROWS = 32
@@ -48,33 +48,35 @@
     rows = o_ref.shape[2]
     rate = math.log2(math.e) / math.sqrt(HD)
     length = info_ref[2]
-    for i in range(seq // QB):
-        keys = (i + 1) * QB
-        scores = dot(q_ref[i * QB : keys, :], k_ref[:keys, :], ((1,), (1,)))
-        col = lax.broadcasted_iota(jnp.int32, (1, keys), 1)
-        scores = scores + jnp.where(col < length, 0.0, neg_large)
-        r = lax.broadcasted_iota(jnp.int32, (QB, QB), 0)
-        c = lax.broadcasted_iota(jnp.int32, (QB, QB), 1)
-        last = jnp.where(c <= r, scores[:, keys - QB :], neg_large)
-        scores = last if i == 0 else jnp.concatenate([scores[:, : keys - QB], last], 1)
-        peak = jnp.max(scores, axis=1, keepdims=True)
-        e = jnp.exp2((scores - peak) * rate)
-        total = jnp.sum(e, axis=1, keepdims=True)
-        out = dot(e.astype(BF), v_ref[:keys, :], ((1,), (0,))) / total
-        out = out.T.astype(BF)
-        for n in range(QB // rows):
-            o_ref[i * (QB // rows) + n] = out[:, n * rows : (n + 1) * rows]
+    key = lax.broadcasted_iota(jnp.int32, (seq, 1), 0)
+    hide = jnp.where(key < length, 0.0, neg_large)
+    r = lax.broadcasted_iota(jnp.int32, (QB, QB), 0)
+    c = lax.broadcasted_iota(jnp.int32, (QB, QB), 1)
+    for h in range(q_ref.shape[1] // HD):
+        at = slice(h * HD, (h + 1) * HD)
+        q_t, v_t = q_ref[:, at].T, v_ref[:, at].T
+        for i in range(seq // QB):
+            keys = (i + 1) * QB
+            scores = dot(k_ref[:keys, at], q_t[:, i * QB : keys], ((1,), (0,))) + hide[:keys]
+            last = jnp.where(r <= c, scores[keys - QB :], neg_large)
+            scores = last if i == 0 else jnp.concatenate([scores[: keys - QB], last], 0)
+            peak = jnp.max(scores, axis=0, keepdims=True)
+            e = jnp.exp2((scores - peak) * rate)
+            total = jnp.sum(e, axis=0, keepdims=True)
+            out = (dot(v_t[:, :keys], e.astype(BF), ((1,), (0,))) / total).astype(BF)
+            for n in range(0, QB, min(rows, QB)):
+                block, first = divmod(i * QB + n, rows)
+                o_ref[block, at, first : first + min(rows, QB)] = out[:, n : n + rows]
 
 
 def attend(info, q, k, v, rows):
     seq, width = q.shape
     heads = width // HD
-    block = pl.BlockSpec((seq, HD), lambda h: (0, h))
+    block = VM
     return pl.pallas_call(
         attend_body,
-        grid=(heads,),
-        in_specs=[SM, block, block, block],
-        out_specs=pl.BlockSpec((seq // rows, HD, rows), lambda h: (0, h, 0)),
+                in_specs=[SM, block, block, block],
+        out_specs=VM,
         out_shape=shape((seq // rows, width, rows)),
         compiler_params=params(),
         cost_estimate=pl.CostEstimate(
@@ -96,24 +98,29 @@
     me, group, length, votes = info_ref[0], info_ref[1], info_ref[2], info_ref[3]
     for m in range(n_tensor):
         turned_ref[m] = ctx_ref[me ^ m].T
-    for c in range(0, dout, COLS):
+    near, far = group % NEAR, group // NEAR
+    columns = [(c, 0, c) for c in range(0, dout, COLS)]
+    if xor_far:
+        cut, spare = w_refs[-1][0].shape[1], w_refs[-1][2].shape[1]
+        own, other = near % 2 * cut, (1 - near % 2) * cut
+        columns = [(pl.multiple_of(own + c, COLS), 0, c) for c in range(0, cut, COLS)]
+        columns += [(pl.multiple_of(other + c, COLS), 1, c) for c in range(0, cut, COLS)]
+        columns += [(2 * cut + c, 2, c) for c in range(0, spare, COLS)]
+    for step, (start, piece, first) in enumerate(columns):
+        to = pl.ds(start, COLS)
         total = None
         for m in range(n_tensor):
-            first = 0
-            for ref in w_refs[m]:
-                if first <= c < first + ref.shape[1]:
-                    w = ref[:, c - first : c - first + COLS]
-                first += ref.shape[1]
+            whole = len(w_refs[m]) == 1
+            w = w_refs[m][0][:, to] if whole else w_refs[m][piece][:, first : first + COLS]
             part = dot(turned_ref[m], w, ((1,), (0,)))
             total = part if total is None else total + part
-        joined_ref[:, c : c + COLS] = total
+        joined_ref[:, to] = total
         sq = total * total
         lanes = sum(sq[:, i : i + 128] for i in range(0, COLS, 128))
-        square_ref[...] = lanes if c == 0 else square_ref[...] + lanes
+        square_ref[...] = lanes if step == 0 else square_ref[...] + lanes
     acc_ref[...] = jnp.zeros_like(acc_ref)
     slice_w = dout // n_dp
     cw = slice_w // chunks
-    near, far = group % NEAR, group // NEAR
     n_far = n_dp // NEAR
 
     def body(r, carry):
@@ -232,11 +239,16 @@
     return words[:n] + words[n : 2 * n], words[2 * n : 2 * n + 1] + words[2 * n + 1 : 2 * n + 2]
 
 
-def grad_body(plan, dout, info_ref, *refs):
+def grad_body(plan, dout, counts, info_ref, *refs):
     n_dp, n_tensor, _, _, xor_far = plan
-    ctx_refs, g_refs, (keep_ref, send_ref) = refs[: NEAR + 1], refs[NEAR + 1 : -2], refs[-2:]
+    keep_ref, send_ref = refs[-2:]
+    ctx_refs, at = [], 0
+    for n in counts:
+        ctx_refs.append(refs[at : at + n])
+        at += n
+    g_refs = refs[at:-2]
     n_y, n_far, tall, cw = keep_ref.shape
-    feats, rows = ctx_refs[0].shape[1:]
+    feats, rows = ctx_refs[0][0].shape[1:]
     wide = n_far * cw
     me = info_ref[0]
     core, y = me % 2, me // 2
@@ -249,9 +261,12 @@
     for s, ref in ((1, send_ref), (0, keep_ref)):
         for a in range(n_y):
             m = (y ^ a if xor_far else a) * 2 + (core ^ s)
-            total = sum(dot(c[m], g[:rows, :], ((1,), (0,))) for c, g in zip(ctx_refs[:-2], g_refs))
-            last = [dot(c[m], g_refs[-1][:rows, :], ((1,), (0,))) for c in ctx_refs[-2:]]
-            total = (total + jnp.concatenate(last, 0)).astype(BF)
+            total = None
+            for parts, g in zip(ctx_refs, g_refs):
+                c = jnp.concatenate([part[m] for part in parts], 0) if len(parts) > 1 else parts[0][m]
+                part = dot(c, g[:rows, :], ((1,), (0,)))
+                total = part if total is None else total + part
+            total = total.astype(BF)
             for b in range(n_far):
                 ref[a, b, :feats, :] = total[:, b * cw : (b + 1) * cw]
                 if tall > feats:
@@ -260,7 +275,7 @@
 
 def gradient(plan, dout, info, ctxs, grads):
     n_dp, n_tensor, chunks, _, _ = plan
-    _, feats, rows = ctxs[0].shape
+    _, feats, rows = ctxs[0][0].shape
     wide = grads[0].shape[1]
     cw = dout // n_dp // chunks
     tall = feats
@@ -268,8 +283,8 @@
         tall += stat_sizes(dout, wide, cw)[2]
     block = shape((n_tensor // 2, n_dp // NEAR, tall, cw))
     return pl.pallas_call(
-        functools.partial(grad_body, plan, dout),
-        in_specs=[SM] + [VM] * (2 * NEAR + 1),
+        functools.partial(grad_body, plan, dout, [len(c) for c in ctxs]),
+        in_specs=[SM] + [VM] * (NEAR + sum(len(c) for c in ctxs)),
         out_specs=[VM, VM],
         out_shape=[block, block],
         compiler_params=params(),
@@ -279,7 +294,7 @@
             transcendentals=0,
         ),
         name="gradient",
-    )(info, *ctxs, *grads)
+    )(info, *[part for parts in ctxs for part in parts], *grads)
 
 
 def merge_body(in_block, feats, keep_ref, got_ref, *out_refs):
@@ -375,6 +390,45 @@
     nears = [[NEAR * f + q for f in range(n_far)] for q in range(NEAR)]
     x = lax.all_to_all(blocks[0], "tensor", 0, 0, tiled=True, axis_index_groups=cores)
     return [lax.all_to_all(x, "dp", 1, 1, tiled=True, axis_index_groups=nears)]
+
+
+def gather_large(n_dp, n_tensor, _, weight, context):
+    ctx = lax.all_to_all(context, "tensor", 0, 0, tiled=True)
+    held = {0: weight}
+    bit = n_tensor // 2
+    while bit:
+        held.update({m | bit: swap(w, "tensor", n_tensor, bit) for m, w in list(held.items())})
+        bit //= 2
+    ctxs = [[ctx]] + [[swap(ctx, "dp", n_dp, q)] for q in range(1, NEAR)]
+    return ctx, ctxs, [[held[m]] for m in range(n_tensor)]
+
+
+def gather_small(n_dp, n_tensor, side, weight, context):
+    barrier = lax.optimization_barrier
+
+    def dp(x, mask):
+        return swap(x, "dp", n_dp, mask)
+
+    def tensor(x, mask):
+        return swap(x, "tensor", n_tensor, mask)
+
+    dout = weight.shape[1]
+    cut = dout * 3 // 8
+    mine = tensor(lax.dynamic_slice_in_dim(weight, side * cut, cut, 1), 2)
+    beside = tensor(weight, 1)
+    rest = weight[:, 2 * cut :]
+    mine, beside, context = barrier((mine, beside, context))
+    other, mine_beside = dp(mine, 1), tensor(mine, 1)
+    ctx = lax.all_to_all(context, "tensor", 0, 0, tiled=True)
+    rest, other, mine_beside, ctx = barrier((rest, other, mine_beside, ctx))
+    rest, other_beside = tensor(rest, 2), tensor(other, 1)
+    half = ctx.shape[1] // 2
+    low, high = ctx[:, :half], ctx[:, half:]
+    low_x, high_z = dp(low, 1), dp(high, 2)
+    rest, low_x, high_z = barrier((rest, low_x, high_z))
+    ctxs = [[ctx], [low_x, dp(high, 1)], [dp(low, 2), high_z], [dp(low_x, 2), dp(high_z, 1)]]
+    far = [mine, other, rest]
+    return ctx, ctxs, [[weight], [beside], far, [mine_beside, other_beside, tensor(rest, 1)]]
 
 
 def on_device(
@@ -400,30 +454,9 @@
     group = lax.axis_index("dp").astype(jnp.int32)
     info = jnp.stack([me, group, lengths[0], vote_counts[0]])
 
-    weight = joining_weight[0]
-    half = n_tensor // 2
-    cut = dout // 2
-    first, second = weight[:, :cut], weight[:, cut:]
-    first = swap(first, "tensor", n_tensor, half)
-    beside = swap(weight, "tensor", n_tensor, 1)
-    context = attend(info, query_states[0], key_states[0], value_states[0], rows)
-    first, beside, context = lax.optimization_barrier((first, beside, context))
-    ctx = lax.all_to_all(context, "tensor", 0, 0, tiled=True)
-    across = swap(first, "tensor", n_tensor, 1)
-    across, second, ctx = lax.optimization_barrier((across, second, ctx))
-    second = swap(second, "tensor", n_tensor, half)
-    beside_x, beside_z = (swap(ctx, "dp", n_dp, q) for q in (1, 2))
-    second, beside_x, beside_z = lax.optimization_barrier((second, beside_x, beside_z))
-    diagonal = [swap(beside_x[:, : width // 2], "dp", n_dp, 2), swap(beside_z[:, width // 2 :], "dp", n_dp, 1)]
-    ctxs = [ctx, beside_x, beside_z, *diagonal]
-    held = {0: [weight], 1: [beside], half: [first, second]}
-    held[half + 1] = [across, swap(second, "tensor", n_tensor, 1)]
-    bit = half // 2
-    while bit > 1:
-        held.update({m ^ bit: [swap(p, "tensor", n_tensor, bit) for p in w] for m, w in list(held.items())})
-        bit //= 2
-    weights = [held[m] for m in range(n_tensor)]
-
+    attended = attend(info, query_states[0], key_states[0], value_states[0], rows)
+    gather = gather_small if xor_far else gather_large
+    ctx, ctxs, weights = gather(n_dp, n_tensor, group & 1, joining_weight[0], attended)
     hidden, grads = join(plan, info, ctx, norm_gain[None, :], next_hidden, weights)
     parts = []
     for j in range(chunks):

time: 90.3 us -> 87.7 us (0.971)
  blocking collectives: 11.8 us -> 0 us
  starting transfers between devices: 24.1 us -> 34.4 us
  local copies, waits for them, and re-layouts: 2.31 us -> 4.9 us
  waiting for transfers between devices: 34.7 us -> 32.9 us
  Pallas kernels: 14.9 us -> 13.1 us
    all_to_all x1 -> x0, blocking collectives: 11.8 us -> none  [on_device(): ctx = lax.all_to_all(context, 'tensor', 0, 0, tiled=True)]
    ppermute x17 -> x21, waiting for transfers between devices: 27.5 us -> 20.3 us  [swap(): return lax.ppermute(x, axis, [(i, i ^ mask) for i in range(n)])]
    ppermute x17 -> x21, starting transfers between devices: 14.8 us -> 21.8 us  [swap(): return lax.ppermute(x, axis, [(i, i ^ mask) for i in range(n)])]
    all_to_all x0 -> x1, waiting for transfers between devices: none -> 5.87 us  [gather_small(): ctx = lax.all_to_all(context, 'tensor', 0, 0, tiled=True)]
    all_to_all x0 -> x1, starting transfers between devices: none -> 3.47 us  [gather_small(): ctx = lax.all_to_all(context, 'tensor', 0, 0, tiled=True)]
    unnamed x16 -> x14, local copies, waits for them, and re-layouts: 0.04 us -> 3.1 us
    slice x3 -> x2, local copies, waits for them, and re-layouts: 2.27 us -> 0.78 us  [the longest x1 0.74 us: gather_small(): rest = weight[:, 2 * cut:]]
    pallas_call x1, Pallas kernels: 7.1 us -> 5.7 us  [join(): pl.pallas_call(functools.partial(join_body, plan, [len(w) for w in weight...]
  transfers between devices with their start and end apart: 23 -> 28, of which waited for: 12 -> 14; matrix products, arithmetic and copies ran while one was open for 3% -> 2% of each run, Pallas kernels for 16% -> 14%
where the time goes in v6:
time: 87.7 us; the launch traced here: 87.4 us
  starting transfers between devices  34.4 us (39%)
  waiting for transfers between devices  32.9 us (38%)
  Pallas kernels  13.1 us (15%)
  local copies, waits for them, and re-layouts  4.9 us (6%)
  between operations  2.05 us (2%)
    ppermute x21, starting transfers between devices, swap(): return lax.ppermute(x, axis, [(i, i ^ mask) for i in range(n)])  21.8 us
    ppermute x21, waiting for transfers between devices, swap(): return lax.ppermute(x, axis, [(i, i ^ mask) for i in range(n)])  20.3 us
    ppermute x6, starting transfers between devices, swap_far(): lax.ppermute(x, ('dp', 'tensor'), [(i, i ^ mask) for i in range(n_dp * n_...  9.09 us
    ppermute x6, waiting for transfers between devices, swap_far(): lax.ppermute(x, ('dp', 'tensor'), [(i, i ^ mask) for i in range(n_dp * n_...  6.73 us
    all_to_all x1, waiting for transfers between devices, gather_small(): ctx = lax.all_to_all(context, 'tensor', 0, 0, tiled=True)  5.87 us
    pallas_call x1, Pallas kernels, join(): pl.pallas_call(functools.partial(join_body, plan, [len(w) for w in weight...  5.7 us
    pallas_call x1, Pallas kernels, attend(): pl.pallas_call(attend_body, in_specs=[SM, block, block, block], out_specs...  4 us
    all_to_all x1, starting transfers between devices, gather_small(): ctx = lax.all_to_all(context, 'tensor', 0, 0, tiled=True)  3.47 us
  transfers between devices with their start and end apart: 28, of which 14 were waited for; matrix products, arithmetic and copies ran while one was open for 2% of the time, Pallas kernels for 14%

profile of v6, /device:TPU:0, one launch (start us, length us, event | category | flops | bytes accessed | tf_op | source)
XLA Modules:
  0.0 87.4 jit_solution(10346204042310692289)
XLA Ops:
  2.2 2.7 %collective-permute-start = (bf16[256,768]{1,0:T(8,128)(2,1)S(1)}, bf16[256,768]{1,0:T(8,128)(2,1)S(1)}, u32[]{:S(2)}, u32[]{:S(2)}) collective-permute-start(bf16[256,768]{1,0:T(8,128)(2,1)S(1)} %dynamic-slice_bitcast_fusion), channel_id=1, source_target_pairs={{0,2},{1,3},{2,0},{3,1},{4,6},{5,7},{6,4},{7,5},{8,10},{9,11},{10,... | collective-permute-start | bytes 1179656 | tf_op jit(solution)/shard_map/ppermute | solution.py:374
  8.3 4.0 %attend.1 = bf16[4,256,256]{2,1,0:T(8,128)(2,1)} custom-call(s32[4]{0:T(128)S(1)} %pad_add_fusion.info_ref, bf16[1024,256]{1,0:T(8,128)(2,1)S(1)} %bitcast.16, bf16[1024,256]{1,0:T(8,128)(2,1)S(1)} %bitcast.17, bf16[1024,256]{1,0:T(8,128)(2,1)S(1)} %bitcast.18), custom_call_target="tpu_custom_call" | custom-call | flops 1073741824 | bytes 2097152 | tf_op jit(solution)/shard_map/attend/pallas_call | solution.py:76
  12.3 2.2 %collective-permute-done.refs_2_ = bf16[256,768]{1,0:T(8,128)(2,1)S(1)} collective-permute-done((bf16[256,768]{1,0:T(8,128)(2,1)S(1)}, bf16[256,768]{1,0:T(8,128)(2,1)S(1)}, u32[]{:S(2)}, u32[]{:S(2)}) %collective-permute-start) | collective-permute-done | bytes 393248 | tf_op jit(solution)/shard_map/ppermute | solution.py:374
  15.6 3.5 %all-to-all-start = ((bf16[4,256,256]{2,1,0:T(8,128)(2,1)}), bf16[4,256,256]{2,1,0:T(8,128)(2,1)S(1)}, u32[]{:S(2)}, u32[]{:S(2)}) async-start(bf16[4,256,256]{2,1,0:T(8,128)(2,1)} %attend.1), calls=%async_computation | async-start | bytes 1048576 | tf_op jit(solution)/shard_map/all_to_all | solution.py:422
  19.5 1.7 %collective-permute-start.2 = (bf16[256,768]{1,0:T(8,128)(2,1)S(1)}, bf16[256,768]{1,0:T(8,128)(2,1)}, u32[]{:S(2)}, u32[]{:S(2)}) collective-permute-start(bf16[256,768]{1,0:T(8,128)(2,1)S(1)} %collective-permute-done.refs_2_), channel_id=1, source_target_pairs={{0,4},{4,0},{8,12},{12,8},{16,20},{20,16},{24,28},{28,24},{1,5},{5... | collective-permute-start | bytes 1179656 | tf_op jit(solution)/shard_map/ppermute | solution.py:374
  22.0 5.9 %all-to-all-done.ctx_ref.refs_0_ = bf16[4,256,256]{2,1,0:T(8,128)(2,1)S(1)} async-done(((bf16[4,256,256]{2,1,0:T(8,128)(2,1)}), bf16[4,256,256]{2,1,0:T(8,128)(2,1)S(1)}, u32[]{:S(2)}, u32[]{:S(2)}) %all-to-all-start) | async-done | bytes 524320 | tf_op jit(solution)/shard_map/all_to_all | solution.py:422
  27.8 2.9 %collective-permute-done.2.refs_3_ = bf16[256,768]{1,0:T(8,128)(2,1)} collective-permute-done((bf16[256,768]{1,0:T(8,128)(2,1)S(1)}, bf16[256,768]{1,0:T(8,128)(2,1)}, u32[]{:S(2)}, u32[]{:S(2)}) %collective-permute-start.2) | collective-permute-done | bytes 393248 | tf_op jit(solution)/shard_map/ppermute | solution.py:374
  30.7 1.9 %collective-permute-start.4 = (bf16[256,512]{1,0:T(8,128)(2,1)}, bf16[256,512]{1,0:T(8,128)(2,1)S(1)}, u32[]{:S(2)}, u32[]{:S(2)}) collective-permute-start(bf16[256,512]{1,0:T(8,128)(2,1)} %slice.12), channel_id=1, source_target_pairs={{0,2},{1,3},{2,0},{3,1},{4,6},{5,7},{6,4},{7,5},{8,10},{9,11},{10,... | collective-permute-start | bytes 786440 | tf_op jit(solution)/shard_map/ppermute | solution.py:374
  32.7 1.9 %collective-permute-start.6 = (bf16[4,128,256]{2,1,0:T(8,128)(2,1)S(1)}, bf16[4,128,256]{2,1,0:T(8,128)(2,1)S(1)}, u32[]{:S(2)}, u32[]{:S(2)}) collective-permute-start(bf16[4,128,256]{2,1,0:T(8,128)(2,1)S(1)} %get-tuple-element.72), channel_id=1, source_target_pairs={{0,8},{4,12},{8,0},{12,4},{16,24},{20,28},{24,16},{28,20},{1,9},{5... | collective-permute-start | bytes 786440 | tf_op jit(solution)/shard_map/ppermute | solution.py:374
  36.1 2.8 %collective-permute-done.4.refs_4_ = bf16[256,512]{1,0:T(8,128)(2,1)S(1)} collective-permute-done((bf16[256,512]{1,0:T(8,128)(2,1)}, bf16[256,512]{1,0:T(8,128)(2,1)S(1)}, u32[]{:S(2)}, u32[]{:S(2)}) %collective-permute-start.4) | collective-permute-done | bytes 262176 | tf_op jit(solution)/shard_map/ppermute | solution.py:374
  41.8 1.5 %collective-permute-start.9 = (bf16[4,128,256]{2,1,0:T(8,128)(2,1)S(1)}, bf16[4,128,256]{2,1,0:T(8,128)(2,1)S(1)}, u32[]{:S(2)}, u32[]{:S(2)}) collective-permute-start(bf16[4,128,256]{2,1,0:T(8,128)(2,1)S(1)} %get-tuple-element.72), channel_id=1, source_target_pairs={{0,4},{4,0},{8,12},{12,8},{16,20},{20,16},{24,28},{28,24},{1,5},{5... | collective-permute-start | bytes 786440 | tf_op jit(solution)/shard_map/ppermute | solution.py:374
  43.7 1.6 %collective-permute-start.11 = (bf16[4,128,256]{2,1,0:T(8,128)(2,1)S(1)}, bf16[4,128,256]{2,1,0:T(8,128)(2,1)S(1)}, u32[]{:S(2)}, u32[]{:S(2)}) collective-permute-start(bf16[4,128,256]{2,1,0:T(8,128)(2,1)S(1)} %collective-permute-done.5.refs_1_), channel_id=1, source_target_pairs={{0,8},{4,12},{8,0},{12,4},{16,24},{20,28},{24,16},{28,20},{1,9},{5... | collective-permute-start | bytes 786440 | tf_op jit(solution)/shard_map/ppermute | solution.py:374
  45.8 5.7 %join.1 = (bf16[256,2048]{1,0:T(8,128)(2,1)}, bf16[288,256]{1,0:T(8,128)(2,1)S(1)}, bf16[288,256]{1,0:T(8,128)(2,1)S(1)}, bf16[288,256]{1,0:T(8,128)(2,1)S(1)}, ...) custom-call(s32[4]{0:T(128)S(1)} %pad_add_fusion.info_ref, ...), custom_call_target="tpu_custom_call" | custom-call | flops 1073741824 | bytes 7340032 | tf_op jit(solution)/shard_map/join/pallas_call | solution.py:201
  53.5 1.6 %collective-permute-start.22 = (bf16[256,256]{1,0:T(8,128)(2,1)S(1)}, bf16[256,256]{1,0:T(8,128)(2,1)S(1)}, u32[]{:S(2)}, u32[]{:S(2)}) collective-permute-start(bf16[256,256]{1,0:T(8,128)(2,1)S(1)} %get-tuple-element.62), channel_id=1, source_target_pairs={{0,12},{4,8},{8,4},{12,0},{16,28},{20,24},{24,20},{28,16},{1,13},{... | collective-permute-start | bytes 393224 | tf_op jit(solution)/shard_map/ppermute | solution.py:374
  55.0 3.0 %collective-permute-done.11.refs_5_ = bf16[4,128,256]{2,1,0:T(8,128)(2,1)S(1)} collective-permute-done((bf16[4,128,256]{2,1,0:T(8,128)(2,1)S(1)}, bf16[4,128,256]{2,1,0:T(8,128)(2,1)S(1)}, u32[]{:S(2)}, u32[]{:S(2)}) %collective-permute-start.11) | collective-permute-done | bytes 262176 | tf_op jit(solution)/shard_map/ppermute | solution.py:374
  58.9 2.6 %collective-permute-start.15 = (bf16[288,256]{1,0:T(8,128)(2,1)S(1)}, bf16[288,256]{1,0:T(8,128)(2,1)S(1)}, u32[]{:S(2)}, u32[]{:S(2)}) collective-permute-start(bf16[288,256]{1,0:T(8,128)(2,1)S(1)} %get-tuple-element.52), channel_id=1, source_target_pairs={{0,12},{4,8},{8,4},{12,0},{16,28},{20,24},{24,20},{28,16},{1,13},{... | collective-permute-start | bytes 442376 | tf_op jit(solution)/shard_map/ppermute | solution.py:374
  61.5 2.1 %collective-permute-done.22.refs_10_ = bf16[256,256]{1,0:T(8,128)(2,1)S(1)} collective-permute-done((bf16[256,256]{1,0:T(8,128)(2,1)S(1)}, bf16[256,256]{1,0:T(8,128)(2,1)S(1)}, u32[]{:S(2)}, u32[]{:S(2)}) %collective-permute-start.22) | collective-permute-done | bytes 131104 | tf_op jit(solution)/shard_map/ppermute | solution.py:374
  65.3 1.6 %collective-permute-done.14.refs_9_ = bf16[288,256]{1,0:T(8,128)(2,1)S(1)} collective-permute-done((bf16[288,256]{1,0:T(8,128)(2,1)S(1)}, bf16[288,256]{1,0:T(8,128)(2,1)S(1)}, u32[]{:S(2)}, u32[]{:S(2)}) %collective-permute-start.14) | collective-permute-done | bytes 147488 | tf_op jit(solution)/shard_map/ppermute | solution.py:374
  66.9 2.4 %collective-permute-done.15.refs_10_ = bf16[288,256]{1,0:T(8,128)(2,1)S(1)} collective-permute-done((bf16[288,256]{1,0:T(8,128)(2,1)S(1)}, bf16[288,256]{1,0:T(8,128)(2,1)S(1)}, u32[]{:S(2)}, u32[]{:S(2)}) %collective-permute-start.15) | collective-permute-done | bytes 147488 | tf_op jit(solution)/shard_map/ppermute | solution.py:374
  70.7 2.7 %collective-permute-start.24 = (bf16[1,1,256,128]{3,2,1,0:T(8,128)(2,1)S(1)}, bf16[1,1,256,128]{3,2,1,0:T(8,128)(2,1)S(1)}, u32[]{:S(2)}, u32[]{:S(2)}) collective-permute-start(bf16[1,1,256,128]{3,2,1,0:T(8,128)(2,1)S(1)} %get-tuple-element.66), channel_id=1, source_target_pairs={{0,16},{1,17},{2,18},{3,19},{4,20},{5,21},{6,22},{7,23},{8,24},{9,... | collective-permute-start | bytes 196616 | tf_op jit(solution)/shard_map/ppermute | solution.py:379
  73.4 1.5 %collective-permute-start.17 = (bf16[1,1,304,128]{3,2,1,0:T(8,128)(2,1)S(1)}, bf16[1,1,304,128]{3,2,1,0:T(8,128)(2,1)S(1)}, u32[]{:S(2)}, u32[]{:S(2)}) collective-permute-start(bf16[1,1,304,128]{3,2,1,0:T(8,128)(2,1)S(1)} %get-tuple-element.56), channel_id=1, source_target_pairs={{0,16},{1,17},{2,18},{3,19},{4,20},{5,21},{6,22},{7,23},{8,24},{9,... | collective-permute-start | bytes 233480 | tf_op jit(solution)/shard_map/ppermute | solution.py:379
  75.2 2.7 %collective-permute-start.19 = (bf16[1,1,304,128]{3,2,1,0:T(8,128)(2,1)S(1)}, bf16[1,1,304,128]{3,2,1,0:T(8,128)(2,1)S(1)}, u32[]{:S(2)}, u32[]{:S(2)}) collective-permute-start(bf16[1,1,304,128]{3,2,1,0:T(8,128)(2,1)S(1)} %get-tuple-element.58), channel_id=1, source_target_pairs={{0,18},{1,19},{2,16},{3,17},{4,22},{5,23},{6,20},{7,21},{8,26},{9,... | collective-permute-start | bytes 233480 | tf_op jit(solution)/shard_map/ppermute | solution.py:379
  79.1 1.7 %collective-permute-start.26 = (bf16[1,1,256,128]{3,2,1,0:T(8,128)(2,1)S(1)}, bf16[1,1,256,128]{3,2,1,0:T(8,128)(2,1)S(1)}, u32[]{:S(2)}, u32[]{:S(2)}) collective-permute-start(bf16[1,1,256,128]{3,2,1,0:T(8,128)(2,1)S(1)} %get-tuple-element.68), channel_id=1, source_target_pairs={{0,18},{1,19},{2,16},{3,17},{4,22},{5,23},{6,20},{7,21},{8,26},{9,... | collective-permute-start | bytes 196616 | tf_op jit(solution)/shard_map/ppermute | solution.py:379
  82.1 4.4 %collective-permute-done.26.refs_7_ = bf16[1,1,256,128]{3,2,1,0:T(8,128)(2,1)S(1)} collective-permute-done((bf16[1,1,256,128]{3,2,1,0:T(8,128)(2,1)S(1)}, bf16[1,1,256,128]{3,2,1,0:T(8,128)(2,1)S(1)}, u32[]{:S(2)}, u32[]{:S(2)}) %collective-permute-start.26) | collective-permute-done | bytes 65568 | tf_op jit(solution)/shard_map/ppermute | solution.py:379
  (57 shorter events, 20.9 us)
Async XLA Ops:
  0.6 13.9 %collective-permute-start.1 = (bf16[256,2048]{1,0:T(8,128)(2,1)}, bf16[256,2048]{1,0:T(8,128)(2,1)S(1)}, u32[]{:S(2)}, u32[]{:S(2)}) collective-permute-start(bf16[256,2048]{1,0:T(8,128)(2,1)} %bitcast.12), channel_id=1, source_target_pairs={{0,1},{1,0},{2,3},{3,2},{4,5},{5,4},{6,7},{7,6},{8,9},{9,8},{10,11... | collective-permute-start | bytes 3145736 | tf_op jit(solution)/shard_map/ppermute | solution.py:374
  2.2 12.4 %collective-permute-start = (bf16[256,768]{1,0:T(8,128)(2,1)S(1)}, bf16[256,768]{1,0:T(8,128)(2,1)S(1)}, u32[]{:S(2)}, u32[]{:S(2)}) collective-permute-start(bf16[256,768]{1,0:T(8,128)(2,1)S(1)} %dynamic-slice_bitcast_fusion), channel_id=1, source_target_pairs={{0,2},{1,3},{2,0},{3,1},{4,6},{5,7},{6,4},{7,5},{8,10},{9,11},{10,... | collective-permute-start | bytes 1179656 | tf_op jit(solution)/shard_map/ppermute | solution.py:374
  15.6 12.3 %all-to-all-start = ((bf16[4,256,256]{2,1,0:T(8,128)(2,1)}), bf16[4,256,256]{2,1,0:T(8,128)(2,1)S(1)}, u32[]{:S(2)}, u32[]{:S(2)}) async-start(bf16[4,256,256]{2,1,0:T(8,128)(2,1)} %attend.1), calls=%async_computation | async-start | bytes 1048576 | tf_op jit(solution)/shard_map/all_to_all | solution.py:422
  19.0 8.8 %collective-permute-start.3 = (bf16[256,768]{1,0:T(8,128)(2,1)S(1)}, bf16[256,768]{1,0:T(8,128)(2,1)S(1)}, u32[]{:S(2)}, u32[]{:S(2)}) collective-permute-start(bf16[256,768]{1,0:T(8,128)(2,1)S(1)} %collective-permute-done.refs_2_), channel_id=1, source_target_pairs={{0,1},{1,0},{2,3},{3,2},{4,5},{5,4},{6,7},{7,6},{8,9},{9,8},{10,11... | collective-permute-start | bytes 1179656 | tf_op jit(solution)/shard_map/ppermute | solution.py:374
  19.5 11.2 %collective-permute-start.2 = (bf16[256,768]{1,0:T(8,128)(2,1)S(1)}, bf16[256,768]{1,0:T(8,128)(2,1)}, u32[]{:S(2)}, u32[]{:S(2)}) collective-permute-start(bf16[256,768]{1,0:T(8,128)(2,1)S(1)} %collective-permute-done.refs_2_), channel_id=1, source_target_pairs={{0,4},{4,0},{8,12},{12,8},{16,20},{20,16},{24,28},{28,24},{1,5},{5... | collective-permute-start | bytes 1179656 | tf_op jit(solution)/shard_map/ppermute | solution.py:374
  30.7 8.1 %collective-permute-start.4 = (bf16[256,512]{1,0:T(8,128)(2,1)}, bf16[256,512]{1,0:T(8,128)(2,1)S(1)}, u32[]{:S(2)}, u32[]{:S(2)}) collective-permute-start(bf16[256,512]{1,0:T(8,128)(2,1)} %slice.12), channel_id=1, source_target_pairs={{0,2},{1,3},{2,0},{3,1},{4,6},{5,7},{6,4},{7,5},{8,10},{9,11},{10,... | collective-permute-start | bytes 786440 | tf_op jit(solution)/shard_map/ppermute | solution.py:374
  32.7 7.6 %collective-permute-start.6 = (bf16[4,128,256]{2,1,0:T(8,128)(2,1)S(1)}, bf16[4,128,256]{2,1,0:T(8,128)(2,1)S(1)}, u32[]{:S(2)}, u32[]{:S(2)}) collective-permute-start(bf16[4,128,256]{2,1,0:T(8,128)(2,1)S(1)} %get-tuple-element.72), channel_id=1, source_target_pairs={{0,8},{4,12},{8,0},{12,4},{16,24},{20,28},{24,16},{28,20},{1,9},{5... | collective-permute-start | bytes 786440 | tf_op jit(solution)/shard_map/ppermute | solution.py:374
  34.6 7.2 %collective-permute-start.5 = (bf16[4,128,256]{2,1,0:T(8,128)(2,1)S(1)}, bf16[4,128,256]{2,1,0:T(8,128)(2,1)S(1)}, u32[]{:S(2)}, u32[]{:S(2)}) collective-permute-start(bf16[4,128,256]{2,1,0:T(8,128)(2,1)S(1)} %get-tuple-element.73), channel_id=1, source_target_pairs={{0,4},{4,0},{8,12},{12,8},{16,20},{20,16},{24,28},{28,24},{1,5},{5... | collective-permute-start | bytes 786440 | tf_op jit(solution)/shard_map/ppermute | solution.py:374
  36.1 9.2 %collective-permute-start.7 = (bf16[256,768]{1,0:T(8,128)(2,1)}, bf16[256,768]{1,0:T(8,128)(2,1)S(1)}, u32[]{:S(2)}, u32[]{:S(2)}) collective-permute-start(bf16[256,768]{1,0:T(8,128)(2,1)} %collective-permute-done.2.refs_3_), channel_id=1, source_target_pairs={{0,1},{1,0},{2,3},{3,2},{4,5},{5,4},{6,7},{7,6},{8,9},{9,8},{10,11... | collective-permute-start | bytes 1179656 | tf_op jit(solution)/shard_map/ppermute | solution.py:374
  41.8 11.3 %collective-permute-start.9 = (bf16[4,128,256]{2,1,0:T(8,128)(2,1)S(1)}, bf16[4,128,256]{2,1,0:T(8,128)(2,1)S(1)}, u32[]{:S(2)}, u32[]{:S(2)}) collective-permute-start(bf16[4,128,256]{2,1,0:T(8,128)(2,1)S(1)} %get-tuple-element.72), channel_id=1, source_target_pairs={{0,4},{4,0},{8,12},{12,8},{16,20},{20,16},{24,28},{28,24},{1,5},{5... | collective-permute-start | bytes 786440 | tf_op jit(solution)/shard_map/ppermute | solution.py:374
  43.3 10.2 %collective-permute-start.10 = (bf16[4,128,256]{2,1,0:T(8,128)(2,1)S(1)}, bf16[4,128,256]{2,1,0:T(8,128)(2,1)S(1)}, u32[]{:S(2)}, u32[]{:S(2)}) collective-permute-start(bf16[4,128,256]{2,1,0:T(8,128)(2,1)S(1)} %get-tuple-element.73), channel_id=1, source_target_pairs={{0,8},{4,12},{8,0},{12,4},{16,24},{20,28},{24,16},{28,20},{1,9},{5... | collective-permute-start | bytes 786440 | tf_op jit(solution)/shard_map/ppermute | solution.py:374
  43.7 14.3 %collective-permute-start.11 = (bf16[4,128,256]{2,1,0:T(8,128)(2,1)S(1)}, bf16[4,128,256]{2,1,0:T(8,128)(2,1)S(1)}, u32[]{:S(2)}, u32[]{:S(2)}) collective-permute-start(bf16[4,128,256]{2,1,0:T(8,128)(2,1)S(1)} %collective-permute-done.5.refs_1_), channel_id=1, source_target_pairs={{0,8},{4,12},{8,0},{12,4},{16,24},{20,28},{24,16},{28,20},{1,9},{5... | collective-permute-start | bytes 786440 | tf_op jit(solution)/shard_map/ppermute | solution.py:374
  45.3 13.3 %collective-permute-start.12 = (bf16[4,128,256]{2,1,0:T(8,128)(2,1)S(1)}, bf16[4,128,256]{2,1,0:T(8,128)(2,1)S(1)}, u32[]{:S(2)}, u32[]{:S(2)}) collective-permute-start(bf16[4,128,256]{2,1,0:T(8,128)(2,1)S(1)} %collective-permute-done.6.refs_4_), channel_id=1, source_target_pairs={{0,4},{4,0},{8,12},{12,8},{16,20},{20,16},{24,28},{28,24},{1,5},{5... | collective-permute-start | bytes 786440 | tf_op jit(solution)/shard_map/ppermute | solution.py:374
  51.5 7.4 %collective-permute-start.20 = (bf16[256,256]{1,0:T(8,128)(2,1)S(1)}, bf16[256,256]{1,0:T(8,128)(2,1)S(1)}, u32[]{:S(2)}, u32[]{:S(2)}) collective-permute-start(bf16[256,256]{1,0:T(8,128)(2,1)S(1)} %get-tuple-element.60), channel_id=1, source_target_pairs={{0,4},{4,0},{8,12},{12,8},{16,20},{20,16},{24,28},{28,24},{1,5},{5... | collective-permute-start | bytes 393224 | tf_op jit(solution)/shard_map/ppermute | solution.py:374
  53.0 8.5 %collective-permute-start.21 = (bf16[256,256]{1,0:T(8,128)(2,1)S(1)}, bf16[256,256]{1,0:T(8,128)(2,1)S(1)}, u32[]{:S(2)}, u32[]{:S(2)}) collective-permute-start(bf16[256,256]{1,0:T(8,128)(2,1)S(1)} %get-tuple-element.61), channel_id=1, source_target_pairs={{0,8},{4,12},{8,0},{12,4},{16,24},{20,28},{24,16},{28,20},{1,9},{5... | collective-permute-start | bytes 393224 | tf_op jit(solution)/shard_map/ppermute | solution.py:374
  53.5 10.2 %collective-permute-start.22 = (bf16[256,256]{1,0:T(8,128)(2,1)S(1)}, bf16[256,256]{1,0:T(8,128)(2,1)S(1)}, u32[]{:S(2)}, u32[]{:S(2)}) collective-permute-start(bf16[256,256]{1,0:T(8,128)(2,1)S(1)} %get-tuple-element.62), channel_id=1, source_target_pairs={{0,12},{4,8},{8,4},{12,0},{16,28},{20,24},{24,20},{28,16},{1,13},{... | collective-permute-start | bytes 393224 | tf_op jit(solution)/shard_map/ppermute | solution.py:374
  58.0 7.3 %collective-permute-start.13 = (bf16[288,256]{1,0:T(8,128)(2,1)S(1)}, bf16[288,256]{1,0:T(8,128)(2,1)S(1)}, u32[]{:S(2)}, u32[]{:S(2)}) collective-permute-start(bf16[288,256]{1,0:T(8,128)(2,1)S(1)} %get-tuple-element.50), channel_id=1, source_target_pairs={{0,4},{4,0},{8,12},{12,8},{16,20},{20,16},{24,28},{28,24},{1,5},{5... | collective-permute-start | bytes 442376 | tf_op jit(solution)/shard_map/ppermute | solution.py:374
  58.6 8.3 %collective-permute-start.14 = (bf16[288,256]{1,0:T(8,128)(2,1)S(1)}, bf16[288,256]{1,0:T(8,128)(2,1)S(1)}, u32[]{:S(2)}, u32[]{:S(2)}) collective-permute-start(bf16[288,256]{1,0:T(8,128)(2,1)S(1)} %get-tuple-element.51), channel_id=1, source_target_pairs={{0,8},{4,12},{8,0},{12,4},{16,24},{20,28},{24,16},{28,20},{1,9},{5... | collective-permute-start | bytes 442376 | tf_op jit(solution)/shard_map/ppermute | solution.py:374
  58.9 10.3 %collective-permute-start.15 = (bf16[288,256]{1,0:T(8,128)(2,1)S(1)}, bf16[288,256]{1,0:T(8,128)(2,1)S(1)}, u32[]{:S(2)}, u32[]{:S(2)}) collective-permute-start(bf16[288,256]{1,0:T(8,128)(2,1)S(1)} %get-tuple-element.52), channel_id=1, source_target_pairs={{0,12},{4,8},{8,4},{12,0},{16,28},{20,24},{24,20},{28,16},{1,13},{... | collective-permute-start | bytes 442376 | tf_op jit(solution)/shard_map/ppermute | solution.py:374
  70.7 8.4 %collective-permute-start.24 = (bf16[1,1,256,128]{3,2,1,0:T(8,128)(2,1)S(1)}, bf16[1,1,256,128]{3,2,1,0:T(8,128)(2,1)S(1)}, u32[]{:S(2)}, u32[]{:S(2)}) collective-permute-start(bf16[1,1,256,128]{3,2,1,0:T(8,128)(2,1)S(1)} %get-tuple-element.66), channel_id=1, source_target_pairs={{0,16},{1,17},{2,18},{3,19},{4,20},{5,21},{6,22},{7,23},{8,24},{9,... | collective-permute-start | bytes 196616 | tf_op jit(solution)/shard_map/ppermute | solution.py:379
  73.4 13.2 %collective-permute-start.17 = (bf16[1,1,304,128]{3,2,1,0:T(8,128)(2,1)S(1)}, bf16[1,1,304,128]{3,2,1,0:T(8,128)(2,1)S(1)}, u32[]{:S(2)}, u32[]{:S(2)}) collective-permute-start(bf16[1,1,304,128]{3,2,1,0:T(8,128)(2,1)S(1)} %get-tuple-element.56), channel_id=1, source_target_pairs={{0,16},{1,17},{2,18},{3,19},{4,20},{5,21},{6,22},{7,23},{8,24},{9,... | collective-permute-start | bytes 233480 | tf_op jit(solution)/shard_map/ppermute | solution.py:379
  74.9 11.7 %collective-permute-start.18 = (bf16[1,1,304,128]{3,2,1,0:T(8,128)(2,1)S(1)}, bf16[1,1,304,128]{3,2,1,0:T(8,128)(2,1)S(1)}, u32[]{:S(2)}, u32[]{:S(2)}) collective-permute-start(bf16[1,1,304,128]{3,2,1,0:T(8,128)(2,1)S(1)} %get-tuple-element.57), channel_id=1, source_target_pairs={{0,2},{1,3},{2,0},{3,1},{4,6},{5,7},{6,4},{7,5},{8,10},{9,11},{10,... | collective-permute-start | bytes 233480 | tf_op jit(solution)/shard_map/ppermute | solution.py:379
  75.2 11.4 %collective-permute-start.19 = (bf16[1,1,304,128]{3,2,1,0:T(8,128)(2,1)S(1)}, bf16[1,1,304,128]{3,2,1,0:T(8,128)(2,1)S(1)}, u32[]{:S(2)}, u32[]{:S(2)}) collective-permute-start(bf16[1,1,304,128]{3,2,1,0:T(8,128)(2,1)S(1)} %get-tuple-element.58), channel_id=1, source_target_pairs={{0,18},{1,19},{2,16},{3,17},{4,22},{5,23},{6,20},{7,21},{8,26},{9,... | collective-permute-start | bytes 233480 | tf_op jit(solution)/shard_map/ppermute | solution.py:379
  79.1 7.5 %collective-permute-start.26 = (bf16[1,1,256,128]{3,2,1,0:T(8,128)(2,1)S(1)}, bf16[1,1,256,128]{3,2,1,0:T(8,128)(2,1)S(1)}, u32[]{:S(2)}, u32[]{:S(2)}) collective-permute-start(bf16[1,1,256,128]{3,2,1,0:T(8,128)(2,1)S(1)} %get-tuple-element.68), channel_id=1, source_target_pairs={{0,18},{1,19},{2,16},{3,17},{4,22},{5,23},{6,20},{7,21},{8,26},{9,... | collective-permute-start | bytes 196616 | tf_op jit(solution)/shard_map/ppermute | solution.py:379
  (11 other events, 74.4 us)

commit v7 on v6

--- a/solution.py
+++ b/solution.py
@@ -78,7 +78,7 @@
                 in_specs=[SM, block, block, block],
         out_specs=VM,
         out_shape=shape((seq // rows, width, rows)),
-        compiler_params=params(),
+        compiler_params=pltpu.CompilerParams(vmem_limit_bytes=60 * MIB),
         cost_estimate=pl.CostEstimate(
             flops=4 * seq * seq * width, bytes_accessed=8 * seq * width, transcendentals=heads * seq * seq
         ),
@@ -413,20 +413,19 @@
         return swap(x, "tensor", n_tensor, mask)
 
     dout = weight.shape[1]
-    cut = dout * 3 // 8
+    cut = dout // 4
     mine = tensor(lax.dynamic_slice_in_dim(weight, side * cut, cut, 1), 2)
     beside = tensor(weight, 1)
     rest = weight[:, 2 * cut :]
-    mine, beside, context = barrier((mine, beside, context))
+    mine, context = barrier((mine, context))
     other, mine_beside = dp(mine, 1), tensor(mine, 1)
     ctx = lax.all_to_all(context, "tensor", 0, 0, tiled=True)
-    rest, other, mine_beside, ctx = barrier((rest, other, mine_beside, ctx))
+    rest, other, mine_beside, beside, ctx = barrier((rest, other, mine_beside, beside, ctx))
     rest, other_beside = tensor(rest, 2), tensor(other, 1)
+    ctx_x, ctx_z = dp(ctx, 1), dp(ctx, 2)
+    rest, other_beside, ctx_x, ctx_z = barrier((rest, other_beside, ctx_x, ctx_z))
     half = ctx.shape[1] // 2
-    low, high = ctx[:, :half], ctx[:, half:]
-    low_x, high_z = dp(low, 1), dp(high, 2)
-    rest, low_x, high_z = barrier((rest, low_x, high_z))
-    ctxs = [[ctx], [low_x, dp(high, 1)], [dp(low, 2), high_z], [dp(low_x, 2), dp(high_z, 1)]]
+    ctxs = [[ctx], [ctx_x], [ctx_z], [dp(ctx_x[:, :half], 2), dp(ctx_z[:, half:], 1)]]
     far = [mine, other, rest]
     return ctx, ctxs, [[weight], [beside], far, [mine_beside, other_beside, tensor(rest, 1)]]
 

time: 87.7 us -> 83.3 us (0.950)
  local copies, waits for them, and re-layouts: 4.9 us -> 1.86 us
  starting transfers between devices: 34.4 us -> 31.7 us
    all_to_all x1, waiting for transfers between devices: 5.87 us -> 0.12 us  [gather_small(): ctx = lax.all_to_all(context, 'tensor', 0, 0, tiled=True)]
    ppermute x21 -> x19, waiting for transfers between devices: 20.3 us -> 25.6 us  [swap(): return lax.ppermute(x, axis, [(i, i ^ mask) for i in range(n)])]
    ppermute x21 -> x19, starting transfers between devices: 21.8 us -> 18.3 us  [swap(): return lax.ppermute(x, axis, [(i, i ^ mask) for i in range(n)])]
    unnamed x14 -> x8, local copies, waits for them, and re-layouts: 3.1 us -> 0.02 us
  transfers between devices with their start and end apart: 28 -> 26, of which waited for: 14 -> 14; matrix products, arithmetic and copies ran while one was open for 2% -> 3% of each run, Pallas kernels for 14% -> 16%
where the time goes in v7:
time: 83.3 us; the launch traced here: 83 us
  waiting for transfers between devices  33 us (40%)
  starting transfers between devices  31.7 us (38%)
  Pallas kernels  13.9 us (17%)
  between operations  2.06 us (2%)
  local copies, waits for them, and re-layouts  1.86 us (2%)
    ppermute x19, waiting for transfers between devices, swap(): return lax.ppermute(x, axis, [(i, i ^ mask) for i in range(n)])  25.6 us
    ppermute x19, starting transfers between devices, swap(): return lax.ppermute(x, axis, [(i, i ^ mask) for i in range(n)])  18.3 us
    ppermute x6, starting transfers between devices, swap_far(): lax.ppermute(x, ('dp', 'tensor'), [(i, i ^ mask) for i in range(n_dp * n_...  9.74 us
    ppermute x6, waiting for transfers between devices, swap_far(): lax.ppermute(x, ('dp', 'tensor'), [(i, i ^ mask) for i in range(n_dp * n_...  7.24 us
    pallas_call x1, Pallas kernels, join(): pl.pallas_call(functools.partial(join_body, plan, [len(w) for w in weight...  5.63 us
    pallas_call x1, Pallas kernels, attend(): pl.pallas_call(attend_body, in_specs=[SM, block, block, block], out_specs...  4.83 us
    all_to_all x1, starting transfers between devices, gather_small(): ctx = lax.all_to_all(context, 'tensor', 0, 0, tiled=True)  3.6 us
    pallas_call x2, Pallas kernels, gradient(): pl.pallas_call(functools.partial(grad_body, plan, dout, [len(c) for c in...  2.5 us
  transfers between devices with their start and end apart: 26, of which 14 were waited for; matrix products, arithmetic and copies ran while one was open for 3% of the time, Pallas kernels for 16%

profile of v7, /device:TPU:0, one launch (start us, length us, event | category | flops | bytes accessed | tf_op | source)
XLA Modules:
  0.0 83.0 jit_solution(13885206971816512470)
XLA Ops:
  2.1 2.6 %collective-permute-start = (bf16[256,512]{1,0:T(8,128)(2,1)S(1)}, bf16[256,512]{1,0:T(8,128)(2,1)S(1)}, u32[]{:S(2)}, u32[]{:S(2)}) collective-permute-start(bf16[256,512]{1,0:T(8,128)(2,1)S(1)} %dynamic-slice_bitcast_fusion), channel_id=1, source_target_pairs={{0,2},{1,3},{2,0},{3,1},{4,6},{5,7},{6,4},{7,5},{8,10},{9,11},{10,... | collective-permute-start | bytes 786440 | tf_op jit(solution)/shard_map/ppermute | solution.py:374
  6.6 4.8 %attend.1 = bf16[4,256,256]{2,1,0:T(8,128)(2,1)} custom-call(s32[4]{0:T(128)} %pad_add_fusion.info_ref, bf16[1024,256]{1,0:T(8,128)(2,1)} %bitcast.16, bf16[1024,256]{1,0:T(8,128)(2,1)} %bitcast.17, bf16[1024,256]{1,0:T(8,128)(2,1)} %bitcast.18), custom_call_target="tpu_custom_call" | custom-call | flops 1073741824 | bytes 2097152 | tf_op jit(solution)/shard_map/attend/pallas_call | solution.py:76
  11.7 3.6 %all-to-all-start = ((bf16[4,256,256]{2,1,0:T(8,128)(2,1)}), bf16[4,256,256]{2,1,0:T(8,128)(2,1)S(1)}, u32[]{:S(2)}, u32[]{:S(2)}) async-start(bf16[4,256,256]{2,1,0:T(8,128)(2,1)} %attend.1), calls=%async_computation | async-start | bytes 1048576 | tf_op jit(solution)/shard_map/all_to_all | solution.py:422
  15.3 1.7 %collective-permute-start.1 = (bf16[256,512]{1,0:T(8,128)(2,1)S(1)}, bf16[256,512]{1,0:T(8,128)(2,1)S(1)}, u32[]{:S(2)}, u32[]{:S(2)}) collective-permute-start(bf16[256,512]{1,0:T(8,128)(2,1)S(1)} %collective-permute-done.refs_2_), channel_id=1, source_target_pairs={{0,4},{4,0},{8,12},{12,8},{16,20},{20,16},{24,28},{28,24},{1,5},{5... | collective-permute-start | bytes 786440 | tf_op jit(solution)/shard_map/ppermute | solution.py:374
  17.9 6.1 %collective-permute-done.1.refs_3_ = bf16[256,512]{1,0:T(8,128)(2,1)S(1)} collective-permute-done((bf16[256,512]{1,0:T(8,128)(2,1)S(1)}, bf16[256,512]{1,0:T(8,128)(2,1)S(1)}, u32[]{:S(2)}, u32[]{:S(2)}) %collective-permute-start.1) | collective-permute-done | bytes 262176 | tf_op jit(solution)/shard_map/ppermute | solution.py:374
  24.1 1.6 %collective-permute-start.6 = (bf16[4,256,256]{2,1,0:T(8,128)(2,1)S(1)}, bf16[4,256,256]{2,1,0:T(8,128)(2,1)S(1)}, u32[]{:S(2)}, u32[]{:S(2)}) collective-permute-start(bf16[4,256,256]{2,1,0:T(8,128)(2,1)S(1)} %all-to-all-done.ctx_ref.refs_0_), channel_id=1, source_target_pairs={{0,4},{4,0},{8,12},{12,8},{16,20},{20,16},{24,28},{28,24},{1,5},{5... | collective-permute-start | bytes 1572872 | tf_op jit(solution)/shard_map/ppermute | solution.py:374
  25.7 1.6 %collective-permute-start.7 = (bf16[4,256,256]{2,1,0:T(8,128)(2,1)S(1)}, bf16[4,256,256]{2,1,0:T(8,128)(2,1)S(1)}, u32[]{:S(2)}, u32[]{:S(2)}) collective-permute-start(bf16[4,256,256]{2,1,0:T(8,128)(2,1)S(1)} %all-to-all-done.ctx_ref.refs_0_), channel_id=1, source_target_pairs={{0,8},{4,12},{8,0},{12,4},{16,24},{20,28},{24,16},{28,20},{1,9},{5... | collective-permute-start | bytes 1572872 | tf_op jit(solution)/shard_map/ppermute | solution.py:374
  27.3 1.6 %collective-permute-start.4 = (bf16[256,1024]{1,0:T(8,128)(2,1)}, bf16[256,1024]{1,0:T(8,128)(2,1)S(1)}, u32[]{:S(2)}, u32[]{:S(2)}) collective-permute-start(bf16[256,1024]{1,0:T(8,128)(2,1)} %slice.12), channel_id=1, source_target_pairs={{0,2},{1,3},{2,0},{3,1},{4,6},{5,7},{6,4},{7,5},{8,10},{9,11},{10,... | collective-permute-start | bytes 1572872 | tf_op jit(solution)/shard_map/ppermute | solution.py:374
  28.9 1.5 %collective-permute-done.5.refs_6_ = bf16[256,512]{1,0:T(8,128)(2,1)S(1)} collective-permute-done((bf16[256,512]{1,0:T(8,128)(2,1)S(1)}, bf16[256,512]{1,0:T(8,128)(2,1)S(1)}, u32[]{:S(2)}, u32[]{:S(2)}) %collective-permute-start.5) | collective-permute-done | bytes 262176 | tf_op jit(solution)/shard_map/ppermute | solution.py:374
  30.4 7.2 %collective-permute-done.6.refs_1_ = bf16[4,256,256]{2,1,0:T(8,128)(2,1)S(1)} collective-permute-done((bf16[4,256,256]{2,1,0:T(8,128)(2,1)S(1)}, bf16[4,256,256]{2,1,0:T(8,128)(2,1)S(1)}, u32[]{:S(2)}, u32[]{:S(2)}) %collective-permute-start.6) | collective-permute-done | bytes 524320 | tf_op jit(solution)/shard_map/ppermute | solution.py:374
  37.6 1.3 %collective-permute-done.7.refs_2_ = bf16[4,256,256]{2,1,0:T(8,128)(2,1)S(1)} collective-permute-done((bf16[4,256,256]{2,1,0:T(8,128)(2,1)S(1)}, bf16[4,256,256]{2,1,0:T(8,128)(2,1)S(1)}, u32[]{:S(2)}, u32[]{:S(2)}) %collective-permute-start.7) | collective-permute-done | bytes 524320 | tf_op jit(solution)/shard_map/ppermute | solution.py:374
  38.9 1.5 %collective-permute-done.4.refs_4_ = bf16[256,1024]{1,0:T(8,128)(2,1)S(1)} collective-permute-done((bf16[256,1024]{1,0:T(8,128)(2,1)}, bf16[256,1024]{1,0:T(8,128)(2,1)S(1)}, u32[]{:S(2)}, u32[]{:S(2)}) %collective-permute-start.4) | collective-permute-done | bytes 524320 | tf_op jit(solution)/shard_map/ppermute | solution.py:374
  42.3 5.6 %join.1 = (bf16[256,2048]{1,0:T(8,128)(2,1)}, bf16[288,256]{1,0:T(8,128)(2,1)S(1)}, bf16[288,256]{1,0:T(8,128)(2,1)S(1)}, bf16[288,256]{1,0:T(8,128)(2,1)S(1)}, ...) custom-call(s32[4]{0:T(128)S(1)} %copy-done.3, ...), custom_call_target="tpu_custom_call" | custom-call | flops 1073741824 | bytes 7340032 | tf_op jit(solution)/shard_map/join/pallas_call | solution.py:201
  48.8 1.5 %collective-permute-start.19 = (bf16[256,256]{1,0:T(8,128)(2,1)S(1)}, bf16[256,256]{1,0:T(8,128)(2,1)S(1)}, u32[]{:S(2)}, u32[]{:S(2)}) collective-permute-start(bf16[256,256]{1,0:T(8,128)(2,1)S(1)} %get-tuple-element.63), channel_id=1, source_target_pairs={{0,8},{4,12},{8,0},{12,4},{16,24},{20,28},{24,16},{28,20},{1,9},{5... | collective-permute-start | bytes 393224 | tf_op jit(solution)/shard_map/ppermute | solution.py:374
  52.3 1.5 %collective-permute-start.12 = (bf16[288,256]{1,0:T(8,128)(2,1)S(1)}, bf16[288,256]{1,0:T(8,128)(2,1)S(1)}, u32[]{:S(2)}, u32[]{:S(2)}) collective-permute-start(bf16[288,256]{1,0:T(8,128)(2,1)S(1)} %get-tuple-element.53), channel_id=1, source_target_pairs={{0,8},{4,12},{8,0},{12,4},{16,24},{20,28},{24,16},{28,20},{1,9},{5... | collective-permute-start | bytes 442376 | tf_op jit(solution)/shard_map/ppermute | solution.py:374
  53.8 1.6 %collective-permute-start.13 = (bf16[288,256]{1,0:T(8,128)(2,1)S(1)}, bf16[288,256]{1,0:T(8,128)(2,1)S(1)}, u32[]{:S(2)}, u32[]{:S(2)}) collective-permute-start(bf16[288,256]{1,0:T(8,128)(2,1)S(1)} %get-tuple-element.54), channel_id=1, source_target_pairs={{0,12},{4,8},{8,4},{12,0},{16,28},{20,24},{24,20},{28,16},{1,13},{... | collective-permute-start | bytes 442376 | tf_op jit(solution)/shard_map/ppermute | solution.py:374
  55.4 3.2 %collective-permute-done.20.refs_8_ = bf16[256,256]{1,0:T(8,128)(2,1)S(1)} collective-permute-done((bf16[256,256]{1,0:T(8,128)(2,1)S(1)}, bf16[256,256]{1,0:T(8,128)(2,1)S(1)}, u32[]{:S(2)}, u32[]{:S(2)}) %collective-permute-start.20) | collective-permute-done | bytes 131104 | tf_op jit(solution)/shard_map/ppermute | solution.py:374
  61.2 2.6 %collective-permute-done.13.refs_8_ = bf16[288,256]{1,0:T(8,128)(2,1)S(1)} collective-permute-done((bf16[288,256]{1,0:T(8,128)(2,1)S(1)}, bf16[288,256]{1,0:T(8,128)(2,1)S(1)}, u32[]{:S(2)}, u32[]{:S(2)}) %collective-permute-start.13) | collective-permute-done | bytes 147488 | tf_op jit(solution)/shard_map/ppermute | solution.py:374
  65.2 2.7 %collective-permute-start.22 = (bf16[1,1,256,128]{3,2,1,0:T(8,128)(2,1)S(1)}, bf16[1,1,256,128]{3,2,1,0:T(8,128)(2,1)S(1)}, u32[]{:S(2)}, u32[]{:S(2)}) collective-permute-start(bf16[1,1,256,128]{3,2,1,0:T(8,128)(2,1)S(1)} %get-tuple-element.68), channel_id=1, source_target_pairs={{0,16},{1,17},{2,18},{3,19},{4,20},{5,21},{6,22},{7,23},{8,24},{9,... | collective-permute-start | bytes 196616 | tf_op jit(solution)/shard_map/ppermute | solution.py:379
  67.9 1.5 %collective-permute-start.15 = (bf16[1,1,304,128]{3,2,1,0:T(8,128)(2,1)S(1)}, bf16[1,1,304,128]{3,2,1,0:T(8,128)(2,1)S(1)}, u32[]{:S(2)}, u32[]{:S(2)}) collective-permute-start(bf16[1,1,304,128]{3,2,1,0:T(8,128)(2,1)S(1)} %get-tuple-element.58), channel_id=1, source_target_pairs={{0,16},{1,17},{2,18},{3,19},{4,20},{5,21},{6,22},{7,23},{8,24},{9,... | collective-permute-start | bytes 233480 | tf_op jit(solution)/shard_map/ppermute | solution.py:379
  70.7 1.7 %collective-permute-start.17 = (bf16[1,1,304,128]{3,2,1,0:T(8,128)(2,1)S(1)}, bf16[1,1,304,128]{3,2,1,0:T(8,128)(2,1)S(1)}, u32[]{:S(2)}, u32[]{:S(2)}) collective-permute-start(bf16[1,1,304,128]{3,2,1,0:T(8,128)(2,1)S(1)} %get-tuple-element.60), channel_id=1, source_target_pairs={{0,18},{1,19},{2,16},{3,17},{4,22},{5,23},{6,20},{7,21},{8,26},{9,... | collective-permute-start | bytes 233480 | tf_op jit(solution)/shard_map/ppermute | solution.py:379
  73.9 1.3 %collective-permute-start.24 = (bf16[1,1,256,128]{3,2,1,0:T(8,128)(2,1)S(1)}, bf16[1,1,256,128]{3,2,1,0:T(8,128)(2,1)S(1)}, u32[]{:S(2)}, u32[]{:S(2)}) collective-permute-start(bf16[1,1,256,128]{3,2,1,0:T(8,128)(2,1)S(1)} %get-tuple-element.70), channel_id=1, source_target_pairs={{0,18},{1,19},{2,16},{3,17},{4,22},{5,23},{6,20},{7,21},{8,26},{9,... | collective-permute-start | bytes 196616 | tf_op jit(solution)/shard_map/ppermute | solution.py:379
  75.3 1.4 %collective-permute-done.23.refs_6_ = bf16[1,1,256,128]{3,2,1,0:T(8,128)(2,1)S(1)} collective-permute-done((bf16[1,1,256,128]{3,2,1,0:T(8,128)(2,1)S(1)}, bf16[1,1,256,128]{3,2,1,0:T(8,128)(2,1)S(1)}, u32[]{:S(2)}, u32[]{:S(2)}) %collective-permute-start.23) | collective-permute-done | bytes 65568 | tf_op jit(solution)/shard_map/ppermute | solution.py:379
  76.6 5.6 %collective-permute-done.24.refs_7_ = bf16[1,1,256,128]{3,2,1,0:T(8,128)(2,1)S(1)} collective-permute-done((bf16[1,1,256,128]{3,2,1,0:T(8,128)(2,1)S(1)}, bf16[1,1,256,128]{3,2,1,0:T(8,128)(2,1)S(1)}, u32[]{:S(2)}, u32[]{:S(2)}) %collective-permute-start.24) | collective-permute-done | bytes 65568 | tf_op jit(solution)/shard_map/ppermute | solution.py:379
  (48 shorter events, 15.8 us)
Async XLA Ops:
  0.6 23.5 %collective-permute-start.3 = (bf16[256,2048]{1,0:T(8,128)(2,1)}, bf16[256,2048]{1,0:T(8,128)(2,1)}, u32[]{:S(2)}, u32[]{:S(2)}) collective-permute-start(bf16[256,2048]{1,0:T(8,128)(2,1)} %bitcast.12), channel_id=1, source_target_pairs={{0,1},{1,0},{2,3},{3,2},{4,5},{5,4},{6,7},{7,6},{8,9},{9,8},{10,11... | collective-permute-start | bytes 3145736 | tf_op jit(solution)/shard_map/ppermute | solution.py:374
  2.1 9.6 %collective-permute-start = (bf16[256,512]{1,0:T(8,128)(2,1)S(1)}, bf16[256,512]{1,0:T(8,128)(2,1)S(1)}, u32[]{:S(2)}, u32[]{:S(2)}) collective-permute-start(bf16[256,512]{1,0:T(8,128)(2,1)S(1)} %dynamic-slice_bitcast_fusion), channel_id=1, source_target_pairs={{0,2},{1,3},{2,0},{3,1},{4,6},{5,7},{6,4},{7,5},{8,10},{9,11},{10,... | collective-permute-start | bytes 786440 | tf_op jit(solution)/shard_map/ppermute | solution.py:374
  11.7 12.4 %all-to-all-start = ((bf16[4,256,256]{2,1,0:T(8,128)(2,1)}), bf16[4,256,256]{2,1,0:T(8,128)(2,1)S(1)}, u32[]{:S(2)}, u32[]{:S(2)}) async-start(bf16[4,256,256]{2,1,0:T(8,128)(2,1)} %attend.1), calls=%async_computation | async-start | bytes 1048576 | tf_op jit(solution)/shard_map/all_to_all | solution.py:422
  15.3 8.7 %collective-permute-start.1 = (bf16[256,512]{1,0:T(8,128)(2,1)S(1)}, bf16[256,512]{1,0:T(8,128)(2,1)S(1)}, u32[]{:S(2)}, u32[]{:S(2)}) collective-permute-start(bf16[256,512]{1,0:T(8,128)(2,1)S(1)} %collective-permute-done.refs_2_), channel_id=1, source_target_pairs={{0,4},{4,0},{8,12},{12,8},{16,20},{20,16},{24,28},{28,24},{1,5},{5... | collective-permute-start | bytes 786440 | tf_op jit(solution)/shard_map/ppermute | solution.py:374
  17.0 7.0 %collective-permute-start.2 = (bf16[256,512]{1,0:T(8,128)(2,1)S(1)}, bf16[256,512]{1,0:T(8,128)(2,1)S(1)}, u32[]{:S(2)}, u32[]{:S(2)}) collective-permute-start(bf16[256,512]{1,0:T(8,128)(2,1)S(1)} %collective-permute-done.refs_2_), channel_id=1, source_target_pairs={{0,1},{1,0},{2,3},{3,2},{4,5},{5,4},{6,7},{7,6},{8,9},{9,8},{10,11... | collective-permute-start | bytes 786440 | tf_op jit(solution)/shard_map/ppermute | solution.py:374
  24.1 13.5 %collective-permute-start.6 = (bf16[4,256,256]{2,1,0:T(8,128)(2,1)S(1)}, bf16[4,256,256]{2,1,0:T(8,128)(2,1)S(1)}, u32[]{:S(2)}, u32[]{:S(2)}) collective-permute-start(bf16[4,256,256]{2,1,0:T(8,128)(2,1)S(1)} %all-to-all-done.ctx_ref.refs_0_), channel_id=1, source_target_pairs={{0,4},{4,0},{8,12},{12,8},{16,20},{20,16},{24,28},{28,24},{1,5},{5... | collective-permute-start | bytes 1572872 | tf_op jit(solution)/shard_map/ppermute | solution.py:374
  25.7 13.2 %collective-permute-start.7 = (bf16[4,256,256]{2,1,0:T(8,128)(2,1)S(1)}, bf16[4,256,256]{2,1,0:T(8,128)(2,1)S(1)}, u32[]{:S(2)}, u32[]{:S(2)}) collective-permute-start(bf16[4,256,256]{2,1,0:T(8,128)(2,1)S(1)} %all-to-all-done.ctx_ref.refs_0_), channel_id=1, source_target_pairs={{0,8},{4,12},{8,0},{12,4},{16,24},{20,28},{24,16},{28,20},{1,9},{5... | collective-permute-start | bytes 1572872 | tf_op jit(solution)/shard_map/ppermute | solution.py:374
  27.3 13.1 %collective-permute-start.4 = (bf16[256,1024]{1,0:T(8,128)(2,1)}, bf16[256,1024]{1,0:T(8,128)(2,1)S(1)}, u32[]{:S(2)}, u32[]{:S(2)}) collective-permute-start(bf16[256,1024]{1,0:T(8,128)(2,1)} %slice.12), channel_id=1, source_target_pairs={{0,2},{1,3},{2,0},{3,1},{4,6},{5,7},{6,4},{7,5},{8,10},{9,11},{10,... | collective-permute-start | bytes 1572872 | tf_op jit(solution)/shard_map/ppermute | solution.py:374
  40.4 11.0 %collective-permute-start.10 = (bf16[4,128,256]{2,1,0:T(8,128)(2,1)S(1)}, bf16[4,128,256]{2,1,0:T(8,128)(2,1)S(1)}, u32[]{:S(2)}, u32[]{:S(2)}) collective-permute-start(bf16[4,128,256]{2,1,0:T(8,128)(2,1)S(1)} %slice.11), channel_id=1, source_target_pairs={{0,4},{4,0},{8,12},{12,8},{16,20},{20,16},{24,28},{28,24},{1,5},{5... | collective-permute-start | bytes 786440 | tf_op jit(solution)/shard_map/ppermute | solution.py:374
  41.1 11.3 %collective-permute-start.9 = (bf16[4,128,256]{2,1,0:T(8,128)(2,1)S(1)}, bf16[4,128,256]{2,1,0:T(8,128)(2,1)S(1)}, u32[]{:S(2)}, u32[]{:S(2)}) collective-permute-start(bf16[4,128,256]{2,1,0:T(8,128)(2,1)S(1)} %slice.10), channel_id=1, source_target_pairs={{0,8},{4,12},{8,0},{12,4},{16,24},{20,28},{24,16},{28,20},{1,9},{5... | collective-permute-start | bytes 786440 | tf_op jit(solution)/shard_map/ppermute | solution.py:374
  47.9 5.9 %collective-permute-start.18 = (bf16[256,256]{1,0:T(8,128)(2,1)S(1)}, bf16[256,256]{1,0:T(8,128)(2,1)S(1)}, u32[]{:S(2)}, u32[]{:S(2)}) collective-permute-start(bf16[256,256]{1,0:T(8,128)(2,1)S(1)} %get-tuple-element.62), channel_id=1, source_target_pairs={{0,4},{4,0},{8,12},{12,8},{16,20},{20,16},{24,28},{28,24},{1,5},{5... | collective-permute-start | bytes 393224 | tf_op jit(solution)/shard_map/ppermute | solution.py:374
  48.8 6.6 %collective-permute-start.19 = (bf16[256,256]{1,0:T(8,128)(2,1)S(1)}, bf16[256,256]{1,0:T(8,128)(2,1)S(1)}, u32[]{:S(2)}, u32[]{:S(2)}) collective-permute-start(bf16[256,256]{1,0:T(8,128)(2,1)S(1)} %get-tuple-element.63), channel_id=1, source_target_pairs={{0,8},{4,12},{8,0},{12,4},{16,24},{20,28},{24,16},{28,20},{1,9},{5... | collective-permute-start | bytes 393224 | tf_op jit(solution)/shard_map/ppermute | solution.py:374
  50.3 8.3 %collective-permute-start.20 = (bf16[256,256]{1,0:T(8,128)(2,1)S(1)}, bf16[256,256]{1,0:T(8,128)(2,1)S(1)}, u32[]{:S(2)}, u32[]{:S(2)}) collective-permute-start(bf16[256,256]{1,0:T(8,128)(2,1)S(1)} %get-tuple-element.64), channel_id=1, source_target_pairs={{0,12},{4,8},{8,4},{12,0},{16,28},{20,24},{24,20},{28,16},{1,13},{... | collective-permute-start | bytes 393224 | tf_op jit(solution)/shard_map/ppermute | solution.py:374
  51.4 8.5 %collective-permute-start.11 = (bf16[288,256]{1,0:T(8,128)(2,1)S(1)}, bf16[288,256]{1,0:T(8,128)(2,1)S(1)}, u32[]{:S(2)}, u32[]{:S(2)}) collective-permute-start(bf16[288,256]{1,0:T(8,128)(2,1)S(1)} %get-tuple-element.52), channel_id=1, source_target_pairs={{0,4},{4,0},{8,12},{12,8},{16,20},{20,16},{24,28},{28,24},{1,5},{5... | collective-permute-start | bytes 442376 | tf_op jit(solution)/shard_map/ppermute | solution.py:374
  52.3 8.8 %collective-permute-start.12 = (bf16[288,256]{1,0:T(8,128)(2,1)S(1)}, bf16[288,256]{1,0:T(8,128)(2,1)S(1)}, u32[]{:S(2)}, u32[]{:S(2)}) collective-permute-start(bf16[288,256]{1,0:T(8,128)(2,1)S(1)} %get-tuple-element.53), channel_id=1, source_target_pairs={{0,8},{4,12},{8,0},{12,4},{16,24},{20,28},{24,16},{28,20},{1,9},{5... | collective-permute-start | bytes 442376 | tf_op jit(solution)/shard_map/ppermute | solution.py:374
  53.8 10.0 %collective-permute-start.13 = (bf16[288,256]{1,0:T(8,128)(2,1)S(1)}, bf16[288,256]{1,0:T(8,128)(2,1)S(1)}, u32[]{:S(2)}, u32[]{:S(2)}) collective-permute-start(bf16[288,256]{1,0:T(8,128)(2,1)S(1)} %get-tuple-element.54), channel_id=1, source_target_pairs={{0,12},{4,8},{8,4},{12,0},{16,28},{20,24},{24,20},{28,16},{1,13},{... | collective-permute-start | bytes 442376 | tf_op jit(solution)/shard_map/ppermute | solution.py:374
  59.8 5.3 %collective-permute-start.21 = (bf16[2,2,256,128]{3,2,1,0:T(8,128)(2,1)S(1)}, bf16[2,2,256,128]{3,2,1,0:T(8,128)(2,1)S(1)}, u32[]{:S(2)}, u32[]{:S(2)}) collective-permute-start(bf16[2,2,256,128]{3,2,1,0:T(8,128)(2,1)S(1)} %get-tuple-element.66), channel_id=1, source_target_pairs={{0,1},{1,0},{2,3},{3,2},{4,5},{5,4},{6,7},{7,6},{8,9},{9,8},{10,11... | collective-permute-start | bytes 786440 | tf_op jit(solution)/shard_map/ppermute | solution.py:374
  65.0 2.8 %collective-permute-start.14 = (bf16[2,2,304,128]{3,2,1,0:T(8,128)(2,1)S(1)}, bf16[2,2,304,128]{3,2,1,0:T(8,128)(2,1)S(1)}, u32[]{:S(2)}, u32[]{:S(2)}) collective-permute-start(bf16[2,2,304,128]{3,2,1,0:T(8,128)(2,1)S(1)} %get-tuple-element.56), channel_id=1, source_target_pairs={{0,1},{1,0},{2,3},{3,2},{4,5},{5,4},{6,7},{7,6},{8,9},{9,8},{10,11... | collective-permute-start | bytes 933896 | tf_op jit(solution)/shard_map/ppermute | solution.py:374
  65.2 8.7 %collective-permute-start.22 = (bf16[1,1,256,128]{3,2,1,0:T(8,128)(2,1)S(1)}, bf16[1,1,256,128]{3,2,1,0:T(8,128)(2,1)S(1)}, u32[]{:S(2)}, u32[]{:S(2)}) collective-permute-start(bf16[1,1,256,128]{3,2,1,0:T(8,128)(2,1)S(1)} %get-tuple-element.68), channel_id=1, source_target_pairs={{0,16},{1,17},{2,18},{3,19},{4,20},{5,21},{6,22},{7,23},{8,24},{9,... | collective-permute-start | bytes 196616 | tf_op jit(solution)/shard_map/ppermute | solution.py:379
  67.9 14.3 %collective-permute-start.15 = (bf16[1,1,304,128]{3,2,1,0:T(8,128)(2,1)S(1)}, bf16[1,1,304,128]{3,2,1,0:T(8,128)(2,1)S(1)}, u32[]{:S(2)}, u32[]{:S(2)}) collective-permute-start(bf16[1,1,304,128]{3,2,1,0:T(8,128)(2,1)S(1)} %get-tuple-element.58), channel_id=1, source_target_pairs={{0,16},{1,17},{2,18},{3,19},{4,20},{5,21},{6,22},{7,23},{8,24},{9,... | collective-permute-start | bytes 233480 | tf_op jit(solution)/shard_map/ppermute | solution.py:379
  69.4 12.8 %collective-permute-start.16 = (bf16[1,1,304,128]{3,2,1,0:T(8,128)(2,1)S(1)}, bf16[1,1,304,128]{3,2,1,0:T(8,128)(2,1)S(1)}, u32[]{:S(2)}, u32[]{:S(2)}) collective-permute-start(bf16[1,1,304,128]{3,2,1,0:T(8,128)(2,1)S(1)} %get-tuple-element.59), channel_id=1, source_target_pairs={{0,2},{1,3},{2,0},{3,1},{4,6},{5,7},{6,4},{7,5},{8,10},{9,11},{10,... | collective-permute-start | bytes 233480 | tf_op jit(solution)/shard_map/ppermute | solution.py:379
  70.7 11.5 %collective-permute-start.17 = (bf16[1,1,304,128]{3,2,1,0:T(8,128)(2,1)S(1)}, bf16[1,1,304,128]{3,2,1,0:T(8,128)(2,1)S(1)}, u32[]{:S(2)}, u32[]{:S(2)}) collective-permute-start(bf16[1,1,304,128]{3,2,1,0:T(8,128)(2,1)S(1)} %get-tuple-element.60), channel_id=1, source_target_pairs={{0,18},{1,19},{2,16},{3,17},{4,22},{5,23},{6,20},{7,21},{8,26},{9,... | collective-permute-start | bytes 233480 | tf_op jit(solution)/shard_map/ppermute | solution.py:379
  72.4 4.3 %collective-permute-start.23 = (bf16[1,1,256,128]{3,2,1,0:T(8,128)(2,1)S(1)}, bf16[1,1,256,128]{3,2,1,0:T(8,128)(2,1)S(1)}, u32[]{:S(2)}, u32[]{:S(2)}) collective-permute-start(bf16[1,1,256,128]{3,2,1,0:T(8,128)(2,1)S(1)} %get-tuple-element.69), channel_id=1, source_target_pairs={{0,2},{1,3},{2,0},{3,1},{4,6},{5,7},{6,4},{7,5},{8,10},{9,11},{10,... | collective-permute-start | bytes 196616 | tf_op jit(solution)/shard_map/ppermute | solution.py:379
  73.9 8.3 %collective-permute-start.24 = (bf16[1,1,256,128]{3,2,1,0:T(8,128)(2,1)S(1)}, bf16[1,1,256,128]{3,2,1,0:T(8,128)(2,1)S(1)}, u32[]{:S(2)}, u32[]{:S(2)}) collective-permute-start(bf16[1,1,256,128]{3,2,1,0:T(8,128)(2,1)S(1)} %get-tuple-element.70), channel_id=1, source_target_pairs={{0,18},{1,19},{2,16},{3,17},{4,22},{5,23},{6,20},{7,21},{8,26},{9,... | collective-permute-start | bytes 196616 | tf_op jit(solution)/shard_map/ppermute | solution.py:379
  (6 other events, 39.2 us)

commit v8 on v7

--- a/solution.py
+++ b/solution.py
@@ -239,41 +239,40 @@
     return words[:n] + words[n : 2 * n], words[2 * n : 2 * n + 1] + words[2 * n + 1 : 2 * n + 2]
 
 
-def grad_body(plan, dout, counts, info_ref, *refs):
+def grad_body(plan, dout, counts, s, info_ref, *refs):
     n_dp, n_tensor, _, _, xor_far = plan
-    keep_ref, send_ref = refs[-2:]
+    ref = refs[-1]
     ctx_refs, at = [], 0
     for n in counts:
         ctx_refs.append(refs[at : at + n])
         at += n
-    g_refs = refs[at:-2]
-    n_y, n_far, tall, cw = keep_ref.shape
+    g_refs = refs[at:-1]
+    n_y, n_far, tall, cw = ref.shape
     feats, rows = ctx_refs[0][0].shape[1:]
     wide = n_far * cw
     me = info_ref[0]
     core, y = me % 2, me // 2
     if tall > feats:
         in_piece, in_block, stat_rows = stat_sizes(dout, wide, cw)
-        sums = sum(ref[rows:, :].astype(F32) for ref in g_refs)
+        sums = sum(g[rows:, :].astype(F32) for g in g_refs)
         gains, scalars = block_sums(sums, in_piece)
         gains = jnp.concatenate([gains[:, b * cw : (b + 1) * cw] for b in range(n_far)], 0)
         words = block_words(gains, scalars[:, :cw], stat_rows, cw)
-    for s, ref in ((1, send_ref), (0, keep_ref)):
-        for a in range(n_y):
-            m = (y ^ a if xor_far else a) * 2 + (core ^ s)
-            total = None
-            for parts, g in zip(ctx_refs, g_refs):
-                c = jnp.concatenate([part[m] for part in parts], 0) if len(parts) > 1 else parts[0][m]
-                part = dot(c, g[:rows, :], ((1,), (0,)))
-                total = part if total is None else total + part
-            total = total.astype(BF)
-            for b in range(n_far):
-                ref[a, b, :feats, :] = total[:, b * cw : (b + 1) * cw]
-                if tall > feats:
-                    ref[a, b, feats:, :] = words
-
-
-def gradient(plan, dout, info, ctxs, grads):
+    for a in range(n_y):
+        m = (y ^ a if xor_far else a) * 2 + (core ^ s)
+        total = None
+        for parts, g in zip(ctx_refs, g_refs):
+            c = jnp.concatenate([part[m] for part in parts], 0) if len(parts) > 1 else parts[0][m]
+            part = dot(c, g[:rows, :], ((1,), (0,)))
+            total = part if total is None else total + part
+        total = total.astype(BF)
+        for b in range(n_far):
+            ref[a, b, :feats, :] = total[:, b * cw : (b + 1) * cw]
+            if tall > feats:
+                ref[a, b, feats:, :] = words
+
+
+def gradient(plan, dout, info, ctxs, grads, s):
     n_dp, n_tensor, chunks, _, _ = plan
     _, feats, rows = ctxs[0][0].shape
     wide = grads[0].shape[1]
@@ -283,14 +282,14 @@
         tall += stat_sizes(dout, wide, cw)[2]
     block = shape((n_tensor // 2, n_dp // NEAR, tall, cw))
     return pl.pallas_call(
-        functools.partial(grad_body, plan, dout, [len(c) for c in ctxs]),
+        functools.partial(grad_body, plan, dout, [len(c) for c in ctxs], s),
         in_specs=[SM] + [VM] * (NEAR + sum(len(c) for c in ctxs)),
-        out_specs=[VM, VM],
-        out_shape=[block, block],
+        out_specs=VM,
+        out_shape=block,
         compiler_params=params(),
         cost_estimate=pl.CostEstimate(
-            flops=2 * NEAR * n_tensor * rows * feats * wide,
-            bytes_accessed=2 * (NEAR * rows * (n_tensor * feats + wide) + n_tensor * feats * wide),
+            flops=NEAR * n_tensor * rows * feats * wide,
+            bytes_accessed=NEAR * rows * (n_tensor * feats + 2 * wide) + n_tensor * feats * wide,
             transcendentals=0,
         ),
         name="gradient",
@@ -460,7 +459,8 @@
     parts = []
     for j in range(chunks):
         near = [grads[j][0]] + [swap(grads[j][q], "dp", n_dp, q) for q in range(1, NEAR)]
-        keep, send = gradient(plan, dout, info, ctxs, near)
+        send = gradient(plan, dout, info, ctxs, near, 1)
+        keep = gradient(plan, dout, info, ctxs, near, 0)
         blocks = merge(plan, dout, width, keep, swap(send, "tensor", n_tensor, 1))
         parts.append(exchange_far(plan, blocks))
     weight_grad, gain_grad, loss = finish(plan, dout, width, parts)

time: 83.3 us -> 84.7 us (1.017)
  Pallas kernels: 13.9 us -> 15.3 us
  starting transfers between devices: 31.7 us -> 30.8 us
    pallas_call x2 -> x4, Pallas kernels: 2.5 us -> 3.9 us  [gradient(): pl.pallas_call(functools.partial(grad_body, plan, dout, [len(c) for c in...]
  transfers between devices with their start and end apart: 26 -> 26, of which waited for: 14 -> 13; matrix products, arithmetic and copies ran while one was open for 3% -> 3% of each run, Pallas kernels for 16% -> 17%
where the time goes in v8:
time: 84.7 us; the launch traced here: 84.4 us
  waiting for transfers between devices  33.8 us (40%)
  starting transfers between devices  30.8 us (36%)
  Pallas kernels  15.3 us (18%)
  between operations  2.09 us (2%)
  local copies, waits for them, and re-layouts  1.87 us (2%)
    ppermute x19, waiting for transfers between devices, swap(): return lax.ppermute(x, axis, [(i, i ^ mask) for i in range(n)])  25.9 us
    ppermute x19, starting transfers between devices, swap(): return lax.ppermute(x, axis, [(i, i ^ mask) for i in range(n)])  18.3 us
    ppermute x6, starting transfers between devices, swap_far(): lax.ppermute(x, ('dp', 'tensor'), [(i, i ^ mask) for i in range(n_dp * n_...  8.9 us
    ppermute x6, waiting for transfers between devices, swap_far(): lax.ppermute(x, ('dp', 'tensor'), [(i, i ^ mask) for i in range(n_dp * n_...  7.73 us
    pallas_call x1, Pallas kernels, join(): pl.pallas_call(functools.partial(join_body, plan, [len(w) for w in weight...  5.63 us
    pallas_call x1, Pallas kernels, attend(): pl.pallas_call(attend_body, in_specs=[SM, block, block, block], out_specs...  4.83 us
    pallas_call x4, Pallas kernels, gradient(): pl.pallas_call(functools.partial(grad_body, plan, dout, [len(c) for c in...  3.9 us
    all_to_all x1, starting transfers between devices, gather_small(): ctx = lax.all_to_all(context, 'tensor', 0, 0, tiled=True)  3.6 us
  transfers between devices with their start and end apart: 26, of which 13 were waited for; matrix products, arithmetic and copies ran while one was open for 3% of the time, Pallas kernels for 17%

profile of v8, /device:TPU:0, one launch (start us, length us, event | category | flops | bytes accessed | tf_op | source)
XLA Modules:
  0.0 84.4 jit_solution(17061690179411044443)
XLA Ops:
  2.1 2.6 %collective-permute-start = (bf16[256,512]{1,0:T(8,128)(2,1)S(1)}, bf16[256,512]{1,0:T(8,128)(2,1)S(1)}, u32[]{:S(2)}, u32[]{:S(2)}) collective-permute-start(bf16[256,512]{1,0:T(8,128)(2,1)S(1)} %dynamic-slice_bitcast_fusion), channel_id=1, source_target_pairs={{0,2},{1,3},{2,0},{3,1},{4,6},{5,7},{6,4},{7,5},{8,10},{9,11},{10,... | collective-permute-start | bytes 786440 | tf_op jit(solution)/shard_map/ppermute | solution.py:373
  6.6 4.8 %attend.1 = bf16[4,256,256]{2,1,0:T(8,128)(2,1)} custom-call(s32[4]{0:T(128)} %pad_add_fusion.info_ref, bf16[1024,256]{1,0:T(8,128)(2,1)} %bitcast.16, bf16[1024,256]{1,0:T(8,128)(2,1)} %bitcast.17, bf16[1024,256]{1,0:T(8,128)(2,1)} %bitcast.18), custom_call_target="tpu_custom_call" | custom-call | flops 1073741824 | bytes 2097152 | tf_op jit(solution)/shard_map/attend/pallas_call | solution.py:76
  11.7 3.6 %all-to-all-start = ((bf16[4,256,256]{2,1,0:T(8,128)(2,1)}), bf16[4,256,256]{2,1,0:T(8,128)(2,1)S(1)}, u32[]{:S(2)}, u32[]{:S(2)}) async-start(bf16[4,256,256]{2,1,0:T(8,128)(2,1)} %attend.1), calls=%async_computation | async-start | bytes 1048576 | tf_op jit(solution)/shard_map/all_to_all | solution.py:421
  15.3 1.7 %collective-permute-start.1 = (bf16[256,512]{1,0:T(8,128)(2,1)S(1)}, bf16[256,512]{1,0:T(8,128)(2,1)S(1)}, u32[]{:S(2)}, u32[]{:S(2)}) collective-permute-start(bf16[256,512]{1,0:T(8,128)(2,1)S(1)} %collective-permute-done.refs_2_), channel_id=1, source_target_pairs={{0,4},{4,0},{8,12},{12,8},{16,20},{20,16},{24,28},{28,24},{1,5},{5... | collective-permute-start | bytes 786440 | tf_op jit(solution)/shard_map/ppermute | solution.py:373
  17.9 6.1 %collective-permute-done.1.refs_3_ = bf16[256,512]{1,0:T(8,128)(2,1)S(1)} collective-permute-done((bf16[256,512]{1,0:T(8,128)(2,1)S(1)}, bf16[256,512]{1,0:T(8,128)(2,1)S(1)}, u32[]{:S(2)}, u32[]{:S(2)}) %collective-permute-start.1) | collective-permute-done | bytes 262176 | tf_op jit(solution)/shard_map/ppermute | solution.py:373
  24.1 1.6 %collective-permute-start.6 = (bf16[4,256,256]{2,1,0:T(8,128)(2,1)S(1)}, bf16[4,256,256]{2,1,0:T(8,128)(2,1)S(1)}, u32[]{:S(2)}, u32[]{:S(2)}) collective-permute-start(bf16[4,256,256]{2,1,0:T(8,128)(2,1)S(1)} %all-to-all-done.ctx_ref.refs_0_), channel_id=1, source_target_pairs={{0,4},{4,0},{8,12},{12,8},{16,20},{20,16},{24,28},{28,24},{1,5},{5... | collective-permute-start | bytes 1572872 | tf_op jit(solution)/shard_map/ppermute | solution.py:373
  25.7 1.6 %collective-permute-start.7 = (bf16[4,256,256]{2,1,0:T(8,128)(2,1)S(1)}, bf16[4,256,256]{2,1,0:T(8,128)(2,1)S(1)}, u32[]{:S(2)}, u32[]{:S(2)}) collective-permute-start(bf16[4,256,256]{2,1,0:T(8,128)(2,1)S(1)} %all-to-all-done.ctx_ref.refs_0_), channel_id=1, source_target_pairs={{0,8},{4,12},{8,0},{12,4},{16,24},{20,28},{24,16},{28,20},{1,9},{5... | collective-permute-start | bytes 1572872 | tf_op jit(solution)/shard_map/ppermute | solution.py:373
  27.3 1.6 %collective-permute-start.4 = (bf16[256,1024]{1,0:T(8,128)(2,1)}, bf16[256,1024]{1,0:T(8,128)(2,1)S(1)}, u32[]{:S(2)}, u32[]{:S(2)}) collective-permute-start(bf16[256,1024]{1,0:T(8,128)(2,1)} %slice.12), channel_id=1, source_target_pairs={{0,2},{1,3},{2,0},{3,1},{4,6},{5,7},{6,4},{7,5},{8,10},{9,11},{10,... | collective-permute-start | bytes 1572872 | tf_op jit(solution)/shard_map/ppermute | solution.py:373
  28.9 1.5 %collective-permute-done.5.refs_6_ = bf16[256,512]{1,0:T(8,128)(2,1)S(1)} collective-permute-done((bf16[256,512]{1,0:T(8,128)(2,1)S(1)}, bf16[256,512]{1,0:T(8,128)(2,1)S(1)}, u32[]{:S(2)}, u32[]{:S(2)}) %collective-permute-start.5) | collective-permute-done | bytes 262176 | tf_op jit(solution)/shard_map/ppermute | solution.py:373
  30.4 7.2 %collective-permute-done.6.refs_1_ = bf16[4,256,256]{2,1,0:T(8,128)(2,1)S(1)} collective-permute-done((bf16[4,256,256]{2,1,0:T(8,128)(2,1)S(1)}, bf16[4,256,256]{2,1,0:T(8,128)(2,1)S(1)}, u32[]{:S(2)}, u32[]{:S(2)}) %collective-permute-start.6) | collective-permute-done | bytes 524320 | tf_op jit(solution)/shard_map/ppermute | solution.py:373
  37.6 1.3 %collective-permute-done.7.refs_2_ = bf16[4,256,256]{2,1,0:T(8,128)(2,1)S(1)} collective-permute-done((bf16[4,256,256]{2,1,0:T(8,128)(2,1)S(1)}, bf16[4,256,256]{2,1,0:T(8,128)(2,1)S(1)}, u32[]{:S(2)}, u32[]{:S(2)}) %collective-permute-start.7) | collective-permute-done | bytes 524320 | tf_op jit(solution)/shard_map/ppermute | solution.py:373
  38.9 1.5 %collective-permute-done.4.refs_4_ = bf16[256,1024]{1,0:T(8,128)(2,1)S(1)} collective-permute-done((bf16[256,1024]{1,0:T(8,128)(2,1)}, bf16[256,1024]{1,0:T(8,128)(2,1)S(1)}, u32[]{:S(2)}, u32[]{:S(2)}) %collective-permute-start.4) | collective-permute-done | bytes 524320 | tf_op jit(solution)/shard_map/ppermute | solution.py:373
  42.3 5.6 %join.1 = (bf16[256,2048]{1,0:T(8,128)(2,1)}, bf16[288,256]{1,0:T(8,128)(2,1)S(1)}, bf16[288,256]{1,0:T(8,128)(2,1)S(1)}, bf16[288,256]{1,0:T(8,128)(2,1)S(1)}, ...) custom-call(s32[4]{0:T(128)S(1)} %copy-done.2, ...), custom_call_target="tpu_custom_call" | custom-call | flops 1073741824 | bytes 7340032 | tf_op jit(solution)/shard_map/join/pallas_call | solution.py:201
  48.8 1.5 %collective-permute-start.19 = (bf16[256,256]{1,0:T(8,128)(2,1)S(1)}, bf16[256,256]{1,0:T(8,128)(2,1)S(1)}, u32[]{:S(2)}, u32[]{:S(2)}) collective-permute-start(bf16[256,256]{1,0:T(8,128)(2,1)S(1)} %get-tuple-element.57), channel_id=1, source_target_pairs={{0,8},{4,12},{8,0},{12,4},{16,24},{20,28},{24,16},{28,20},{1,9},{5... | collective-permute-start | bytes 393224 | tf_op jit(solution)/shard_map/ppermute | solution.py:373
  52.3 1.5 %collective-permute-start.12 = (bf16[288,256]{1,0:T(8,128)(2,1)S(1)}, bf16[288,256]{1,0:T(8,128)(2,1)S(1)}, u32[]{:S(2)}, u32[]{:S(2)}) collective-permute-start(bf16[288,256]{1,0:T(8,128)(2,1)S(1)} %get-tuple-element.49), channel_id=1, source_target_pairs={{0,8},{4,12},{8,0},{12,4},{16,24},{20,28},{24,16},{28,20},{1,9},{5... | collective-permute-start | bytes 442376 | tf_op jit(solution)/shard_map/ppermute | solution.py:373
  53.8 1.6 %collective-permute-start.13 = (bf16[288,256]{1,0:T(8,128)(2,1)S(1)}, bf16[288,256]{1,0:T(8,128)(2,1)S(1)}, u32[]{:S(2)}, u32[]{:S(2)}) collective-permute-start(bf16[288,256]{1,0:T(8,128)(2,1)S(1)} %get-tuple-element.50), channel_id=1, source_target_pairs={{0,12},{4,8},{8,4},{12,0},{16,28},{20,24},{24,20},{28,16},{1,13},{... | collective-permute-start | bytes 442376 | tf_op jit(solution)/shard_map/ppermute | solution.py:373
  55.4 3.2 %collective-permute-done.20.refs_8_ = bf16[256,256]{1,0:T(8,128)(2,1)S(1)} collective-permute-done((bf16[256,256]{1,0:T(8,128)(2,1)S(1)}, bf16[256,256]{1,0:T(8,128)(2,1)S(1)}, u32[]{:S(2)}, u32[]{:S(2)}) %collective-permute-start.20) | collective-permute-done | bytes 131104 | tf_op jit(solution)/shard_map/ppermute | solution.py:373
  59.7 1.5 %collective-permute-done.12.refs_7_ = bf16[288,256]{1,0:T(8,128)(2,1)S(1)} collective-permute-done((bf16[288,256]{1,0:T(8,128)(2,1)S(1)}, bf16[288,256]{1,0:T(8,128)(2,1)S(1)}, u32[]{:S(2)}, u32[]{:S(2)}) %collective-permute-start.12) | collective-permute-done | bytes 147488 | tf_op jit(solution)/shard_map/ppermute | solution.py:373
  61.2 2.6 %collective-permute-done.13.refs_8_ = bf16[288,256]{1,0:T(8,128)(2,1)S(1)} collective-permute-done((bf16[288,256]{1,0:T(8,128)(2,1)S(1)}, bf16[288,256]{1,0:T(8,128)(2,1)S(1)}, u32[]{:S(2)}, u32[]{:S(2)}) %collective-permute-start.13) | collective-permute-done | bytes 147488 | tf_op jit(solution)/shard_map/ppermute | solution.py:373
  65.9 2.7 %collective-permute-start.22 = (bf16[1,1,256,128]{3,2,1,0:T(8,128)(2,1)S(1)}, bf16[1,1,256,128]{3,2,1,0:T(8,128)(2,1)S(1)}, u32[]{:S(2)}, u32[]{:S(2)}) collective-permute-start(bf16[1,1,256,128]{3,2,1,0:T(8,128)(2,1)S(1)} %get-tuple-element.60), channel_id=1, source_target_pairs={{0,16},{1,17},{2,18},{3,19},{4,20},{5,21},{6,22},{7,23},{8,24},{9,... | collective-permute-start | bytes 196616 | tf_op jit(solution)/shard_map/ppermute | solution.py:378
  71.3 2.8 %collective-permute-start.17 = (bf16[1,1,304,128]{3,2,1,0:T(8,128)(2,1)S(1)}, bf16[1,1,304,128]{3,2,1,0:T(8,128)(2,1)S(1)}, u32[]{:S(2)}, u32[]{:S(2)}) collective-permute-start(bf16[1,1,304,128]{3,2,1,0:T(8,128)(2,1)S(1)} %get-tuple-element.54), channel_id=1, source_target_pairs={{0,18},{1,19},{2,16},{3,17},{4,22},{5,23},{6,20},{7,21},{8,26},{9,... | collective-permute-start | bytes 233480 | tf_op jit(solution)/shard_map/ppermute | solution.py:378
  74.1 1.3 %collective-permute-start.23 = (bf16[1,1,256,128]{3,2,1,0:T(8,128)(2,1)S(1)}, bf16[1,1,256,128]{3,2,1,0:T(8,128)(2,1)S(1)}, u32[]{:S(2)}, u32[]{:S(2)}) collective-permute-start(bf16[1,1,256,128]{3,2,1,0:T(8,128)(2,1)S(1)} %get-tuple-element.61), channel_id=1, source_target_pairs={{0,2},{1,3},{2,0},{3,1},{4,6},{5,7},{6,4},{7,5},{8,10},{9,11},{10,... | collective-permute-start | bytes 196616 | tf_op jit(solution)/shard_map/ppermute | solution.py:378
  75.9 2.5 %collective-permute-done.23.refs_6_ = bf16[1,1,256,128]{3,2,1,0:T(8,128)(2,1)S(1)} collective-permute-done((bf16[1,1,256,128]{3,2,1,0:T(8,128)(2,1)S(1)}, bf16[1,1,256,128]{3,2,1,0:T(8,128)(2,1)S(1)}, u32[]{:S(2)}, u32[]{:S(2)}) %collective-permute-start.23) | collective-permute-done | bytes 65568 | tf_op jit(solution)/shard_map/ppermute | solution.py:378
  78.3 5.3 %collective-permute-done.24.refs_7_ = bf16[1,1,256,128]{3,2,1,0:T(8,128)(2,1)S(1)} collective-permute-done((bf16[1,1,256,128]{3,2,1,0:T(8,128)(2,1)S(1)}, bf16[1,1,256,128]{3,2,1,0:T(8,128)(2,1)S(1)}, u32[]{:S(2)}, u32[]{:S(2)}) %collective-permute-start.24) | collective-permute-done | bytes 65568 | tf_op jit(solution)/shard_map/ppermute | solution.py:378
  (50 shorter events, 15.4 us)
Async XLA Ops:
  0.6 23.5 %collective-permute-start.3 = (bf16[256,2048]{1,0:T(8,128)(2,1)}, bf16[256,2048]{1,0:T(8,128)(2,1)}, u32[]{:S(2)}, u32[]{:S(2)}) collective-permute-start(bf16[256,2048]{1,0:T(8,128)(2,1)} %bitcast.12), channel_id=1, source_target_pairs={{0,1},{1,0},{2,3},{3,2},{4,5},{5,4},{6,7},{7,6},{8,9},{9,8},{10,11... | collective-permute-start | bytes 3145736 | tf_op jit(solution)/shard_map/ppermute | solution.py:373
  2.1 9.6 %collective-permute-start = (bf16[256,512]{1,0:T(8,128)(2,1)S(1)}, bf16[256,512]{1,0:T(8,128)(2,1)S(1)}, u32[]{:S(2)}, u32[]{:S(2)}) collective-permute-start(bf16[256,512]{1,0:T(8,128)(2,1)S(1)} %dynamic-slice_bitcast_fusion), channel_id=1, source_target_pairs={{0,2},{1,3},{2,0},{3,1},{4,6},{5,7},{6,4},{7,5},{8,10},{9,11},{10,... | collective-permute-start | bytes 786440 | tf_op jit(solution)/shard_map/ppermute | solution.py:373
  11.7 12.4 %all-to-all-start = ((bf16[4,256,256]{2,1,0:T(8,128)(2,1)}), bf16[4,256,256]{2,1,0:T(8,128)(2,1)S(1)}, u32[]{:S(2)}, u32[]{:S(2)}) async-start(bf16[4,256,256]{2,1,0:T(8,128)(2,1)} %attend.1), calls=%async_computation | async-start | bytes 1048576 | tf_op jit(solution)/shard_map/all_to_all | solution.py:421
  15.3 8.7 %collective-permute-start.1 = (bf16[256,512]{1,0:T(8,128)(2,1)S(1)}, bf16[256,512]{1,0:T(8,128)(2,1)S(1)}, u32[]{:S(2)}, u32[]{:S(2)}) collective-permute-start(bf16[256,512]{1,0:T(8,128)(2,1)S(1)} %collective-permute-done.refs_2_), channel_id=1, source_target_pairs={{0,4},{4,0},{8,12},{12,8},{16,20},{20,16},{24,28},{28,24},{1,5},{5... | collective-permute-start | bytes 786440 | tf_op jit(solution)/shard_map/ppermute | solution.py:373
  17.0 7.0 %collective-permute-start.2 = (bf16[256,512]{1,0:T(8,128)(2,1)S(1)}, bf16[256,512]{1,0:T(8,128)(2,1)S(1)}, u32[]{:S(2)}, u32[]{:S(2)}) collective-permute-start(bf16[256,512]{1,0:T(8,128)(2,1)S(1)} %collective-permute-done.refs_2_), channel_id=1, source_target_pairs={{0,1},{1,0},{2,3},{3,2},{4,5},{5,4},{6,7},{7,6},{8,9},{9,8},{10,11... | collective-permute-start | bytes 786440 | tf_op jit(solution)/shard_map/ppermute | solution.py:373
  24.1 13.5 %collective-permute-start.6 = (bf16[4,256,256]{2,1,0:T(8,128)(2,1)S(1)}, bf16[4,256,256]{2,1,0:T(8,128)(2,1)S(1)}, u32[]{:S(2)}, u32[]{:S(2)}) collective-permute-start(bf16[4,256,256]{2,1,0:T(8,128)(2,1)S(1)} %all-to-all-done.ctx_ref.refs_0_), channel_id=1, source_target_pairs={{0,4},{4,0},{8,12},{12,8},{16,20},{20,16},{24,28},{28,24},{1,5},{5... | collective-permute-start | bytes 1572872 | tf_op jit(solution)/shard_map/ppermute | solution.py:373
  25.7 13.2 %collective-permute-start.7 = (bf16[4,256,256]{2,1,0:T(8,128)(2,1)S(1)}, bf16[4,256,256]{2,1,0:T(8,128)(2,1)S(1)}, u32[]{:S(2)}, u32[]{:S(2)}) collective-permute-start(bf16[4,256,256]{2,1,0:T(8,128)(2,1)S(1)} %all-to-all-done.ctx_ref.refs_0_), channel_id=1, source_target_pairs={{0,8},{4,12},{8,0},{12,4},{16,24},{20,28},{24,16},{28,20},{1,9},{5... | collective-permute-start | bytes 1572872 | tf_op jit(solution)/shard_map/ppermute | solution.py:373
  27.3 13.1 %collective-permute-start.4 = (bf16[256,1024]{1,0:T(8,128)(2,1)}, bf16[256,1024]{1,0:T(8,128)(2,1)S(1)}, u32[]{:S(2)}, u32[]{:S(2)}) collective-permute-start(bf16[256,1024]{1,0:T(8,128)(2,1)} %slice.12), channel_id=1, source_target_pairs={{0,2},{1,3},{2,0},{3,1},{4,6},{5,7},{6,4},{7,5},{8,10},{9,11},{10,... | collective-permute-start | bytes 1572872 | tf_op jit(solution)/shard_map/ppermute | solution.py:373
  40.4 11.0 %collective-permute-start.10 = (bf16[4,128,256]{2,1,0:T(8,128)(2,1)S(1)}, bf16[4,128,256]{2,1,0:T(8,128)(2,1)S(1)}, u32[]{:S(2)}, u32[]{:S(2)}) collective-permute-start(bf16[4,128,256]{2,1,0:T(8,128)(2,1)S(1)} %slice.11), channel_id=1, source_target_pairs={{0,4},{4,0},{8,12},{12,8},{16,20},{20,16},{24,28},{28,24},{1,5},{5... | collective-permute-start | bytes 786440 | tf_op jit(solution)/shard_map/ppermute | solution.py:373
  41.1 11.3 %collective-permute-start.9 = (bf16[4,128,256]{2,1,0:T(8,128)(2,1)S(1)}, bf16[4,128,256]{2,1,0:T(8,128)(2,1)S(1)}, u32[]{:S(2)}, u32[]{:S(2)}) collective-permute-start(bf16[4,128,256]{2,1,0:T(8,128)(2,1)S(1)} %slice.10), channel_id=1, source_target_pairs={{0,8},{4,12},{8,0},{12,4},{16,24},{20,28},{24,16},{28,20},{1,9},{5... | collective-permute-start | bytes 786440 | tf_op jit(solution)/shard_map/ppermute | solution.py:373
  47.9 5.9 %collective-permute-start.18 = (bf16[256,256]{1,0:T(8,128)(2,1)S(1)}, bf16[256,256]{1,0:T(8,128)(2,1)S(1)}, u32[]{:S(2)}, u32[]{:S(2)}) collective-permute-start(bf16[256,256]{1,0:T(8,128)(2,1)S(1)} %get-tuple-element.56), channel_id=1, source_target_pairs={{0,4},{4,0},{8,12},{12,8},{16,20},{20,16},{24,28},{28,24},{1,5},{5... | collective-permute-start | bytes 393224 | tf_op jit(solution)/shard_map/ppermute | solution.py:373
  48.8 6.6 %collective-permute-start.19 = (bf16[256,256]{1,0:T(8,128)(2,1)S(1)}, bf16[256,256]{1,0:T(8,128)(2,1)S(1)}, u32[]{:S(2)}, u32[]{:S(2)}) collective-permute-start(bf16[256,256]{1,0:T(8,128)(2,1)S(1)} %get-tuple-element.57), channel_id=1, source_target_pairs={{0,8},{4,12},{8,0},{12,4},{16,24},{20,28},{24,16},{28,20},{1,9},{5... | collective-permute-start | bytes 393224 | tf_op jit(solution)/shard_map/ppermute | solution.py:373
  50.3 8.3 %collective-permute-start.20 = (bf16[256,256]{1,0:T(8,128)(2,1)S(1)}, bf16[256,256]{1,0:T(8,128)(2,1)S(1)}, u32[]{:S(2)}, u32[]{:S(2)}) collective-permute-start(bf16[256,256]{1,0:T(8,128)(2,1)S(1)} %get-tuple-element.58), channel_id=1, source_target_pairs={{0,12},{4,8},{8,4},{12,0},{16,28},{20,24},{24,20},{28,16},{1,13},{... | collective-permute-start | bytes 393224 | tf_op jit(solution)/shard_map/ppermute | solution.py:373
  51.4 8.2 %collective-permute-start.11 = (bf16[288,256]{1,0:T(8,128)(2,1)S(1)}, bf16[288,256]{1,0:T(8,128)(2,1)S(1)}, u32[]{:S(2)}, u32[]{:S(2)}) collective-permute-start(bf16[288,256]{1,0:T(8,128)(2,1)S(1)} %get-tuple-element.48), channel_id=1, source_target_pairs={{0,4},{4,0},{8,12},{12,8},{16,20},{20,16},{24,28},{28,24},{1,5},{5... | collective-permute-start | bytes 442376 | tf_op jit(solution)/shard_map/ppermute | solution.py:373
  52.3 8.8 %collective-permute-start.12 = (bf16[288,256]{1,0:T(8,128)(2,1)S(1)}, bf16[288,256]{1,0:T(8,128)(2,1)S(1)}, u32[]{:S(2)}, u32[]{:S(2)}) collective-permute-start(bf16[288,256]{1,0:T(8,128)(2,1)S(1)} %get-tuple-element.49), channel_id=1, source_target_pairs={{0,8},{4,12},{8,0},{12,4},{16,24},{20,28},{24,16},{28,20},{1,9},{5... | collective-permute-start | bytes 442376 | tf_op jit(solution)/shard_map/ppermute | solution.py:373
  53.8 10.0 %collective-permute-start.13 = (bf16[288,256]{1,0:T(8,128)(2,1)S(1)}, bf16[288,256]{1,0:T(8,128)(2,1)S(1)}, u32[]{:S(2)}, u32[]{:S(2)}) collective-permute-start(bf16[288,256]{1,0:T(8,128)(2,1)S(1)} %get-tuple-element.50), channel_id=1, source_target_pairs={{0,12},{4,8},{8,4},{12,0},{16,28},{20,24},{24,20},{28,16},{1,13},{... | collective-permute-start | bytes 442376 | tf_op jit(solution)/shard_map/ppermute | solution.py:373
  59.6 6.2 %collective-permute-start.21 = (bf16[2,2,256,128]{3,2,1,0:T(8,128)(2,1)S(1)}, bf16[2,2,256,128]{3,2,1,0:T(8,128)(2,1)S(1)}, u32[]{:S(2)}, u32[]{:S(2)}) collective-permute-start(bf16[2,2,256,128]{3,2,1,0:T(8,128)(2,1)S(1)} %gradient.7), channel_id=1, source_target_pairs={{0,1},{1,0},{2,3},{3,2},{4,5},{5,4},{6,7},{7,6},{8,9},{9,8},{10,11... | collective-permute-start | bytes 786440 | tf_op jit(solution)/shard_map/ppermute | solution.py:373
  64.8 4.8 %collective-permute-start.14 = (bf16[2,2,304,128]{3,2,1,0:T(8,128)(2,1)S(1)}, bf16[2,2,304,128]{3,2,1,0:T(8,128)(2,1)S(1)}, u32[]{:S(2)}, u32[]{:S(2)}) collective-permute-start(bf16[2,2,304,128]{3,2,1,0:T(8,128)(2,1)S(1)} %gradient.5), channel_id=1, source_target_pairs={{0,1},{1,0},{2,3},{3,2},{4,5},{5,4},{6,7},{7,6},{8,9},{9,8},{10,11... | collective-permute-start | bytes 933896 | tf_op jit(solution)/shard_map/ppermute | solution.py:373
  65.9 9.5 %collective-permute-start.22 = (bf16[1,1,256,128]{3,2,1,0:T(8,128)(2,1)S(1)}, bf16[1,1,256,128]{3,2,1,0:T(8,128)(2,1)S(1)}, u32[]{:S(2)}, u32[]{:S(2)}) collective-permute-start(bf16[1,1,256,128]{3,2,1,0:T(8,128)(2,1)S(1)} %get-tuple-element.60), channel_id=1, source_target_pairs={{0,16},{1,17},{2,18},{3,19},{4,20},{5,21},{6,22},{7,23},{8,24},{9,... | collective-permute-start | bytes 196616 | tf_op jit(solution)/shard_map/ppermute | solution.py:378
  69.6 14.0 %collective-permute-start.15 = (bf16[1,1,304,128]{3,2,1,0:T(8,128)(2,1)S(1)}, bf16[1,1,304,128]{3,2,1,0:T(8,128)(2,1)S(1)}, u32[]{:S(2)}, u32[]{:S(2)}) collective-permute-start(bf16[1,1,304,128]{3,2,1,0:T(8,128)(2,1)S(1)} %get-tuple-element.52), channel_id=1, source_target_pairs={{0,16},{1,17},{2,18},{3,19},{4,20},{5,21},{6,22},{7,23},{8,24},{9,... | collective-permute-start | bytes 233480 | tf_op jit(solution)/shard_map/ppermute | solution.py:378
  70.0 13.6 %collective-permute-start.16 = (bf16[1,1,304,128]{3,2,1,0:T(8,128)(2,1)S(1)}, bf16[1,1,304,128]{3,2,1,0:T(8,128)(2,1)S(1)}, u32[]{:S(2)}, u32[]{:S(2)}) collective-permute-start(bf16[1,1,304,128]{3,2,1,0:T(8,128)(2,1)S(1)} %get-tuple-element.53), channel_id=1, source_target_pairs={{0,2},{1,3},{2,0},{3,1},{4,6},{5,7},{6,4},{7,5},{8,10},{9,11},{10,... | collective-permute-start | bytes 233480 | tf_op jit(solution)/shard_map/ppermute | solution.py:378
  71.3 12.3 %collective-permute-start.17 = (bf16[1,1,304,128]{3,2,1,0:T(8,128)(2,1)S(1)}, bf16[1,1,304,128]{3,2,1,0:T(8,128)(2,1)S(1)}, u32[]{:S(2)}, u32[]{:S(2)}) collective-permute-start(bf16[1,1,304,128]{3,2,1,0:T(8,128)(2,1)S(1)} %get-tuple-element.54), channel_id=1, source_target_pairs={{0,18},{1,19},{2,16},{3,17},{4,22},{5,23},{6,20},{7,21},{8,26},{9,... | collective-permute-start | bytes 233480 | tf_op jit(solution)/shard_map/ppermute | solution.py:378
  74.1 4.3 %collective-permute-start.23 = (bf16[1,1,256,128]{3,2,1,0:T(8,128)(2,1)S(1)}, bf16[1,1,256,128]{3,2,1,0:T(8,128)(2,1)S(1)}, u32[]{:S(2)}, u32[]{:S(2)}) collective-permute-start(bf16[1,1,256,128]{3,2,1,0:T(8,128)(2,1)S(1)} %get-tuple-element.61), channel_id=1, source_target_pairs={{0,2},{1,3},{2,0},{3,1},{4,6},{5,7},{6,4},{7,5},{8,10},{9,11},{10,... | collective-permute-start | bytes 196616 | tf_op jit(solution)/shard_map/ppermute | solution.py:378
  75.4 8.2 %collective-permute-start.24 = (bf16[1,1,256,128]{3,2,1,0:T(8,128)(2,1)S(1)}, bf16[1,1,256,128]{3,2,1,0:T(8,128)(2,1)S(1)}, u32[]{:S(2)}, u32[]{:S(2)}) collective-permute-start(bf16[1,1,256,128]{3,2,1,0:T(8,128)(2,1)S(1)} %get-tuple-element.62), channel_id=1, source_target_pairs={{0,18},{1,19},{2,16},{3,17},{4,22},{5,23},{6,20},{7,21},{8,26},{9,... | collective-permute-start | bytes 196616 | tf_op jit(solution)/shard_map/ppermute | solution.py:378
  (6 other events, 39.2 us)

commit v9 on v7

--- a/solution.py
+++ b/solution.py
@@ -303,21 +303,19 @@
         gains, scalars = block_sums(keep_ref[0, 0, feats:, :], in_block)
         more, others = block_sums(got_ref[0, 0, feats:, :], in_block)
         words = block_words(gains + more, scalars + others, tall - feats, cw)
+    each = out_refs[0].shape[0] * out_refs[0].shape[1]
     for i in range(n_y * n_far):
         a, b = divmod(i, n_far)
         total = keep_ref[a, b, :feats, :].astype(F32) + got_ref[a, b, :feats, :].astype(F32)
-        ref, at = (out_refs[0], (a, b)) if len(out_refs) == 1 else (out_refs[i], (0, 0))
+        ref, at = out_refs[i // each], divmod(i % each, out_refs[0].shape[1])
         ref[(*at, slice(0, feats), slice(None))] = total.astype(BF)
         if tall > feats:
             ref[(*at, slice(feats, tall), slice(None))] = words
 
 
-def merge(plan, dout, feats, keep, got):
+def merge(dims, dout, feats, keep, got):
     n_y, n_far, tall, cw = keep.shape
-    if plan[4]:
-        outs = [shape((1, 1, tall, cw))] * (n_y * n_far)
-    else:
-        outs = [shape(keep.shape)]
+    outs = [shape((*dims, tall, cw))] * (n_y * n_far // math.prod(dims))
     return pl.pallas_call(
         functools.partial(merge_body, dout // cw, feats),
         in_specs=[VM, VM],
@@ -379,17 +377,29 @@
     return lax.ppermute(x, ("dp", "tensor"), [(i, i ^ mask) for i in range(n_dp * n_tensor)])
 
 
-def exchange_far(plan, blocks):
-    n_dp, n_tensor, _, _, xor_far = plan
-    n_far = n_dp // NEAR
-    if xor_far:
-        return [blocks[0]] + [
-            swap_far(block, n_dp, n_tensor, *divmod(i, n_far)) for i, block in enumerate(blocks) if i
+def exchange_far(plan, two_steps, dout, feats, keep, got):
+    n_dp, n_tensor, _, _, pairwise = plan
+    n_y, n_far = n_tensor // 2, n_dp // NEAR
+    if not pairwise:
+        groups = [
+            [(NEAR * f + q) * n_tensor + 2 * y + c for y in range(n_y) for f in range(n_far)]
+            for q in range(NEAR)
+            for c in range(2)
         ]
-    cores = [[2 * y + c for y in range(n_tensor // 2)] for c in range(2)]
-    nears = [[NEAR * f + q for f in range(n_far)] for q in range(NEAR)]
-    x = lax.all_to_all(blocks[0], "tensor", 0, 0, tiled=True, axis_index_groups=cores)
-    return [lax.all_to_all(x, "dp", 1, 1, tiled=True, axis_index_groups=nears)]
+        (x,) = merge((n_y, n_far), dout, feats, keep, got)
+        x = x.reshape(n_y * n_far, *x.shape[2:])
+        x = lax.all_to_all(x, ("dp", "tensor"), 0, 0, tiled=True, axis_index_groups=groups)
+        return [x.reshape(keep.shape)]
+
+    def far(x, a, b):
+        return swap_far(x, n_dp, n_tensor, a, b)
+
+    if two_steps:
+        own, across = merge((1, 2), dout, feats, keep, got)
+        own, beyond = merge((1, 1), dout, feats, own, far(across, 1, 0))
+        return [own, far(beyond, 0, 1)]
+    blocks = merge((1, 1), dout, feats, keep, got)
+    return [blocks[0], far(blocks[1], 0, 1), far(blocks[2], 1, 0), far(blocks[3], 1, 1)]
 
 
 def gather_large(n_dp, n_tensor, _, weight, context):
@@ -447,7 +457,7 @@
     dout = norm_gain.shape[0]
     rows = next_hidden.shape[0]
     chunks = 2 if dout // n_dp >= 256 else 1
-    xor_far = (n_tensor // 2) * (n_dp // NEAR) <= 4
+    xor_far = (n_tensor, n_dp // NEAR) == (4, 2)
     plan = (n_dp, n_tensor, chunks, seq, xor_far)
     me = lax.axis_index("tensor").astype(jnp.int32)
     group = lax.axis_index("dp").astype(jnp.int32)
@@ -461,8 +471,8 @@
     for j in range(chunks):
         near = [grads[j][0]] + [swap(grads[j][q], "dp", n_dp, q) for q in range(1, NEAR)]
         keep, send = gradient(plan, dout, info, ctxs, near)
-        blocks = merge(plan, dout, width, keep, swap(send, "tensor", n_tensor, 1))
-        parts.append(exchange_far(plan, blocks))
+        got = swap(send, "tensor", n_tensor, 1)
+        parts.append(exchange_far(plan, j == chunks - 1, dout, width, keep, got))
     weight_grad, gain_grad, loss = finish(plan, dout, width, parts)
     return (hidden, weight_grad[None], gain_grad.reshape(dout), loss.reshape(()))
 

time: 83.3 us -> 81.2 us (0.975)
  waiting for transfers between devices: 33 us -> 31.8 us
  starting transfers between devices: 31.7 us -> 30.7 us
    ppermute x6 -> x5, waiting for transfers between devices: 7.24 us -> 5.86 us  [swap_far(): lax.ppermute(x, ('dp', 'tensor'), [(i, i ^ mask) for i in range(n_dp * n_...]
    ppermute x6 -> x5, starting transfers between devices: 9.74 us -> 8.78 us  [swap_far(): lax.ppermute(x, ('dp', 'tensor'), [(i, i ^ mask) for i in range(n_dp * n_...]
  transfers between devices with their start and end apart: 26 -> 25, of which waited for: 14 -> 14; matrix products, arithmetic and copies ran while one was open for 3% -> 3% of each run, Pallas kernels for 16% -> 16%
where the time goes in v9:
time: 81.2 us; the launch traced here: 80.9 us
  waiting for transfers between devices  31.8 us (39%)
  starting transfers between devices  30.7 us (38%)
  Pallas kernels  13.9 us (17%)
  between operations  2.06 us (3%)
  local copies, waits for them, and re-layouts  1.86 us (2%)
    ppermute x19, waiting for transfers between devices, swap(): return lax.ppermute(x, axis, [(i, i ^ mask) for i in range(n)])  25.8 us
    ppermute x19, starting transfers between devices, swap(): return lax.ppermute(x, axis, [(i, i ^ mask) for i in range(n)])  18.3 us
    ppermute x5, starting transfers between devices, swap_far(): lax.ppermute(x, ('dp', 'tensor'), [(i, i ^ mask) for i in range(n_dp * n_...  8.78 us
    ppermute x5, waiting for transfers between devices, swap_far(): lax.ppermute(x, ('dp', 'tensor'), [(i, i ^ mask) for i in range(n_dp * n_...  5.86 us
    pallas_call x1, Pallas kernels, join(): pl.pallas_call(functools.partial(join_body, plan, [len(w) for w in weight...  5.63 us
    pallas_call x1, Pallas kernels, attend(): pl.pallas_call(attend_body, in_specs=[SM, block, block, block], out_specs...  4.83 us
    all_to_all x1, starting transfers between devices, gather_small(): ctx = lax.all_to_all(context, 'tensor', 0, 0, tiled=True)  3.6 us
    pallas_call x2, Pallas kernels, gradient(): pl.pallas_call(functools.partial(grad_body, plan, dout, [len(c) for c in...  2.5 us
  transfers between devices with their start and end apart: 25, of which 14 were waited for; matrix products, arithmetic and copies ran while one was open for 3% of the time, Pallas kernels for 16%

profile of v9, /device:TPU:0, one launch (start us, length us, event | category | flops | bytes accessed | tf_op | source)
XLA Modules:
  0.0 80.9 jit_solution(10514555161933211209)
XLA Ops:
  2.1 2.6 %collective-permute-start = (bf16[256,512]{1,0:T(8,128)(2,1)S(1)}, bf16[256,512]{1,0:T(8,128)(2,1)S(1)}, u32[]{:S(2)}, u32[]{:S(2)}) collective-permute-start(bf16[256,512]{1,0:T(8,128)(2,1)S(1)} %dynamic-slice_bitcast_fusion), channel_id=1, source_target_pairs={{0,2},{1,3},{2,0},{3,1},{4,6},{5,7},{6,4},{7,5},{8,10},{9,11},{10,... | collective-permute-start | bytes 786440 | tf_op jit(solution)/shard_map/ppermute | solution.py:372
  6.6 4.8 %attend.1 = bf16[4,256,256]{2,1,0:T(8,128)(2,1)} custom-call(s32[4]{0:T(128)} %pad_add_fusion.info_ref, bf16[1024,256]{1,0:T(8,128)(2,1)} %bitcast.16, bf16[1024,256]{1,0:T(8,128)(2,1)} %bitcast.17, bf16[1024,256]{1,0:T(8,128)(2,1)} %bitcast.18), custom_call_target="tpu_custom_call" | custom-call | flops 1073741824 | bytes 2097152 | tf_op jit(solution)/shard_map/attend/pallas_call | solution.py:76
  11.7 3.6 %all-to-all-start = ((bf16[4,256,256]{2,1,0:T(8,128)(2,1)}), bf16[4,256,256]{2,1,0:T(8,128)(2,1)S(1)}, u32[]{:S(2)}, u32[]{:S(2)}) async-start(bf16[4,256,256]{2,1,0:T(8,128)(2,1)} %attend.1), calls=%async_computation | async-start | bytes 1048576 | tf_op jit(solution)/shard_map/all_to_all | solution.py:432
  15.3 1.7 %collective-permute-start.1 = (bf16[256,512]{1,0:T(8,128)(2,1)S(1)}, bf16[256,512]{1,0:T(8,128)(2,1)S(1)}, u32[]{:S(2)}, u32[]{:S(2)}) collective-permute-start(bf16[256,512]{1,0:T(8,128)(2,1)S(1)} %collective-permute-done.refs_2_), channel_id=1, source_target_pairs={{0,4},{4,0},{8,12},{12,8},{16,20},{20,16},{24,28},{28,24},{1,5},{5... | collective-permute-start | bytes 786440 | tf_op jit(solution)/shard_map/ppermute | solution.py:372
  17.9 6.1 %collective-permute-done.1.refs_3_ = bf16[256,512]{1,0:T(8,128)(2,1)S(1)} collective-permute-done((bf16[256,512]{1,0:T(8,128)(2,1)S(1)}, bf16[256,512]{1,0:T(8,128)(2,1)S(1)}, u32[]{:S(2)}, u32[]{:S(2)}) %collective-permute-start.1) | collective-permute-done | bytes 262176 | tf_op jit(solution)/shard_map/ppermute | solution.py:372
  24.1 1.6 %collective-permute-start.6 = (bf16[4,256,256]{2,1,0:T(8,128)(2,1)S(1)}, bf16[4,256,256]{2,1,0:T(8,128)(2,1)S(1)}, u32[]{:S(2)}, u32[]{:S(2)}) collective-permute-start(bf16[4,256,256]{2,1,0:T(8,128)(2,1)S(1)} %all-to-all-done.ctx_ref.refs_0_), channel_id=1, source_target_pairs={{0,4},{4,0},{8,12},{12,8},{16,20},{20,16},{24,28},{28,24},{1,5},{5... | collective-permute-start | bytes 1572872 | tf_op jit(solution)/shard_map/ppermute | solution.py:372
  25.7 1.6 %collective-permute-start.7 = (bf16[4,256,256]{2,1,0:T(8,128)(2,1)S(1)}, bf16[4,256,256]{2,1,0:T(8,128)(2,1)S(1)}, u32[]{:S(2)}, u32[]{:S(2)}) collective-permute-start(bf16[4,256,256]{2,1,0:T(8,128)(2,1)S(1)} %all-to-all-done.ctx_ref.refs_0_), channel_id=1, source_target_pairs={{0,8},{4,12},{8,0},{12,4},{16,24},{20,28},{24,16},{28,20},{1,9},{5... | collective-permute-start | bytes 1572872 | tf_op jit(solution)/shard_map/ppermute | solution.py:372
  27.3 1.6 %collective-permute-start.4 = (bf16[256,1024]{1,0:T(8,128)(2,1)}, bf16[256,1024]{1,0:T(8,128)(2,1)S(1)}, u32[]{:S(2)}, u32[]{:S(2)}) collective-permute-start(bf16[256,1024]{1,0:T(8,128)(2,1)} %slice.12), channel_id=1, source_target_pairs={{0,2},{1,3},{2,0},{3,1},{4,6},{5,7},{6,4},{7,5},{8,10},{9,11},{10,... | collective-permute-start | bytes 1572872 | tf_op jit(solution)/shard_map/ppermute | solution.py:372
  28.9 1.5 %collective-permute-done.5.refs_6_ = bf16[256,512]{1,0:T(8,128)(2,1)S(1)} collective-permute-done((bf16[256,512]{1,0:T(8,128)(2,1)S(1)}, bf16[256,512]{1,0:T(8,128)(2,1)S(1)}, u32[]{:S(2)}, u32[]{:S(2)}) %collective-permute-start.5) | collective-permute-done | bytes 262176 | tf_op jit(solution)/shard_map/ppermute | solution.py:372
  30.4 7.2 %collective-permute-done.6.refs_1_ = bf16[4,256,256]{2,1,0:T(8,128)(2,1)S(1)} collective-permute-done((bf16[4,256,256]{2,1,0:T(8,128)(2,1)S(1)}, bf16[4,256,256]{2,1,0:T(8,128)(2,1)S(1)}, u32[]{:S(2)}, u32[]{:S(2)}) %collective-permute-start.6) | collective-permute-done | bytes 524320 | tf_op jit(solution)/shard_map/ppermute | solution.py:372
  37.6 1.3 %collective-permute-done.7.refs_2_ = bf16[4,256,256]{2,1,0:T(8,128)(2,1)S(1)} collective-permute-done((bf16[4,256,256]{2,1,0:T(8,128)(2,1)S(1)}, bf16[4,256,256]{2,1,0:T(8,128)(2,1)S(1)}, u32[]{:S(2)}, u32[]{:S(2)}) %collective-permute-start.7) | collective-permute-done | bytes 524320 | tf_op jit(solution)/shard_map/ppermute | solution.py:372
  38.9 1.5 %collective-permute-done.4.refs_4_ = bf16[256,1024]{1,0:T(8,128)(2,1)S(1)} collective-permute-done((bf16[256,1024]{1,0:T(8,128)(2,1)}, bf16[256,1024]{1,0:T(8,128)(2,1)S(1)}, u32[]{:S(2)}, u32[]{:S(2)}) %collective-permute-start.4) | collective-permute-done | bytes 524320 | tf_op jit(solution)/shard_map/ppermute | solution.py:372
  42.3 5.6 %join.1 = (bf16[256,2048]{1,0:T(8,128)(2,1)}, bf16[288,256]{1,0:T(8,128)(2,1)S(1)}, bf16[288,256]{1,0:T(8,128)(2,1)S(1)}, bf16[288,256]{1,0:T(8,128)(2,1)S(1)}, ...) custom-call(s32[4]{0:T(128)S(1)} %copy-done.3, ...), custom_call_target="tpu_custom_call" | custom-call | flops 1073741824 | bytes 7340032 | tf_op jit(solution)/shard_map/join/pallas_call | solution.py:201
  48.8 1.5 %collective-permute-start.19 = (bf16[256,256]{1,0:T(8,128)(2,1)S(1)}, bf16[256,256]{1,0:T(8,128)(2,1)S(1)}, u32[]{:S(2)}, u32[]{:S(2)}) collective-permute-start(bf16[256,256]{1,0:T(8,128)(2,1)S(1)} %get-tuple-element.63), channel_id=1, source_target_pairs={{0,8},{4,12},{8,0},{12,4},{16,24},{20,28},{24,16},{28,20},{1,9},{5... | collective-permute-start | bytes 393224 | tf_op jit(solution)/shard_map/ppermute | solution.py:372
  52.3 1.5 %collective-permute-start.12 = (bf16[288,256]{1,0:T(8,128)(2,1)S(1)}, bf16[288,256]{1,0:T(8,128)(2,1)S(1)}, u32[]{:S(2)}, u32[]{:S(2)}) collective-permute-start(bf16[288,256]{1,0:T(8,128)(2,1)S(1)} %get-tuple-element.53), channel_id=1, source_target_pairs={{0,8},{4,12},{8,0},{12,4},{16,24},{20,28},{24,16},{28,20},{1,9},{5... | collective-permute-start | bytes 442376 | tf_op jit(solution)/shard_map/ppermute | solution.py:372
  53.8 1.6 %collective-permute-start.13 = (bf16[288,256]{1,0:T(8,128)(2,1)S(1)}, bf16[288,256]{1,0:T(8,128)(2,1)S(1)}, u32[]{:S(2)}, u32[]{:S(2)}) collective-permute-start(bf16[288,256]{1,0:T(8,128)(2,1)S(1)} %get-tuple-element.54), channel_id=1, source_target_pairs={{0,12},{4,8},{8,4},{12,0},{16,28},{20,24},{24,20},{28,16},{1,13},{... | collective-permute-start | bytes 442376 | tf_op jit(solution)/shard_map/ppermute | solution.py:372
  55.4 3.2 %collective-permute-done.20.refs_8_ = bf16[256,256]{1,0:T(8,128)(2,1)S(1)} collective-permute-done((bf16[256,256]{1,0:T(8,128)(2,1)S(1)}, bf16[256,256]{1,0:T(8,128)(2,1)S(1)}, u32[]{:S(2)}, u32[]{:S(2)}) %collective-permute-start.20) | collective-permute-done | bytes 131104 | tf_op jit(solution)/shard_map/ppermute | solution.py:372
  61.2 2.6 %collective-permute-done.13.refs_8_ = bf16[288,256]{1,0:T(8,128)(2,1)S(1)} collective-permute-done((bf16[288,256]{1,0:T(8,128)(2,1)S(1)}, bf16[288,256]{1,0:T(8,128)(2,1)S(1)}, u32[]{:S(2)}, u32[]{:S(2)}) %collective-permute-start.13) | collective-permute-done | bytes 147488 | tf_op jit(solution)/shard_map/ppermute | solution.py:372
  63.8 1.3 %gradient.2 = (bf16[2,2,304,128]{3,2,1,0:T(8,128)(2,1)S(1)}, bf16[2,2,304,128]{3,2,1,0:T(8,128)(2,1)S(1)}) custom-call(s32[4]{0:T(128)S(1)} %copy-done.3, bf16[4,256,256]{2,1,0:T(8,128)(2,1)S(1)} %all-to-all-done.ctx_ref.refs_0_, bf16[4,256,256]{2,1,0:T(8,128)(2,1)S(1)} %collective-permute-done.6.refs_1_, ...), custom_call_target="tpu_custom_call" | custom-call | flops 536870912 | bytes 3145728 | tf_op jit(solution)/shard_map/gradient/pallas_call | solution.py:285
  65.2 1.4 %collective-permute-start.22 = (bf16[1,2,256,128]{3,2,1,0:T(8,128)(2,1)S(1)}, bf16[1,2,256,128]{3,2,1,0:T(8,128)(2,1)S(1)}, u32[]{:S(2)}, u32[]{:S(2)}) collective-permute-start(bf16[1,2,256,128]{3,2,1,0:T(8,128)(2,1)S(1)} %get-tuple-element.68), channel_id=1, source_target_pairs={{0,2},{1,3},{2,0},{3,1},{4,6},{5,7},{6,4},{7,5},{8,10},{9,11},{10,... | collective-permute-start | bytes 393224 | tf_op jit(solution)/shard_map/ppermute | solution.py:377
  66.8 2.7 %collective-permute-start.15 = (bf16[1,1,304,128]{3,2,1,0:T(8,128)(2,1)S(1)}, bf16[1,1,304,128]{3,2,1,0:T(8,128)(2,1)S(1)}, u32[]{:S(2)}, u32[]{:S(2)}) collective-permute-start(bf16[1,1,304,128]{3,2,1,0:T(8,128)(2,1)S(1)} %get-tuple-element.58), channel_id=1, source_target_pairs={{0,16},{1,17},{2,18},{3,19},{4,20},{5,21},{6,22},{7,23},{8,24},{9,... | collective-permute-start | bytes 233480 | tf_op jit(solution)/shard_map/ppermute | solution.py:377
  69.4 1.3 %collective-permute-start.16 = (bf16[1,1,304,128]{3,2,1,0:T(8,128)(2,1)S(1)}, bf16[1,1,304,128]{3,2,1,0:T(8,128)(2,1)S(1)}, u32[]{:S(2)}, u32[]{:S(2)}) collective-permute-start(bf16[1,1,304,128]{3,2,1,0:T(8,128)(2,1)S(1)} %get-tuple-element.59), channel_id=1, source_target_pairs={{0,2},{1,3},{2,0},{3,1},{4,6},{5,7},{6,4},{7,5},{8,10},{9,11},{10,... | collective-permute-start | bytes 233480 | tf_op jit(solution)/shard_map/ppermute | solution.py:377
  71.3 3.0 %collective-permute-start.23 = (bf16[1,1,256,128]{3,2,1,0:T(8,128)(2,1)S(1)}, bf16[1,1,256,128]{3,2,1,0:T(8,128)(2,1)S(1)}, u32[]{:S(2)}, u32[]{:S(2)}) collective-permute-start(bf16[1,1,256,128]{3,2,1,0:T(8,128)(2,1)S(1)} %get-tuple-element.70), channel_id=1, source_target_pairs={{0,16},{1,17},{2,18},{3,19},{4,20},{5,21},{6,22},{7,23},{8,24},{9,... | collective-permute-start | bytes 196616 | tf_op jit(solution)/shard_map/ppermute | solution.py:377
  74.2 5.4 %collective-permute-done.17.refs_3_ = bf16[1,1,304,128]{3,2,1,0:T(8,128)(2,1)S(1)} collective-permute-done((bf16[1,1,304,128]{3,2,1,0:T(8,128)(2,1)S(1)}, bf16[1,1,304,128]{3,2,1,0:T(8,128)(2,1)S(1)}, u32[]{:S(2)}, u32[]{:S(2)}) %collective-permute-start.17) | collective-permute-done | bytes 77856 | tf_op jit(solution)/shard_map/ppermute | solution.py:377
  (47 shorter events, 12.9 us)
Async XLA Ops:
  0.6 23.5 %collective-permute-start.3 = (bf16[256,2048]{1,0:T(8,128)(2,1)}, bf16[256,2048]{1,0:T(8,128)(2,1)}, u32[]{:S(2)}, u32[]{:S(2)}) collective-permute-start(bf16[256,2048]{1,0:T(8,128)(2,1)} %bitcast.12), channel_id=1, source_target_pairs={{0,1},{1,0},{2,3},{3,2},{4,5},{5,4},{6,7},{7,6},{8,9},{9,8},{10,11... | collective-permute-start | bytes 3145736 | tf_op jit(solution)/shard_map/ppermute | solution.py:372
  2.1 9.6 %collective-permute-start = (bf16[256,512]{1,0:T(8,128)(2,1)S(1)}, bf16[256,512]{1,0:T(8,128)(2,1)S(1)}, u32[]{:S(2)}, u32[]{:S(2)}) collective-permute-start(bf16[256,512]{1,0:T(8,128)(2,1)S(1)} %dynamic-slice_bitcast_fusion), channel_id=1, source_target_pairs={{0,2},{1,3},{2,0},{3,1},{4,6},{5,7},{6,4},{7,5},{8,10},{9,11},{10,... | collective-permute-start | bytes 786440 | tf_op jit(solution)/shard_map/ppermute | solution.py:372
  11.7 12.4 %all-to-all-start = ((bf16[4,256,256]{2,1,0:T(8,128)(2,1)}), bf16[4,256,256]{2,1,0:T(8,128)(2,1)S(1)}, u32[]{:S(2)}, u32[]{:S(2)}) async-start(bf16[4,256,256]{2,1,0:T(8,128)(2,1)} %attend.1), calls=%async_computation | async-start | bytes 1048576 | tf_op jit(solution)/shard_map/all_to_all | solution.py:432
  15.3 8.7 %collective-permute-start.1 = (bf16[256,512]{1,0:T(8,128)(2,1)S(1)}, bf16[256,512]{1,0:T(8,128)(2,1)S(1)}, u32[]{:S(2)}, u32[]{:S(2)}) collective-permute-start(bf16[256,512]{1,0:T(8,128)(2,1)S(1)} %collective-permute-done.refs_2_), channel_id=1, source_target_pairs={{0,4},{4,0},{8,12},{12,8},{16,20},{20,16},{24,28},{28,24},{1,5},{5... | collective-permute-start | bytes 786440 | tf_op jit(solution)/shard_map/ppermute | solution.py:372
  17.0 7.0 %collective-permute-start.2 = (bf16[256,512]{1,0:T(8,128)(2,1)S(1)}, bf16[256,512]{1,0:T(8,128)(2,1)S(1)}, u32[]{:S(2)}, u32[]{:S(2)}) collective-permute-start(bf16[256,512]{1,0:T(8,128)(2,1)S(1)} %collective-permute-done.refs_2_), channel_id=1, source_target_pairs={{0,1},{1,0},{2,3},{3,2},{4,5},{5,4},{6,7},{7,6},{8,9},{9,8},{10,11... | collective-permute-start | bytes 786440 | tf_op jit(solution)/shard_map/ppermute | solution.py:372
  24.1 13.5 %collective-permute-start.6 = (bf16[4,256,256]{2,1,0:T(8,128)(2,1)S(1)}, bf16[4,256,256]{2,1,0:T(8,128)(2,1)S(1)}, u32[]{:S(2)}, u32[]{:S(2)}) collective-permute-start(bf16[4,256,256]{2,1,0:T(8,128)(2,1)S(1)} %all-to-all-done.ctx_ref.refs_0_), channel_id=1, source_target_pairs={{0,4},{4,0},{8,12},{12,8},{16,20},{20,16},{24,28},{28,24},{1,5},{5... | collective-permute-start | bytes 1572872 | tf_op jit(solution)/shard_map/ppermute | solution.py:372
  25.7 13.2 %collective-permute-start.7 = (bf16[4,256,256]{2,1,0:T(8,128)(2,1)S(1)}, bf16[4,256,256]{2,1,0:T(8,128)(2,1)S(1)}, u32[]{:S(2)}, u32[]{:S(2)}) collective-permute-start(bf16[4,256,256]{2,1,0:T(8,128)(2,1)S(1)} %all-to-all-done.ctx_ref.refs_0_), channel_id=1, source_target_pairs={{0,8},{4,12},{8,0},{12,4},{16,24},{20,28},{24,16},{28,20},{1,9},{5... | collective-permute-start | bytes 1572872 | tf_op jit(solution)/shard_map/ppermute | solution.py:372
  27.3 13.1 %collective-permute-start.4 = (bf16[256,1024]{1,0:T(8,128)(2,1)}, bf16[256,1024]{1,0:T(8,128)(2,1)S(1)}, u32[]{:S(2)}, u32[]{:S(2)}) collective-permute-start(bf16[256,1024]{1,0:T(8,128)(2,1)} %slice.12), channel_id=1, source_target_pairs={{0,2},{1,3},{2,0},{3,1},{4,6},{5,7},{6,4},{7,5},{8,10},{9,11},{10,... | collective-permute-start | bytes 1572872 | tf_op jit(solution)/shard_map/ppermute | solution.py:372
  40.4 1.9 %collective-permute-start.8 = (bf16[256,1024]{1,0:T(8,128)(2,1)S(1)}, bf16[256,1024]{1,0:T(8,128)(2,1)S(1)}, u32[]{:S(2)}, u32[]{:S(2)}) collective-permute-start(bf16[256,1024]{1,0:T(8,128)(2,1)S(1)} %collective-permute-done.4.refs_4_), channel_id=1, source_target_pairs={{0,1},{1,0},{2,3},{3,2},{4,5},{5,4},{6,7},{7,6},{8,9},{9,8},{10,11... | collective-permute-start | bytes 1572872 | tf_op jit(solution)/shard_map/ppermute | solution.py:372
  40.4 11.0 %collective-permute-start.10 = (bf16[4,128,256]{2,1,0:T(8,128)(2,1)S(1)}, bf16[4,128,256]{2,1,0:T(8,128)(2,1)S(1)}, u32[]{:S(2)}, u32[]{:S(2)}) collective-permute-start(bf16[4,128,256]{2,1,0:T(8,128)(2,1)S(1)} %slice.11), channel_id=1, source_target_pairs={{0,4},{4,0},{8,12},{12,8},{16,20},{20,16},{24,28},{28,24},{1,5},{5... | collective-permute-start | bytes 786440 | tf_op jit(solution)/shard_map/ppermute | solution.py:372
  41.1 11.3 %collective-permute-start.9 = (bf16[4,128,256]{2,1,0:T(8,128)(2,1)S(1)}, bf16[4,128,256]{2,1,0:T(8,128)(2,1)S(1)}, u32[]{:S(2)}, u32[]{:S(2)}) collective-permute-start(bf16[4,128,256]{2,1,0:T(8,128)(2,1)S(1)} %slice.10), channel_id=1, source_target_pairs={{0,8},{4,12},{8,0},{12,4},{16,24},{20,28},{24,16},{28,20},{1,9},{5... | collective-permute-start | bytes 786440 | tf_op jit(solution)/shard_map/ppermute | solution.py:372
  47.9 5.9 %collective-permute-start.18 = (bf16[256,256]{1,0:T(8,128)(2,1)S(1)}, bf16[256,256]{1,0:T(8,128)(2,1)S(1)}, u32[]{:S(2)}, u32[]{:S(2)}) collective-permute-start(bf16[256,256]{1,0:T(8,128)(2,1)S(1)} %get-tuple-element.62), channel_id=1, source_target_pairs={{0,4},{4,0},{8,12},{12,8},{16,20},{20,16},{24,28},{28,24},{1,5},{5... | collective-permute-start | bytes 393224 | tf_op jit(solution)/shard_map/ppermute | solution.py:372
  48.8 6.6 %collective-permute-start.19 = (bf16[256,256]{1,0:T(8,128)(2,1)S(1)}, bf16[256,256]{1,0:T(8,128)(2,1)S(1)}, u32[]{:S(2)}, u32[]{:S(2)}) collective-permute-start(bf16[256,256]{1,0:T(8,128)(2,1)S(1)} %get-tuple-element.63), channel_id=1, source_target_pairs={{0,8},{4,12},{8,0},{12,4},{16,24},{20,28},{24,16},{28,20},{1,9},{5... | collective-permute-start | bytes 393224 | tf_op jit(solution)/shard_map/ppermute | solution.py:372
  50.3 8.3 %collective-permute-start.20 = (bf16[256,256]{1,0:T(8,128)(2,1)S(1)}, bf16[256,256]{1,0:T(8,128)(2,1)S(1)}, u32[]{:S(2)}, u32[]{:S(2)}) collective-permute-start(bf16[256,256]{1,0:T(8,128)(2,1)S(1)} %get-tuple-element.64), channel_id=1, source_target_pairs={{0,12},{4,8},{8,4},{12,0},{16,28},{20,24},{24,20},{28,16},{1,13},{... | collective-permute-start | bytes 393224 | tf_op jit(solution)/shard_map/ppermute | solution.py:372
  51.4 8.5 %collective-permute-start.11 = (bf16[288,256]{1,0:T(8,128)(2,1)S(1)}, bf16[288,256]{1,0:T(8,128)(2,1)S(1)}, u32[]{:S(2)}, u32[]{:S(2)}) collective-permute-start(bf16[288,256]{1,0:T(8,128)(2,1)S(1)} %get-tuple-element.52), channel_id=1, source_target_pairs={{0,4},{4,0},{8,12},{12,8},{16,20},{20,16},{24,28},{28,24},{1,5},{5... | collective-permute-start | bytes 442376 | tf_op jit(solution)/shard_map/ppermute | solution.py:372
  52.3 8.8 %collective-permute-start.12 = (bf16[288,256]{1,0:T(8,128)(2,1)S(1)}, bf16[288,256]{1,0:T(8,128)(2,1)S(1)}, u32[]{:S(2)}, u32[]{:S(2)}) collective-permute-start(bf16[288,256]{1,0:T(8,128)(2,1)S(1)} %get-tuple-element.53), channel_id=1, source_target_pairs={{0,8},{4,12},{8,0},{12,4},{16,24},{20,28},{24,16},{28,20},{1,9},{5... | collective-permute-start | bytes 442376 | tf_op jit(solution)/shard_map/ppermute | solution.py:372
  53.8 10.0 %collective-permute-start.13 = (bf16[288,256]{1,0:T(8,128)(2,1)S(1)}, bf16[288,256]{1,0:T(8,128)(2,1)S(1)}, u32[]{:S(2)}, u32[]{:S(2)}) collective-permute-start(bf16[288,256]{1,0:T(8,128)(2,1)S(1)} %get-tuple-element.54), channel_id=1, source_target_pairs={{0,12},{4,8},{8,4},{12,0},{16,28},{20,24},{24,20},{28,16},{1,13},{... | collective-permute-start | bytes 442376 | tf_op jit(solution)/shard_map/ppermute | solution.py:372
  59.8 5.3 %collective-permute-start.21 = (bf16[2,2,256,128]{3,2,1,0:T(8,128)(2,1)S(1)}, bf16[2,2,256,128]{3,2,1,0:T(8,128)(2,1)S(1)}, u32[]{:S(2)}, u32[]{:S(2)}) collective-permute-start(bf16[2,2,256,128]{3,2,1,0:T(8,128)(2,1)S(1)} %get-tuple-element.66), channel_id=1, source_target_pairs={{0,1},{1,0},{2,3},{3,2},{4,5},{5,4},{6,7},{7,6},{8,9},{9,8},{10,11... | collective-permute-start | bytes 786440 | tf_op jit(solution)/shard_map/ppermute | solution.py:372
  65.0 1.7 %collective-permute-start.14 = (bf16[2,2,304,128]{3,2,1,0:T(8,128)(2,1)S(1)}, bf16[2,2,304,128]{3,2,1,0:T(8,128)(2,1)S(1)}, u32[]{:S(2)}, u32[]{:S(2)}) collective-permute-start(bf16[2,2,304,128]{3,2,1,0:T(8,128)(2,1)S(1)} %get-tuple-element.56), channel_id=1, source_target_pairs={{0,1},{1,0},{2,3},{3,2},{4,5},{5,4},{6,7},{7,6},{8,9},{9,8},{10,11... | collective-permute-start | bytes 933896 | tf_op jit(solution)/shard_map/ppermute | solution.py:372
  65.2 6.0 %collective-permute-start.22 = (bf16[1,2,256,128]{3,2,1,0:T(8,128)(2,1)S(1)}, bf16[1,2,256,128]{3,2,1,0:T(8,128)(2,1)S(1)}, u32[]{:S(2)}, u32[]{:S(2)}) collective-permute-start(bf16[1,2,256,128]{3,2,1,0:T(8,128)(2,1)S(1)} %get-tuple-element.68), channel_id=1, source_target_pairs={{0,2},{1,3},{2,0},{3,1},{4,6},{5,7},{6,4},{7,5},{8,10},{9,11},{10,... | collective-permute-start | bytes 393224 | tf_op jit(solution)/shard_map/ppermute | solution.py:377
  66.8 7.5 %collective-permute-start.15 = (bf16[1,1,304,128]{3,2,1,0:T(8,128)(2,1)S(1)}, bf16[1,1,304,128]{3,2,1,0:T(8,128)(2,1)S(1)}, u32[]{:S(2)}, u32[]{:S(2)}) collective-permute-start(bf16[1,1,304,128]{3,2,1,0:T(8,128)(2,1)S(1)} %get-tuple-element.58), channel_id=1, source_target_pairs={{0,16},{1,17},{2,18},{3,19},{4,20},{5,21},{6,22},{7,23},{8,24},{9,... | collective-permute-start | bytes 233480 | tf_op jit(solution)/shard_map/ppermute | solution.py:377
  69.4 4.8 %collective-permute-start.16 = (bf16[1,1,304,128]{3,2,1,0:T(8,128)(2,1)S(1)}, bf16[1,1,304,128]{3,2,1,0:T(8,128)(2,1)S(1)}, u32[]{:S(2)}, u32[]{:S(2)}) collective-permute-start(bf16[1,1,304,128]{3,2,1,0:T(8,128)(2,1)S(1)} %get-tuple-element.59), channel_id=1, source_target_pairs={{0,2},{1,3},{2,0},{3,1},{4,6},{5,7},{6,4},{7,5},{8,10},{9,11},{10,... | collective-permute-start | bytes 233480 | tf_op jit(solution)/shard_map/ppermute | solution.py:377
  70.7 8.9 %collective-permute-start.17 = (bf16[1,1,304,128]{3,2,1,0:T(8,128)(2,1)S(1)}, bf16[1,1,304,128]{3,2,1,0:T(8,128)(2,1)S(1)}, u32[]{:S(2)}, u32[]{:S(2)}) collective-permute-start(bf16[1,1,304,128]{3,2,1,0:T(8,128)(2,1)S(1)} %get-tuple-element.60), channel_id=1, source_target_pairs={{0,18},{1,19},{2,16},{3,17},{4,22},{5,23},{6,20},{7,21},{8,26},{9,... | collective-permute-start | bytes 233480 | tf_op jit(solution)/shard_map/ppermute | solution.py:377
  71.3 8.8 %collective-permute-start.23 = (bf16[1,1,256,128]{3,2,1,0:T(8,128)(2,1)S(1)}, bf16[1,1,256,128]{3,2,1,0:T(8,128)(2,1)S(1)}, u32[]{:S(2)}, u32[]{:S(2)}) collective-permute-start(bf16[1,1,256,128]{3,2,1,0:T(8,128)(2,1)S(1)} %get-tuple-element.70), channel_id=1, source_target_pairs={{0,16},{1,17},{2,18},{3,19},{4,20},{5,21},{6,22},{7,23},{8,24},{9,... | collective-permute-start | bytes 196616 | tf_op jit(solution)/shard_map/ppermute | solution.py:377
  (5 other events, 37.3 us)

commit v10 on v9

--- a/solution.py
+++ b/solution.py
@@ -36,7 +36,7 @@
 
 
 def params():
-    return pltpu.CompilerParams(vmem_limit_bytes=48 * MIB)
+    return pltpu.CompilerParams(vmem_limit_bytes=32 * MIB)
 
 
 VM = pl.BlockSpec(memory_space=pltpu.VMEM)
@@ -86,38 +86,75 @@
     )(info, q, k, v)
 
 
-def join_body(plan, counts, info_ref, ctx_ref, gain_ref, next_ref, *refs):
-    n_dp, n_tensor, chunks, seq, xor_far = plan
+def mix_body(n_tensor, counts, info_ref, ctx_ref, *refs):
     w_refs, at = [], 0
     for n in counts:
         w_refs.append(refs[at : at + n])
         at += n
-    hidden_ref, grad_refs = refs[at], refs[at + 1 : -5]
-    turned_ref, joined_ref, square_ref, acc_ref, slope_ref = refs[-5:]
-    rows, dout = joined_ref.shape
-    me, group, length, votes = info_ref[0], info_ref[1], info_ref[2], info_ref[3]
+    part_ref, square_ref, turned_ref = refs[at:]
+    dout = part_ref.shape[1]
+    me, side = info_ref[0], info_ref[1] % 2
     for m in range(n_tensor):
         turned_ref[m] = ctx_ref[me ^ m].T
-    near, far = group % NEAR, group // NEAR
     columns = [(c, 0, c) for c in range(0, dout, COLS)]
-    if xor_far:
-        cut, spare = w_refs[-1][0].shape[1], w_refs[-1][2].shape[1]
-        own, other = near % 2 * cut, (1 - near % 2) * cut
-        columns = [(pl.multiple_of(own + c, COLS), 0, c) for c in range(0, cut, COLS)]
-        columns += [(pl.multiple_of(other + c, COLS), 1, c) for c in range(0, cut, COLS)]
-        columns += [(2 * cut + c, 2, c) for c in range(0, spare, COLS)]
+    if max(counts) > 1:
+        cut = w_refs[-1][0].shape[1]
+        columns = [(pl.multiple_of(side * cut + c, COLS), 0, c) for c in range(0, cut, COLS)]
+        columns += [(pl.multiple_of((1 - side) * cut + c, COLS), 1, c) for c in range(0, cut, COLS)]
+        columns += [(c, None, c) for c in range(2 * cut, dout, COLS)]
     for step, (start, piece, first) in enumerate(columns):
         to = pl.ds(start, COLS)
         total = None
         for m in range(n_tensor):
             whole = len(w_refs[m]) == 1
+            if not whole and piece is None:
+                continue
             w = w_refs[m][0][:, to] if whole else w_refs[m][piece][:, first : first + COLS]
             part = dot(turned_ref[m], w, ((1,), (0,)))
             total = part if total is None else total + part
-        joined_ref[:, to] = total
+        part_ref[:, to] = total
+        if piece is not None:
+            sq = total * total
+            lanes = sum(sq[:, i : i + 128] for i in range(0, COLS, 128))
+            square_ref[...] = lanes if step == 0 else square_ref[...] + lanes
+
+
+def mix(info, ctx, weights):
+    n_tensor, width, rows = ctx.shape
+    dout = weights[0][0].shape[1]
+    counts = [len(w) for w in weights]
+    return pl.pallas_call(
+        functools.partial(mix_body, n_tensor, counts),
+        in_specs=[SM] + [VM] * (1 + sum(counts)),
+        out_specs=[VM] * 3,
+        out_shape=[shape((rows, dout), F32), shape((rows, 128), F32), shape((n_tensor, rows, width))],
+        compiler_params=params(),
+        cost_estimate=pl.CostEstimate(
+            flops=2 * rows * dout * width * n_tensor,
+            bytes_accessed=2 * dout * (width * n_tensor + 2 * rows),
+            transcendentals=0,
+        ),
+        name="mix",
+    )(info, ctx, *[w for held in weights for w in held])
+
+
+def join_body(plan, n_late, info_ref, part_ref, early_ref, turned_ref, gain_ref, next_ref, *refs):
+    n_dp, n_tensor, chunks, seq, xor_far = plan
+    late_refs, hidden_ref, grad_refs = refs[:n_late], refs[n_late], refs[n_late + 1 : -4]
+    joined_ref, square_ref, acc_ref, slope_ref = refs[-4:]
+    rows, dout = joined_ref.shape
+    step = acc_ref.shape[0]
+    me, group, length, votes = info_ref[0], info_ref[1], info_ref[2], info_ref[3]
+    near, far = group % NEAR, group // NEAR
+    square_ref[...] = early_ref[...]
+    ready = dout - late_refs[0].shape[1] if n_late else dout
+    for c in range(ready, dout, COLS):
+        total = part_ref[:, c : c + COLS]
+        for m, ref in enumerate(late_refs, n_tensor - n_late):
+            total += dot(turned_ref[m], ref[:, c - ready : c - ready + COLS], ((1,), (0,)))
+        joined_ref[:, c : c + COLS] = total
         sq = total * total
-        lanes = sum(sq[:, i : i + 128] for i in range(0, COLS, 128))
-        square_ref[...] = lanes if step == 0 else square_ref[...] + lanes
+        square_ref[...] += sum(sq[:, i : i + 128] for i in range(0, COLS, 128))
     acc_ref[...] = jnp.zeros_like(acc_ref)
     slice_w = dout // n_dp
     cw = slice_w // chunks
@@ -125,16 +162,16 @@
 
     def body(r, carry):
         loss, weights = carry
-        at = pl.ds(pl.multiple_of(r * ROWS, ROWS), ROWS)
+        at = pl.ds(pl.multiple_of(r * step, step), step)
         inv = lax.rsqrt(jnp.sum(square_ref[at, :], axis=1, keepdims=True) * (1.0 / dout) + 1e-06)
-        pos = (me * rows + r * ROWS) % seq + lax.broadcasted_iota(jnp.int32, (ROWS, 1), 0)
+        pos = (me * rows + r * step) % seq + lax.broadcasted_iota(jnp.int32, (step, 1), 0)
         weight = jnp.where(pos < length - 1, votes.astype(F32), 0.0)
         scaled = weight * (loss_scale * 2.0 / dout)
-        miss = jnp.zeros((ROWS, 128), F32)
-        lean = jnp.zeros((ROWS, 128), F32)
+        miss = jnp.zeros((step, 128), F32)
+        lean = jnp.zeros((step, 128), F32)
         for c in range(0, dout, 512):
             cs = slice(c, c + 512)
-            normed = joined_ref[at, cs] * inv
+            normed = (part_ref if c < ready else joined_ref)[at, cs] * inv
             gain = gain_ref[:, cs]
             predicted = normed * gain
             hidden_ref[at, cs] = predicted.astype(BF)
@@ -167,8 +204,8 @@
         loss = loss + weight * (jnp.sum(miss, axis=1, keepdims=True) * (1.0 / dout))
         return loss, weights + weight
 
-    zero = jnp.zeros((ROWS, 1), F32)
-    loss, weights = lax.fori_loop(0, rows // ROWS, body, (zero, zero))
+    zero = jnp.zeros((step, 1), F32)
+    loss, weights = lax.fori_loop(0, rows // step, body, (zero, zero))
     wide = n_far * cw
     gain_sum = jnp.sum(acc_ref[...], axis=0, keepdims=True)
     gain_sum = jnp.concatenate([gain_sum[:, i : i + wide] for i in range(0, dout, wide)], 0)
@@ -187,9 +224,10 @@
             grad_refs[0][q, rows:, :] = words
 
 
-def join(plan, info, ctx, gain, next_hidden, weights):
+def join(plan, info, early, gain, next_hidden, late):
     n_dp, n_tensor, chunks, _, _ = plan
-    _, width, rows = ctx.shape
+    _, rows, width = early[2].shape
+    step = min(ROWS, rows)
     dout = gain.shape[1]
     wide = dout // NEAR // chunks
     tall = [rows + STAT_ROWS] + [rows] * (chunks - 1)
@@ -199,25 +237,24 @@
     else:
         grads = [shape((NEAR, n, wide)) for n in tall]
     out = pl.pallas_call(
-        functools.partial(join_body, plan, [len(w) for w in weights]),
-        in_specs=[SM] + [VM] * (3 + sum(len(w) for w in weights)),
+        functools.partial(join_body, plan, len(late)),
+        in_specs=[SM] + [VM] * (5 + len(late)),
         out_specs=[VM] * (1 + len(grads)),
         out_shape=[shape((rows, dout)), *grads],
         scratch_shapes=[
-            pltpu.VMEM((n_tensor, rows, width), BF),
             pltpu.VMEM((rows, dout), F32),
             pltpu.VMEM((rows, 128), F32),
-            pltpu.VMEM((ROWS, dout), F32),
-            pltpu.VMEM((ROWS, dout), F32),
+            pltpu.VMEM((step, dout), F32),
+            pltpu.VMEM((step, dout), F32),
         ],
         compiler_params=params(),
         cost_estimate=pl.CostEstimate(
-            flops=2 * rows * dout * width * n_tensor,
-            bytes_accessed=2 * dout * (width * n_tensor + 3 * rows),
+            flops=rows * dout * width,
+            bytes_accessed=2 * dout * (width + 5 * rows),
             transcendentals=rows,
         ),
         name="join",
-    )(info, ctx, gain, next_hidden, *[w for held in weights for w in held])
+    )(info, *early, gain, next_hidden, *late)
     if aligned:
         return out[0], [out[1 + j * NEAR : 1 + (j + 1) * NEAR] for j in range(chunks)]
     return out[0], [[g[q] for q in range(NEAR)] for g in out[1:]]
@@ -402,7 +439,7 @@
     return [blocks[0], far(blocks[1], 0, 1), far(blocks[2], 1, 0), far(blocks[3], 1, 1)]
 
 
-def gather_large(n_dp, n_tensor, _, weight, context):
+def gather_large(n_dp, n_tensor, _, info, weight, context):
     ctx = lax.all_to_all(context, "tensor", 0, 0, tiled=True)
     held = {0: weight}
     bit = n_tensor // 2
@@ -410,10 +447,10 @@
         held.update({m | bit: swap(w, "tensor", n_tensor, bit) for m, w in list(held.items())})
         bit //= 2
     ctxs = [[ctx]] + [[swap(ctx, "dp", n_dp, q)] for q in range(1, NEAR)]
-    return ctx, ctxs, [[held[m]] for m in range(n_tensor)]
-
-
-def gather_small(n_dp, n_tensor, side, weight, context):
+    return ctxs, mix(info, ctx, [[held[m]] for m in range(n_tensor)]), []
+
+
+def gather_small(n_dp, n_tensor, side, info, weight, context):
     barrier = lax.optimization_barrier
 
     def dp(x, mask):
@@ -433,11 +470,11 @@
     rest, other, mine_beside, beside, ctx = barrier((rest, other, mine_beside, beside, ctx))
     rest, other_beside = tensor(rest, 2), tensor(other, 1)
     ctx_x, ctx_z = dp(ctx, 1), dp(ctx, 2)
-    rest, other_beside, ctx_x, ctx_z = barrier((rest, other_beside, ctx_x, ctx_z))
+    early = mix(info, ctx, [[weight], [beside], [mine, other], [mine_beside, other_beside]])
+    rest, early, ctx_x, ctx_z = barrier((rest, early, ctx_x, ctx_z))
     half = ctx.shape[1] // 2
     ctxs = [[ctx], [ctx_x], [ctx_z], [dp(ctx_x[:, :half], 2), dp(ctx_z[:, half:], 1)]]
-    far = [mine, other, rest]
-    return ctx, ctxs, [[weight], [beside], far, [mine_beside, other_beside, tensor(rest, 1)]]
+    return ctxs, early, [rest, tensor(rest, 1)]
 
 
 def on_device(
@@ -465,8 +502,8 @@
 
     attended = attend(info, query_states[0], key_states[0], value_states[0], rows)
     gather = gather_small if xor_far else gather_large
-    ctx, ctxs, weights = gather(n_dp, n_tensor, group & 1, joining_weight[0], attended)
-    hidden, grads = join(plan, info, ctx, norm_gain[None, :], next_hidden, weights)
+    ctxs, early, late = gather(n_dp, n_tensor, group & 1, info, joining_weight[0], attended)
+    hidden, grads = join(plan, info, early, norm_gain[None, :], next_hidden, late)
     parts = []
     for j in range(chunks):
         near = [grads[j][0]] + [swap(grads[j][q], "dp", n_dp, q) for q in range(1, NEAR)]

time: 81.2 us -> 79.7 us (0.982)
  waiting for transfers between devices: 31.8 us -> 29.6 us
    ppermute x19, waiting for transfers between devices: 25.8 us -> 23.7 us  [swap(): return lax.ppermute(x, axis, [(i, i ^ mask) for i in range(n)])]
    pallas_call x1 -> x2, Pallas kernels: 5.63 us -> 6.29 us  [the longest x1 4.04 us: join(): pl.pallas_call(functools.partial(join_body, plan, len(late)), in_specs=[S...]
  transfers between devices with their start and end apart: 25 -> 25, of which waited for: 14 -> 14; matrix products, arithmetic and copies ran while one was open for 3% -> 3% of each run, Pallas kernels for 16% -> 17%
where the time goes in v10:
time: 79.7 us; the launch traced here: 79.4 us
  starting transfers between devices  30.7 us (39%)
  waiting for transfers between devices  29.6 us (37%)
  Pallas kernels  14.7 us (18%)
  between operations  2.04 us (3%)
  local copies, waits for them, and re-layouts  1.85 us (2%)
    ppermute x19, waiting for transfers between devices, swap(): return lax.ppermute(x, axis, [(i, i ^ mask) for i in range(n)])  23.7 us
    ppermute x19, starting transfers between devices, swap(): return lax.ppermute(x, axis, [(i, i ^ mask) for i in range(n)])  18.5 us
    ppermute x5, starting transfers between devices, swap_far(): lax.ppermute(x, ('dp', 'tensor'), [(i, i ^ mask) for i in range(n_dp * n_...  8.78 us
    ppermute x5, waiting for transfers between devices, swap_far(): lax.ppermute(x, ('dp', 'tensor'), [(i, i ^ mask) for i in range(n_dp * n_...  5.7 us
    pallas_call x1, Pallas kernels, attend(): pl.pallas_call(attend_body, in_specs=[SM, block, block, block], out_specs...  4.92 us
    pallas_call x1, Pallas kernels, join(): pl.pallas_call(functools.partial(join_body, plan, len(late)), in_specs=[S...  4.04 us
    all_to_all x1, starting transfers between devices, gather_small(): ctx = lax.all_to_all(context, 'tensor', 0, 0, tiled=True)  3.47 us
    pallas_call x2, Pallas kernels, gradient(): pl.pallas_call(functools.partial(grad_body, plan, dout, [len(c) for c in...  2.49 us
  transfers between devices with their start and end apart: 25, of which 14 were waited for; matrix products, arithmetic and copies ran while one was open for 3% of the time, Pallas kernels for 17%

profile of v10, /device:TPU:0, one launch (start us, length us, event | category | flops | bytes accessed | tf_op | source)
XLA Modules:
  0.0 79.4 jit_solution(870252139380492221)
XLA Ops:
  2.1 2.6 %collective-permute-start = (bf16[256,512]{1,0:T(8,128)(2,1)S(1)}, bf16[256,512]{1,0:T(8,128)(2,1)S(1)}, u32[]{:S(2)}, u32[]{:S(2)}) collective-permute-start(bf16[256,512]{1,0:T(8,128)(2,1)S(1)} %dynamic-slice_bitcast_fusion), channel_id=1, source_target_pairs={{0,2},{1,3},{2,0},{3,1},{4,6},{5,7},{6,4},{7,5},{8,10},{9,11},{10,... | collective-permute-start | bytes 786440 | tf_op jit(solution)/shard_map/ppermute | solution.py:409
  6.6 4.9 %attend.1 = bf16[4,256,256]{2,1,0:T(8,128)(2,1)} custom-call(s32[4]{0:T(128)} %pad_add_fusion.info_ref, bf16[1024,256]{1,0:T(8,128)(2,1)} %bitcast.16, bf16[1024,256]{1,0:T(8,128)(2,1)} %bitcast.17, bf16[1024,256]{1,0:T(8,128)(2,1)} %bitcast.18), custom_call_target="tpu_custom_call" | custom-call | flops 1073741824 | bytes 2097152 | tf_op jit(solution)/shard_map/attend/pallas_call | solution.py:76
  11.7 3.5 %all-to-all-start = ((bf16[4,256,256]{2,1,0:T(8,128)(2,1)}), bf16[4,256,256]{2,1,0:T(8,128)(2,1)S(1)}, u32[]{:S(2)}, u32[]{:S(2)}) async-start(bf16[4,256,256]{2,1,0:T(8,128)(2,1)} %attend.1), calls=%async_computation | async-start | bytes 1048576 | tf_op jit(solution)/shard_map/all_to_all | solution.py:469
  15.2 1.8 %collective-permute-start.1 = (bf16[256,512]{1,0:T(8,128)(2,1)S(1)}, bf16[256,512]{1,0:T(8,128)(2,1)S(1)}, u32[]{:S(2)}, u32[]{:S(2)}) collective-permute-start(bf16[256,512]{1,0:T(8,128)(2,1)S(1)} %collective-permute-done.refs_2_), channel_id=1, source_target_pairs={{0,4},{4,0},{8,12},{12,8},{16,20},{20,16},{24,28},{28,24},{1,5},{5... | collective-permute-start | bytes 786440 | tf_op jit(solution)/shard_map/ppermute | solution.py:409
  17.9 5.9 %collective-permute-done.1.refs_3_ = bf16[256,512]{1,0:T(8,128)(2,1)S(1)} collective-permute-done((bf16[256,512]{1,0:T(8,128)(2,1)S(1)}, bf16[256,512]{1,0:T(8,128)(2,1)S(1)}, u32[]{:S(2)}, u32[]{:S(2)}) %collective-permute-start.1) | collective-permute-done | bytes 262176 | tf_op jit(solution)/shard_map/ppermute | solution.py:409
  24.0 1.7 %collective-permute-start.6 = (bf16[4,256,256]{2,1,0:T(8,128)(2,1)S(1)}, bf16[4,256,256]{2,1,0:T(8,128)(2,1)S(1)}, u32[]{:S(2)}, u32[]{:S(2)}) collective-permute-start(bf16[4,256,256]{2,1,0:T(8,128)(2,1)S(1)} %all-to-all-done.ctx_ref.refs_0_), channel_id=1, source_target_pairs={{0,4},{4,0},{8,12},{12,8},{16,20},{20,16},{24,28},{28,24},{1,5},{5... | collective-permute-start | bytes 1572872 | tf_op jit(solution)/shard_map/ppermute | solution.py:409
  25.7 1.6 %collective-permute-start.7 = (bf16[4,256,256]{2,1,0:T(8,128)(2,1)S(1)}, bf16[4,256,256]{2,1,0:T(8,128)(2,1)S(1)}, u32[]{:S(2)}, u32[]{:S(2)}) collective-permute-start(bf16[4,256,256]{2,1,0:T(8,128)(2,1)S(1)} %all-to-all-done.ctx_ref.refs_0_), channel_id=1, source_target_pairs={{0,8},{4,12},{8,0},{12,4},{16,24},{20,28},{24,16},{28,20},{1,9},{5... | collective-permute-start | bytes 1572872 | tf_op jit(solution)/shard_map/ppermute | solution.py:409
  27.3 1.6 %collective-permute-start.4 = (bf16[256,1024]{1,0:T(8,128)(2,1)}, bf16[256,1024]{1,0:T(8,128)(2,1)S(1)}, u32[]{:S(2)}, u32[]{:S(2)}) collective-permute-start(bf16[256,1024]{1,0:T(8,128)(2,1)} %slice.12), channel_id=1, source_target_pairs={{0,2},{1,3},{2,0},{3,1},{4,6},{5,7},{6,4},{7,5},{8,10},{9,11},{10,... | collective-permute-start | bytes 1572872 | tf_op jit(solution)/shard_map/ppermute | solution.py:409
  28.9 1.5 %collective-permute-done.5.refs_5_ = bf16[256,512]{1,0:T(8,128)(2,1)S(1)} collective-permute-done((bf16[256,512]{1,0:T(8,128)(2,1)S(1)}, bf16[256,512]{1,0:T(8,128)(2,1)S(1)}, u32[]{:S(2)}, u32[]{:S(2)}) %collective-permute-start.5) | collective-permute-done | bytes 262176 | tf_op jit(solution)/shard_map/ppermute | solution.py:409
  30.4 2.2 %mix.1 = (f32[256,2048]{1,0:T(8,128)S(1)}, f32[256,128]{1,0:T(8,128)S(1)}, bf16[4,256,256]{2,1,0:T(8,128)(2,1)S(1)}) custom-call(s32[4]{0:T(128)S(1)} %copy-done.3, bf16[4,256,256]{2,1,0:T(8,128)(2,1)S(1)} %all-to-all-done.ctx_ref.refs_0_, bf16[256,2048]{1,0:T(8,128)(2,1)S(1)} %bitcast.14, bf16[256,2048]{1,0:T(8,128)(2,1)} %collective-permute-done.3.refs_1_, ...), custom_call_target="tpu_custom_call" | custom-call | flops 1073741824 | bytes 6291456 | tf_op jit(solution)/shard_map/mix/pallas_call | solution.py:126
  32.7 4.8 %collective-permute-done.6.refs_1_ = bf16[4,256,256]{2,1,0:T(8,128)(2,1)S(1)} collective-permute-done((bf16[4,256,256]{2,1,0:T(8,128)(2,1)S(1)}, bf16[4,256,256]{2,1,0:T(8,128)(2,1)S(1)}, u32[]{:S(2)}, u32[]{:S(2)}) %collective-permute-start.6) | collective-permute-done | bytes 524320 | tf_op jit(solution)/shard_map/ppermute | solution.py:409
  37.4 1.4 %collective-permute-done.7.refs_2_ = bf16[4,256,256]{2,1,0:T(8,128)(2,1)S(1)} collective-permute-done((bf16[4,256,256]{2,1,0:T(8,128)(2,1)S(1)}, bf16[4,256,256]{2,1,0:T(8,128)(2,1)S(1)}, u32[]{:S(2)}, u32[]{:S(2)}) %collective-permute-start.7) | collective-permute-done | bytes 524320 | tf_op jit(solution)/shard_map/ppermute | solution.py:409
  38.9 1.5 %collective-permute-done.4.refs_0_ = bf16[256,1024]{1,0:T(8,128)(2,1)S(1)} collective-permute-done((bf16[256,1024]{1,0:T(8,128)(2,1)}, bf16[256,1024]{1,0:T(8,128)(2,1)S(1)}, u32[]{:S(2)}, u32[]{:S(2)}) %collective-permute-start.4) | collective-permute-done | bytes 524320 | tf_op jit(solution)/shard_map/ppermute | solution.py:409
  42.3 4.0 %join.1 = (bf16[256,2048]{1,0:T(8,128)(2,1)}, bf16[288,256]{1,0:T(8,128)(2,1)S(1)}, bf16[288,256]{1,0:T(8,128)(2,1)S(1)}, bf16[288,256]{1,0:T(8,128)(2,1)S(1)}, ...) custom-call(s32[4]{0:T(128)S(1)} %copy-done.3, ...), custom_call_target="tpu_custom_call" | custom-call | flops 134217728 | bytes 6291456 | tf_op jit(solution)/shard_map/join/pallas_call | solution.py:239
  47.1 1.6 %collective-permute-start.19 = (bf16[256,256]{1,0:T(8,128)(2,1)S(1)}, bf16[256,256]{1,0:T(8,128)(2,1)S(1)}, u32[]{:S(2)}, u32[]{:S(2)}) collective-permute-start(bf16[256,256]{1,0:T(8,128)(2,1)S(1)} %get-tuple-element.73), channel_id=1, source_target_pairs={{0,8},{4,12},{8,0},{12,4},{16,24},{20,28},{24,16},{28,20},{1,9},{5... | collective-permute-start | bytes 393224 | tf_op jit(solution)/shard_map/ppermute | solution.py:409
  50.6 1.6 %collective-permute-start.12 = (bf16[288,256]{1,0:T(8,128)(2,1)S(1)}, bf16[288,256]{1,0:T(8,128)(2,1)S(1)}, u32[]{:S(2)}, u32[]{:S(2)}) collective-permute-start(bf16[288,256]{1,0:T(8,128)(2,1)S(1)} %get-tuple-element.63), channel_id=1, source_target_pairs={{0,8},{4,12},{8,0},{12,4},{16,24},{20,28},{24,16},{28,20},{1,9},{5... | collective-permute-start | bytes 442376 | tf_op jit(solution)/shard_map/ppermute | solution.py:409
  52.2 1.6 %collective-permute-start.13 = (bf16[288,256]{1,0:T(8,128)(2,1)S(1)}, bf16[288,256]{1,0:T(8,128)(2,1)S(1)}, u32[]{:S(2)}, u32[]{:S(2)}) collective-permute-start(bf16[288,256]{1,0:T(8,128)(2,1)S(1)} %get-tuple-element.64), channel_id=1, source_target_pairs={{0,12},{4,8},{8,4},{12,0},{16,28},{20,24},{24,20},{28,16},{1,13},{... | collective-permute-start | bytes 442376 | tf_op jit(solution)/shard_map/ppermute | solution.py:409
  53.8 3.2 %collective-permute-done.20.refs_8_ = bf16[256,256]{1,0:T(8,128)(2,1)S(1)} collective-permute-done((bf16[256,256]{1,0:T(8,128)(2,1)S(1)}, bf16[256,256]{1,0:T(8,128)(2,1)S(1)}, u32[]{:S(2)}, u32[]{:S(2)}) %collective-permute-start.20) | collective-permute-done | bytes 131104 | tf_op jit(solution)/shard_map/ppermute | solution.py:409
  59.5 3.0 %collective-permute-done.13.refs_8_ = bf16[288,256]{1,0:T(8,128)(2,1)S(1)} collective-permute-done((bf16[288,256]{1,0:T(8,128)(2,1)S(1)}, bf16[288,256]{1,0:T(8,128)(2,1)S(1)}, u32[]{:S(2)}, u32[]{:S(2)}) %collective-permute-start.13) | collective-permute-done | bytes 147488 | tf_op jit(solution)/shard_map/ppermute | solution.py:409
  63.9 1.4 %collective-permute-start.22 = (bf16[1,2,256,128]{3,2,1,0:T(8,128)(2,1)S(1)}, bf16[1,2,256,128]{3,2,1,0:T(8,128)(2,1)S(1)}, u32[]{:S(2)}, u32[]{:S(2)}) collective-permute-start(bf16[1,2,256,128]{3,2,1,0:T(8,128)(2,1)S(1)} %get-tuple-element.78), channel_id=1, source_target_pairs={{0,2},{1,3},{2,0},{3,1},{4,6},{5,7},{6,4},{7,5},{8,10},{9,11},{10,... | collective-permute-start | bytes 393224 | tf_op jit(solution)/shard_map/ppermute | solution.py:414
  65.4 2.7 %collective-permute-start.15 = (bf16[1,1,304,128]{3,2,1,0:T(8,128)(2,1)S(1)}, bf16[1,1,304,128]{3,2,1,0:T(8,128)(2,1)S(1)}, u32[]{:S(2)}, u32[]{:S(2)}) collective-permute-start(bf16[1,1,304,128]{3,2,1,0:T(8,128)(2,1)S(1)} %get-tuple-element.68), channel_id=1, source_target_pairs={{0,16},{1,17},{2,18},{3,19},{4,20},{5,21},{6,22},{7,23},{8,24},{9,... | collective-permute-start | bytes 233480 | tf_op jit(solution)/shard_map/ppermute | solution.py:414
  68.1 1.3 %collective-permute-start.16 = (bf16[1,1,304,128]{3,2,1,0:T(8,128)(2,1)S(1)}, bf16[1,1,304,128]{3,2,1,0:T(8,128)(2,1)S(1)}, u32[]{:S(2)}, u32[]{:S(2)}) collective-permute-start(bf16[1,1,304,128]{3,2,1,0:T(8,128)(2,1)S(1)} %get-tuple-element.69), channel_id=1, source_target_pairs={{0,2},{1,3},{2,0},{3,1},{4,6},{5,7},{6,4},{7,5},{8,10},{9,11},{10,... | collective-permute-start | bytes 233480 | tf_op jit(solution)/shard_map/ppermute | solution.py:414
  69.9 3.0 %collective-permute-start.23 = (bf16[1,1,256,128]{3,2,1,0:T(8,128)(2,1)S(1)}, bf16[1,1,256,128]{3,2,1,0:T(8,128)(2,1)S(1)}, u32[]{:S(2)}, u32[]{:S(2)}) collective-permute-start(bf16[1,1,256,128]{3,2,1,0:T(8,128)(2,1)S(1)} %get-tuple-element.80), channel_id=1, source_target_pairs={{0,16},{1,17},{2,18},{3,19},{4,20},{5,21},{6,22},{7,23},{8,24},{9,... | collective-permute-start | bytes 196616 | tf_op jit(solution)/shard_map/ppermute | solution.py:414
  72.9 5.1 %collective-permute-done.17.refs_3_ = bf16[1,1,304,128]{3,2,1,0:T(8,128)(2,1)S(1)} collective-permute-done((bf16[1,1,304,128]{3,2,1,0:T(8,128)(2,1)S(1)}, bf16[1,1,304,128]{3,2,1,0:T(8,128)(2,1)S(1)}, u32[]{:S(2)}, u32[]{:S(2)}) %collective-permute-start.17) | collective-permute-done | bytes 77856 | tf_op jit(solution)/shard_map/ppermute | solution.py:414
  (48 shorter events, 13.9 us)
Async XLA Ops:
  0.6 23.3 %collective-permute-start.3 = (bf16[256,2048]{1,0:T(8,128)(2,1)}, bf16[256,2048]{1,0:T(8,128)(2,1)}, u32[]{:S(2)}, u32[]{:S(2)}) collective-permute-start(bf16[256,2048]{1,0:T(8,128)(2,1)} %bitcast.12), channel_id=1, source_target_pairs={{0,1},{1,0},{2,3},{3,2},{4,5},{5,4},{6,7},{7,6},{8,9},{9,8},{10,11... | collective-permute-start | bytes 3145736 | tf_op jit(solution)/shard_map/ppermute | solution.py:409
  2.1 9.6 %collective-permute-start = (bf16[256,512]{1,0:T(8,128)(2,1)S(1)}, bf16[256,512]{1,0:T(8,128)(2,1)S(1)}, u32[]{:S(2)}, u32[]{:S(2)}) collective-permute-start(bf16[256,512]{1,0:T(8,128)(2,1)S(1)} %dynamic-slice_bitcast_fusion), channel_id=1, source_target_pairs={{0,2},{1,3},{2,0},{3,1},{4,6},{5,7},{6,4},{7,5},{8,10},{9,11},{10,... | collective-permute-start | bytes 786440 | tf_op jit(solution)/shard_map/ppermute | solution.py:409
  11.7 12.3 %all-to-all-start = ((bf16[4,256,256]{2,1,0:T(8,128)(2,1)}), bf16[4,256,256]{2,1,0:T(8,128)(2,1)S(1)}, u32[]{:S(2)}, u32[]{:S(2)}) async-start(bf16[4,256,256]{2,1,0:T(8,128)(2,1)} %attend.1), calls=%async_computation | async-start | bytes 1048576 | tf_op jit(solution)/shard_map/all_to_all | solution.py:469
  15.2 8.7 %collective-permute-start.1 = (bf16[256,512]{1,0:T(8,128)(2,1)S(1)}, bf16[256,512]{1,0:T(8,128)(2,1)S(1)}, u32[]{:S(2)}, u32[]{:S(2)}) collective-permute-start(bf16[256,512]{1,0:T(8,128)(2,1)S(1)} %collective-permute-done.refs_2_), channel_id=1, source_target_pairs={{0,4},{4,0},{8,12},{12,8},{16,20},{20,16},{24,28},{28,24},{1,5},{5... | collective-permute-start | bytes 786440 | tf_op jit(solution)/shard_map/ppermute | solution.py:409
  16.9 6.9 %collective-permute-start.2 = (bf16[256,512]{1,0:T(8,128)(2,1)S(1)}, bf16[256,512]{1,0:T(8,128)(2,1)S(1)}, u32[]{:S(2)}, u32[]{:S(2)}) collective-permute-start(bf16[256,512]{1,0:T(8,128)(2,1)S(1)} %collective-permute-done.refs_2_), channel_id=1, source_target_pairs={{0,1},{1,0},{2,3},{3,2},{4,5},{5,4},{6,7},{7,6},{8,9},{9,8},{10,11... | collective-permute-start | bytes 786440 | tf_op jit(solution)/shard_map/ppermute | solution.py:409
  24.0 13.5 %collective-permute-start.6 = (bf16[4,256,256]{2,1,0:T(8,128)(2,1)S(1)}, bf16[4,256,256]{2,1,0:T(8,128)(2,1)S(1)}, u32[]{:S(2)}, u32[]{:S(2)}) collective-permute-start(bf16[4,256,256]{2,1,0:T(8,128)(2,1)S(1)} %all-to-all-done.ctx_ref.refs_0_), channel_id=1, source_target_pairs={{0,4},{4,0},{8,12},{12,8},{16,20},{20,16},{24,28},{28,24},{1,5},{5... | collective-permute-start | bytes 1572872 | tf_op jit(solution)/shard_map/ppermute | solution.py:409
  25.7 13.2 %collective-permute-start.7 = (bf16[4,256,256]{2,1,0:T(8,128)(2,1)S(1)}, bf16[4,256,256]{2,1,0:T(8,128)(2,1)S(1)}, u32[]{:S(2)}, u32[]{:S(2)}) collective-permute-start(bf16[4,256,256]{2,1,0:T(8,128)(2,1)S(1)} %all-to-all-done.ctx_ref.refs_0_), channel_id=1, source_target_pairs={{0,8},{4,12},{8,0},{12,4},{16,24},{20,28},{24,16},{28,20},{1,9},{5... | collective-permute-start | bytes 1572872 | tf_op jit(solution)/shard_map/ppermute | solution.py:409
  27.3 13.1 %collective-permute-start.4 = (bf16[256,1024]{1,0:T(8,128)(2,1)}, bf16[256,1024]{1,0:T(8,128)(2,1)S(1)}, u32[]{:S(2)}, u32[]{:S(2)}) collective-permute-start(bf16[256,1024]{1,0:T(8,128)(2,1)} %slice.12), channel_id=1, source_target_pairs={{0,2},{1,3},{2,0},{3,1},{4,6},{5,7},{6,4},{7,5},{8,10},{9,11},{10,... | collective-permute-start | bytes 1572872 | tf_op jit(solution)/shard_map/ppermute | solution.py:409
  40.4 1.9 %collective-permute-start.8 = (bf16[256,1024]{1,0:T(8,128)(2,1)S(1)}, bf16[256,1024]{1,0:T(8,128)(2,1)S(1)}, u32[]{:S(2)}, u32[]{:S(2)}) collective-permute-start(bf16[256,1024]{1,0:T(8,128)(2,1)S(1)} %collective-permute-done.4.refs_0_), channel_id=1, source_target_pairs={{0,1},{1,0},{2,3},{3,2},{4,5},{5,4},{6,7},{7,6},{8,9},{9,8},{10,11... | collective-permute-start | bytes 1572872 | tf_op jit(solution)/shard_map/ppermute | solution.py:409
  40.4 9.4 %collective-permute-start.10 = (bf16[4,128,256]{2,1,0:T(8,128)(2,1)S(1)}, bf16[4,128,256]{2,1,0:T(8,128)(2,1)S(1)}, u32[]{:S(2)}, u32[]{:S(2)}) collective-permute-start(bf16[4,128,256]{2,1,0:T(8,128)(2,1)S(1)} %slice.11), channel_id=1, source_target_pairs={{0,4},{4,0},{8,12},{12,8},{16,20},{20,16},{24,28},{28,24},{1,5},{5... | collective-permute-start | bytes 786440 | tf_op jit(solution)/shard_map/ppermute | solution.py:409
  41.0 9.6 %collective-permute-start.9 = (bf16[4,128,256]{2,1,0:T(8,128)(2,1)S(1)}, bf16[4,128,256]{2,1,0:T(8,128)(2,1)S(1)}, u32[]{:S(2)}, u32[]{:S(2)}) collective-permute-start(bf16[4,128,256]{2,1,0:T(8,128)(2,1)S(1)} %slice.10), channel_id=1, source_target_pairs={{0,8},{4,12},{8,0},{12,4},{16,24},{20,28},{24,16},{28,20},{1,9},{5... | collective-permute-start | bytes 786440 | tf_op jit(solution)/shard_map/ppermute | solution.py:409
  46.3 5.9 %collective-permute-start.18 = (bf16[256,256]{1,0:T(8,128)(2,1)S(1)}, bf16[256,256]{1,0:T(8,128)(2,1)S(1)}, u32[]{:S(2)}, u32[]{:S(2)}) collective-permute-start(bf16[256,256]{1,0:T(8,128)(2,1)S(1)} %get-tuple-element.72), channel_id=1, source_target_pairs={{0,4},{4,0},{8,12},{12,8},{16,20},{20,16},{24,28},{28,24},{1,5},{5... | collective-permute-start | bytes 393224 | tf_op jit(solution)/shard_map/ppermute | solution.py:409
  47.1 6.7 %collective-permute-start.19 = (bf16[256,256]{1,0:T(8,128)(2,1)S(1)}, bf16[256,256]{1,0:T(8,128)(2,1)S(1)}, u32[]{:S(2)}, u32[]{:S(2)}) collective-permute-start(bf16[256,256]{1,0:T(8,128)(2,1)S(1)} %get-tuple-element.73), channel_id=1, source_target_pairs={{0,8},{4,12},{8,0},{12,4},{16,24},{20,28},{24,16},{28,20},{1,9},{5... | collective-permute-start | bytes 393224 | tf_op jit(solution)/shard_map/ppermute | solution.py:409
  48.7 8.4 %collective-permute-start.20 = (bf16[256,256]{1,0:T(8,128)(2,1)S(1)}, bf16[256,256]{1,0:T(8,128)(2,1)S(1)}, u32[]{:S(2)}, u32[]{:S(2)}) collective-permute-start(bf16[256,256]{1,0:T(8,128)(2,1)S(1)} %get-tuple-element.74), channel_id=1, source_target_pairs={{0,12},{4,8},{8,4},{12,0},{16,28},{20,24},{24,20},{28,16},{1,13},{... | collective-permute-start | bytes 393224 | tf_op jit(solution)/shard_map/ppermute | solution.py:409
  49.8 8.5 %collective-permute-start.11 = (bf16[288,256]{1,0:T(8,128)(2,1)S(1)}, bf16[288,256]{1,0:T(8,128)(2,1)S(1)}, u32[]{:S(2)}, u32[]{:S(2)}) collective-permute-start(bf16[288,256]{1,0:T(8,128)(2,1)S(1)} %get-tuple-element.62), channel_id=1, source_target_pairs={{0,4},{4,0},{8,12},{12,8},{16,20},{20,16},{24,28},{28,24},{1,5},{5... | collective-permute-start | bytes 442376 | tf_op jit(solution)/shard_map/ppermute | solution.py:409
  50.6 8.9 %collective-permute-start.12 = (bf16[288,256]{1,0:T(8,128)(2,1)S(1)}, bf16[288,256]{1,0:T(8,128)(2,1)S(1)}, u32[]{:S(2)}, u32[]{:S(2)}) collective-permute-start(bf16[288,256]{1,0:T(8,128)(2,1)S(1)} %get-tuple-element.63), channel_id=1, source_target_pairs={{0,8},{4,12},{8,0},{12,4},{16,24},{20,28},{24,16},{28,20},{1,9},{5... | collective-permute-start | bytes 442376 | tf_op jit(solution)/shard_map/ppermute | solution.py:409
  52.2 10.2 %collective-permute-start.13 = (bf16[288,256]{1,0:T(8,128)(2,1)S(1)}, bf16[288,256]{1,0:T(8,128)(2,1)S(1)}, u32[]{:S(2)}, u32[]{:S(2)}) collective-permute-start(bf16[288,256]{1,0:T(8,128)(2,1)S(1)} %get-tuple-element.64), channel_id=1, source_target_pairs={{0,12},{4,8},{8,4},{12,0},{16,28},{20,24},{24,20},{28,16},{1,13},{... | collective-permute-start | bytes 442376 | tf_op jit(solution)/shard_map/ppermute | solution.py:409
  58.3 5.5 %collective-permute-start.21 = (bf16[2,2,256,128]{3,2,1,0:T(8,128)(2,1)S(1)}, bf16[2,2,256,128]{3,2,1,0:T(8,128)(2,1)S(1)}, u32[]{:S(2)}, u32[]{:S(2)}) collective-permute-start(bf16[2,2,256,128]{3,2,1,0:T(8,128)(2,1)S(1)} %get-tuple-element.76), channel_id=1, source_target_pairs={{0,1},{1,0},{2,3},{3,2},{4,5},{5,4},{6,7},{7,6},{8,9},{9,8},{10,11... | collective-permute-start | bytes 786440 | tf_op jit(solution)/shard_map/ppermute | solution.py:409
  63.7 1.7 %collective-permute-start.14 = (bf16[2,2,304,128]{3,2,1,0:T(8,128)(2,1)S(1)}, bf16[2,2,304,128]{3,2,1,0:T(8,128)(2,1)S(1)}, u32[]{:S(2)}, u32[]{:S(2)}) collective-permute-start(bf16[2,2,304,128]{3,2,1,0:T(8,128)(2,1)S(1)} %get-tuple-element.66), channel_id=1, source_target_pairs={{0,1},{1,0},{2,3},{3,2},{4,5},{5,4},{6,7},{7,6},{8,9},{9,8},{10,11... | collective-permute-start | bytes 933896 | tf_op jit(solution)/shard_map/ppermute | solution.py:409
  63.9 6.0 %collective-permute-start.22 = (bf16[1,2,256,128]{3,2,1,0:T(8,128)(2,1)S(1)}, bf16[1,2,256,128]{3,2,1,0:T(8,128)(2,1)S(1)}, u32[]{:S(2)}, u32[]{:S(2)}) collective-permute-start(bf16[1,2,256,128]{3,2,1,0:T(8,128)(2,1)S(1)} %get-tuple-element.78), channel_id=1, source_target_pairs={{0,2},{1,3},{2,0},{3,1},{4,6},{5,7},{6,4},{7,5},{8,10},{9,11},{10,... | collective-permute-start | bytes 393224 | tf_op jit(solution)/shard_map/ppermute | solution.py:414
  65.4 7.5 %collective-permute-start.15 = (bf16[1,1,304,128]{3,2,1,0:T(8,128)(2,1)S(1)}, bf16[1,1,304,128]{3,2,1,0:T(8,128)(2,1)S(1)}, u32[]{:S(2)}, u32[]{:S(2)}) collective-permute-start(bf16[1,1,304,128]{3,2,1,0:T(8,128)(2,1)S(1)} %get-tuple-element.68), channel_id=1, source_target_pairs={{0,16},{1,17},{2,18},{3,19},{4,20},{5,21},{6,22},{7,23},{8,24},{9,... | collective-permute-start | bytes 233480 | tf_op jit(solution)/shard_map/ppermute | solution.py:414
  68.1 4.8 %collective-permute-start.16 = (bf16[1,1,304,128]{3,2,1,0:T(8,128)(2,1)S(1)}, bf16[1,1,304,128]{3,2,1,0:T(8,128)(2,1)S(1)}, u32[]{:S(2)}, u32[]{:S(2)}) collective-permute-start(bf16[1,1,304,128]{3,2,1,0:T(8,128)(2,1)S(1)} %get-tuple-element.69), channel_id=1, source_target_pairs={{0,2},{1,3},{2,0},{3,1},{4,6},{5,7},{6,4},{7,5},{8,10},{9,11},{10,... | collective-permute-start | bytes 233480 | tf_op jit(solution)/shard_map/ppermute | solution.py:414
  69.4 8.6 %collective-permute-start.17 = (bf16[1,1,304,128]{3,2,1,0:T(8,128)(2,1)S(1)}, bf16[1,1,304,128]{3,2,1,0:T(8,128)(2,1)S(1)}, u32[]{:S(2)}, u32[]{:S(2)}) collective-permute-start(bf16[1,1,304,128]{3,2,1,0:T(8,128)(2,1)S(1)} %get-tuple-element.70), channel_id=1, source_target_pairs={{0,18},{1,19},{2,16},{3,17},{4,22},{5,23},{6,20},{7,21},{8,26},{9,... | collective-permute-start | bytes 233480 | tf_op jit(solution)/shard_map/ppermute | solution.py:414
  69.9 8.7 %collective-permute-start.23 = (bf16[1,1,256,128]{3,2,1,0:T(8,128)(2,1)S(1)}, bf16[1,1,256,128]{3,2,1,0:T(8,128)(2,1)S(1)}, u32[]{:S(2)}, u32[]{:S(2)}) collective-permute-start(bf16[1,1,256,128]{3,2,1,0:T(8,128)(2,1)S(1)} %get-tuple-element.80), channel_id=1, source_target_pairs={{0,16},{1,17},{2,18},{3,19},{4,20},{5,21},{6,22},{7,23},{8,24},{9,... | collective-permute-start | bytes 196616 | tf_op jit(solution)/shard_map/ppermute | solution.py:414
  (5 other events, 84.6 us)

commit v11 on v10

--- a/solution.py
+++ b/solution.py
@@ -43,11 +43,12 @@
 SM = pl.BlockSpec(memory_space=pltpu.SMEM)
 
 
-def attend_body(info_ref, q_ref, k_ref, v_ref, o_ref):
+def attend_body(len_ref, me_ref, q_ref, k_ref, v_ref, *out_refs):
     seq = q_ref.shape[0]
+    o_ref = out_refs[-1]
     rows = o_ref.shape[2]
     rate = math.log2(math.e) / math.sqrt(HD)
-    length = info_ref[2]
+    length = len_ref[0]
     key = lax.broadcasted_iota(jnp.int32, (seq, 1), 0)
     hide = jnp.where(key < length, 0.0, neg_large)
     r = lax.broadcasted_iota(jnp.int32, (QB, QB), 0)
@@ -67,26 +68,29 @@
             for n in range(0, QB, min(rows, QB)):
                 block, first = divmod(i * QB + n, rows)
                 o_ref[block, at, first : first + min(rows, QB)] = out[:, n : n + rows]
-
-
-def attend(info, q, k, v, rows):
+    for m, ref in enumerate(out_refs[:-1]):
+        ref[...] = o_ref[me_ref[0] ^ m]
+
+
+def attend(lengths, me, q, k, v, rows, split):
     seq, width = q.shape
     heads = width // HD
-    block = VM
+    blocks = seq // rows
     return pl.pallas_call(
         attend_body,
-                in_specs=[SM, block, block, block],
-        out_specs=VM,
-        out_shape=shape((seq // rows, width, rows)),
+        in_specs=[SM, SM, VM, VM, VM],
+        out_specs=[VM] * (blocks if split else 1),
+        out_shape=[shape((width, rows))] * blocks if split else [shape((blocks, width, rows))],
+        scratch_shapes=[pltpu.VMEM((blocks, width, rows), BF)] if split else [],
         compiler_params=pltpu.CompilerParams(vmem_limit_bytes=60 * MIB),
         cost_estimate=pl.CostEstimate(
             flops=4 * seq * seq * width, bytes_accessed=8 * seq * width, transcendentals=heads * seq * seq
         ),
         name="attend",
-    )(info, q, k, v)
-
-
-def mix_body(n_tensor, counts, info_ref, ctx_ref, *refs):
+    )(lengths, me, q, k, v)
+
+
+def mix_body(n_tensor, counts, split, info_ref, ctx_ref, *refs):
     w_refs, at = [], 0
     for n in counts:
         w_refs.append(refs[at : at + n])
@@ -95,7 +99,7 @@
     dout = part_ref.shape[1]
     me, side = info_ref[0], info_ref[1] % 2
     for m in range(n_tensor):
-        turned_ref[m] = ctx_ref[me ^ m].T
+        turned_ref[m] = ctx_ref[m if split else me ^ m].T
     columns = [(c, 0, c) for c in range(0, dout, COLS)]
     if max(counts) > 1:
         cut = w_refs[-1][0].shape[1]
@@ -119,12 +123,12 @@
             square_ref[...] = lanes if step == 0 else square_ref[...] + lanes
 
 
-def mix(info, ctx, weights):
+def mix(info, ctx, weights, split):
     n_tensor, width, rows = ctx.shape
     dout = weights[0][0].shape[1]
     counts = [len(w) for w in weights]
     return pl.pallas_call(
-        functools.partial(mix_body, n_tensor, counts),
+        functools.partial(mix_body, n_tensor, counts, split),
         in_specs=[SM] + [VM] * (1 + sum(counts)),
         out_specs=[VM] * 3,
         out_shape=[shape((rows, dout), F32), shape((rows, 128), F32), shape((n_tensor, rows, width))],
@@ -288,7 +292,7 @@
     feats, rows = ctx_refs[0][0].shape[1:]
     wide = n_far * cw
     me = info_ref[0]
-    core, y = me % 2, me // 2
+    core = me % 2
     if tall > feats:
         in_piece, in_block, stat_rows = stat_sizes(dout, wide, cw)
         sums = sum(ref[rows:, :].astype(F32) for ref in g_refs)
@@ -297,7 +301,7 @@
         words = block_words(gains, scalars[:, :cw], stat_rows, cw)
     for s, ref in ((1, send_ref), (0, keep_ref)):
         for a in range(n_y):
-            m = (y ^ a if xor_far else a) * 2 + (core ^ s)
+            m = a * 2 + (s if xor_far else core ^ s)
             total = None
             for parts, g in zip(ctx_refs, g_refs):
                 c = jnp.concatenate([part[m] for part in parts], 0) if len(parts) > 1 else parts[0][m]
@@ -440,14 +444,14 @@
 
 
 def gather_large(n_dp, n_tensor, _, info, weight, context):
-    ctx = lax.all_to_all(context, "tensor", 0, 0, tiled=True)
+    ctx = lax.all_to_all(context[0], "tensor", 0, 0, tiled=True)
     held = {0: weight}
     bit = n_tensor // 2
     while bit:
         held.update({m | bit: swap(w, "tensor", n_tensor, bit) for m, w in list(held.items())})
         bit //= 2
     ctxs = [[ctx]] + [[swap(ctx, "dp", n_dp, q)] for q in range(1, NEAR)]
-    return ctxs, mix(info, ctx, [[held[m]] for m in range(n_tensor)]), []
+    return ctxs, mix(info, ctx, [[held[m]] for m in range(n_tensor)], False), []
 
 
 def gather_small(n_dp, n_tensor, side, info, weight, context):
@@ -464,13 +468,13 @@
     mine = tensor(lax.dynamic_slice_in_dim(weight, side * cut, cut, 1), 2)
     beside = tensor(weight, 1)
     rest = weight[:, 2 * cut :]
-    mine, context = barrier((mine, context))
+    mine, beside, context = barrier((mine, beside, context))
+    ctx = jnp.stack([context[0]] + [tensor(context[m], m) for m in range(1, n_tensor)])
     other, mine_beside = dp(mine, 1), tensor(mine, 1)
-    ctx = lax.all_to_all(context, "tensor", 0, 0, tiled=True)
-    rest, other, mine_beside, beside, ctx = barrier((rest, other, mine_beside, beside, ctx))
+    rest, other, mine_beside, ctx = barrier((rest, other, mine_beside, ctx))
     rest, other_beside = tensor(rest, 2), tensor(other, 1)
     ctx_x, ctx_z = dp(ctx, 1), dp(ctx, 2)
-    early = mix(info, ctx, [[weight], [beside], [mine, other], [mine_beside, other_beside]])
+    early = mix(info, ctx, [[weight], [beside], [mine, other], [mine_beside, other_beside]], True)
     rest, early, ctx_x, ctx_z = barrier((rest, early, ctx_x, ctx_z))
     half = ctx.shape[1] // 2
     ctxs = [[ctx], [ctx_x], [ctx_z], [dp(ctx_x[:, :half], 2), dp(ctx_z[:, half:], 1)]]
@@ -500,7 +504,7 @@
     group = lax.axis_index("dp").astype(jnp.int32)
     info = jnp.stack([me, group, lengths[0], vote_counts[0]])
 
-    attended = attend(info, query_states[0], key_states[0], value_states[0], rows)
+    attended = attend(lengths, me.reshape(1), query_states[0], key_states[0], value_states[0], rows, xor_far)
     gather = gather_small if xor_far else gather_large
     ctxs, early, late = gather(n_dp, n_tensor, group & 1, info, joining_weight[0], attended)
     hidden, grads = join(plan, info, early, norm_gain[None, :], next_hidden, late)

time: 79.7 us -> 78.3 us (0.982)
  starting transfers between devices: 30.7 us -> 27.6 us
  waiting for transfers between devices: 29.6 us -> 32.4 us
  local copies, waits for them, and re-layouts: 1.85 us -> 1.05 us
  Pallas kernels: 14.7 us -> 13.9 us
    all_to_all x1 -> x0, starting transfers between devices: 3.47 us -> none  [gather_small(): ctx = lax.all_to_all(context, 'tensor', 0, 0, tiled=True)]
    ppermute x19 -> x22, waiting for transfers between devices: 23.7 us -> 26.5 us  [swap(): return lax.ppermute(x, axis, [(i, i ^ mask) for i in range(n)])]
    ppermute x19 -> x22, starting transfers between devices: 18.5 us -> 19.6 us  [swap(): return lax.ppermute(x, axis, [(i, i ^ mask) for i in range(n)])]
    another operation x0 -> x1, other arithmetic: none -> 0.97 us  [gather_small(): jnp.stack([context[0]] + [tensor(context[m], m) for m in range(1, n_tenso...]
  transfers between devices with their start and end apart: 25 -> 27, of which waited for: 14 -> 16; matrix products, arithmetic and copies ran while one was open for 3% -> 3% of each run, Pallas kernels for 17% -> 17%
where the time goes in v11:
time: 78.3 us; the launch traced here: 78.1 us
  waiting for transfers between devices  32.4 us (41%)
  starting transfers between devices  27.6 us (35%)
  Pallas kernels  13.9 us (18%)
  between operations  2.07 us (3%)
  local copies, waits for them, and re-layouts  1.05 us (1%)
  other arithmetic  1.05 us (1%)
    ppermute x22, waiting for transfers between devices, swap(): return lax.ppermute(x, axis, [(i, i ^ mask) for i in range(n)])  26.5 us
    ppermute x22, starting transfers between devices, swap(): return lax.ppermute(x, axis, [(i, i ^ mask) for i in range(n)])  19.6 us
    ppermute x5, starting transfers between devices, swap_far(): lax.ppermute(x, ('dp', 'tensor'), [(i, i ^ mask) for i in range(n_dp * n_...  8 us
    ppermute x5, waiting for transfers between devices, swap_far(): lax.ppermute(x, ('dp', 'tensor'), [(i, i ^ mask) for i in range(n_dp * n_...  5.86 us
    pallas_call x1, Pallas kernels, attend(): pl.pallas_call(attend_body, in_specs=[SM, SM, VM, VM, VM], out_specs=[VM]...  4.82 us
    pallas_call x1, Pallas kernels, join(): pl.pallas_call(functools.partial(join_body, plan, len(late)), in_specs=[S...  4.05 us
    pallas_call x2, Pallas kernels, gradient(): pl.pallas_call(functools.partial(grad_body, plan, dout, [len(c) for c in...  2.5 us
  transfers between devices with their start and end apart: 27, of which 16 were waited for; matrix products, arithmetic and copies ran while one was open for 3% of the time, Pallas kernels for 17%

profile of v11, /device:TPU:0, one launch (start us, length us, event | category | flops | bytes accessed | tf_op | source)
XLA Modules:
  0.0 78.1 jit_solution(12617329325301979847)
XLA Ops:
  2.1 2.6 %collective-permute-start = (bf16[256,512]{1,0:T(8,128)(2,1)S(1)}, bf16[256,512]{1,0:T(8,128)(2,1)S(1)}, u32[]{:S(2)}, u32[]{:S(2)}) collective-permute-start(bf16[256,512]{1,0:T(8,128)(2,1)S(1)} %dynamic-slice_bitcast_fusion), channel_id=1, source_target_pairs={{0,2},{1,3},{2,0},{3,1},{4,6},{5,7},{6,4},{7,5},{8,10},{9,11},{10,... | collective-permute-start | bytes 786440 | tf_op jit(solution)/shard_map/ppermute | solution.py:413
  5.4 4.8 %attend.1 = (bf16[256,256]{1,0:T(8,128)(2,1)}, bf16[256,256]{1,0:T(8,128)(2,1)}, bf16[256,256]{1,0:T(8,128)(2,1)}, bf16[256,256]{1,0:T(8,128)(2,1)}) custom-call(s32[1]{0:T(128)S(6)} %copy.12.len_ref, s32[1]{0:T(128)} %bitcast.me_ref, bf16[1024,256]{1,0:T(8,128)(2,1)} %bitcast.24, bf16[1024,256]{1,0:T(8,128)(2,1)} %bitcast.25, bf16[1024,256]{1,0:T(8,128)(2,1)} %bitcast.26), custom_call_target="tpu_custom_call" | custom-call | flops 1073741824 | bytes 2097152 | tf_op jit(solution)/shard_map/attend/pallas_call | solution.py:79
  10.2 1.5 %collective-permute-done.refs_2_ = bf16[256,512]{1,0:T(8,128)(2,1)S(1)} collective-permute-done((bf16[256,512]{1,0:T(8,128)(2,1)S(1)}, bf16[256,512]{1,0:T(8,128)(2,1)S(1)}, u32[]{:S(2)}, u32[]{:S(2)}) %collective-permute-start) | collective-permute-done | bytes 262176 | tf_op jit(solution)/shard_map/ppermute | solution.py:413
  11.7 1.7 %collective-permute-start.2 = (bf16[256,512]{1,0:T(8,128)(2,1)S(1)}, bf16[256,512]{1,0:T(8,128)(2,1)S(1)}, u32[]{:S(2)}, u32[]{:S(2)}) collective-permute-start(bf16[256,512]{1,0:T(8,128)(2,1)S(1)} %collective-permute-done.refs_2_), channel_id=1, source_target_pairs={{0,4},{4,0},{8,12},{12,8},{16,20},{20,16},{24,28},{28,24},{1,5},{5... | collective-permute-start | bytes 786440 | tf_op jit(solution)/shard_map/ppermute | solution.py:413
  13.4 1.6 %collective-permute-start.6 = (bf16[256,256]{1,0:T(8,128)(2,1)}, bf16[256,256]{1,0:T(8,128)(2,1)S(1)}, u32[]{:S(2)}, u32[]{:S(2)}) collective-permute-start(bf16[256,256]{1,0:T(8,128)(2,1)} %get-tuple-element.59), channel_id=1, source_target_pairs={{0,3},{1,2},{2,1},{3,0},{4,7},{5,6},{6,5},{7,4},{8,11},{9,10},{10,... | collective-permute-start | bytes 393224 | tf_op jit(solution)/shard_map/ppermute | solution.py:413
  15.6 3.6 %collective-permute-done.6 = bf16[256,256]{1,0:T(8,128)(2,1)S(1)} collective-permute-done((bf16[256,256]{1,0:T(8,128)(2,1)}, bf16[256,256]{1,0:T(8,128)(2,1)S(1)}, u32[]{:S(2)}, u32[]{:S(2)}) %collective-permute-start.6) | collective-permute-done | bytes 131104 | tf_op jit(solution)/shard_map/ppermute | solution.py:413
  19.2 3.0 %collective-permute-done.5 = bf16[256,256]{1,0:T(8,128)(2,1)S(1)} collective-permute-done((bf16[256,256]{1,0:T(8,128)(2,1)}, bf16[256,256]{1,0:T(8,128)(2,1)S(1)}, u32[]{:S(2)}, u32[]{:S(2)}) %collective-permute-start.5) | collective-permute-done | bytes 131104 | tf_op jit(solution)/shard_map/ppermute | solution.py:413
  23.2 1.6 %collective-permute-start.10 = (bf16[4,256,256]{2,1,0:T(8,128)(2,1)S(1)}, bf16[4,256,256]{2,1,0:T(8,128)(2,1)S(1)}, u32[]{:S(2)}, u32[]{:S(2)}) collective-permute-start(bf16[4,256,256]{2,1,0:T(8,128)(2,1)S(1)} %pad_maximum_fusion.ctx_ref.refs_0_), channel_id=1, source_target_pairs={{0,8},{4,12},{8,0},{12,4},{16,24},{20,28},{24,16},{28,20},{1,9},{5... | collective-permute-start | bytes 1572872 | tf_op jit(solution)/shard_map/ppermute | solution.py:413
  24.9 1.5 %collective-permute-start.7 = (bf16[256,1024]{1,0:T(8,128)(2,1)S(1)}, bf16[256,1024]{1,0:T(8,128)(2,1)S(1)}, u32[]{:S(2)}, u32[]{:S(2)}) collective-permute-start(bf16[256,1024]{1,0:T(8,128)(2,1)S(1)} %slice.12), channel_id=1, source_target_pairs={{0,2},{1,3},{2,0},{3,1},{4,6},{5,7},{6,4},{7,5},{8,10},{9,11},{10,... | collective-permute-start | bytes 1572872 | tf_op jit(solution)/shard_map/ppermute | solution.py:413
  28.5 1.6 %mix.1 = (f32[256,2048]{1,0:T(8,128)S(1)}, f32[256,128]{1,0:T(8,128)S(1)}, bf16[4,256,256]{2,1,0:T(8,128)(2,1)S(1)}) custom-call(s32[4]{0:T(128)S(1)} %pad_add_fusion.info_ref, bf16[4,256,256]{2,1,0:T(8,128)(2,1)S(1)} %pad_maximum_fusion.ctx_ref.refs_0_, bf16[256,2048]{1,0:T(8,128)(2,1)S(1)} %bitcast.18, ...), custom_call_target="tpu_custom_call" | custom-call | flops 1073741824 | bytes 6291456 | tf_op jit(solution)/shard_map/mix/pallas_call | solution.py:130
  30.0 6.6 %collective-permute-done.10.refs_2_ = bf16[4,256,256]{2,1,0:T(8,128)(2,1)S(1)} collective-permute-done((bf16[4,256,256]{2,1,0:T(8,128)(2,1)S(1)}, bf16[4,256,256]{2,1,0:T(8,128)(2,1)S(1)}, u32[]{:S(2)}, u32[]{:S(2)}) %collective-permute-start.10) | collective-permute-done | bytes 524320 | tf_op jit(solution)/shard_map/ppermute | solution.py:413
  36.6 1.3 %collective-permute-done.7.refs_0_ = bf16[256,1024]{1,0:T(8,128)(2,1)S(1)} collective-permute-done((bf16[256,1024]{1,0:T(8,128)(2,1)S(1)}, bf16[256,1024]{1,0:T(8,128)(2,1)S(1)}, u32[]{:S(2)}, u32[]{:S(2)}) %collective-permute-start.7) | collective-permute-done | bytes 524320 | tf_op jit(solution)/shard_map/ppermute | solution.py:413
  41.0 4.0 %join.1 = (bf16[256,2048]{1,0:T(8,128)(2,1)}, bf16[288,256]{1,0:T(8,128)(2,1)S(1)}, bf16[288,256]{1,0:T(8,128)(2,1)S(1)}, bf16[288,256]{1,0:T(8,128)(2,1)S(1)}, ...) custom-call(s32[4]{0:T(128)S(1)} %pad_add_fusion.info_ref, ...), custom_call_target="tpu_custom_call" | custom-call | flops 134217728 | bytes 6291456 | tf_op jit(solution)/shard_map/join/pallas_call | solution.py:243
  45.8 1.6 %collective-permute-start.22 = (bf16[256,256]{1,0:T(8,128)(2,1)S(1)}, bf16[256,256]{1,0:T(8,128)(2,1)S(1)}, u32[]{:S(2)}, u32[]{:S(2)}) collective-permute-start(bf16[256,256]{1,0:T(8,128)(2,1)S(1)} %get-tuple-element.87), channel_id=1, source_target_pairs={{0,8},{4,12},{8,0},{12,4},{16,24},{20,28},{24,16},{28,20},{1,9},{5... | collective-permute-start | bytes 393224 | tf_op jit(solution)/shard_map/ppermute | solution.py:413
  49.3 1.6 %collective-permute-start.15 = (bf16[288,256]{1,0:T(8,128)(2,1)S(1)}, bf16[288,256]{1,0:T(8,128)(2,1)S(1)}, u32[]{:S(2)}, u32[]{:S(2)}) collective-permute-start(bf16[288,256]{1,0:T(8,128)(2,1)S(1)} %get-tuple-element.77), channel_id=1, source_target_pairs={{0,8},{4,12},{8,0},{12,4},{16,24},{20,28},{24,16},{28,20},{1,9},{5... | collective-permute-start | bytes 442376 | tf_op jit(solution)/shard_map/ppermute | solution.py:413
  50.9 1.3 %collective-permute-done.21.refs_6_ = bf16[256,256]{1,0:T(8,128)(2,1)S(1)} collective-permute-done((bf16[256,256]{1,0:T(8,128)(2,1)S(1)}, bf16[256,256]{1,0:T(8,128)(2,1)S(1)}, u32[]{:S(2)}, u32[]{:S(2)}) %collective-permute-start.21) | collective-permute-done | bytes 131104 | tf_op jit(solution)/shard_map/ppermute | solution.py:413
  52.2 1.9 %collective-permute-start.16 = (bf16[288,256]{1,0:T(8,128)(2,1)S(1)}, bf16[288,256]{1,0:T(8,128)(2,1)S(1)}, u32[]{:S(2)}, u32[]{:S(2)}) collective-permute-start(bf16[288,256]{1,0:T(8,128)(2,1)S(1)} %get-tuple-element.78), channel_id=1, source_target_pairs={{0,12},{4,8},{8,4},{12,0},{16,28},{20,24},{24,20},{28,16},{1,13},{... | collective-permute-start | bytes 442376 | tf_op jit(solution)/shard_map/ppermute | solution.py:413
  54.0 1.7 %collective-permute-done.23.refs_8_ = bf16[256,256]{1,0:T(8,128)(2,1)S(1)} collective-permute-done((bf16[256,256]{1,0:T(8,128)(2,1)S(1)}, bf16[256,256]{1,0:T(8,128)(2,1)S(1)}, u32[]{:S(2)}, u32[]{:S(2)}) %collective-permute-start.23) | collective-permute-done | bytes 131104 | tf_op jit(solution)/shard_map/ppermute | solution.py:413
  55.7 1.2 %gradient.3 = (bf16[2,2,256,128]{3,2,1,0:T(8,128)(2,1)S(1)}, bf16[2,2,256,128]{3,2,1,0:T(8,128)(2,1)S(1)}) custom-call(s32[4]{0:T(128)S(1)} %pad_add_fusion.info_ref, bf16[4,256,256]{2,1,0:T(8,128)(2,1)S(1)} %pad_maximum_fusion.ctx_ref.refs_0_, bf16[4,256,256]{2,1,0:T(8,128)(2,1)S(1)} %collective-permute-done.9.refs_1_, ...), custom_call_target="tpu_custom_call" | custom-call | flops 536870912 | bytes 3145728 | tf_op jit(solution)/shard_map/gradient/pallas_call | solution.py:326
  58.2 2.7 %collective-permute-done.16.refs_8_ = bf16[288,256]{1,0:T(8,128)(2,1)S(1)} collective-permute-done((bf16[288,256]{1,0:T(8,128)(2,1)S(1)}, bf16[288,256]{1,0:T(8,128)(2,1)S(1)}, u32[]{:S(2)}, u32[]{:S(2)}) %collective-permute-start.16) | collective-permute-done | bytes 147488 | tf_op jit(solution)/shard_map/ppermute | solution.py:413
  60.9 1.2 %gradient.2 = (bf16[2,2,304,128]{3,2,1,0:T(8,128)(2,1)S(1)}, bf16[2,2,304,128]{3,2,1,0:T(8,128)(2,1)S(1)}) custom-call(s32[4]{0:T(128)S(1)} %pad_add_fusion.info_ref, bf16[4,256,256]{2,1,0:T(8,128)(2,1)S(1)} %pad_maximum_fusion.ctx_ref.refs_0_, bf16[4,256,256]{2,1,0:T(8,128)(2,1)S(1)} %collective-permute-done.9.refs_1_, ...), custom_call_target="tpu_custom_call" | custom-call | flops 536870912 | bytes 3145728 | tf_op jit(solution)/shard_map/gradient/pallas_call | solution.py:326
  63.9 2.7 %collective-permute-start.18 = (bf16[1,1,304,128]{3,2,1,0:T(8,128)(2,1)S(1)}, bf16[1,1,304,128]{3,2,1,0:T(8,128)(2,1)S(1)}, u32[]{:S(2)}, u32[]{:S(2)}) collective-permute-start(bf16[1,1,304,128]{3,2,1,0:T(8,128)(2,1)S(1)} %get-tuple-element.82), channel_id=1, source_target_pairs={{0,16},{1,17},{2,18},{3,19},{4,20},{5,21},{6,22},{7,23},{8,24},{9,... | collective-permute-start | bytes 233480 | tf_op jit(solution)/shard_map/ppermute | solution.py:418
  68.4 3.0 %collective-permute-start.26 = (bf16[1,1,256,128]{3,2,1,0:T(8,128)(2,1)S(1)}, bf16[1,1,256,128]{3,2,1,0:T(8,128)(2,1)S(1)}, u32[]{:S(2)}, u32[]{:S(2)}) collective-permute-start(bf16[1,1,256,128]{3,2,1,0:T(8,128)(2,1)S(1)} %get-tuple-element.94), channel_id=1, source_target_pairs={{0,16},{1,17},{2,18},{3,19},{4,20},{5,21},{6,22},{7,23},{8,24},{9,... | collective-permute-start | bytes 196616 | tf_op jit(solution)/shard_map/ppermute | solution.py:418
  71.4 4.8 %collective-permute-done.20.refs_3_ = bf16[1,1,304,128]{3,2,1,0:T(8,128)(2,1)S(1)} collective-permute-done((bf16[1,1,304,128]{3,2,1,0:T(8,128)(2,1)S(1)}, bf16[1,1,304,128]{3,2,1,0:T(8,128)(2,1)S(1)}, u32[]{:S(2)}, u32[]{:S(2)}) %collective-permute-start.20) | collective-permute-done | bytes 77856 | tf_op jit(solution)/shard_map/ppermute | solution.py:418
  (51 shorter events, 16.8 us)
Async XLA Ops:
  0.6 11.1 %collective-permute-start.1 = (bf16[256,2048]{1,0:T(8,128)(2,1)}, bf16[256,2048]{1,0:T(8,128)(2,1)S(1)}, u32[]{:S(2)}, u32[]{:S(2)}) collective-permute-start(bf16[256,2048]{1,0:T(8,128)(2,1)} %bitcast.16), channel_id=1, source_target_pairs={{0,1},{1,0},{2,3},{3,2},{4,5},{5,4},{6,7},{7,6},{8,9},{9,8},{10,11... | collective-permute-start | bytes 3145736 | tf_op jit(solution)/shard_map/ppermute | solution.py:413
  2.1 9.6 %collective-permute-start = (bf16[256,512]{1,0:T(8,128)(2,1)S(1)}, bf16[256,512]{1,0:T(8,128)(2,1)S(1)}, u32[]{:S(2)}, u32[]{:S(2)}) collective-permute-start(bf16[256,512]{1,0:T(8,128)(2,1)S(1)} %dynamic-slice_bitcast_fusion), channel_id=1, source_target_pairs={{0,2},{1,3},{2,0},{3,1},{4,6},{5,7},{6,4},{7,5},{8,10},{9,11},{10,... | collective-permute-start | bytes 786440 | tf_op jit(solution)/shard_map/ppermute | solution.py:413
  11.7 11.5 %collective-permute-start.2 = (bf16[256,512]{1,0:T(8,128)(2,1)S(1)}, bf16[256,512]{1,0:T(8,128)(2,1)S(1)}, u32[]{:S(2)}, u32[]{:S(2)}) collective-permute-start(bf16[256,512]{1,0:T(8,128)(2,1)S(1)} %collective-permute-done.refs_2_), channel_id=1, source_target_pairs={{0,4},{4,0},{8,12},{12,8},{16,20},{20,16},{24,28},{28,24},{1,5},{5... | collective-permute-start | bytes 786440 | tf_op jit(solution)/shard_map/ppermute | solution.py:413
  13.4 9.8 %collective-permute-start.3 = (bf16[256,512]{1,0:T(8,128)(2,1)S(1)}, bf16[256,512]{1,0:T(8,128)(2,1)S(1)}, u32[]{:S(2)}, u32[]{:S(2)}) collective-permute-start(bf16[256,512]{1,0:T(8,128)(2,1)S(1)} %collective-permute-done.refs_2_), channel_id=1, source_target_pairs={{0,1},{1,0},{2,3},{3,2},{4,5},{5,4},{6,7},{7,6},{8,9},{9,8},{10,11... | collective-permute-start | bytes 786440 | tf_op jit(solution)/shard_map/ppermute | solution.py:413
  13.4 5.8 %collective-permute-start.6 = (bf16[256,256]{1,0:T(8,128)(2,1)}, bf16[256,256]{1,0:T(8,128)(2,1)S(1)}, u32[]{:S(2)}, u32[]{:S(2)}) collective-permute-start(bf16[256,256]{1,0:T(8,128)(2,1)} %get-tuple-element.59), channel_id=1, source_target_pairs={{0,3},{1,2},{2,1},{3,0},{4,7},{5,6},{6,5},{7,4},{8,11},{9,10},{10,... | collective-permute-start | bytes 393224 | tf_op jit(solution)/shard_map/ppermute | solution.py:413
  15.0 4.2 %collective-permute-start.4 = (bf16[256,256]{1,0:T(8,128)(2,1)}, bf16[256,256]{1,0:T(8,128)(2,1)S(1)}, u32[]{:S(2)}, u32[]{:S(2)}) collective-permute-start(bf16[256,256]{1,0:T(8,128)(2,1)} %get-tuple-element.57), channel_id=1, source_target_pairs={{0,1},{1,0},{2,3},{3,2},{4,5},{5,4},{6,7},{7,6},{8,9},{9,8},{10,11... | collective-permute-start | bytes 393224 | tf_op jit(solution)/shard_map/ppermute | solution.py:413
  15.0 7.2 %collective-permute-start.5 = (bf16[256,256]{1,0:T(8,128)(2,1)}, bf16[256,256]{1,0:T(8,128)(2,1)S(1)}, u32[]{:S(2)}, u32[]{:S(2)}) collective-permute-start(bf16[256,256]{1,0:T(8,128)(2,1)} %get-tuple-element.58), channel_id=1, source_target_pairs={{0,2},{1,3},{2,0},{3,1},{4,6},{5,7},{6,4},{7,5},{8,10},{9,11},{10,... | collective-permute-start | bytes 393224 | tf_op jit(solution)/shard_map/ppermute | solution.py:413
  23.2 13.4 %collective-permute-start.10 = (bf16[4,256,256]{2,1,0:T(8,128)(2,1)S(1)}, bf16[4,256,256]{2,1,0:T(8,128)(2,1)S(1)}, u32[]{:S(2)}, u32[]{:S(2)}) collective-permute-start(bf16[4,256,256]{2,1,0:T(8,128)(2,1)S(1)} %pad_maximum_fusion.ctx_ref.refs_0_), channel_id=1, source_target_pairs={{0,8},{4,12},{8,0},{12,4},{16,24},{20,28},{24,16},{28,20},{1,9},{5... | collective-permute-start | bytes 1572872 | tf_op jit(solution)/shard_map/ppermute | solution.py:413
  24.9 13.0 %collective-permute-start.7 = (bf16[256,1024]{1,0:T(8,128)(2,1)S(1)}, bf16[256,1024]{1,0:T(8,128)(2,1)S(1)}, u32[]{:S(2)}, u32[]{:S(2)}) collective-permute-start(bf16[256,1024]{1,0:T(8,128)(2,1)S(1)} %slice.12), channel_id=1, source_target_pairs={{0,2},{1,3},{2,0},{3,1},{4,6},{5,7},{6,4},{7,5},{8,10},{9,11},{10,... | collective-permute-start | bytes 1572872 | tf_op jit(solution)/shard_map/ppermute | solution.py:413
  26.4 12.7 %collective-permute-start.9 = (bf16[4,256,256]{2,1,0:T(8,128)(2,1)S(1)}, bf16[4,256,256]{2,1,0:T(8,128)(2,1)S(1)}, u32[]{:S(2)}, u32[]{:S(2)}) collective-permute-start(bf16[4,256,256]{2,1,0:T(8,128)(2,1)S(1)} %pad_maximum_fusion.ctx_ref.refs_0_), channel_id=1, source_target_pairs={{0,4},{4,0},{8,12},{12,8},{16,20},{20,16},{24,28},{28,24},{1,5},{5... | collective-permute-start | bytes 1572872 | tf_op jit(solution)/shard_map/ppermute | solution.py:413
  39.1 9.4 %collective-permute-start.12 = (bf16[4,128,256]{2,1,0:T(8,128)(2,1)S(1)}, bf16[4,128,256]{2,1,0:T(8,128)(2,1)S(1)}, u32[]{:S(2)}, u32[]{:S(2)}) collective-permute-start(bf16[4,128,256]{2,1,0:T(8,128)(2,1)S(1)} %slice.10), channel_id=1, source_target_pairs={{0,8},{4,12},{8,0},{12,4},{16,24},{20,28},{24,16},{28,20},{1,9},{5... | collective-permute-start | bytes 786440 | tf_op jit(solution)/shard_map/ppermute | solution.py:413
  39.7 9.7 %collective-permute-start.13 = (bf16[4,128,256]{2,1,0:T(8,128)(2,1)S(1)}, bf16[4,128,256]{2,1,0:T(8,128)(2,1)S(1)}, u32[]{:S(2)}, u32[]{:S(2)}) collective-permute-start(bf16[4,128,256]{2,1,0:T(8,128)(2,1)S(1)} %slice.11), channel_id=1, source_target_pairs={{0,4},{4,0},{8,12},{12,8},{16,20},{20,16},{24,28},{28,24},{1,5},{5... | collective-permute-start | bytes 786440 | tf_op jit(solution)/shard_map/ppermute | solution.py:413
  45.1 7.1 %collective-permute-start.21 = (bf16[256,256]{1,0:T(8,128)(2,1)S(1)}, bf16[256,256]{1,0:T(8,128)(2,1)S(1)}, u32[]{:S(2)}, u32[]{:S(2)}) collective-permute-start(bf16[256,256]{1,0:T(8,128)(2,1)S(1)} %get-tuple-element.86), channel_id=1, source_target_pairs={{0,4},{4,0},{8,12},{12,8},{16,20},{20,16},{24,28},{28,24},{1,5},{5... | collective-permute-start | bytes 393224 | tf_op jit(solution)/shard_map/ppermute | solution.py:413
  45.8 8.2 %collective-permute-start.22 = (bf16[256,256]{1,0:T(8,128)(2,1)S(1)}, bf16[256,256]{1,0:T(8,128)(2,1)S(1)}, u32[]{:S(2)}, u32[]{:S(2)}) collective-permute-start(bf16[256,256]{1,0:T(8,128)(2,1)S(1)} %get-tuple-element.87), channel_id=1, source_target_pairs={{0,8},{4,12},{8,0},{12,4},{16,24},{20,28},{24,16},{28,20},{1,9},{5... | collective-permute-start | bytes 393224 | tf_op jit(solution)/shard_map/ppermute | solution.py:413
  47.4 8.3 %collective-permute-start.23 = (bf16[256,256]{1,0:T(8,128)(2,1)S(1)}, bf16[256,256]{1,0:T(8,128)(2,1)S(1)}, u32[]{:S(2)}, u32[]{:S(2)}) collective-permute-start(bf16[256,256]{1,0:T(8,128)(2,1)S(1)} %get-tuple-element.88), channel_id=1, source_target_pairs={{0,12},{4,8},{8,4},{12,0},{16,28},{20,24},{24,20},{28,16},{1,13},{... | collective-permute-start | bytes 393224 | tf_op jit(solution)/shard_map/ppermute | solution.py:413
  48.6 8.7 %collective-permute-start.14 = (bf16[288,256]{1,0:T(8,128)(2,1)S(1)}, bf16[288,256]{1,0:T(8,128)(2,1)S(1)}, u32[]{:S(2)}, u32[]{:S(2)}) collective-permute-start(bf16[288,256]{1,0:T(8,128)(2,1)S(1)} %get-tuple-element.76), channel_id=1, source_target_pairs={{0,4},{4,0},{8,12},{12,8},{16,20},{20,16},{24,28},{28,24},{1,5},{5... | collective-permute-start | bytes 442376 | tf_op jit(solution)/shard_map/ppermute | solution.py:413
  49.3 8.9 %collective-permute-start.15 = (bf16[288,256]{1,0:T(8,128)(2,1)S(1)}, bf16[288,256]{1,0:T(8,128)(2,1)S(1)}, u32[]{:S(2)}, u32[]{:S(2)}) collective-permute-start(bf16[288,256]{1,0:T(8,128)(2,1)S(1)} %get-tuple-element.77), channel_id=1, source_target_pairs={{0,8},{4,12},{8,0},{12,4},{16,24},{20,28},{24,16},{28,20},{1,9},{5... | collective-permute-start | bytes 442376 | tf_op jit(solution)/shard_map/ppermute | solution.py:413
  52.2 8.8 %collective-permute-start.16 = (bf16[288,256]{1,0:T(8,128)(2,1)S(1)}, bf16[288,256]{1,0:T(8,128)(2,1)S(1)}, u32[]{:S(2)}, u32[]{:S(2)}) collective-permute-start(bf16[288,256]{1,0:T(8,128)(2,1)S(1)} %get-tuple-element.78), channel_id=1, source_target_pairs={{0,12},{4,8},{8,4},{12,0},{16,28},{20,24},{24,20},{28,16},{1,13},{... | collective-permute-start | bytes 442376 | tf_op jit(solution)/shard_map/ppermute | solution.py:413
  57.0 5.3 %collective-permute-start.24 = (bf16[2,2,256,128]{3,2,1,0:T(8,128)(2,1)S(1)}, bf16[2,2,256,128]{3,2,1,0:T(8,128)(2,1)S(1)}, u32[]{:S(2)}, u32[]{:S(2)}) collective-permute-start(bf16[2,2,256,128]{3,2,1,0:T(8,128)(2,1)S(1)} %get-tuple-element.90), channel_id=1, source_target_pairs={{0,1},{1,0},{2,3},{3,2},{4,5},{5,4},{6,7},{7,6},{8,9},{9,8},{10,11... | collective-permute-start | bytes 786440 | tf_op jit(solution)/shard_map/ppermute | solution.py:413
  62.4 6.0 %collective-permute-start.25 = (bf16[1,2,256,128]{3,2,1,0:T(8,128)(2,1)S(1)}, bf16[1,2,256,128]{3,2,1,0:T(8,128)(2,1)S(1)}, u32[]{:S(2)}, u32[]{:S(2)}) collective-permute-start(bf16[1,2,256,128]{3,2,1,0:T(8,128)(2,1)S(1)} %get-tuple-element.92), channel_id=1, source_target_pairs={{0,2},{1,3},{2,0},{3,1},{4,6},{5,7},{6,4},{7,5},{8,10},{9,11},{10,... | collective-permute-start | bytes 393224 | tf_op jit(solution)/shard_map/ppermute | solution.py:418
  63.9 7.5 %collective-permute-start.18 = (bf16[1,1,304,128]{3,2,1,0:T(8,128)(2,1)S(1)}, bf16[1,1,304,128]{3,2,1,0:T(8,128)(2,1)S(1)}, u32[]{:S(2)}, u32[]{:S(2)}) collective-permute-start(bf16[1,1,304,128]{3,2,1,0:T(8,128)(2,1)S(1)} %get-tuple-element.82), channel_id=1, source_target_pairs={{0,16},{1,17},{2,18},{3,19},{4,20},{5,21},{6,22},{7,23},{8,24},{9,... | collective-permute-start | bytes 233480 | tf_op jit(solution)/shard_map/ppermute | solution.py:418
  66.6 4.8 %collective-permute-start.19 = (bf16[1,1,304,128]{3,2,1,0:T(8,128)(2,1)S(1)}, bf16[1,1,304,128]{3,2,1,0:T(8,128)(2,1)S(1)}, u32[]{:S(2)}, u32[]{:S(2)}) collective-permute-start(bf16[1,1,304,128]{3,2,1,0:T(8,128)(2,1)S(1)} %get-tuple-element.83), channel_id=1, source_target_pairs={{0,2},{1,3},{2,0},{3,1},{4,6},{5,7},{6,4},{7,5},{8,10},{9,11},{10,... | collective-permute-start | bytes 233480 | tf_op jit(solution)/shard_map/ppermute | solution.py:418
  67.2 9.1 %collective-permute-start.20 = (bf16[1,1,304,128]{3,2,1,0:T(8,128)(2,1)S(1)}, bf16[1,1,304,128]{3,2,1,0:T(8,128)(2,1)S(1)}, u32[]{:S(2)}, u32[]{:S(2)}) collective-permute-start(bf16[1,1,304,128]{3,2,1,0:T(8,128)(2,1)S(1)} %get-tuple-element.84), channel_id=1, source_target_pairs={{0,18},{1,19},{2,16},{3,17},{4,22},{5,23},{6,20},{7,21},{8,26},{9,... | collective-permute-start | bytes 233480 | tf_op jit(solution)/shard_map/ppermute | solution.py:418
  68.4 8.8 %collective-permute-start.26 = (bf16[1,1,256,128]{3,2,1,0:T(8,128)(2,1)S(1)}, bf16[1,1,256,128]{3,2,1,0:T(8,128)(2,1)S(1)}, u32[]{:S(2)}, u32[]{:S(2)}) collective-permute-start(bf16[1,1,256,128]{3,2,1,0:T(8,128)(2,1)S(1)} %get-tuple-element.94), channel_id=1, source_target_pairs={{0,16},{1,17},{2,18},{3,19},{4,20},{5,21},{6,22},{7,23},{8,24},{9,... | collective-permute-start | bytes 196616 | tf_op jit(solution)/shard_map/ppermute | solution.py:418
  (6 other events, 45.3 us)

commit v12 on v11

--- a/solution.py
+++ b/solution.py
@@ -475,10 +475,12 @@
     rest, other_beside = tensor(rest, 2), tensor(other, 1)
     ctx_x, ctx_z = dp(ctx, 1), dp(ctx, 2)
     early = mix(info, ctx, [[weight], [beside], [mine, other], [mine_beside, other_beside]], True)
-    rest, early, ctx_x, ctx_z = barrier((rest, early, ctx_x, ctx_z))
+    rest, early = barrier((rest, early))
+    late = [rest, tensor(rest, 1)]
+    late, ctx_x, ctx_z = barrier((late, ctx_x, ctx_z))
     half = ctx.shape[1] // 2
     ctxs = [[ctx], [ctx_x], [ctx_z], [dp(ctx_x[:, :half], 2), dp(ctx_z[:, half:], 1)]]
-    return ctxs, early, [rest, tensor(rest, 1)]
+    return ctxs, early, late
 
 
 def on_device(

time: 78.3 us -> 80.2 us (1.024)
  starting transfers between devices: 27.6 us -> 29.3 us
    ppermute x22, starting transfers between devices: 19.6 us -> 21.7 us  [swap(): return lax.ppermute(x, axis, [(i, i ^ mask) for i in range(n)])]
  transfers between devices with their start and end apart: 27 -> 27, of which waited for: 16 -> 12; matrix products, arithmetic and copies ran while one was open for 3% -> 3% of each run, Pallas kernels for 17% -> 16%
where the time goes in v12:
time: 80.2 us; the launch traced here: 80 us
  waiting for transfers between devices  32.7 us (41%)
  starting transfers between devices  29.3 us (37%)
  Pallas kernels  13.9 us (17%)
  between operations  2.09 us (3%)
  local copies, waits for them, and re-layouts  1.06 us (1%)
  other arithmetic  1.05 us (1%)
    ppermute x22, waiting for transfers between devices, swap(): return lax.ppermute(x, axis, [(i, i ^ mask) for i in range(n)])  26.8 us
    ppermute x22, starting transfers between devices, swap(): return lax.ppermute(x, axis, [(i, i ^ mask) for i in range(n)])  21.7 us
    ppermute x5, starting transfers between devices, swap_far(): lax.ppermute(x, ('dp', 'tensor'), [(i, i ^ mask) for i in range(n_dp * n_...  7.58 us
    ppermute x5, waiting for transfers between devices, swap_far(): lax.ppermute(x, ('dp', 'tensor'), [(i, i ^ mask) for i in range(n_dp * n_...  5.86 us
    pallas_call x1, Pallas kernels, attend(): pl.pallas_call(attend_body, in_specs=[SM, SM, VM, VM, VM], out_specs=[VM]...  4.82 us
    pallas_call x1, Pallas kernels, join(): pl.pallas_call(functools.partial(join_body, plan, len(late)), in_specs=[S...  4.05 us
    pallas_call x2, Pallas kernels, gradient(): pl.pallas_call(functools.partial(grad_body, plan, dout, [len(c) for c in...  2.5 us
  transfers between devices with their start and end apart: 27, of which 12 were waited for; matrix products, arithmetic and copies ran while one was open for 3% of the time, Pallas kernels for 16%

profile of v12, /device:TPU:0, one launch (start us, length us, event | category | flops | bytes accessed | tf_op | source)
XLA Modules:
  0.0 80.0 jit_solution(10368915509074528790)
XLA Ops:
  2.1 2.6 %collective-permute-start = (bf16[256,512]{1,0:T(8,128)(2,1)S(1)}, bf16[256,512]{1,0:T(8,128)(2,1)S(1)}, u32[]{:S(2)}, u32[]{:S(2)}) collective-permute-start(bf16[256,512]{1,0:T(8,128)(2,1)S(1)} %dynamic-slice_bitcast_fusion), channel_id=1, source_target_pairs={{0,2},{1,3},{2,0},{3,1},{4,6},{5,7},{6,4},{7,5},{8,10},{9,11},{10,... | collective-permute-start | bytes 786440 | tf_op jit(solution)/shard_map/ppermute | solution.py:413
  5.4 4.8 %attend.1 = (bf16[256,256]{1,0:T(8,128)(2,1)}, bf16[256,256]{1,0:T(8,128)(2,1)}, bf16[256,256]{1,0:T(8,128)(2,1)}, bf16[256,256]{1,0:T(8,128)(2,1)}) custom-call(s32[1]{0:T(128)S(6)} %copy.12.len_ref, s32[1]{0:T(128)} %bitcast.me_ref, bf16[1024,256]{1,0:T(8,128)(2,1)} %bitcast.24, bf16[1024,256]{1,0:T(8,128)(2,1)} %bitcast.25, bf16[1024,256]{1,0:T(8,128)(2,1)} %bitcast.26), custom_call_target="tpu_custom_call" | custom-call | flops 1073741824 | bytes 2097152 | tf_op jit(solution)/shard_map/attend/pallas_call | solution.py:79
  10.2 1.5 %collective-permute-done.refs_2_ = bf16[256,512]{1,0:T(8,128)(2,1)S(1)} collective-permute-done((bf16[256,512]{1,0:T(8,128)(2,1)S(1)}, bf16[256,512]{1,0:T(8,128)(2,1)S(1)}, u32[]{:S(2)}, u32[]{:S(2)}) %collective-permute-start) | collective-permute-done | bytes 262176 | tf_op jit(solution)/shard_map/ppermute | solution.py:413
  11.7 1.7 %collective-permute-start.2 = (bf16[256,512]{1,0:T(8,128)(2,1)S(1)}, bf16[256,512]{1,0:T(8,128)(2,1)S(1)}, u32[]{:S(2)}, u32[]{:S(2)}) collective-permute-start(bf16[256,512]{1,0:T(8,128)(2,1)S(1)} %collective-permute-done.refs_2_), channel_id=1, source_target_pairs={{0,4},{4,0},{8,12},{12,8},{16,20},{20,16},{24,28},{28,24},{1,5},{5... | collective-permute-start | bytes 786440 | tf_op jit(solution)/shard_map/ppermute | solution.py:413
  13.6 1.5 %collective-permute-start.5 = (bf16[256,256]{1,0:T(8,128)(2,1)}, bf16[256,256]{1,0:T(8,128)(2,1)S(1)}, u32[]{:S(2)}, u32[]{:S(2)}) collective-permute-start(bf16[256,256]{1,0:T(8,128)(2,1)} %get-tuple-element.60), channel_id=1, source_target_pairs={{0,2},{1,3},{2,0},{3,1},{4,6},{5,7},{6,4},{7,5},{8,10},{9,11},{10,... | collective-permute-start | bytes 393224 | tf_op jit(solution)/shard_map/ppermute | solution.py:413
  15.3 4.8 %collective-permute-done.5 = bf16[256,256]{1,0:T(8,128)(2,1)S(1)} collective-permute-done((bf16[256,256]{1,0:T(8,128)(2,1)}, bf16[256,256]{1,0:T(8,128)(2,1)S(1)}, u32[]{:S(2)}, u32[]{:S(2)}) %collective-permute-start.5) | collective-permute-done | bytes 131104 | tf_op jit(solution)/shard_map/ppermute | solution.py:413
  20.2 1.5 %collective-permute-done.6 = bf16[256,256]{1,0:T(8,128)(2,1)S(1)} collective-permute-done((bf16[256,256]{1,0:T(8,128)(2,1)}, bf16[256,256]{1,0:T(8,128)(2,1)S(1)}, u32[]{:S(2)}, u32[]{:S(2)}) %collective-permute-start.6) | collective-permute-done | bytes 131104 | tf_op jit(solution)/shard_map/ppermute | solution.py:413
  22.7 1.6 %collective-permute-start.7 = (bf16[256,1024]{1,0:T(8,128)(2,1)S(1)}, bf16[256,1024]{1,0:T(8,128)(2,1)S(1)}, u32[]{:S(2)}, u32[]{:S(2)}) collective-permute-start(bf16[256,1024]{1,0:T(8,128)(2,1)S(1)} %slice.12), channel_id=1, source_target_pairs={{0,2},{1,3},{2,0},{3,1},{4,6},{5,7},{6,4},{7,5},{8,10},{9,11},{10,... | collective-permute-start | bytes 1572872 | tf_op jit(solution)/shard_map/ppermute | solution.py:413
  25.2 1.6 %collective-permute-start.11 = (bf16[4,256,256]{2,1,0:T(8,128)(2,1)S(1)}, bf16[4,256,256]{2,1,0:T(8,128)(2,1)S(1)}, u32[]{:S(2)}, u32[]{:S(2)}) collective-permute-start(bf16[4,256,256]{2,1,0:T(8,128)(2,1)S(1)} %pad_maximum_fusion.ctx_ref.refs_0_), channel_id=1, source_target_pairs={{0,8},{4,12},{8,0},{12,4},{16,24},{20,28},{24,16},{28,20},{1,9},{5... | collective-permute-start | bytes 1572872 | tf_op jit(solution)/shard_map/ppermute | solution.py:413
  27.3 1.6 %mix.1 = (f32[256,2048]{1,0:T(8,128)S(1)}, f32[256,128]{1,0:T(8,128)S(1)}, bf16[4,256,256]{2,1,0:T(8,128)(2,1)S(1)}) custom-call(s32[4]{0:T(128)S(1)} %pad_add_fusion.info_ref, bf16[4,256,256]{2,1,0:T(8,128)(2,1)S(1)} %pad_maximum_fusion.ctx_ref.refs_0_, bf16[256,2048]{1,0:T(8,128)(2,1)S(1)} %bitcast.18, ...), custom_call_target="tpu_custom_call" | custom-call | flops 1073741824 | bytes 6291456 | tf_op jit(solution)/shard_map/mix/pallas_call | solution.py:130
  28.9 8.1 %collective-permute-done.7.refs_0_ = bf16[256,1024]{1,0:T(8,128)(2,1)S(1)} collective-permute-done((bf16[256,1024]{1,0:T(8,128)(2,1)S(1)}, bf16[256,1024]{1,0:T(8,128)(2,1)S(1)}, u32[]{:S(2)}, u32[]{:S(2)}) %collective-permute-start.7) | collective-permute-done | bytes 524320 | tf_op jit(solution)/shard_map/ppermute | solution.py:413
  37.1 2.3 %collective-permute-done.11.refs_2_ = bf16[4,256,256]{2,1,0:T(8,128)(2,1)S(1)} collective-permute-done((bf16[4,256,256]{2,1,0:T(8,128)(2,1)S(1)}, bf16[4,256,256]{2,1,0:T(8,128)(2,1)S(1)}, u32[]{:S(2)}, u32[]{:S(2)}) %collective-permute-start.11) | collective-permute-done | bytes 524320 | tf_op jit(solution)/shard_map/ppermute | solution.py:413
  39.4 1.3 %collective-permute-done.10.refs_1_ = bf16[4,256,256]{2,1,0:T(8,128)(2,1)S(1)} collective-permute-done((bf16[4,256,256]{2,1,0:T(8,128)(2,1)S(1)}, bf16[4,256,256]{2,1,0:T(8,128)(2,1)S(1)}, u32[]{:S(2)}, u32[]{:S(2)}) %collective-permute-start.10) | collective-permute-done | bytes 524320 | tf_op jit(solution)/shard_map/ppermute | solution.py:413
  41.8 4.1 %join.1 = (bf16[256,2048]{1,0:T(8,128)(2,1)}, bf16[288,256]{1,0:T(8,128)(2,1)S(1)}, bf16[288,256]{1,0:T(8,128)(2,1)S(1)}, bf16[288,256]{1,0:T(8,128)(2,1)S(1)}, ...) custom-call(s32[4]{0:T(128)S(1)} %pad_add_fusion.info_ref, ...), custom_call_target="tpu_custom_call" | custom-call | flops 134217728 | bytes 6291456 | tf_op jit(solution)/shard_map/join/pallas_call | solution.py:243
  45.8 1.5 %collective-permute-start.21 = (bf16[256,256]{1,0:T(8,128)(2,1)S(1)}, bf16[256,256]{1,0:T(8,128)(2,1)S(1)}, u32[]{:S(2)}, u32[]{:S(2)}) collective-permute-start(bf16[256,256]{1,0:T(8,128)(2,1)S(1)} %get-tuple-element.90), channel_id=1, source_target_pairs={{0,4},{4,0},{8,12},{12,8},{16,20},{20,16},{24,28},{28,24},{1,5},{5... | collective-permute-start | bytes 393224 | tf_op jit(solution)/shard_map/ppermute | solution.py:413
  47.3 1.6 %collective-permute-start.22 = (bf16[256,256]{1,0:T(8,128)(2,1)S(1)}, bf16[256,256]{1,0:T(8,128)(2,1)S(1)}, u32[]{:S(2)}, u32[]{:S(2)}) collective-permute-start(bf16[256,256]{1,0:T(8,128)(2,1)S(1)} %get-tuple-element.91), channel_id=1, source_target_pairs={{0,8},{4,12},{8,0},{12,4},{16,24},{20,28},{24,16},{28,20},{1,9},{5... | collective-permute-start | bytes 393224 | tf_op jit(solution)/shard_map/ppermute | solution.py:413
  49.3 2.2 %collective-permute-done.21.refs_6_ = bf16[256,256]{1,0:T(8,128)(2,1)S(1)} collective-permute-done((bf16[256,256]{1,0:T(8,128)(2,1)S(1)}, bf16[256,256]{1,0:T(8,128)(2,1)S(1)}, u32[]{:S(2)}, u32[]{:S(2)}) %collective-permute-start.21) | collective-permute-done | bytes 131104 | tf_op jit(solution)/shard_map/ppermute | solution.py:413
  51.5 2.6 %collective-permute-start.14 = (bf16[288,256]{1,0:T(8,128)(2,1)S(1)}, bf16[288,256]{1,0:T(8,128)(2,1)S(1)}, u32[]{:S(2)}, u32[]{:S(2)}) collective-permute-start(bf16[288,256]{1,0:T(8,128)(2,1)S(1)} %get-tuple-element.80), channel_id=1, source_target_pairs={{0,4},{4,0},{8,12},{12,8},{16,20},{20,16},{24,28},{28,24},{1,5},{5... | collective-permute-start | bytes 442376 | tf_op jit(solution)/shard_map/ppermute | solution.py:413
  54.1 2.7 %collective-permute-start.15 = (bf16[288,256]{1,0:T(8,128)(2,1)S(1)}, bf16[288,256]{1,0:T(8,128)(2,1)S(1)}, u32[]{:S(2)}, u32[]{:S(2)}) collective-permute-start(bf16[288,256]{1,0:T(8,128)(2,1)S(1)} %get-tuple-element.81), channel_id=1, source_target_pairs={{0,8},{4,12},{8,0},{12,4},{16,24},{20,28},{24,16},{28,20},{1,9},{5... | collective-permute-start | bytes 442376 | tf_op jit(solution)/shard_map/ppermute | solution.py:413
  60.0 2.9 %collective-permute-done.16.refs_8_ = bf16[288,256]{1,0:T(8,128)(2,1)S(1)} collective-permute-done((bf16[288,256]{1,0:T(8,128)(2,1)S(1)}, bf16[288,256]{1,0:T(8,128)(2,1)S(1)}, u32[]{:S(2)}, u32[]{:S(2)}) %collective-permute-start.16) | collective-permute-done | bytes 147488 | tf_op jit(solution)/shard_map/ppermute | solution.py:413
  64.5 1.4 %collective-permute-done.17.got_ref = bf16[2,2,304,128]{3,2,1,0:T(8,128)(2,1)S(1)} collective-permute-done((bf16[2,2,304,128]{3,2,1,0:T(8,128)(2,1)S(1)}, bf16[2,2,304,128]{3,2,1,0:T(8,128)(2,1)S(1)}, u32[]{:S(2)}, u32[]{:S(2)}) %collective-permute-start.17) | collective-permute-done | bytes 311328 | tf_op jit(solution)/shard_map/ppermute | solution.py:413
  65.9 2.7 %collective-permute-start.18 = (bf16[1,1,304,128]{3,2,1,0:T(8,128)(2,1)S(1)}, bf16[1,1,304,128]{3,2,1,0:T(8,128)(2,1)S(1)}, u32[]{:S(2)}, u32[]{:S(2)}) collective-permute-start(bf16[1,1,304,128]{3,2,1,0:T(8,128)(2,1)S(1)} %get-tuple-element.86), channel_id=1, source_target_pairs={{0,16},{1,17},{2,18},{3,19},{4,20},{5,21},{6,22},{7,23},{8,24},{9,... | collective-permute-start | bytes 233480 | tf_op jit(solution)/shard_map/ppermute | solution.py:418
  70.4 3.0 %collective-permute-start.26 = (bf16[1,1,256,128]{3,2,1,0:T(8,128)(2,1)S(1)}, bf16[1,1,256,128]{3,2,1,0:T(8,128)(2,1)S(1)}, u32[]{:S(2)}, u32[]{:S(2)}) collective-permute-start(bf16[1,1,256,128]{3,2,1,0:T(8,128)(2,1)S(1)} %get-tuple-element.98), channel_id=1, source_target_pairs={{0,16},{1,17},{2,18},{3,19},{4,20},{5,21},{6,22},{7,23},{8,24},{9,... | collective-permute-start | bytes 196616 | tf_op jit(solution)/shard_map/ppermute | solution.py:418
  73.4 5.0 %collective-permute-done.20.refs_3_ = bf16[1,1,304,128]{3,2,1,0:T(8,128)(2,1)S(1)} collective-permute-done((bf16[1,1,304,128]{3,2,1,0:T(8,128)(2,1)S(1)}, bf16[1,1,304,128]{3,2,1,0:T(8,128)(2,1)S(1)}, u32[]{:S(2)}, u32[]{:S(2)}) %collective-permute-start.20) | collective-permute-done | bytes 77856 | tf_op jit(solution)/shard_map/ppermute | solution.py:418
  (51 shorter events, 13.4 us)
Async XLA Ops:
  0.6 11.1 %collective-permute-start.1 = (bf16[256,2048]{1,0:T(8,128)(2,1)}, bf16[256,2048]{1,0:T(8,128)(2,1)S(1)}, u32[]{:S(2)}, u32[]{:S(2)}) collective-permute-start(bf16[256,2048]{1,0:T(8,128)(2,1)} %bitcast.16), channel_id=1, source_target_pairs={{0,1},{1,0},{2,3},{3,2},{4,5},{5,4},{6,7},{7,6},{8,9},{9,8},{10,11... | collective-permute-start | bytes 3145736 | tf_op jit(solution)/shard_map/ppermute | solution.py:413
  2.1 9.6 %collective-permute-start = (bf16[256,512]{1,0:T(8,128)(2,1)S(1)}, bf16[256,512]{1,0:T(8,128)(2,1)S(1)}, u32[]{:S(2)}, u32[]{:S(2)}) collective-permute-start(bf16[256,512]{1,0:T(8,128)(2,1)S(1)} %dynamic-slice_bitcast_fusion), channel_id=1, source_target_pairs={{0,2},{1,3},{2,0},{3,1},{4,6},{5,7},{6,4},{7,5},{8,10},{9,11},{10,... | collective-permute-start | bytes 786440 | tf_op jit(solution)/shard_map/ppermute | solution.py:413
  11.7 11.0 %collective-permute-start.3 = (bf16[256,512]{1,0:T(8,128)(2,1)S(1)}, bf16[256,512]{1,0:T(8,128)(2,1)S(1)}, u32[]{:S(2)}, u32[]{:S(2)}) collective-permute-start(bf16[256,512]{1,0:T(8,128)(2,1)S(1)} %collective-permute-done.refs_2_), channel_id=1, source_target_pairs={{0,1},{1,0},{2,3},{3,2},{4,5},{5,4},{6,7},{7,6},{8,9},{9,8},{10,11... | collective-permute-start | bytes 786440 | tf_op jit(solution)/shard_map/ppermute | solution.py:413
  11.7 11.0 %collective-permute-start.2 = (bf16[256,512]{1,0:T(8,128)(2,1)S(1)}, bf16[256,512]{1,0:T(8,128)(2,1)S(1)}, u32[]{:S(2)}, u32[]{:S(2)}) collective-permute-start(bf16[256,512]{1,0:T(8,128)(2,1)S(1)} %collective-permute-done.refs_2_), channel_id=1, source_target_pairs={{0,4},{4,0},{8,12},{12,8},{16,20},{20,16},{24,28},{28,24},{1,5},{5... | collective-permute-start | bytes 786440 | tf_op jit(solution)/shard_map/ppermute | solution.py:413
  13.6 6.5 %collective-permute-start.5 = (bf16[256,256]{1,0:T(8,128)(2,1)}, bf16[256,256]{1,0:T(8,128)(2,1)S(1)}, u32[]{:S(2)}, u32[]{:S(2)}) collective-permute-start(bf16[256,256]{1,0:T(8,128)(2,1)} %get-tuple-element.60), channel_id=1, source_target_pairs={{0,2},{1,3},{2,0},{3,1},{4,6},{5,7},{6,4},{7,5},{8,10},{9,11},{10,... | collective-permute-start | bytes 393224 | tf_op jit(solution)/shard_map/ppermute | solution.py:413
  15.2 6.5 %collective-permute-start.6 = (bf16[256,256]{1,0:T(8,128)(2,1)}, bf16[256,256]{1,0:T(8,128)(2,1)S(1)}, u32[]{:S(2)}, u32[]{:S(2)}) collective-permute-start(bf16[256,256]{1,0:T(8,128)(2,1)} %get-tuple-element.61), channel_id=1, source_target_pairs={{0,3},{1,2},{2,1},{3,0},{4,7},{5,6},{6,5},{7,4},{8,11},{9,10},{10,... | collective-permute-start | bytes 393224 | tf_op jit(solution)/shard_map/ppermute | solution.py:413
  22.7 14.4 %collective-permute-start.7 = (bf16[256,1024]{1,0:T(8,128)(2,1)S(1)}, bf16[256,1024]{1,0:T(8,128)(2,1)S(1)}, u32[]{:S(2)}, u32[]{:S(2)}) collective-permute-start(bf16[256,1024]{1,0:T(8,128)(2,1)S(1)} %slice.12), channel_id=1, source_target_pairs={{0,2},{1,3},{2,0},{3,1},{4,6},{5,7},{6,4},{7,5},{8,10},{9,11},{10,... | collective-permute-start | bytes 1572872 | tf_op jit(solution)/shard_map/ppermute | solution.py:413
  25.2 14.2 %collective-permute-start.11 = (bf16[4,256,256]{2,1,0:T(8,128)(2,1)S(1)}, bf16[4,256,256]{2,1,0:T(8,128)(2,1)S(1)}, u32[]{:S(2)}, u32[]{:S(2)}) collective-permute-start(bf16[4,256,256]{2,1,0:T(8,128)(2,1)S(1)} %pad_maximum_fusion.ctx_ref.refs_0_), channel_id=1, source_target_pairs={{0,8},{4,12},{8,0},{12,4},{16,24},{20,28},{24,16},{28,20},{1,9},{5... | collective-permute-start | bytes 1572872 | tf_op jit(solution)/shard_map/ppermute | solution.py:413
  26.8 13.9 %collective-permute-start.10 = (bf16[4,256,256]{2,1,0:T(8,128)(2,1)S(1)}, bf16[4,256,256]{2,1,0:T(8,128)(2,1)S(1)}, u32[]{:S(2)}, u32[]{:S(2)}) collective-permute-start(bf16[4,256,256]{2,1,0:T(8,128)(2,1)S(1)} %pad_maximum_fusion.ctx_ref.refs_0_), channel_id=1, source_target_pairs={{0,4},{4,0},{8,12},{12,8},{16,20},{20,16},{24,28},{28,24},{1,5},{5... | collective-permute-start | bytes 1572872 | tf_op jit(solution)/shard_map/ppermute | solution.py:413
  37.1 3.6 %collective-permute-start.9 = (bf16[256,1024]{1,0:T(8,128)(2,1)S(1)}, bf16[256,1024]{1,0:T(8,128)(2,1)S(1)}, u32[]{:S(2)}, u32[]{:S(2)}) collective-permute-start(bf16[256,1024]{1,0:T(8,128)(2,1)S(1)} %collective-permute-done.7.refs_0_), channel_id=1, source_target_pairs={{0,1},{1,0},{2,3},{3,2},{4,5},{5,4},{6,7},{7,6},{8,9},{9,8},{10,11... | collective-permute-start | bytes 1572872 | tf_op jit(solution)/shard_map/ppermute | solution.py:413
  40.7 17.2 %collective-permute-start.13 = (bf16[4,128,256]{2,1,0:T(8,128)(2,1)S(1)}, bf16[4,128,256]{2,1,0:T(8,128)(2,1)S(1)}, u32[]{:S(2)}, u32[]{:S(2)}) collective-permute-start(bf16[4,128,256]{2,1,0:T(8,128)(2,1)S(1)} %slice.11), channel_id=1, source_target_pairs={{0,4},{4,0},{8,12},{12,8},{16,20},{20,16},{24,28},{28,24},{1,5},{5... | collective-permute-start | bytes 786440 | tf_op jit(solution)/shard_map/ppermute | solution.py:413
  41.3 16.6 %collective-permute-start.12 = (bf16[4,128,256]{2,1,0:T(8,128)(2,1)S(1)}, bf16[4,128,256]{2,1,0:T(8,128)(2,1)S(1)}, u32[]{:S(2)}, u32[]{:S(2)}) collective-permute-start(bf16[4,128,256]{2,1,0:T(8,128)(2,1)S(1)} %slice.10), channel_id=1, source_target_pairs={{0,8},{4,12},{8,0},{12,4},{16,24},{20,28},{24,16},{28,20},{1,9},{5... | collective-permute-start | bytes 786440 | tf_op jit(solution)/shard_map/ppermute | solution.py:413
  45.8 5.7 %collective-permute-start.21 = (bf16[256,256]{1,0:T(8,128)(2,1)S(1)}, bf16[256,256]{1,0:T(8,128)(2,1)S(1)}, u32[]{:S(2)}, u32[]{:S(2)}) collective-permute-start(bf16[256,256]{1,0:T(8,128)(2,1)S(1)} %get-tuple-element.90), channel_id=1, source_target_pairs={{0,4},{4,0},{8,12},{12,8},{16,20},{20,16},{24,28},{28,24},{1,5},{5... | collective-permute-start | bytes 393224 | tf_op jit(solution)/shard_map/ppermute | solution.py:413
  47.3 6.8 %collective-permute-start.22 = (bf16[256,256]{1,0:T(8,128)(2,1)S(1)}, bf16[256,256]{1,0:T(8,128)(2,1)S(1)}, u32[]{:S(2)}, u32[]{:S(2)}) collective-permute-start(bf16[256,256]{1,0:T(8,128)(2,1)S(1)} %get-tuple-element.91), channel_id=1, source_target_pairs={{0,8},{4,12},{8,0},{12,4},{16,24},{20,28},{24,16},{28,20},{1,9},{5... | collective-permute-start | bytes 393224 | tf_op jit(solution)/shard_map/ppermute | solution.py:413
  48.9 8.0 %collective-permute-start.23 = (bf16[256,256]{1,0:T(8,128)(2,1)S(1)}, bf16[256,256]{1,0:T(8,128)(2,1)S(1)}, u32[]{:S(2)}, u32[]{:S(2)}) collective-permute-start(bf16[256,256]{1,0:T(8,128)(2,1)S(1)} %get-tuple-element.92), channel_id=1, source_target_pairs={{0,12},{4,8},{8,4},{12,0},{16,28},{20,24},{24,20},{28,16},{1,13},{... | collective-permute-start | bytes 393224 | tf_op jit(solution)/shard_map/ppermute | solution.py:413
  51.5 7.7 %collective-permute-start.14 = (bf16[288,256]{1,0:T(8,128)(2,1)S(1)}, bf16[288,256]{1,0:T(8,128)(2,1)S(1)}, u32[]{:S(2)}, u32[]{:S(2)}) collective-permute-start(bf16[288,256]{1,0:T(8,128)(2,1)S(1)} %get-tuple-element.80), channel_id=1, source_target_pairs={{0,4},{4,0},{8,12},{12,8},{16,20},{20,16},{24,28},{28,24},{1,5},{5... | collective-permute-start | bytes 442376 | tf_op jit(solution)/shard_map/ppermute | solution.py:413
  54.1 5.9 %collective-permute-start.15 = (bf16[288,256]{1,0:T(8,128)(2,1)S(1)}, bf16[288,256]{1,0:T(8,128)(2,1)S(1)}, u32[]{:S(2)}, u32[]{:S(2)}) collective-permute-start(bf16[288,256]{1,0:T(8,128)(2,1)S(1)} %get-tuple-element.81), channel_id=1, source_target_pairs={{0,8},{4,12},{8,0},{12,4},{16,24},{20,28},{24,16},{28,20},{1,9},{5... | collective-permute-start | bytes 442376 | tf_op jit(solution)/shard_map/ppermute | solution.py:413
  56.9 6.0 %collective-permute-start.16 = (bf16[288,256]{1,0:T(8,128)(2,1)S(1)}, bf16[288,256]{1,0:T(8,128)(2,1)S(1)}, u32[]{:S(2)}, u32[]{:S(2)}) collective-permute-start(bf16[288,256]{1,0:T(8,128)(2,1)S(1)} %get-tuple-element.82), channel_id=1, source_target_pairs={{0,12},{4,8},{8,4},{12,0},{16,28},{20,24},{24,20},{28,16},{1,13},{... | collective-permute-start | bytes 442376 | tf_op jit(solution)/shard_map/ppermute | solution.py:413
  59.2 5.1 %collective-permute-start.24 = (bf16[2,2,256,128]{3,2,1,0:T(8,128)(2,1)S(1)}, bf16[2,2,256,128]{3,2,1,0:T(8,128)(2,1)S(1)}, u32[]{:S(2)}, u32[]{:S(2)}) collective-permute-start(bf16[2,2,256,128]{3,2,1,0:T(8,128)(2,1)S(1)} %get-tuple-element.94), channel_id=1, source_target_pairs={{0,1},{1,0},{2,3},{3,2},{4,5},{5,4},{6,7},{7,6},{8,9},{9,8},{10,11... | collective-permute-start | bytes 786440 | tf_op jit(solution)/shard_map/ppermute | solution.py:413
  64.3 6.0 %collective-permute-start.25 = (bf16[1,2,256,128]{3,2,1,0:T(8,128)(2,1)S(1)}, bf16[1,2,256,128]{3,2,1,0:T(8,128)(2,1)S(1)}, u32[]{:S(2)}, u32[]{:S(2)}) collective-permute-start(bf16[1,2,256,128]{3,2,1,0:T(8,128)(2,1)S(1)} %get-tuple-element.96), channel_id=1, source_target_pairs={{0,2},{1,3},{2,0},{3,1},{4,6},{5,7},{6,4},{7,5},{8,10},{9,11},{10,... | collective-permute-start | bytes 393224 | tf_op jit(solution)/shard_map/ppermute | solution.py:418
  65.9 7.5 %collective-permute-start.18 = (bf16[1,1,304,128]{3,2,1,0:T(8,128)(2,1)S(1)}, bf16[1,1,304,128]{3,2,1,0:T(8,128)(2,1)S(1)}, u32[]{:S(2)}, u32[]{:S(2)}) collective-permute-start(bf16[1,1,304,128]{3,2,1,0:T(8,128)(2,1)S(1)} %get-tuple-element.86), channel_id=1, source_target_pairs={{0,16},{1,17},{2,18},{3,19},{4,20},{5,21},{6,22},{7,23},{8,24},{9,... | collective-permute-start | bytes 233480 | tf_op jit(solution)/shard_map/ppermute | solution.py:418
  68.6 4.8 %collective-permute-start.19 = (bf16[1,1,304,128]{3,2,1,0:T(8,128)(2,1)S(1)}, bf16[1,1,304,128]{3,2,1,0:T(8,128)(2,1)S(1)}, u32[]{:S(2)}, u32[]{:S(2)}) collective-permute-start(bf16[1,1,304,128]{3,2,1,0:T(8,128)(2,1)S(1)} %get-tuple-element.87), channel_id=1, source_target_pairs={{0,2},{1,3},{2,0},{3,1},{4,6},{5,7},{6,4},{7,5},{8,10},{9,11},{10,... | collective-permute-start | bytes 233480 | tf_op jit(solution)/shard_map/ppermute | solution.py:418
  69.2 9.2 %collective-permute-start.20 = (bf16[1,1,304,128]{3,2,1,0:T(8,128)(2,1)S(1)}, bf16[1,1,304,128]{3,2,1,0:T(8,128)(2,1)S(1)}, u32[]{:S(2)}, u32[]{:S(2)}) collective-permute-start(bf16[1,1,304,128]{3,2,1,0:T(8,128)(2,1)S(1)} %get-tuple-element.88), channel_id=1, source_target_pairs={{0,18},{1,19},{2,16},{3,17},{4,22},{5,23},{6,20},{7,21},{8,26},{9,... | collective-permute-start | bytes 233480 | tf_op jit(solution)/shard_map/ppermute | solution.py:418
  70.4 8.8 %collective-permute-start.26 = (bf16[1,1,256,128]{3,2,1,0:T(8,128)(2,1)S(1)}, bf16[1,1,256,128]{3,2,1,0:T(8,128)(2,1)S(1)}, u32[]{:S(2)}, u32[]{:S(2)}) collective-permute-start(bf16[1,1,256,128]{3,2,1,0:T(8,128)(2,1)S(1)} %get-tuple-element.98), channel_id=1, source_target_pairs={{0,16},{1,17},{2,18},{3,19},{4,20},{5,21},{6,22},{7,23},{8,24},{9,... | collective-permute-start | bytes 196616 | tf_op jit(solution)/shard_map/ppermute | solution.py:418
  (6 other events, 53.0 us)

commit v13 on v11

--- a/solution.py
+++ b/solution.py
@@ -43,10 +43,21 @@
 SM = pl.BlockSpec(memory_space=pltpu.SMEM)
 
 
-def attend_body(len_ref, me_ref, q_ref, k_ref, v_ref, *out_refs):
+def attend_body(n_out, len_ref, me_ref, q_hbm, k_hbm, v_hbm, *refs):
+    out_refs, (q_ref, k_ref, v_ref, sems) = refs[:n_out], refs[n_out : n_out + 4]
+    o_ref = refs[-1] if n_out > 1 else out_refs[0]
     seq = q_ref.shape[0]
-    o_ref = out_refs[-1]
     rows = o_ref.shape[2]
+
+    def copies(h):
+        at = slice(h * HD, (h + 1) * HD)
+        pairs = ((q_hbm, q_ref), (k_hbm, k_ref), (v_hbm, v_ref))
+        return [pltpu.make_async_copy(a.at[:, at], b.at[:, at], sems.at[h, i]) for i, (a, b) in enumerate(pairs)]
+
+    loads = [copies(h) for h in range(q_ref.shape[1] // HD)]
+    for load in loads:
+        for copy in load:
+            copy.start()
     rate = math.log2(math.e) / math.sqrt(HD)
     length = len_ref[0]
     key = lax.broadcasted_iota(jnp.int32, (seq, 1), 0)
@@ -55,6 +66,8 @@
     c = lax.broadcasted_iota(jnp.int32, (QB, QB), 1)
     for h in range(q_ref.shape[1] // HD):
         at = slice(h * HD, (h + 1) * HD)
+        for copy in loads[h]:
+            copy.wait()
         q_t, v_t = q_ref[:, at].T, v_ref[:, at].T
         for i in range(seq // QB):
             keys = (i + 1) * QB
@@ -68,7 +81,7 @@
             for n in range(0, QB, min(rows, QB)):
                 block, first = divmod(i * QB + n, rows)
                 o_ref[block, at, first : first + min(rows, QB)] = out[:, n : n + rows]
-    for m, ref in enumerate(out_refs[:-1]):
+    for m, ref in enumerate(out_refs if n_out > 1 else []):
         ref[...] = o_ref[me_ref[0] ^ m]
 
 
@@ -76,18 +89,40 @@
     seq, width = q.shape
     heads = width // HD
     blocks = seq // rows
+    hbm = pl.BlockSpec(memory_space=pl.ANY)
     return pl.pallas_call(
-        attend_body,
-        in_specs=[SM, SM, VM, VM, VM],
+        functools.partial(attend_body, blocks if split else 1),
+        in_specs=[SM, SM, hbm, hbm, hbm],
         out_specs=[VM] * (blocks if split else 1),
         out_shape=[shape((width, rows))] * blocks if split else [shape((blocks, width, rows))],
-        scratch_shapes=[pltpu.VMEM((blocks, width, rows), BF)] if split else [],
+        scratch_shapes=[pltpu.VMEM((seq, width), BF)] * 3
+        + [pltpu.SemaphoreType.DMA((heads, 3))]
+        + ([pltpu.VMEM((blocks, width, rows), BF)] if split else []),
         compiler_params=pltpu.CompilerParams(vmem_limit_bytes=60 * MIB),
         cost_estimate=pl.CostEstimate(
             flops=4 * seq * seq * width, bytes_accessed=8 * seq * width, transcendentals=heads * seq * seq
         ),
         name="attend",
     )(lengths, me, q, k, v)
+
+
+def stack_body(*refs):
+    for i, ref in enumerate(refs[:-1]):
+        refs[-1][i] = ref[...]
+
+
+def stack(arrays):
+    return pl.pallas_call(
+        stack_body,
+        in_specs=[VM] * len(arrays),
+        out_specs=VM,
+        out_shape=shape((len(arrays), *arrays[0].shape)),
+        compiler_params=params(),
+        cost_estimate=pl.CostEstimate(
+            flops=0, bytes_accessed=4 * len(arrays) * arrays[0].size, transcendentals=0
+        ),
+        name="stack",
+    )(*arrays)
 
 
 def mix_body(n_tensor, counts, split, info_ref, ctx_ref, *refs):
@@ -469,7 +504,7 @@
     beside = tensor(weight, 1)
     rest = weight[:, 2 * cut :]
     mine, beside, context = barrier((mine, beside, context))
-    ctx = jnp.stack([context[0]] + [tensor(context[m], m) for m in range(1, n_tensor)])
+    ctx = stack([context[0]] + [tensor(context[m], m) for m in range(1, n_tensor)])
     other, mine_beside = dp(mine, 1), tensor(mine, 1)
     rest, other, mine_beside, ctx = barrier((rest, other, mine_beside, ctx))
     rest, other_beside = tensor(rest, 2), tensor(other, 1)

time: 78.3 us -> 78.7 us (level)
  other arithmetic: 1.05 us -> 0.08 us
  local copies, waits for them, and re-layouts: 1.05 us -> 1.96 us
    another operation x1 -> x0, other arithmetic: 0.97 us -> none  [gather_small(): jnp.stack([context[0]] + [tensor(context[m], m) for m in range(1, n_tenso...]
    unnamed x6 -> x8, local copies, waits for them, and re-layouts: 0.01 us -> 0.92 us
    pallas_call x1 -> x2, Pallas kernels: 4.82 us -> 4.98 us  [the longest x1 4.95 us: attend(): pl.pallas_call(functools.partial(attend_body, blocks if split else 1), in...]
  transfers between devices with their start and end apart: 27 -> 27, of which waited for: 16 -> 16; matrix products, arithmetic and copies ran while one was open for 3% -> 1% of each run, Pallas kernels for 17% -> 17%
where the time goes in v13:
time: 78.7 us; the launch traced here: 78.5 us
  waiting for transfers between devices  32.9 us (42%)
  starting transfers between devices  27.4 us (35%)
  Pallas kernels  14 us (18%)
  between operations  2.08 us (3%)
  local copies, waits for them, and re-layouts  1.96 us (2%)
    ppermute x22, waiting for transfers between devices, swap(): return lax.ppermute(x, axis, [(i, i ^ mask) for i in range(n)])  27.1 us
    ppermute x22, starting transfers between devices, swap(): return lax.ppermute(x, axis, [(i, i ^ mask) for i in range(n)])  19.4 us
    ppermute x5, starting transfers between devices, swap_far(): lax.ppermute(x, ('dp', 'tensor'), [(i, i ^ mask) for i in range(n_dp * n_...  8.03 us
    ppermute x5, waiting for transfers between devices, swap_far(): lax.ppermute(x, ('dp', 'tensor'), [(i, i ^ mask) for i in range(n_dp * n_...  5.86 us
    pallas_call x1, Pallas kernels, attend(): pl.pallas_call(functools.partial(attend_body, blocks if split else 1), in...  4.95 us
    pallas_call x1, Pallas kernels, join(): pl.pallas_call(functools.partial(join_body, plan, len(late)), in_specs=[S...  4.05 us
    pallas_call x2, Pallas kernels, gradient(): pl.pallas_call(functools.partial(grad_body, plan, dout, [len(c) for c in...  2.49 us
  transfers between devices with their start and end apart: 27, of which 16 were waited for; matrix products, arithmetic and copies ran while one was open for 1% of the time, Pallas kernels for 17%

profile of v13, /device:TPU:0, one launch (start us, length us, event | category | flops | bytes accessed | tf_op | source)
XLA Modules:
  0.0 78.5 jit_solution(6960816842162556704)
XLA Ops:
  2.1 2.6 %collective-permute-start = (bf16[256,512]{1,0:T(8,128)(2,1)S(1)}, bf16[256,512]{1,0:T(8,128)(2,1)S(1)}, u32[]{:S(2)}, u32[]{:S(2)}) collective-permute-start(bf16[256,512]{1,0:T(8,128)(2,1)S(1)} %dynamic-slice_bitcast_fusion), channel_id=1, source_target_pairs={{0,2},{1,3},{2,0},{3,1},{4,6},{5,7},{6,4},{7,5},{8,10},{9,11},{10,... | collective-permute-start | bytes 786440 | tf_op jit(solution)/shard_map/ppermute | solution.py:448
  5.4 4.9 %attend.1 = (bf16[256,256]{1,0:T(8,128)(2,1)}, bf16[256,256]{1,0:T(8,128)(2,1)}, bf16[256,256]{1,0:T(8,128)(2,1)}, bf16[256,256]{1,0:T(8,128)(2,1)}) custom-call(s32[1]{0:T(128)S(6)} %copy.12.len_ref, s32[1]{0:T(128)} %bitcast.me_ref, bf16[1024,256]{1,0:T(8,128)(2,1)} %bitcast.16, bf16[1024,256]{1,0:T(8,128)(2,1)} %bitcast.17, bf16[1024,256]{1,0:T(8,128)(2,1)} %bitcast.18), custom_call_target="tpu_custom_call" | custom-call | flops 1073741824 | bytes 2097152 | tf_op jit(solution)/shard_map/attend/pallas_call | solution.py:93
  10.3 1.3 %collective-permute-done.refs_2_ = bf16[256,512]{1,0:T(8,128)(2,1)S(1)} collective-permute-done((bf16[256,512]{1,0:T(8,128)(2,1)S(1)}, bf16[256,512]{1,0:T(8,128)(2,1)S(1)}, u32[]{:S(2)}, u32[]{:S(2)}) %collective-permute-start) | collective-permute-done | bytes 262176 | tf_op jit(solution)/shard_map/ppermute | solution.py:448
  11.7 1.7 %collective-permute-start.2 = (bf16[256,512]{1,0:T(8,128)(2,1)S(1)}, bf16[256,512]{1,0:T(8,128)(2,1)S(1)}, u32[]{:S(2)}, u32[]{:S(2)}) collective-permute-start(bf16[256,512]{1,0:T(8,128)(2,1)S(1)} %collective-permute-done.refs_2_), channel_id=1, source_target_pairs={{0,4},{4,0},{8,12},{12,8},{16,20},{20,16},{24,28},{28,24},{1,5},{5... | collective-permute-start | bytes 786440 | tf_op jit(solution)/shard_map/ppermute | solution.py:448
  13.9 1.5 %collective-permute-start.5 = (bf16[256,256]{1,0:T(8,128)(2,1)}, bf16[256,256]{1,0:T(8,128)(2,1)S(1)}, u32[]{:S(2)}, u32[]{:S(2)}) collective-permute-start(bf16[256,256]{1,0:T(8,128)(2,1)} %get-tuple-element.58), channel_id=1, source_target_pairs={{0,2},{1,3},{2,0},{3,1},{4,6},{5,7},{6,4},{7,5},{8,10},{9,11},{10,... | collective-permute-start | bytes 393224 | tf_op jit(solution)/shard_map/ppermute | solution.py:448
  15.5 4.9 %collective-permute-done.5.refs_2_ = bf16[256,256]{1,0:T(8,128)(2,1)S(1)} collective-permute-done((bf16[256,256]{1,0:T(8,128)(2,1)}, bf16[256,256]{1,0:T(8,128)(2,1)S(1)}, u32[]{:S(2)}, u32[]{:S(2)}) %collective-permute-start.5) | collective-permute-done | bytes 131104 | tf_op jit(solution)/shard_map/ppermute | solution.py:448
  22.5 1.6 %collective-permute-start.10 = (bf16[4,256,256]{2,1,0:T(8,128)(2,1)S(1)}, bf16[4,256,256]{2,1,0:T(8,128)(2,1)S(1)}, u32[]{:S(2)}, u32[]{:S(2)}) collective-permute-start(bf16[4,256,256]{2,1,0:T(8,128)(2,1)S(1)} %stack.13.ctx_ref.refs_0_), channel_id=1, source_target_pairs={{0,8},{4,12},{8,0},{12,4},{16,24},{20,28},{24,16},{28,20},{1,9},{5... | collective-permute-start | bytes 1572872 | tf_op jit(solution)/shard_map/ppermute | solution.py:448
  24.1 1.4 %collective-permute-start.7 = (bf16[256,1024]{1,0:T(8,128)(2,1)S(1)}, bf16[256,1024]{1,0:T(8,128)(2,1)S(1)}, u32[]{:S(2)}, u32[]{:S(2)}) collective-permute-start(bf16[256,1024]{1,0:T(8,128)(2,1)S(1)} %slice.12), channel_id=1, source_target_pairs={{0,2},{1,3},{2,0},{3,1},{4,6},{5,7},{6,4},{7,5},{8,10},{9,11},{10,... | collective-permute-start | bytes 1572872 | tf_op jit(solution)/shard_map/ppermute | solution.py:448
  27.6 1.6 %mix.1 = (f32[256,2048]{1,0:T(8,128)S(1)}, f32[256,128]{1,0:T(8,128)S(1)}, bf16[4,256,256]{2,1,0:T(8,128)(2,1)S(1)}) custom-call(s32[4]{0:T(128)S(1)} %pad_add_fusion.info_ref, bf16[4,256,256]{2,1,0:T(8,128)(2,1)S(1)} %stack.13.ctx_ref.refs_0_, bf16[256,2048]{1,0:T(8,128)(2,1)S(1)} %bitcast.14, bf16[256,2048]{1,0:T(8,128)(2,1)S(1)} %collective-permute-done.1.refs_1_, ...), custom_call_target="tpu_custom_call" | custom-call | flops 1073741824 | bytes 6291456 | tf_op jit(solution)/shard_map/mix/pallas_call | solution.py:165
  29.1 7.9 %collective-permute-done.10.refs_2_ = bf16[4,256,256]{2,1,0:T(8,128)(2,1)S(1)} collective-permute-done((bf16[4,256,256]{2,1,0:T(8,128)(2,1)S(1)}, bf16[4,256,256]{2,1,0:T(8,128)(2,1)S(1)}, u32[]{:S(2)}, u32[]{:S(2)}) %collective-permute-start.10) | collective-permute-done | bytes 524320 | tf_op jit(solution)/shard_map/ppermute | solution.py:448
  37.0 1.3 %collective-permute-done.7.refs_0_ = bf16[256,1024]{1,0:T(8,128)(2,1)S(1)} collective-permute-done((bf16[256,1024]{1,0:T(8,128)(2,1)S(1)}, bf16[256,1024]{1,0:T(8,128)(2,1)S(1)}, u32[]{:S(2)}, u32[]{:S(2)}) %collective-permute-start.7) | collective-permute-done | bytes 524320 | tf_op jit(solution)/shard_map/ppermute | solution.py:448
  41.5 4.1 %join.1 = (bf16[256,2048]{1,0:T(8,128)(2,1)}, bf16[288,256]{1,0:T(8,128)(2,1)S(1)}, bf16[288,256]{1,0:T(8,128)(2,1)S(1)}, bf16[288,256]{1,0:T(8,128)(2,1)S(1)}, ...) custom-call(s32[4]{0:T(128)S(1)} %pad_add_fusion.info_ref, ...), custom_call_target="tpu_custom_call" | custom-call | flops 134217728 | bytes 6291456 | tf_op jit(solution)/shard_map/join/pallas_call | solution.py:278
  46.3 1.6 %collective-permute-start.22 = (bf16[256,256]{1,0:T(8,128)(2,1)S(1)}, bf16[256,256]{1,0:T(8,128)(2,1)S(1)}, u32[]{:S(2)}, u32[]{:S(2)}) collective-permute-start(bf16[256,256]{1,0:T(8,128)(2,1)S(1)} %get-tuple-element.87), channel_id=1, source_target_pairs={{0,8},{4,12},{8,0},{12,4},{16,24},{20,28},{24,16},{28,20},{1,9},{5... | collective-permute-start | bytes 393224 | tf_op jit(solution)/shard_map/ppermute | solution.py:448
  49.8 1.6 %collective-permute-start.15 = (bf16[288,256]{1,0:T(8,128)(2,1)S(1)}, bf16[288,256]{1,0:T(8,128)(2,1)S(1)}, u32[]{:S(2)}, u32[]{:S(2)}) collective-permute-start(bf16[288,256]{1,0:T(8,128)(2,1)S(1)} %get-tuple-element.77), channel_id=1, source_target_pairs={{0,8},{4,12},{8,0},{12,4},{16,24},{20,28},{24,16},{28,20},{1,9},{5... | collective-permute-start | bytes 442376 | tf_op jit(solution)/shard_map/ppermute | solution.py:448
  51.4 1.3 %collective-permute-done.21.refs_6_ = bf16[256,256]{1,0:T(8,128)(2,1)S(1)} collective-permute-done((bf16[256,256]{1,0:T(8,128)(2,1)S(1)}, bf16[256,256]{1,0:T(8,128)(2,1)S(1)}, u32[]{:S(2)}, u32[]{:S(2)}) %collective-permute-start.21) | collective-permute-done | bytes 131104 | tf_op jit(solution)/shard_map/ppermute | solution.py:448
  52.6 1.9 %collective-permute-start.16 = (bf16[288,256]{1,0:T(8,128)(2,1)S(1)}, bf16[288,256]{1,0:T(8,128)(2,1)S(1)}, u32[]{:S(2)}, u32[]{:S(2)}) collective-permute-start(bf16[288,256]{1,0:T(8,128)(2,1)S(1)} %get-tuple-element.78), channel_id=1, source_target_pairs={{0,12},{4,8},{8,4},{12,0},{16,28},{20,24},{24,20},{28,16},{1,13},{... | collective-permute-start | bytes 442376 | tf_op jit(solution)/shard_map/ppermute | solution.py:448
  54.5 1.7 %collective-permute-done.23.refs_8_ = bf16[256,256]{1,0:T(8,128)(2,1)S(1)} collective-permute-done((bf16[256,256]{1,0:T(8,128)(2,1)S(1)}, bf16[256,256]{1,0:T(8,128)(2,1)S(1)}, u32[]{:S(2)}, u32[]{:S(2)}) %collective-permute-start.23) | collective-permute-done | bytes 131104 | tf_op jit(solution)/shard_map/ppermute | solution.py:448
  56.2 1.2 %gradient.3 = (bf16[2,2,256,128]{3,2,1,0:T(8,128)(2,1)S(1)}, bf16[2,2,256,128]{3,2,1,0:T(8,128)(2,1)S(1)}) custom-call(s32[4]{0:T(128)S(1)} %pad_add_fusion.info_ref, bf16[4,256,256]{2,1,0:T(8,128)(2,1)S(1)} %stack.13.ctx_ref.refs_0_, bf16[4,256,256]{2,1,0:T(8,128)(2,1)S(1)} %collective-permute-done.9.refs_1_, ...), custom_call_target="tpu_custom_call" | custom-call | flops 536870912 | bytes 3145728 | tf_op jit(solution)/shard_map/gradient/pallas_call | solution.py:361
  58.7 2.7 %collective-permute-done.16.refs_8_ = bf16[288,256]{1,0:T(8,128)(2,1)S(1)} collective-permute-done((bf16[288,256]{1,0:T(8,128)(2,1)S(1)}, bf16[288,256]{1,0:T(8,128)(2,1)S(1)}, u32[]{:S(2)}, u32[]{:S(2)}) %collective-permute-start.16) | collective-permute-done | bytes 147488 | tf_op jit(solution)/shard_map/ppermute | solution.py:448
  61.4 1.2 %gradient.2 = (bf16[2,2,304,128]{3,2,1,0:T(8,128)(2,1)S(1)}, bf16[2,2,304,128]{3,2,1,0:T(8,128)(2,1)S(1)}) custom-call(s32[4]{0:T(128)S(1)} %pad_add_fusion.info_ref, bf16[4,256,256]{2,1,0:T(8,128)(2,1)S(1)} %stack.13.ctx_ref.refs_0_, bf16[4,256,256]{2,1,0:T(8,128)(2,1)S(1)} %collective-permute-done.9.refs_1_, ...), custom_call_target="tpu_custom_call" | custom-call | flops 536870912 | bytes 3145728 | tf_op jit(solution)/shard_map/gradient/pallas_call | solution.py:361
  64.4 2.7 %collective-permute-start.18 = (bf16[1,1,304,128]{3,2,1,0:T(8,128)(2,1)S(1)}, bf16[1,1,304,128]{3,2,1,0:T(8,128)(2,1)S(1)}, u32[]{:S(2)}, u32[]{:S(2)}) collective-permute-start(bf16[1,1,304,128]{3,2,1,0:T(8,128)(2,1)S(1)} %get-tuple-element.82), channel_id=1, source_target_pairs={{0,16},{1,17},{2,18},{3,19},{4,20},{5,21},{6,22},{7,23},{8,24},{9,... | collective-permute-start | bytes 233480 | tf_op jit(solution)/shard_map/ppermute | solution.py:453
  67.6 1.2 %collective-permute-start.20 = (bf16[1,1,304,128]{3,2,1,0:T(8,128)(2,1)S(1)}, bf16[1,1,304,128]{3,2,1,0:T(8,128)(2,1)S(1)}, u32[]{:S(2)}, u32[]{:S(2)}) collective-permute-start(bf16[1,1,304,128]{3,2,1,0:T(8,128)(2,1)S(1)} %get-tuple-element.84), channel_id=1, source_target_pairs={{0,18},{1,19},{2,16},{3,17},{4,22},{5,23},{6,20},{7,21},{8,26},{9,... | collective-permute-start | bytes 233480 | tf_op jit(solution)/shard_map/ppermute | solution.py:453
  68.9 3.0 %collective-permute-start.26 = (bf16[1,1,256,128]{3,2,1,0:T(8,128)(2,1)S(1)}, bf16[1,1,256,128]{3,2,1,0:T(8,128)(2,1)S(1)}, u32[]{:S(2)}, u32[]{:S(2)}) collective-permute-start(bf16[1,1,256,128]{3,2,1,0:T(8,128)(2,1)S(1)} %get-tuple-element.94), channel_id=1, source_target_pairs={{0,16},{1,17},{2,18},{3,19},{4,20},{5,21},{6,22},{7,23},{8,24},{9,... | collective-permute-start | bytes 196616 | tf_op jit(solution)/shard_map/ppermute | solution.py:453
  71.8 4.8 %collective-permute-done.20.refs_3_ = bf16[1,1,304,128]{3,2,1,0:T(8,128)(2,1)S(1)} collective-permute-done((bf16[1,1,304,128]{3,2,1,0:T(8,128)(2,1)S(1)}, bf16[1,1,304,128]{3,2,1,0:T(8,128)(2,1)S(1)}, u32[]{:S(2)}, u32[]{:S(2)}) %collective-permute-start.20) | collective-permute-done | bytes 77856 | tf_op jit(solution)/shard_map/ppermute | solution.py:453
  (53 shorter events, 16.6 us)
Async XLA Ops:
  0.6 11.1 %collective-permute-start.1 = (bf16[256,2048]{1,0:T(8,128)(2,1)}, bf16[256,2048]{1,0:T(8,128)(2,1)S(1)}, u32[]{:S(2)}, u32[]{:S(2)}) collective-permute-start(bf16[256,2048]{1,0:T(8,128)(2,1)} %bitcast.12), channel_id=1, source_target_pairs={{0,1},{1,0},{2,3},{3,2},{4,5},{5,4},{6,7},{7,6},{8,9},{9,8},{10,11... | collective-permute-start | bytes 3145736 | tf_op jit(solution)/shard_map/ppermute | solution.py:448
  2.1 9.6 %collective-permute-start = (bf16[256,512]{1,0:T(8,128)(2,1)S(1)}, bf16[256,512]{1,0:T(8,128)(2,1)S(1)}, u32[]{:S(2)}, u32[]{:S(2)}) collective-permute-start(bf16[256,512]{1,0:T(8,128)(2,1)S(1)} %dynamic-slice_bitcast_fusion), channel_id=1, source_target_pairs={{0,2},{1,3},{2,0},{3,1},{4,6},{5,7},{6,4},{7,5},{8,10},{9,11},{10,... | collective-permute-start | bytes 786440 | tf_op jit(solution)/shard_map/ppermute | solution.py:448
  11.7 10.7 %collective-permute-start.2 = (bf16[256,512]{1,0:T(8,128)(2,1)S(1)}, bf16[256,512]{1,0:T(8,128)(2,1)S(1)}, u32[]{:S(2)}, u32[]{:S(2)}) collective-permute-start(bf16[256,512]{1,0:T(8,128)(2,1)S(1)} %collective-permute-done.refs_2_), channel_id=1, source_target_pairs={{0,4},{4,0},{8,12},{12,8},{16,20},{20,16},{24,28},{28,24},{1,5},{5... | collective-permute-start | bytes 786440 | tf_op jit(solution)/shard_map/ppermute | solution.py:448
  13.4 9.0 %collective-permute-start.3 = (bf16[256,512]{1,0:T(8,128)(2,1)S(1)}, bf16[256,512]{1,0:T(8,128)(2,1)S(1)}, u32[]{:S(2)}, u32[]{:S(2)}) collective-permute-start(bf16[256,512]{1,0:T(8,128)(2,1)S(1)} %collective-permute-done.refs_2_), channel_id=1, source_target_pairs={{0,1},{1,0},{2,3},{3,2},{4,5},{5,4},{6,7},{7,6},{8,9},{9,8},{10,11... | collective-permute-start | bytes 786440 | tf_op jit(solution)/shard_map/ppermute | solution.py:448
  13.4 2.1 %collective-permute-start.4 = (bf16[256,256]{1,0:T(8,128)(2,1)}, bf16[256,256]{1,0:T(8,128)(2,1)S(1)}, u32[]{:S(2)}, u32[]{:S(2)}) collective-permute-start(bf16[256,256]{1,0:T(8,128)(2,1)} %get-tuple-element.57), channel_id=1, source_target_pairs={{0,1},{1,0},{2,3},{3,2},{4,5},{5,4},{6,7},{7,6},{8,9},{9,8},{10,11... | collective-permute-start | bytes 393224 | tf_op jit(solution)/shard_map/ppermute | solution.py:448
  13.9 6.5 %collective-permute-start.5 = (bf16[256,256]{1,0:T(8,128)(2,1)}, bf16[256,256]{1,0:T(8,128)(2,1)S(1)}, u32[]{:S(2)}, u32[]{:S(2)}) collective-permute-start(bf16[256,256]{1,0:T(8,128)(2,1)} %get-tuple-element.58), channel_id=1, source_target_pairs={{0,2},{1,3},{2,0},{3,1},{4,6},{5,7},{6,4},{7,5},{8,10},{9,11},{10,... | collective-permute-start | bytes 393224 | tf_op jit(solution)/shard_map/ppermute | solution.py:448
  15.4 6.0 %collective-permute-start.6 = (bf16[256,256]{1,0:T(8,128)(2,1)}, bf16[256,256]{1,0:T(8,128)(2,1)S(1)}, u32[]{:S(2)}, u32[]{:S(2)}) collective-permute-start(bf16[256,256]{1,0:T(8,128)(2,1)} %get-tuple-element.59), channel_id=1, source_target_pairs={{0,3},{1,2},{2,1},{3,0},{4,7},{5,6},{6,5},{7,4},{8,11},{9,10},{10,... | collective-permute-start | bytes 393224 | tf_op jit(solution)/shard_map/ppermute | solution.py:448
  22.5 14.6 %collective-permute-start.10 = (bf16[4,256,256]{2,1,0:T(8,128)(2,1)S(1)}, bf16[4,256,256]{2,1,0:T(8,128)(2,1)S(1)}, u32[]{:S(2)}, u32[]{:S(2)}) collective-permute-start(bf16[4,256,256]{2,1,0:T(8,128)(2,1)S(1)} %stack.13.ctx_ref.refs_0_), channel_id=1, source_target_pairs={{0,8},{4,12},{8,0},{12,4},{16,24},{20,28},{24,16},{28,20},{1,9},{5... | collective-permute-start | bytes 1572872 | tf_op jit(solution)/shard_map/ppermute | solution.py:448
  24.1 14.3 %collective-permute-start.7 = (bf16[256,1024]{1,0:T(8,128)(2,1)S(1)}, bf16[256,1024]{1,0:T(8,128)(2,1)S(1)}, u32[]{:S(2)}, u32[]{:S(2)}) collective-permute-start(bf16[256,1024]{1,0:T(8,128)(2,1)S(1)} %slice.12), channel_id=1, source_target_pairs={{0,2},{1,3},{2,0},{3,1},{4,6},{5,7},{6,4},{7,5},{8,10},{9,11},{10,... | collective-permute-start | bytes 1572872 | tf_op jit(solution)/shard_map/ppermute | solution.py:448
  25.5 14.1 %collective-permute-start.9 = (bf16[4,256,256]{2,1,0:T(8,128)(2,1)S(1)}, bf16[4,256,256]{2,1,0:T(8,128)(2,1)S(1)}, u32[]{:S(2)}, u32[]{:S(2)}) collective-permute-start(bf16[4,256,256]{2,1,0:T(8,128)(2,1)S(1)} %stack.13.ctx_ref.refs_0_), channel_id=1, source_target_pairs={{0,4},{4,0},{8,12},{12,8},{16,20},{20,16},{24,28},{28,24},{1,5},{5... | collective-permute-start | bytes 1572872 | tf_op jit(solution)/shard_map/ppermute | solution.py:448
  39.6 9.4 %collective-permute-start.12 = (bf16[4,128,256]{2,1,0:T(8,128)(2,1)S(1)}, bf16[4,128,256]{2,1,0:T(8,128)(2,1)S(1)}, u32[]{:S(2)}, u32[]{:S(2)}) collective-permute-start(bf16[4,128,256]{2,1,0:T(8,128)(2,1)S(1)} %slice.10), channel_id=1, source_target_pairs={{0,8},{4,12},{8,0},{12,4},{16,24},{20,28},{24,16},{28,20},{1,9},{5... | collective-permute-start | bytes 786440 | tf_op jit(solution)/shard_map/ppermute | solution.py:448
  40.1 9.7 %collective-permute-start.13 = (bf16[4,128,256]{2,1,0:T(8,128)(2,1)S(1)}, bf16[4,128,256]{2,1,0:T(8,128)(2,1)S(1)}, u32[]{:S(2)}, u32[]{:S(2)}) collective-permute-start(bf16[4,128,256]{2,1,0:T(8,128)(2,1)S(1)} %slice.11), channel_id=1, source_target_pairs={{0,4},{4,0},{8,12},{12,8},{16,20},{20,16},{24,28},{28,24},{1,5},{5... | collective-permute-start | bytes 786440 | tf_op jit(solution)/shard_map/ppermute | solution.py:448
  45.5 7.1 %collective-permute-start.21 = (bf16[256,256]{1,0:T(8,128)(2,1)S(1)}, bf16[256,256]{1,0:T(8,128)(2,1)S(1)}, u32[]{:S(2)}, u32[]{:S(2)}) collective-permute-start(bf16[256,256]{1,0:T(8,128)(2,1)S(1)} %get-tuple-element.86), channel_id=1, source_target_pairs={{0,4},{4,0},{8,12},{12,8},{16,20},{20,16},{24,28},{28,24},{1,5},{5... | collective-permute-start | bytes 393224 | tf_op jit(solution)/shard_map/ppermute | solution.py:448
  46.3 8.2 %collective-permute-start.22 = (bf16[256,256]{1,0:T(8,128)(2,1)S(1)}, bf16[256,256]{1,0:T(8,128)(2,1)S(1)}, u32[]{:S(2)}, u32[]{:S(2)}) collective-permute-start(bf16[256,256]{1,0:T(8,128)(2,1)S(1)} %get-tuple-element.87), channel_id=1, source_target_pairs={{0,8},{4,12},{8,0},{12,4},{16,24},{20,28},{24,16},{28,20},{1,9},{5... | collective-permute-start | bytes 393224 | tf_op jit(solution)/shard_map/ppermute | solution.py:448
  47.9 8.3 %collective-permute-start.23 = (bf16[256,256]{1,0:T(8,128)(2,1)S(1)}, bf16[256,256]{1,0:T(8,128)(2,1)S(1)}, u32[]{:S(2)}, u32[]{:S(2)}) collective-permute-start(bf16[256,256]{1,0:T(8,128)(2,1)S(1)} %get-tuple-element.88), channel_id=1, source_target_pairs={{0,12},{4,8},{8,4},{12,0},{16,28},{20,24},{24,20},{28,16},{1,13},{... | collective-permute-start | bytes 393224 | tf_op jit(solution)/shard_map/ppermute | solution.py:448
  49.0 8.7 %collective-permute-start.14 = (bf16[288,256]{1,0:T(8,128)(2,1)S(1)}, bf16[288,256]{1,0:T(8,128)(2,1)S(1)}, u32[]{:S(2)}, u32[]{:S(2)}) collective-permute-start(bf16[288,256]{1,0:T(8,128)(2,1)S(1)} %get-tuple-element.76), channel_id=1, source_target_pairs={{0,4},{4,0},{8,12},{12,8},{16,20},{20,16},{24,28},{28,24},{1,5},{5... | collective-permute-start | bytes 442376 | tf_op jit(solution)/shard_map/ppermute | solution.py:448
  49.8 8.9 %collective-permute-start.15 = (bf16[288,256]{1,0:T(8,128)(2,1)S(1)}, bf16[288,256]{1,0:T(8,128)(2,1)S(1)}, u32[]{:S(2)}, u32[]{:S(2)}) collective-permute-start(bf16[288,256]{1,0:T(8,128)(2,1)S(1)} %get-tuple-element.77), channel_id=1, source_target_pairs={{0,8},{4,12},{8,0},{12,4},{16,24},{20,28},{24,16},{28,20},{1,9},{5... | collective-permute-start | bytes 442376 | tf_op jit(solution)/shard_map/ppermute | solution.py:448
  52.6 8.8 %collective-permute-start.16 = (bf16[288,256]{1,0:T(8,128)(2,1)S(1)}, bf16[288,256]{1,0:T(8,128)(2,1)S(1)}, u32[]{:S(2)}, u32[]{:S(2)}) collective-permute-start(bf16[288,256]{1,0:T(8,128)(2,1)S(1)} %get-tuple-element.78), channel_id=1, source_target_pairs={{0,12},{4,8},{8,4},{12,0},{16,28},{20,24},{24,20},{28,16},{1,13},{... | collective-permute-start | bytes 442376 | tf_op jit(solution)/shard_map/ppermute | solution.py:448
  57.4 5.3 %collective-permute-start.24 = (bf16[2,2,256,128]{3,2,1,0:T(8,128)(2,1)S(1)}, bf16[2,2,256,128]{3,2,1,0:T(8,128)(2,1)S(1)}, u32[]{:S(2)}, u32[]{:S(2)}) collective-permute-start(bf16[2,2,256,128]{3,2,1,0:T(8,128)(2,1)S(1)} %get-tuple-element.90), channel_id=1, source_target_pairs={{0,1},{1,0},{2,3},{3,2},{4,5},{5,4},{6,7},{7,6},{8,9},{9,8},{10,11... | collective-permute-start | bytes 786440 | tf_op jit(solution)/shard_map/ppermute | solution.py:448
  62.8 6.0 %collective-permute-start.25 = (bf16[1,2,256,128]{3,2,1,0:T(8,128)(2,1)S(1)}, bf16[1,2,256,128]{3,2,1,0:T(8,128)(2,1)S(1)}, u32[]{:S(2)}, u32[]{:S(2)}) collective-permute-start(bf16[1,2,256,128]{3,2,1,0:T(8,128)(2,1)S(1)} %get-tuple-element.92), channel_id=1, source_target_pairs={{0,2},{1,3},{2,0},{3,1},{4,6},{5,7},{6,4},{7,5},{8,10},{9,11},{10,... | collective-permute-start | bytes 393224 | tf_op jit(solution)/shard_map/ppermute | solution.py:453
  64.4 7.5 %collective-permute-start.18 = (bf16[1,1,304,128]{3,2,1,0:T(8,128)(2,1)S(1)}, bf16[1,1,304,128]{3,2,1,0:T(8,128)(2,1)S(1)}, u32[]{:S(2)}, u32[]{:S(2)}) collective-permute-start(bf16[1,1,304,128]{3,2,1,0:T(8,128)(2,1)S(1)} %get-tuple-element.82), channel_id=1, source_target_pairs={{0,16},{1,17},{2,18},{3,19},{4,20},{5,21},{6,22},{7,23},{8,24},{9,... | collective-permute-start | bytes 233480 | tf_op jit(solution)/shard_map/ppermute | solution.py:453
  67.0 4.8 %collective-permute-start.19 = (bf16[1,1,304,128]{3,2,1,0:T(8,128)(2,1)S(1)}, bf16[1,1,304,128]{3,2,1,0:T(8,128)(2,1)S(1)}, u32[]{:S(2)}, u32[]{:S(2)}) collective-permute-start(bf16[1,1,304,128]{3,2,1,0:T(8,128)(2,1)S(1)} %get-tuple-element.83), channel_id=1, source_target_pairs={{0,2},{1,3},{2,0},{3,1},{4,6},{5,7},{6,4},{7,5},{8,10},{9,11},{10,... | collective-permute-start | bytes 233480 | tf_op jit(solution)/shard_map/ppermute | solution.py:453
  67.6 9.1 %collective-permute-start.20 = (bf16[1,1,304,128]{3,2,1,0:T(8,128)(2,1)S(1)}, bf16[1,1,304,128]{3,2,1,0:T(8,128)(2,1)S(1)}, u32[]{:S(2)}, u32[]{:S(2)}) collective-permute-start(bf16[1,1,304,128]{3,2,1,0:T(8,128)(2,1)S(1)} %get-tuple-element.84), channel_id=1, source_target_pairs={{0,18},{1,19},{2,16},{3,17},{4,22},{5,23},{6,20},{7,21},{8,26},{9,... | collective-permute-start | bytes 233480 | tf_op jit(solution)/shard_map/ppermute | solution.py:453
  68.9 8.8 %collective-permute-start.26 = (bf16[1,1,256,128]{3,2,1,0:T(8,128)(2,1)S(1)}, bf16[1,1,256,128]{3,2,1,0:T(8,128)(2,1)S(1)}, u32[]{:S(2)}, u32[]{:S(2)}) collective-permute-start(bf16[1,1,256,128]{3,2,1,0:T(8,128)(2,1)S(1)} %get-tuple-element.94), channel_id=1, source_target_pairs={{0,16},{1,17},{2,18},{3,19},{4,20},{5,21},{6,22},{7,23},{8,24},{9,... | collective-permute-start | bytes 196616 | tf_op jit(solution)/shard_map/ppermute | solution.py:453
  (7 other events, 48.7 us)

commit v14 on v11

--- a/solution.py
+++ b/solution.py
@@ -466,13 +466,12 @@
     dout = weight.shape[1]
     cut = dout // 4
     mine = tensor(lax.dynamic_slice_in_dim(weight, side * cut, cut, 1), 2)
-    beside = tensor(weight, 1)
     rest = weight[:, 2 * cut :]
-    mine, beside, context = barrier((mine, beside, context))
+    mine, context = barrier((mine, context))
     ctx = jnp.stack([context[0]] + [tensor(context[m], m) for m in range(1, n_tensor)])
     other, mine_beside = dp(mine, 1), tensor(mine, 1)
-    rest, other, mine_beside, ctx = barrier((rest, other, mine_beside, ctx))
-    rest, other_beside = tensor(rest, 2), tensor(other, 1)
+    rest, other, mine_beside, ctx, own = barrier((rest, other, mine_beside, ctx, weight))
+    rest, other_beside, beside = tensor(rest, 2), tensor(other, 1), tensor(own, 1)
     ctx_x, ctx_z = dp(ctx, 1), dp(ctx, 2)
     early = mix(info, ctx, [[weight], [beside], [mine, other], [mine_beside, other_beside]], True)
     rest, early, ctx_x, ctx_z = barrier((rest, early, ctx_x, ctx_z))
@@ -513,7 +512,7 @@
         near = [grads[j][0]] + [swap(grads[j][q], "dp", n_dp, q) for q in range(1, NEAR)]
         keep, send = gradient(plan, dout, info, ctxs, near)
         got = swap(send, "tensor", n_tensor, 1)
-        parts.append(exchange_far(plan, j == chunks - 1, dout, width, keep, got))
+        parts.append(exchange_far(plan, True, dout, width, keep, got))
     weight_grad, gain_grad, loss = finish(plan, dout, width, parts)
     return (hidden, weight_grad[None], gain_grad.reshape(dout), loss.reshape(()))
 

time: 78.3 us -> 79.6 us (1.017)
  waiting for transfers between devices: 32.4 us -> 35 us
  starting transfers between devices: 27.6 us -> 26.3 us
    ppermute x5 -> x4, waiting for transfers between devices: 5.86 us -> 8.62 us  [swap_far(): lax.ppermute(x, ('dp', 'tensor'), [(i, i ^ mask) for i in range(n_dp * n_...]
    ppermute x5 -> x4, starting transfers between devices: 8 us -> 6.31 us  [swap_far(): lax.ppermute(x, ('dp', 'tensor'), [(i, i ^ mask) for i in range(n_dp * n_...]
  transfers between devices with their start and end apart: 27 -> 26, of which waited for: 16 -> 15; matrix products, arithmetic and copies ran while one was open for 3% -> 1% of each run, Pallas kernels for 17% -> 17%
where the time goes in v14:
time: 79.6 us; the launch traced here: 79.4 us
  waiting for transfers between devices  35 us (44%)
  starting transfers between devices  26.3 us (33%)
  Pallas kernels  13.9 us (17%)
  between operations  2.09 us (3%)
  local copies, waits for them, and re-layouts  1.06 us (1%)
  other arithmetic  1.05 us (1%)
    ppermute x22, waiting for transfers between devices, swap(): return lax.ppermute(x, axis, [(i, i ^ mask) for i in range(n)])  26.4 us
    ppermute x22, starting transfers between devices, swap(): return lax.ppermute(x, axis, [(i, i ^ mask) for i in range(n)])  20 us
    ppermute x4, waiting for transfers between devices, swap_far(): lax.ppermute(x, ('dp', 'tensor'), [(i, i ^ mask) for i in range(n_dp * n_...  8.62 us
    ppermute x4, starting transfers between devices, swap_far(): lax.ppermute(x, ('dp', 'tensor'), [(i, i ^ mask) for i in range(n_dp * n_...  6.31 us
    pallas_call x1, Pallas kernels, attend(): pl.pallas_call(attend_body, in_specs=[SM, SM, VM, VM, VM], out_specs=[VM]...  4.82 us
    pallas_call x1, Pallas kernels, join(): pl.pallas_call(functools.partial(join_body, plan, len(late)), in_specs=[S...  4.05 us
    pallas_call x2, Pallas kernels, gradient(): pl.pallas_call(functools.partial(grad_body, plan, dout, [len(c) for c in...  2.5 us
  transfers between devices with their start and end apart: 26, of which 15 were waited for; matrix products, arithmetic and copies ran while one was open for 1% of the time, Pallas kernels for 17%

profile of v14, /device:TPU:0, one launch (start us, length us, event | category | flops | bytes accessed | tf_op | source)
XLA Modules:
  0.0 79.4 jit_solution(12964451184267715897)
XLA Ops:
  1.6 3.0 %collective-permute-start = (bf16[256,512]{1,0:T(8,128)(2,1)S(1)}, bf16[256,512]{1,0:T(8,128)(2,1)S(1)}, u32[]{:S(2)}, u32[]{:S(2)}) collective-permute-start(bf16[256,512]{1,0:T(8,128)(2,1)S(1)} %dynamic-slice_bitcast_fusion), channel_id=1, source_target_pairs={{0,2},{1,3},{2,0},{3,1},{4,6},{5,7},{6,4},{7,5},{8,10},{9,11},{10,... | collective-permute-start | bytes 786440 | tf_op jit(solution)/shard_map/ppermute | solution.py:413
  5.3 4.8 %attend.1 = (bf16[256,256]{1,0:T(8,128)(2,1)}, bf16[256,256]{1,0:T(8,128)(2,1)}, bf16[256,256]{1,0:T(8,128)(2,1)}, bf16[256,256]{1,0:T(8,128)(2,1)}) custom-call(s32[1]{0:T(128)S(6)} %copy.12.len_ref, s32[1]{0:T(128)} %bitcast.me_ref, bf16[1024,256]{1,0:T(8,128)(2,1)} %bitcast.24, bf16[1024,256]{1,0:T(8,128)(2,1)} %bitcast.25, bf16[1024,256]{1,0:T(8,128)(2,1)} %bitcast.26), custom_call_target="tpu_custom_call" | custom-call | flops 1073741824 | bytes 2097152 | tf_op jit(solution)/shard_map/attend/pallas_call | solution.py:79
  11.0 1.7 %collective-permute-start.1 = (bf16[256,512]{1,0:T(8,128)(2,1)S(1)}, bf16[256,512]{1,0:T(8,128)(2,1)S(1)}, u32[]{:S(2)}, u32[]{:S(2)}) collective-permute-start(bf16[256,512]{1,0:T(8,128)(2,1)S(1)} %collective-permute-done.refs_2_), channel_id=1, source_target_pairs={{0,4},{4,0},{8,12},{12,8},{16,20},{20,16},{24,28},{28,24},{1,5},{5... | collective-permute-start | bytes 786440 | tf_op jit(solution)/shard_map/ppermute | solution.py:413
  12.7 1.6 %collective-permute-start.5 = (bf16[256,256]{1,0:T(8,128)(2,1)}, bf16[256,256]{1,0:T(8,128)(2,1)S(1)}, u32[]{:S(2)}, u32[]{:S(2)}) collective-permute-start(bf16[256,256]{1,0:T(8,128)(2,1)} %get-tuple-element.59), channel_id=1, source_target_pairs={{0,3},{1,2},{2,1},{3,0},{4,7},{5,6},{6,5},{7,4},{8,11},{9,10},{10,... | collective-permute-start | bytes 393224 | tf_op jit(solution)/shard_map/ppermute | solution.py:413
  14.9 3.6 %collective-permute-done.5 = bf16[256,256]{1,0:T(8,128)(2,1)S(1)} collective-permute-done((bf16[256,256]{1,0:T(8,128)(2,1)}, bf16[256,256]{1,0:T(8,128)(2,1)S(1)}, u32[]{:S(2)}, u32[]{:S(2)}) %collective-permute-start.5) | collective-permute-done | bytes 131104 | tf_op jit(solution)/shard_map/ppermute | solution.py:413
  18.5 3.0 %collective-permute-done.4 = bf16[256,256]{1,0:T(8,128)(2,1)S(1)} collective-permute-done((bf16[256,256]{1,0:T(8,128)(2,1)}, bf16[256,256]{1,0:T(8,128)(2,1)S(1)}, u32[]{:S(2)}, u32[]{:S(2)}) %collective-permute-start.4) | collective-permute-done | bytes 131104 | tf_op jit(solution)/shard_map/ppermute | solution.py:413
  22.6 1.6 %collective-permute-start.10 = (bf16[4,256,256]{2,1,0:T(8,128)(2,1)S(1)}, bf16[4,256,256]{2,1,0:T(8,128)(2,1)S(1)}, u32[]{:S(2)}, u32[]{:S(2)}) collective-permute-start(bf16[4,256,256]{2,1,0:T(8,128)(2,1)S(1)} %pad_maximum_fusion.ctx_ref.refs_0_), channel_id=1, source_target_pairs={{0,8},{4,12},{8,0},{12,4},{16,24},{20,28},{24,16},{28,20},{1,9},{5... | collective-permute-start | bytes 1572872 | tf_op jit(solution)/shard_map/ppermute | solution.py:413
  24.2 1.5 %collective-permute-start.6 = (bf16[256,1024]{1,0:T(8,128)(2,1)S(1)}, bf16[256,1024]{1,0:T(8,128)(2,1)S(1)}, u32[]{:S(2)}, u32[]{:S(2)}) collective-permute-start(bf16[256,1024]{1,0:T(8,128)(2,1)S(1)} %slice.12), channel_id=1, source_target_pairs={{0,2},{1,3},{2,0},{3,1},{4,6},{5,7},{6,4},{7,5},{8,10},{9,11},{10,... | collective-permute-start | bytes 1572872 | tf_op jit(solution)/shard_map/ppermute | solution.py:413
  27.8 1.5 %mix.1 = (f32[256,2048]{1,0:T(8,128)S(1)}, f32[256,128]{1,0:T(8,128)S(1)}, bf16[4,256,256]{2,1,0:T(8,128)(2,1)S(1)}) custom-call(s32[4]{0:T(128)S(1)} %pad_add_fusion.info_ref, bf16[4,256,256]{2,1,0:T(8,128)(2,1)S(1)} %pad_maximum_fusion.ctx_ref.refs_0_, bf16[256,2048]{1,0:T(8,128)(2,1)S(1)} %bitcast.18, ...), custom_call_target="tpu_custom_call" | custom-call | flops 1073741824 | bytes 6291456 | tf_op jit(solution)/shard_map/mix/pallas_call | solution.py:130
  29.4 7.5 %collective-permute-done.10.refs_2_ = bf16[4,256,256]{2,1,0:T(8,128)(2,1)S(1)} collective-permute-done((bf16[4,256,256]{2,1,0:T(8,128)(2,1)S(1)}, bf16[4,256,256]{2,1,0:T(8,128)(2,1)S(1)}, u32[]{:S(2)}, u32[]{:S(2)}) %collective-permute-start.10) | collective-permute-done | bytes 524320 | tf_op jit(solution)/shard_map/ppermute | solution.py:413
  36.9 1.3 %collective-permute-done.6.refs_0_ = bf16[256,1024]{1,0:T(8,128)(2,1)S(1)} collective-permute-done((bf16[256,1024]{1,0:T(8,128)(2,1)S(1)}, bf16[256,1024]{1,0:T(8,128)(2,1)S(1)}, u32[]{:S(2)}, u32[]{:S(2)}) %collective-permute-start.6) | collective-permute-done | bytes 524320 | tf_op jit(solution)/shard_map/ppermute | solution.py:413
  41.4 4.1 %join.1 = (bf16[256,2048]{1,0:T(8,128)(2,1)}, bf16[288,256]{1,0:T(8,128)(2,1)S(1)}, bf16[288,256]{1,0:T(8,128)(2,1)S(1)}, bf16[288,256]{1,0:T(8,128)(2,1)S(1)}, ...) custom-call(s32[4]{0:T(128)S(1)} %pad_add_fusion.info_ref, ...), custom_call_target="tpu_custom_call" | custom-call | flops 134217728 | bytes 6291456 | tf_op jit(solution)/shard_map/join/pallas_call | solution.py:243
  46.2 1.6 %collective-permute-start.15 = (bf16[288,256]{1,0:T(8,128)(2,1)S(1)}, bf16[288,256]{1,0:T(8,128)(2,1)S(1)}, u32[]{:S(2)}, u32[]{:S(2)}) collective-permute-start(bf16[288,256]{1,0:T(8,128)(2,1)S(1)} %get-tuple-element.77), channel_id=1, source_target_pairs={{0,8},{4,12},{8,0},{12,4},{16,24},{20,28},{24,16},{28,20},{1,9},{5... | collective-permute-start | bytes 442376 | tf_op jit(solution)/shard_map/ppermute | solution.py:413
  49.7 1.6 %collective-permute-start.21 = (bf16[256,256]{1,0:T(8,128)(2,1)S(1)}, bf16[256,256]{1,0:T(8,128)(2,1)S(1)}, u32[]{:S(2)}, u32[]{:S(2)}) collective-permute-start(bf16[256,256]{1,0:T(8,128)(2,1)S(1)} %get-tuple-element.87), channel_id=1, source_target_pairs={{0,8},{4,12},{8,0},{12,4},{16,24},{20,28},{24,16},{28,20},{1,9},{5... | collective-permute-start | bytes 393224 | tf_op jit(solution)/shard_map/ppermute | solution.py:413
  51.2 1.6 %collective-permute-done.14.refs_6_ = bf16[288,256]{1,0:T(8,128)(2,1)S(1)} collective-permute-done((bf16[288,256]{1,0:T(8,128)(2,1)S(1)}, bf16[288,256]{1,0:T(8,128)(2,1)S(1)}, u32[]{:S(2)}, u32[]{:S(2)}) %collective-permute-start.14) | collective-permute-done | bytes 147488 | tf_op jit(solution)/shard_map/ppermute | solution.py:413
  52.9 2.2 %collective-permute-start.22 = (bf16[256,256]{1,0:T(8,128)(2,1)S(1)}, bf16[256,256]{1,0:T(8,128)(2,1)S(1)}, u32[]{:S(2)}, u32[]{:S(2)}) collective-permute-start(bf16[256,256]{1,0:T(8,128)(2,1)S(1)} %get-tuple-element.88), channel_id=1, source_target_pairs={{0,12},{4,8},{8,4},{12,0},{16,28},{20,24},{24,20},{28,16},{1,13},{... | collective-permute-start | bytes 393224 | tf_op jit(solution)/shard_map/ppermute | solution.py:413
  55.1 1.7 %collective-permute-done.16.refs_8_ = bf16[288,256]{1,0:T(8,128)(2,1)S(1)} collective-permute-done((bf16[288,256]{1,0:T(8,128)(2,1)S(1)}, bf16[288,256]{1,0:T(8,128)(2,1)S(1)}, u32[]{:S(2)}, u32[]{:S(2)}) %collective-permute-start.16) | collective-permute-done | bytes 147488 | tf_op jit(solution)/shard_map/ppermute | solution.py:413
  56.8 1.2 %gradient.2 = (bf16[2,2,304,128]{3,2,1,0:T(8,128)(2,1)S(1)}, bf16[2,2,304,128]{3,2,1,0:T(8,128)(2,1)S(1)}) custom-call(s32[4]{0:T(128)S(1)} %pad_add_fusion.info_ref, bf16[4,256,256]{2,1,0:T(8,128)(2,1)S(1)} %pad_maximum_fusion.ctx_ref.refs_0_, bf16[4,256,256]{2,1,0:T(8,128)(2,1)S(1)} %collective-permute-done.9.refs_1_, ...), custom_call_target="tpu_custom_call" | custom-call | flops 536870912 | bytes 3145728 | tf_op jit(solution)/shard_map/gradient/pallas_call | solution.py:326
  58.9 2.4 %collective-permute-done.22.refs_8_ = bf16[256,256]{1,0:T(8,128)(2,1)S(1)} collective-permute-done((bf16[256,256]{1,0:T(8,128)(2,1)S(1)}, bf16[256,256]{1,0:T(8,128)(2,1)S(1)}, u32[]{:S(2)}, u32[]{:S(2)}) %collective-permute-start.22) | collective-permute-done | bytes 131104 | tf_op jit(solution)/shard_map/ppermute | solution.py:413
  61.3 1.3 %gradient.3 = (bf16[2,2,256,128]{3,2,1,0:T(8,128)(2,1)S(1)}, bf16[2,2,256,128]{3,2,1,0:T(8,128)(2,1)S(1)}) custom-call(s32[4]{0:T(128)S(1)} %pad_add_fusion.info_ref, bf16[4,256,256]{2,1,0:T(8,128)(2,1)S(1)} %pad_maximum_fusion.ctx_ref.refs_0_, bf16[4,256,256]{2,1,0:T(8,128)(2,1)S(1)} %collective-permute-done.9.refs_1_, ...), custom_call_target="tpu_custom_call" | custom-call | flops 536870912 | bytes 3145728 | tf_op jit(solution)/shard_map/gradient/pallas_call | solution.py:326
  64.9 4.7 %collective-permute-done.18.got_ref = bf16[1,2,304,128]{3,2,1,0:T(8,128)(2,1)S(1)} collective-permute-done((bf16[1,2,304,128]{3,2,1,0:T(8,128)(2,1)S(1)}, bf16[1,2,304,128]{3,2,1,0:T(8,128)(2,1)S(1)}, u32[]{:S(2)}, u32[]{:S(2)}) %collective-permute-start.18) | collective-permute-done | bytes 155680 | tf_op jit(solution)/shard_map/ppermute | solution.py:418
  69.6 2.7 %collective-permute-start.19 = (bf16[1,1,304,128]{3,2,1,0:T(8,128)(2,1)S(1)}, bf16[1,1,304,128]{3,2,1,0:T(8,128)(2,1)S(1)}, u32[]{:S(2)}, u32[]{:S(2)}) collective-permute-start(bf16[1,1,304,128]{3,2,1,0:T(8,128)(2,1)S(1)} %get-tuple-element.84), channel_id=1, source_target_pairs={{0,16},{1,17},{2,18},{3,19},{4,20},{5,21},{6,22},{7,23},{8,24},{9,... | collective-permute-start | bytes 233480 | tf_op jit(solution)/shard_map/ppermute | solution.py:418
  72.3 2.4 %collective-permute-start.25 = (bf16[1,1,256,128]{3,2,1,0:T(8,128)(2,1)S(1)}, bf16[1,1,256,128]{3,2,1,0:T(8,128)(2,1)S(1)}, u32[]{:S(2)}, u32[]{:S(2)}) collective-permute-start(bf16[1,1,256,128]{3,2,1,0:T(8,128)(2,1)S(1)} %get-tuple-element.94), channel_id=1, source_target_pairs={{0,16},{1,17},{2,18},{3,19},{4,20},{5,21},{6,22},{7,23},{8,24},{9,... | collective-permute-start | bytes 196616 | tf_op jit(solution)/shard_map/ppermute | solution.py:418
  74.7 4.0 %collective-permute-done.25.refs_3_ = bf16[1,1,256,128]{3,2,1,0:T(8,128)(2,1)S(1)} collective-permute-done((bf16[1,1,256,128]{3,2,1,0:T(8,128)(2,1)S(1)}, bf16[1,1,256,128]{3,2,1,0:T(8,128)(2,1)S(1)}, u32[]{:S(2)}, u32[]{:S(2)}) %collective-permute-start.25) | collective-permute-done | bytes 65568 | tf_op jit(solution)/shard_map/ppermute | solution.py:418
  (50 shorter events, 14.7 us)
Async XLA Ops:
  1.6 9.3 %collective-permute-start = (bf16[256,512]{1,0:T(8,128)(2,1)S(1)}, bf16[256,512]{1,0:T(8,128)(2,1)S(1)}, u32[]{:S(2)}, u32[]{:S(2)}) collective-permute-start(bf16[256,512]{1,0:T(8,128)(2,1)S(1)} %dynamic-slice_bitcast_fusion), channel_id=1, source_target_pairs={{0,2},{1,3},{2,0},{3,1},{4,6},{5,7},{6,4},{7,5},{8,10},{9,11},{10,... | collective-permute-start | bytes 786440 | tf_op jit(solution)/shard_map/ppermute | solution.py:413
  11.0 11.5 %collective-permute-start.1 = (bf16[256,512]{1,0:T(8,128)(2,1)S(1)}, bf16[256,512]{1,0:T(8,128)(2,1)S(1)}, u32[]{:S(2)}, u32[]{:S(2)}) collective-permute-start(bf16[256,512]{1,0:T(8,128)(2,1)S(1)} %collective-permute-done.refs_2_), channel_id=1, source_target_pairs={{0,4},{4,0},{8,12},{12,8},{16,20},{20,16},{24,28},{28,24},{1,5},{5... | collective-permute-start | bytes 786440 | tf_op jit(solution)/shard_map/ppermute | solution.py:413
  12.7 9.8 %collective-permute-start.2 = (bf16[256,512]{1,0:T(8,128)(2,1)S(1)}, bf16[256,512]{1,0:T(8,128)(2,1)S(1)}, u32[]{:S(2)}, u32[]{:S(2)}) collective-permute-start(bf16[256,512]{1,0:T(8,128)(2,1)S(1)} %collective-permute-done.refs_2_), channel_id=1, source_target_pairs={{0,1},{1,0},{2,3},{3,2},{4,5},{5,4},{6,7},{7,6},{8,9},{9,8},{10,11... | collective-permute-start | bytes 786440 | tf_op jit(solution)/shard_map/ppermute | solution.py:413
  12.7 5.8 %collective-permute-start.5 = (bf16[256,256]{1,0:T(8,128)(2,1)}, bf16[256,256]{1,0:T(8,128)(2,1)S(1)}, u32[]{:S(2)}, u32[]{:S(2)}) collective-permute-start(bf16[256,256]{1,0:T(8,128)(2,1)} %get-tuple-element.59), channel_id=1, source_target_pairs={{0,3},{1,2},{2,1},{3,0},{4,7},{5,6},{6,5},{7,4},{8,11},{9,10},{10,... | collective-permute-start | bytes 393224 | tf_op jit(solution)/shard_map/ppermute | solution.py:413
  14.3 4.2 %collective-permute-start.3 = (bf16[256,256]{1,0:T(8,128)(2,1)}, bf16[256,256]{1,0:T(8,128)(2,1)S(1)}, u32[]{:S(2)}, u32[]{:S(2)}) collective-permute-start(bf16[256,256]{1,0:T(8,128)(2,1)} %get-tuple-element.57), channel_id=1, source_target_pairs={{0,1},{1,0},{2,3},{3,2},{4,5},{5,4},{6,7},{7,6},{8,9},{9,8},{10,11... | collective-permute-start | bytes 393224 | tf_op jit(solution)/shard_map/ppermute | solution.py:413
  14.3 7.2 %collective-permute-start.4 = (bf16[256,256]{1,0:T(8,128)(2,1)}, bf16[256,256]{1,0:T(8,128)(2,1)S(1)}, u32[]{:S(2)}, u32[]{:S(2)}) collective-permute-start(bf16[256,256]{1,0:T(8,128)(2,1)} %get-tuple-element.58), channel_id=1, source_target_pairs={{0,2},{1,3},{2,0},{3,1},{4,6},{5,7},{6,4},{7,5},{8,10},{9,11},{10,... | collective-permute-start | bytes 393224 | tf_op jit(solution)/shard_map/ppermute | solution.py:413
  22.5 5.3 %collective-permute-start.7 = (bf16[256,2048]{1,0:T(8,128)(2,1)S(1)}, bf16[256,2048]{1,0:T(8,128)(2,1)S(1)}, u32[]{:S(2)}, u32[]{:S(2)}) collective-permute-start(bf16[256,2048]{1,0:T(8,128)(2,1)S(1)} %bitcast.17), channel_id=1, source_target_pairs={{0,1},{1,0},{2,3},{3,2},{4,5},{5,4},{6,7},{7,6},{8,9},{9,8},{10,11... | collective-permute-start | bytes 3145736 | tf_op jit(solution)/shard_map/ppermute | solution.py:413
  22.6 14.3 %collective-permute-start.10 = (bf16[4,256,256]{2,1,0:T(8,128)(2,1)S(1)}, bf16[4,256,256]{2,1,0:T(8,128)(2,1)S(1)}, u32[]{:S(2)}, u32[]{:S(2)}) collective-permute-start(bf16[4,256,256]{2,1,0:T(8,128)(2,1)S(1)} %pad_maximum_fusion.ctx_ref.refs_0_), channel_id=1, source_target_pairs={{0,8},{4,12},{8,0},{12,4},{16,24},{20,28},{24,16},{28,20},{1,9},{5... | collective-permute-start | bytes 1572872 | tf_op jit(solution)/shard_map/ppermute | solution.py:413
  24.2 14.0 %collective-permute-start.6 = (bf16[256,1024]{1,0:T(8,128)(2,1)S(1)}, bf16[256,1024]{1,0:T(8,128)(2,1)S(1)}, u32[]{:S(2)}, u32[]{:S(2)}) collective-permute-start(bf16[256,1024]{1,0:T(8,128)(2,1)S(1)} %slice.12), channel_id=1, source_target_pairs={{0,2},{1,3},{2,0},{3,1},{4,6},{5,7},{6,4},{7,5},{8,10},{9,11},{10,... | collective-permute-start | bytes 1572872 | tf_op jit(solution)/shard_map/ppermute | solution.py:413
  25.7 13.7 %collective-permute-start.9 = (bf16[4,256,256]{2,1,0:T(8,128)(2,1)S(1)}, bf16[4,256,256]{2,1,0:T(8,128)(2,1)S(1)}, u32[]{:S(2)}, u32[]{:S(2)}) collective-permute-start(bf16[4,256,256]{2,1,0:T(8,128)(2,1)S(1)} %pad_maximum_fusion.ctx_ref.refs_0_), channel_id=1, source_target_pairs={{0,4},{4,0},{8,12},{12,8},{16,20},{20,16},{24,28},{28,24},{1,5},{5... | collective-permute-start | bytes 1572872 | tf_op jit(solution)/shard_map/ppermute | solution.py:413
  39.4 1.9 %collective-permute-start.11 = (bf16[256,1024]{1,0:T(8,128)(2,1)S(1)}, bf16[256,1024]{1,0:T(8,128)(2,1)S(1)}, u32[]{:S(2)}, u32[]{:S(2)}) collective-permute-start(bf16[256,1024]{1,0:T(8,128)(2,1)S(1)} %collective-permute-done.6.refs_0_), channel_id=1, source_target_pairs={{0,1},{1,0},{2,3},{3,2},{4,5},{5,4},{6,7},{7,6},{8,9},{9,8},{10,11... | collective-permute-start | bytes 1572872 | tf_op jit(solution)/shard_map/ppermute | solution.py:413
  39.5 9.4 %collective-permute-start.12 = (bf16[4,128,256]{2,1,0:T(8,128)(2,1)S(1)}, bf16[4,128,256]{2,1,0:T(8,128)(2,1)S(1)}, u32[]{:S(2)}, u32[]{:S(2)}) collective-permute-start(bf16[4,128,256]{2,1,0:T(8,128)(2,1)S(1)} %slice.10), channel_id=1, source_target_pairs={{0,8},{4,12},{8,0},{12,4},{16,24},{20,28},{24,16},{28,20},{1,9},{5... | collective-permute-start | bytes 786440 | tf_op jit(solution)/shard_map/ppermute | solution.py:413
  40.0 9.7 %collective-permute-start.13 = (bf16[4,128,256]{2,1,0:T(8,128)(2,1)S(1)}, bf16[4,128,256]{2,1,0:T(8,128)(2,1)S(1)}, u32[]{:S(2)}, u32[]{:S(2)}) collective-permute-start(bf16[4,128,256]{2,1,0:T(8,128)(2,1)S(1)} %slice.11), channel_id=1, source_target_pairs={{0,4},{4,0},{8,12},{12,8},{16,20},{20,16},{24,28},{28,24},{1,5},{5... | collective-permute-start | bytes 786440 | tf_op jit(solution)/shard_map/ppermute | solution.py:413
  45.4 7.4 %collective-permute-start.14 = (bf16[288,256]{1,0:T(8,128)(2,1)S(1)}, bf16[288,256]{1,0:T(8,128)(2,1)S(1)}, u32[]{:S(2)}, u32[]{:S(2)}) collective-permute-start(bf16[288,256]{1,0:T(8,128)(2,1)S(1)} %get-tuple-element.76), channel_id=1, source_target_pairs={{0,4},{4,0},{8,12},{12,8},{16,20},{20,16},{24,28},{28,24},{1,5},{5... | collective-permute-start | bytes 442376 | tf_op jit(solution)/shard_map/ppermute | solution.py:413
  46.2 8.9 %collective-permute-start.15 = (bf16[288,256]{1,0:T(8,128)(2,1)S(1)}, bf16[288,256]{1,0:T(8,128)(2,1)S(1)}, u32[]{:S(2)}, u32[]{:S(2)}) collective-permute-start(bf16[288,256]{1,0:T(8,128)(2,1)S(1)} %get-tuple-element.77), channel_id=1, source_target_pairs={{0,8},{4,12},{8,0},{12,4},{16,24},{20,28},{24,16},{28,20},{1,9},{5... | collective-permute-start | bytes 442376 | tf_op jit(solution)/shard_map/ppermute | solution.py:413
  47.7 9.0 %collective-permute-start.16 = (bf16[288,256]{1,0:T(8,128)(2,1)S(1)}, bf16[288,256]{1,0:T(8,128)(2,1)S(1)}, u32[]{:S(2)}, u32[]{:S(2)}) collective-permute-start(bf16[288,256]{1,0:T(8,128)(2,1)S(1)} %get-tuple-element.78), channel_id=1, source_target_pairs={{0,12},{4,8},{8,4},{12,0},{16,28},{20,24},{24,20},{28,16},{1,13},{... | collective-permute-start | bytes 442376 | tf_op jit(solution)/shard_map/ppermute | solution.py:413
  48.9 9.2 %collective-permute-start.20 = (bf16[256,256]{1,0:T(8,128)(2,1)S(1)}, bf16[256,256]{1,0:T(8,128)(2,1)S(1)}, u32[]{:S(2)}, u32[]{:S(2)}) collective-permute-start(bf16[256,256]{1,0:T(8,128)(2,1)S(1)} %get-tuple-element.86), channel_id=1, source_target_pairs={{0,4},{4,0},{8,12},{12,8},{16,20},{20,16},{24,28},{28,24},{1,5},{5... | collective-permute-start | bytes 393224 | tf_op jit(solution)/shard_map/ppermute | solution.py:413
  49.7 9.2 %collective-permute-start.21 = (bf16[256,256]{1,0:T(8,128)(2,1)S(1)}, bf16[256,256]{1,0:T(8,128)(2,1)S(1)}, u32[]{:S(2)}, u32[]{:S(2)}) collective-permute-start(bf16[256,256]{1,0:T(8,128)(2,1)S(1)} %get-tuple-element.87), channel_id=1, source_target_pairs={{0,8},{4,12},{8,0},{12,4},{16,24},{20,28},{24,16},{28,20},{1,9},{5... | collective-permute-start | bytes 393224 | tf_op jit(solution)/shard_map/ppermute | solution.py:413
  52.9 8.4 %collective-permute-start.22 = (bf16[256,256]{1,0:T(8,128)(2,1)S(1)}, bf16[256,256]{1,0:T(8,128)(2,1)S(1)}, u32[]{:S(2)}, u32[]{:S(2)}) collective-permute-start(bf16[256,256]{1,0:T(8,128)(2,1)S(1)} %get-tuple-element.88), channel_id=1, source_target_pairs={{0,12},{4,8},{8,4},{12,0},{16,28},{20,24},{24,20},{28,16},{1,13},{... | collective-permute-start | bytes 393224 | tf_op jit(solution)/shard_map/ppermute | solution.py:413
  58.0 4.6 %collective-permute-start.17 = (bf16[2,2,304,128]{3,2,1,0:T(8,128)(2,1)S(1)}, bf16[2,2,304,128]{3,2,1,0:T(8,128)(2,1)S(1)}, u32[]{:S(2)}, u32[]{:S(2)}) collective-permute-start(bf16[2,2,304,128]{3,2,1,0:T(8,128)(2,1)S(1)} %get-tuple-element.80), channel_id=1, source_target_pairs={{0,1},{1,0},{2,3},{3,2},{4,5},{5,4},{6,7},{7,6},{8,9},{9,8},{10,11... | collective-permute-start | bytes 933896 | tf_op jit(solution)/shard_map/ppermute | solution.py:413
  62.7 6.9 %collective-permute-start.18 = (bf16[1,2,304,128]{3,2,1,0:T(8,128)(2,1)S(1)}, bf16[1,2,304,128]{3,2,1,0:T(8,128)(2,1)S(1)}, u32[]{:S(2)}, u32[]{:S(2)}) collective-permute-start(bf16[1,2,304,128]{3,2,1,0:T(8,128)(2,1)S(1)} %get-tuple-element.82), channel_id=1, source_target_pairs={{0,2},{1,3},{2,0},{3,1},{4,6},{5,7},{6,4},{7,5},{8,10},{9,11},{10,... | collective-permute-start | bytes 466952 | tf_op jit(solution)/shard_map/ppermute | solution.py:418
  64.2 8.1 %collective-permute-start.24 = (bf16[1,2,256,128]{3,2,1,0:T(8,128)(2,1)S(1)}, bf16[1,2,256,128]{3,2,1,0:T(8,128)(2,1)S(1)}, u32[]{:S(2)}, u32[]{:S(2)}) collective-permute-start(bf16[1,2,256,128]{3,2,1,0:T(8,128)(2,1)S(1)} %get-tuple-element.92), channel_id=1, source_target_pairs={{0,2},{1,3},{2,0},{3,1},{4,6},{5,7},{6,4},{7,5},{8,10},{9,11},{10,... | collective-permute-start | bytes 393224 | tf_op jit(solution)/shard_map/ppermute | solution.py:418
  69.6 9.0 %collective-permute-start.19 = (bf16[1,1,304,128]{3,2,1,0:T(8,128)(2,1)S(1)}, bf16[1,1,304,128]{3,2,1,0:T(8,128)(2,1)S(1)}, u32[]{:S(2)}, u32[]{:S(2)}) collective-permute-start(bf16[1,1,304,128]{3,2,1,0:T(8,128)(2,1)S(1)} %get-tuple-element.84), channel_id=1, source_target_pairs={{0,16},{1,17},{2,18},{3,19},{4,20},{5,21},{6,22},{7,23},{8,24},{9,... | collective-permute-start | bytes 233480 | tf_op jit(solution)/shard_map/ppermute | solution.py:418
  72.3 6.3 %collective-permute-start.25 = (bf16[1,1,256,128]{3,2,1,0:T(8,128)(2,1)S(1)}, bf16[1,1,256,128]{3,2,1,0:T(8,128)(2,1)S(1)}, u32[]{:S(2)}, u32[]{:S(2)}) collective-permute-start(bf16[1,1,256,128]{3,2,1,0:T(8,128)(2,1)S(1)} %get-tuple-element.94), channel_id=1, source_target_pairs={{0,16},{1,17},{2,18},{3,19},{4,20},{5,21},{6,22},{7,23},{8,24},{9,... | collective-permute-start | bytes 196616 | tf_op jit(solution)/shard_map/ppermute | solution.py:418
  (5 other events, 45.1 us)

commit v15 on v11

--- a/solution.py
+++ b/solution.py
@@ -10,9 +10,10 @@
 
 HD = 128
 QB = 128
-ROWS = 128
+ROWS = 256
 COLS = 256
 NEAR = 4
+SHORTEST = 256
 STAT_ROWS = 32
 
 loss_scale = 65536.0
@@ -58,7 +59,9 @@
         q_t, v_t = q_ref[:, at].T, v_ref[:, at].T
         for i in range(seq // QB):
             keys = (i + 1) * QB
-            scores = dot(k_ref[:keys, at], q_t[:, i * QB : keys], ((1,), (0,))) + hide[:keys]
+            scores = dot(k_ref[:keys, at], q_t[:, i * QB : keys], ((1,), (0,)))
+            if keys > SHORTEST:
+                scores = jnp.concatenate([scores[:SHORTEST], scores[SHORTEST:] + hide[SHORTEST:keys]], 0)
             last = jnp.where(r <= c, scores[keys - QB :], neg_large)
             scores = last if i == 0 else jnp.concatenate([scores[: keys - QB], last], 0)
             peak = jnp.max(scores, axis=0, keepdims=True)

time: 78.3 us -> 77.6 us (level)
  waiting for transfers between devices: 32.4 us -> 33.4 us
  starting transfers between devices: 27.6 us -> 26.7 us
  Pallas kernels: 13.9 us -> 13.1 us
    ppermute x22, waiting for transfers between devices: 26.5 us -> 27.6 us  [swap(): return lax.ppermute(x, axis, [(i, i ^ mask) for i in range(n)])]
    ppermute x22, starting transfers between devices: 19.6 us -> 18.7 us  [swap(): return lax.ppermute(x, axis, [(i, i ^ mask) for i in range(n)])]
  transfers between devices with their start and end apart: 27 -> 27, of which waited for: 16 -> 16; matrix products, arithmetic and copies ran while one was open for 3% -> 3% of each run, Pallas kernels for 17% -> 16%
where the time goes in v15:
time: 77.6 us; the launch traced here: 77.4 us
  waiting for transfers between devices  33.4 us (43%)
  starting transfers between devices  26.7 us (34%)
  Pallas kernels  13.1 us (17%)
  between operations  2.07 us (3%)
  local copies, waits for them, and re-layouts  1.05 us (1%)
  other arithmetic  1.05 us (1%)
    ppermute x22, waiting for transfers between devices, swap(): return lax.ppermute(x, axis, [(i, i ^ mask) for i in range(n)])  27.6 us
    ppermute x22, starting transfers between devices, swap(): return lax.ppermute(x, axis, [(i, i ^ mask) for i in range(n)])  18.7 us
    ppermute x5, starting transfers between devices, swap_far(): lax.ppermute(x, ('dp', 'tensor'), [(i, i ^ mask) for i in range(n_dp * n_...  8 us
    ppermute x5, waiting for transfers between devices, swap_far(): lax.ppermute(x, ('dp', 'tensor'), [(i, i ^ mask) for i in range(n_dp * n_...  5.86 us
    pallas_call x1, Pallas kernels, attend(): pl.pallas_call(attend_body, in_specs=[SM, SM, VM, VM, VM], out_specs=[VM]...  4.74 us
    pallas_call x1, Pallas kernels, join(): pl.pallas_call(functools.partial(join_body, plan, len(late)), in_specs=[S...  3.38 us
    pallas_call x2, Pallas kernels, gradient(): pl.pallas_call(functools.partial(grad_body, plan, dout, [len(c) for c in...  2.5 us
    pallas_call x1, Pallas kernels, mix(): pl.pallas_call(functools.partial(mix_body, n_tensor, counts, split), in_s...  1.56 us
  transfers between devices with their start and end apart: 27, of which 16 were waited for; matrix products, arithmetic and copies ran while one was open for 3% of the time, Pallas kernels for 16%

profile of v15, /device:TPU:0, one launch (start us, length us, event | category | flops | bytes accessed | tf_op | source)
XLA Modules:
  0.0 77.4 jit_solution(11793625096596609691)
XLA Ops:
  2.1 2.6 %collective-permute-start = (bf16[256,512]{1,0:T(8,128)(2,1)S(1)}, bf16[256,512]{1,0:T(8,128)(2,1)S(1)}, u32[]{:S(2)}, u32[]{:S(2)}) collective-permute-start(bf16[256,512]{1,0:T(8,128)(2,1)S(1)} %dynamic-slice_bitcast_fusion), channel_id=1, source_target_pairs={{0,2},{1,3},{2,0},{3,1},{4,6},{5,7},{6,4},{7,5},{8,10},{9,11},{10,... | collective-permute-start | bytes 786440 | tf_op jit(solution)/shard_map/ppermute | solution.py:416
  5.4 4.7 %attend.1 = (bf16[256,256]{1,0:T(8,128)(2,1)}, bf16[256,256]{1,0:T(8,128)(2,1)}, bf16[256,256]{1,0:T(8,128)(2,1)}, bf16[256,256]{1,0:T(8,128)(2,1)}) custom-call(s32[1]{0:T(128)S(6)} %copy.12.len_ref, s32[1]{0:T(128)} %bitcast.me_ref, bf16[1024,256]{1,0:T(8,128)(2,1)} %bitcast.24, bf16[1024,256]{1,0:T(8,128)(2,1)} %bitcast.25, bf16[1024,256]{1,0:T(8,128)(2,1)} %bitcast.26), custom_call_target="tpu_custom_call" | custom-call | flops 1073741824 | bytes 2097152 | tf_op jit(solution)/shard_map/attend/pallas_call | solution.py:82
  10.1 1.6 %collective-permute-done.refs_2_ = bf16[256,512]{1,0:T(8,128)(2,1)S(1)} collective-permute-done((bf16[256,512]{1,0:T(8,128)(2,1)S(1)}, bf16[256,512]{1,0:T(8,128)(2,1)S(1)}, u32[]{:S(2)}, u32[]{:S(2)}) %collective-permute-start) | collective-permute-done | bytes 262176 | tf_op jit(solution)/shard_map/ppermute | solution.py:416
  11.7 1.7 %collective-permute-start.2 = (bf16[256,512]{1,0:T(8,128)(2,1)S(1)}, bf16[256,512]{1,0:T(8,128)(2,1)S(1)}, u32[]{:S(2)}, u32[]{:S(2)}) collective-permute-start(bf16[256,512]{1,0:T(8,128)(2,1)S(1)} %collective-permute-done.refs_2_), channel_id=1, source_target_pairs={{0,4},{4,0},{8,12},{12,8},{16,20},{20,16},{24,28},{28,24},{1,5},{5... | collective-permute-start | bytes 786440 | tf_op jit(solution)/shard_map/ppermute | solution.py:416
  13.4 1.6 %collective-permute-start.6 = (bf16[256,256]{1,0:T(8,128)(2,1)}, bf16[256,256]{1,0:T(8,128)(2,1)S(1)}, u32[]{:S(2)}, u32[]{:S(2)}) collective-permute-start(bf16[256,256]{1,0:T(8,128)(2,1)} %get-tuple-element.59), channel_id=1, source_target_pairs={{0,3},{1,2},{2,1},{3,0},{4,7},{5,6},{6,5},{7,4},{8,11},{9,10},{10,... | collective-permute-start | bytes 393224 | tf_op jit(solution)/shard_map/ppermute | solution.py:416
  15.6 3.6 %collective-permute-done.6 = bf16[256,256]{1,0:T(8,128)(2,1)S(1)} collective-permute-done((bf16[256,256]{1,0:T(8,128)(2,1)}, bf16[256,256]{1,0:T(8,128)(2,1)S(1)}, u32[]{:S(2)}, u32[]{:S(2)}) %collective-permute-start.6) | collective-permute-done | bytes 131104 | tf_op jit(solution)/shard_map/ppermute | solution.py:416
  19.2 3.0 %collective-permute-done.5 = bf16[256,256]{1,0:T(8,128)(2,1)S(1)} collective-permute-done((bf16[256,256]{1,0:T(8,128)(2,1)}, bf16[256,256]{1,0:T(8,128)(2,1)S(1)}, u32[]{:S(2)}, u32[]{:S(2)}) %collective-permute-start.5) | collective-permute-done | bytes 131104 | tf_op jit(solution)/shard_map/ppermute | solution.py:416
  23.2 1.6 %collective-permute-start.10 = (bf16[4,256,256]{2,1,0:T(8,128)(2,1)S(1)}, bf16[4,256,256]{2,1,0:T(8,128)(2,1)S(1)}, u32[]{:S(2)}, u32[]{:S(2)}) collective-permute-start(bf16[4,256,256]{2,1,0:T(8,128)(2,1)S(1)} %pad_maximum_fusion.ctx_ref.refs_0_), channel_id=1, source_target_pairs={{0,8},{4,12},{8,0},{12,4},{16,24},{20,28},{24,16},{28,20},{1,9},{5... | collective-permute-start | bytes 1572872 | tf_op jit(solution)/shard_map/ppermute | solution.py:416
  24.9 1.5 %collective-permute-start.7 = (bf16[256,1024]{1,0:T(8,128)(2,1)S(1)}, bf16[256,1024]{1,0:T(8,128)(2,1)S(1)}, u32[]{:S(2)}, u32[]{:S(2)}) collective-permute-start(bf16[256,1024]{1,0:T(8,128)(2,1)S(1)} %slice.12), channel_id=1, source_target_pairs={{0,2},{1,3},{2,0},{3,1},{4,6},{5,7},{6,4},{7,5},{8,10},{9,11},{10,... | collective-permute-start | bytes 1572872 | tf_op jit(solution)/shard_map/ppermute | solution.py:416
  28.5 1.6 %mix.1 = (f32[256,2048]{1,0:T(8,128)S(1)}, f32[256,128]{1,0:T(8,128)S(1)}, bf16[4,256,256]{2,1,0:T(8,128)(2,1)S(1)}) custom-call(s32[4]{0:T(128)S(1)} %pad_add_fusion.info_ref, bf16[4,256,256]{2,1,0:T(8,128)(2,1)S(1)} %pad_maximum_fusion.ctx_ref.refs_0_, bf16[256,2048]{1,0:T(8,128)(2,1)S(1)} %bitcast.18, ...), custom_call_target="tpu_custom_call" | custom-call | flops 1073741824 | bytes 6291456 | tf_op jit(solution)/shard_map/mix/pallas_call | solution.py:133
  30.0 6.6 %collective-permute-done.10.refs_2_ = bf16[4,256,256]{2,1,0:T(8,128)(2,1)S(1)} collective-permute-done((bf16[4,256,256]{2,1,0:T(8,128)(2,1)S(1)}, bf16[4,256,256]{2,1,0:T(8,128)(2,1)S(1)}, u32[]{:S(2)}, u32[]{:S(2)}) %collective-permute-start.10) | collective-permute-done | bytes 524320 | tf_op jit(solution)/shard_map/ppermute | solution.py:416
  36.6 1.3 %collective-permute-done.7.refs_0_ = bf16[256,1024]{1,0:T(8,128)(2,1)S(1)} collective-permute-done((bf16[256,1024]{1,0:T(8,128)(2,1)S(1)}, bf16[256,1024]{1,0:T(8,128)(2,1)S(1)}, u32[]{:S(2)}, u32[]{:S(2)}) %collective-permute-start.7) | collective-permute-done | bytes 524320 | tf_op jit(solution)/shard_map/ppermute | solution.py:416
  41.0 3.4 %join.1 = (bf16[256,2048]{1,0:T(8,128)(2,1)}, bf16[288,256]{1,0:T(8,128)(2,1)S(1)}, bf16[288,256]{1,0:T(8,128)(2,1)S(1)}, bf16[288,256]{1,0:T(8,128)(2,1)S(1)}, ...) custom-call(s32[4]{0:T(128)S(1)} %pad_add_fusion.info_ref, ...), custom_call_target="tpu_custom_call" | custom-call | flops 134217728 | bytes 6291456 | tf_op jit(solution)/shard_map/join/pallas_call | solution.py:246
  45.2 1.6 %collective-permute-start.22 = (bf16[256,256]{1,0:T(8,128)(2,1)S(1)}, bf16[256,256]{1,0:T(8,128)(2,1)S(1)}, u32[]{:S(2)}, u32[]{:S(2)}) collective-permute-start(bf16[256,256]{1,0:T(8,128)(2,1)S(1)} %get-tuple-element.87), channel_id=1, source_target_pairs={{0,8},{4,12},{8,0},{12,4},{16,24},{20,28},{24,16},{28,20},{1,9},{5... | collective-permute-start | bytes 393224 | tf_op jit(solution)/shard_map/ppermute | solution.py:416
  48.9 1.6 %collective-permute-start.15 = (bf16[288,256]{1,0:T(8,128)(2,1)S(1)}, bf16[288,256]{1,0:T(8,128)(2,1)S(1)}, u32[]{:S(2)}, u32[]{:S(2)}) collective-permute-start(bf16[288,256]{1,0:T(8,128)(2,1)S(1)} %get-tuple-element.77), channel_id=1, source_target_pairs={{0,8},{4,12},{8,0},{12,4},{16,24},{20,28},{24,16},{28,20},{1,9},{5... | collective-permute-start | bytes 442376 | tf_op jit(solution)/shard_map/ppermute | solution.py:416
  50.5 3.5 %collective-permute-done.21.refs_6_ = bf16[256,256]{1,0:T(8,128)(2,1)S(1)} collective-permute-done((bf16[256,256]{1,0:T(8,128)(2,1)S(1)}, bf16[256,256]{1,0:T(8,128)(2,1)S(1)}, u32[]{:S(2)}, u32[]{:S(2)}) %collective-permute-start.21) | collective-permute-done | bytes 131104 | tf_op jit(solution)/shard_map/ppermute | solution.py:416
  53.9 1.3 %collective-permute-start.16 = (bf16[288,256]{1,0:T(8,128)(2,1)S(1)}, bf16[288,256]{1,0:T(8,128)(2,1)S(1)}, u32[]{:S(2)}, u32[]{:S(2)}) collective-permute-start(bf16[288,256]{1,0:T(8,128)(2,1)S(1)} %get-tuple-element.78), channel_id=1, source_target_pairs={{0,12},{4,8},{8,4},{12,0},{16,28},{20,24},{24,20},{28,16},{1,13},{... | collective-permute-start | bytes 442376 | tf_op jit(solution)/shard_map/ppermute | solution.py:416
  55.2 1.3 %gradient.3 = (bf16[2,2,256,128]{3,2,1,0:T(8,128)(2,1)S(1)}, bf16[2,2,256,128]{3,2,1,0:T(8,128)(2,1)S(1)}) custom-call(s32[4]{0:T(128)S(1)} %pad_add_fusion.info_ref, bf16[4,256,256]{2,1,0:T(8,128)(2,1)S(1)} %pad_maximum_fusion.ctx_ref.refs_0_, bf16[4,256,256]{2,1,0:T(8,128)(2,1)S(1)} %collective-permute-done.9.refs_1_, ...), custom_call_target="tpu_custom_call" | custom-call | flops 536870912 | bytes 3145728 | tf_op jit(solution)/shard_map/gradient/pallas_call | solution.py:329
  56.6 1.4 %collective-permute-done.14.refs_6_ = bf16[288,256]{1,0:T(8,128)(2,1)S(1)} collective-permute-done((bf16[288,256]{1,0:T(8,128)(2,1)S(1)}, bf16[288,256]{1,0:T(8,128)(2,1)S(1)}, u32[]{:S(2)}, u32[]{:S(2)}) %collective-permute-start.14) | collective-permute-done | bytes 147488 | tf_op jit(solution)/shard_map/ppermute | solution.py:416
  57.9 2.3 %collective-permute-done.16.refs_8_ = bf16[288,256]{1,0:T(8,128)(2,1)S(1)} collective-permute-done((bf16[288,256]{1,0:T(8,128)(2,1)S(1)}, bf16[288,256]{1,0:T(8,128)(2,1)S(1)}, u32[]{:S(2)}, u32[]{:S(2)}) %collective-permute-start.16) | collective-permute-done | bytes 147488 | tf_op jit(solution)/shard_map/ppermute | solution.py:416
  60.3 1.2 %gradient.2 = (bf16[2,2,304,128]{3,2,1,0:T(8,128)(2,1)S(1)}, bf16[2,2,304,128]{3,2,1,0:T(8,128)(2,1)S(1)}) custom-call(s32[4]{0:T(128)S(1)} %pad_add_fusion.info_ref, bf16[4,256,256]{2,1,0:T(8,128)(2,1)S(1)} %pad_maximum_fusion.ctx_ref.refs_0_, bf16[4,256,256]{2,1,0:T(8,128)(2,1)S(1)} %collective-permute-done.9.refs_1_, ...), custom_call_target="tpu_custom_call" | custom-call | flops 536870912 | bytes 3145728 | tf_op jit(solution)/shard_map/gradient/pallas_call | solution.py:329
  63.3 2.7 %collective-permute-start.18 = (bf16[1,1,304,128]{3,2,1,0:T(8,128)(2,1)S(1)}, bf16[1,1,304,128]{3,2,1,0:T(8,128)(2,1)S(1)}, u32[]{:S(2)}, u32[]{:S(2)}) collective-permute-start(bf16[1,1,304,128]{3,2,1,0:T(8,128)(2,1)S(1)} %get-tuple-element.82), channel_id=1, source_target_pairs={{0,16},{1,17},{2,18},{3,19},{4,20},{5,21},{6,22},{7,23},{8,24},{9,... | collective-permute-start | bytes 233480 | tf_op jit(solution)/shard_map/ppermute | solution.py:421
  67.8 3.0 %collective-permute-start.26 = (bf16[1,1,256,128]{3,2,1,0:T(8,128)(2,1)S(1)}, bf16[1,1,256,128]{3,2,1,0:T(8,128)(2,1)S(1)}, u32[]{:S(2)}, u32[]{:S(2)}) collective-permute-start(bf16[1,1,256,128]{3,2,1,0:T(8,128)(2,1)S(1)} %get-tuple-element.94), channel_id=1, source_target_pairs={{0,16},{1,17},{2,18},{3,19},{4,20},{5,21},{6,22},{7,23},{8,24},{9,... | collective-permute-start | bytes 196616 | tf_op jit(solution)/shard_map/ppermute | solution.py:421
  70.7 5.2 %collective-permute-done.20.refs_3_ = bf16[1,1,304,128]{3,2,1,0:T(8,128)(2,1)S(1)} collective-permute-done((bf16[1,1,304,128]{3,2,1,0:T(8,128)(2,1)S(1)}, bf16[1,1,304,128]{3,2,1,0:T(8,128)(2,1)S(1)}, u32[]{:S(2)}, u32[]{:S(2)}) %collective-permute-start.20) | collective-permute-done | bytes 77856 | tf_op jit(solution)/shard_map/ppermute | solution.py:421
  (51 shorter events, 15.5 us)
Async XLA Ops:
  0.6 11.1 %collective-permute-start.1 = (bf16[256,2048]{1,0:T(8,128)(2,1)}, bf16[256,2048]{1,0:T(8,128)(2,1)S(1)}, u32[]{:S(2)}, u32[]{:S(2)}) collective-permute-start(bf16[256,2048]{1,0:T(8,128)(2,1)} %bitcast.16), channel_id=1, source_target_pairs={{0,1},{1,0},{2,3},{3,2},{4,5},{5,4},{6,7},{7,6},{8,9},{9,8},{10,11... | collective-permute-start | bytes 3145736 | tf_op jit(solution)/shard_map/ppermute | solution.py:416
  2.1 9.6 %collective-permute-start = (bf16[256,512]{1,0:T(8,128)(2,1)S(1)}, bf16[256,512]{1,0:T(8,128)(2,1)S(1)}, u32[]{:S(2)}, u32[]{:S(2)}) collective-permute-start(bf16[256,512]{1,0:T(8,128)(2,1)S(1)} %dynamic-slice_bitcast_fusion), channel_id=1, source_target_pairs={{0,2},{1,3},{2,0},{3,1},{4,6},{5,7},{6,4},{7,5},{8,10},{9,11},{10,... | collective-permute-start | bytes 786440 | tf_op jit(solution)/shard_map/ppermute | solution.py:416
  11.7 11.5 %collective-permute-start.2 = (bf16[256,512]{1,0:T(8,128)(2,1)S(1)}, bf16[256,512]{1,0:T(8,128)(2,1)S(1)}, u32[]{:S(2)}, u32[]{:S(2)}) collective-permute-start(bf16[256,512]{1,0:T(8,128)(2,1)S(1)} %collective-permute-done.refs_2_), channel_id=1, source_target_pairs={{0,4},{4,0},{8,12},{12,8},{16,20},{20,16},{24,28},{28,24},{1,5},{5... | collective-permute-start | bytes 786440 | tf_op jit(solution)/shard_map/ppermute | solution.py:416
  13.4 9.8 %collective-permute-start.3 = (bf16[256,512]{1,0:T(8,128)(2,1)S(1)}, bf16[256,512]{1,0:T(8,128)(2,1)S(1)}, u32[]{:S(2)}, u32[]{:S(2)}) collective-permute-start(bf16[256,512]{1,0:T(8,128)(2,1)S(1)} %collective-permute-done.refs_2_), channel_id=1, source_target_pairs={{0,1},{1,0},{2,3},{3,2},{4,5},{5,4},{6,7},{7,6},{8,9},{9,8},{10,11... | collective-permute-start | bytes 786440 | tf_op jit(solution)/shard_map/ppermute | solution.py:416
  13.4 5.8 %collective-permute-start.6 = (bf16[256,256]{1,0:T(8,128)(2,1)}, bf16[256,256]{1,0:T(8,128)(2,1)S(1)}, u32[]{:S(2)}, u32[]{:S(2)}) collective-permute-start(bf16[256,256]{1,0:T(8,128)(2,1)} %get-tuple-element.59), channel_id=1, source_target_pairs={{0,3},{1,2},{2,1},{3,0},{4,7},{5,6},{6,5},{7,4},{8,11},{9,10},{10,... | collective-permute-start | bytes 393224 | tf_op jit(solution)/shard_map/ppermute | solution.py:416
  15.0 4.2 %collective-permute-start.4 = (bf16[256,256]{1,0:T(8,128)(2,1)}, bf16[256,256]{1,0:T(8,128)(2,1)S(1)}, u32[]{:S(2)}, u32[]{:S(2)}) collective-permute-start(bf16[256,256]{1,0:T(8,128)(2,1)} %get-tuple-element.57), channel_id=1, source_target_pairs={{0,1},{1,0},{2,3},{3,2},{4,5},{5,4},{6,7},{7,6},{8,9},{9,8},{10,11... | collective-permute-start | bytes 393224 | tf_op jit(solution)/shard_map/ppermute | solution.py:416
  15.0 7.2 %collective-permute-start.5 = (bf16[256,256]{1,0:T(8,128)(2,1)}, bf16[256,256]{1,0:T(8,128)(2,1)S(1)}, u32[]{:S(2)}, u32[]{:S(2)}) collective-permute-start(bf16[256,256]{1,0:T(8,128)(2,1)} %get-tuple-element.58), channel_id=1, source_target_pairs={{0,2},{1,3},{2,0},{3,1},{4,6},{5,7},{6,4},{7,5},{8,10},{9,11},{10,... | collective-permute-start | bytes 393224 | tf_op jit(solution)/shard_map/ppermute | solution.py:416
  23.2 13.4 %collective-permute-start.10 = (bf16[4,256,256]{2,1,0:T(8,128)(2,1)S(1)}, bf16[4,256,256]{2,1,0:T(8,128)(2,1)S(1)}, u32[]{:S(2)}, u32[]{:S(2)}) collective-permute-start(bf16[4,256,256]{2,1,0:T(8,128)(2,1)S(1)} %pad_maximum_fusion.ctx_ref.refs_0_), channel_id=1, source_target_pairs={{0,8},{4,12},{8,0},{12,4},{16,24},{20,28},{24,16},{28,20},{1,9},{5... | collective-permute-start | bytes 1572872 | tf_op jit(solution)/shard_map/ppermute | solution.py:416
  24.9 13.0 %collective-permute-start.7 = (bf16[256,1024]{1,0:T(8,128)(2,1)S(1)}, bf16[256,1024]{1,0:T(8,128)(2,1)S(1)}, u32[]{:S(2)}, u32[]{:S(2)}) collective-permute-start(bf16[256,1024]{1,0:T(8,128)(2,1)S(1)} %slice.12), channel_id=1, source_target_pairs={{0,2},{1,3},{2,0},{3,1},{4,6},{5,7},{6,4},{7,5},{8,10},{9,11},{10,... | collective-permute-start | bytes 1572872 | tf_op jit(solution)/shard_map/ppermute | solution.py:416
  26.4 12.7 %collective-permute-start.9 = (bf16[4,256,256]{2,1,0:T(8,128)(2,1)S(1)}, bf16[4,256,256]{2,1,0:T(8,128)(2,1)S(1)}, u32[]{:S(2)}, u32[]{:S(2)}) collective-permute-start(bf16[4,256,256]{2,1,0:T(8,128)(2,1)S(1)} %pad_maximum_fusion.ctx_ref.refs_0_), channel_id=1, source_target_pairs={{0,4},{4,0},{8,12},{12,8},{16,20},{20,16},{24,28},{28,24},{1,5},{5... | collective-permute-start | bytes 1572872 | tf_op jit(solution)/shard_map/ppermute | solution.py:416
  39.1 9.2 %collective-permute-start.12 = (bf16[4,128,256]{2,1,0:T(8,128)(2,1)S(1)}, bf16[4,128,256]{2,1,0:T(8,128)(2,1)S(1)}, u32[]{:S(2)}, u32[]{:S(2)}) collective-permute-start(bf16[4,128,256]{2,1,0:T(8,128)(2,1)S(1)} %slice.10), channel_id=1, source_target_pairs={{0,8},{4,12},{8,0},{12,4},{16,24},{20,28},{24,16},{28,20},{1,9},{5... | collective-permute-start | bytes 786440 | tf_op jit(solution)/shard_map/ppermute | solution.py:416
  39.7 9.2 %collective-permute-start.13 = (bf16[4,128,256]{2,1,0:T(8,128)(2,1)S(1)}, bf16[4,128,256]{2,1,0:T(8,128)(2,1)S(1)}, u32[]{:S(2)}, u32[]{:S(2)}) collective-permute-start(bf16[4,128,256]{2,1,0:T(8,128)(2,1)S(1)} %slice.11), channel_id=1, source_target_pairs={{0,4},{4,0},{8,12},{12,8},{16,20},{20,16},{24,28},{28,24},{1,5},{5... | collective-permute-start | bytes 786440 | tf_op jit(solution)/shard_map/ppermute | solution.py:416
  44.4 9.5 %collective-permute-start.21 = (bf16[256,256]{1,0:T(8,128)(2,1)S(1)}, bf16[256,256]{1,0:T(8,128)(2,1)S(1)}, u32[]{:S(2)}, u32[]{:S(2)}) collective-permute-start(bf16[256,256]{1,0:T(8,128)(2,1)S(1)} %get-tuple-element.86), channel_id=1, source_target_pairs={{0,4},{4,0},{8,12},{12,8},{16,20},{20,16},{24,28},{28,24},{1,5},{5... | collective-permute-start | bytes 393224 | tf_op jit(solution)/shard_map/ppermute | solution.py:416
  45.2 10.0 %collective-permute-start.22 = (bf16[256,256]{1,0:T(8,128)(2,1)S(1)}, bf16[256,256]{1,0:T(8,128)(2,1)S(1)}, u32[]{:S(2)}, u32[]{:S(2)}) collective-permute-start(bf16[256,256]{1,0:T(8,128)(2,1)S(1)} %get-tuple-element.87), channel_id=1, source_target_pairs={{0,8},{4,12},{8,0},{12,4},{16,24},{20,28},{24,16},{28,20},{1,9},{5... | collective-permute-start | bytes 393224 | tf_op jit(solution)/shard_map/ppermute | solution.py:416
  46.8 8.5 %collective-permute-start.23 = (bf16[256,256]{1,0:T(8,128)(2,1)S(1)}, bf16[256,256]{1,0:T(8,128)(2,1)S(1)}, u32[]{:S(2)}, u32[]{:S(2)}) collective-permute-start(bf16[256,256]{1,0:T(8,128)(2,1)S(1)} %get-tuple-element.88), channel_id=1, source_target_pairs={{0,12},{4,8},{8,4},{12,0},{16,28},{20,24},{24,20},{28,16},{1,13},{... | collective-permute-start | bytes 393224 | tf_op jit(solution)/shard_map/ppermute | solution.py:416
  48.3 9.6 %collective-permute-start.14 = (bf16[288,256]{1,0:T(8,128)(2,1)S(1)}, bf16[288,256]{1,0:T(8,128)(2,1)S(1)}, u32[]{:S(2)}, u32[]{:S(2)}) collective-permute-start(bf16[288,256]{1,0:T(8,128)(2,1)S(1)} %get-tuple-element.76), channel_id=1, source_target_pairs={{0,4},{4,0},{8,12},{12,8},{16,20},{20,16},{24,28},{28,24},{1,5},{5... | collective-permute-start | bytes 442376 | tf_op jit(solution)/shard_map/ppermute | solution.py:416
  48.9 9.0 %collective-permute-start.15 = (bf16[288,256]{1,0:T(8,128)(2,1)S(1)}, bf16[288,256]{1,0:T(8,128)(2,1)S(1)}, u32[]{:S(2)}, u32[]{:S(2)}) collective-permute-start(bf16[288,256]{1,0:T(8,128)(2,1)S(1)} %get-tuple-element.77), channel_id=1, source_target_pairs={{0,8},{4,12},{8,0},{12,4},{16,24},{20,28},{24,16},{28,20},{1,9},{5... | collective-permute-start | bytes 442376 | tf_op jit(solution)/shard_map/ppermute | solution.py:416
  53.9 6.3 %collective-permute-start.16 = (bf16[288,256]{1,0:T(8,128)(2,1)S(1)}, bf16[288,256]{1,0:T(8,128)(2,1)S(1)}, u32[]{:S(2)}, u32[]{:S(2)}) collective-permute-start(bf16[288,256]{1,0:T(8,128)(2,1)S(1)} %get-tuple-element.78), channel_id=1, source_target_pairs={{0,12},{4,8},{8,4},{12,0},{16,28},{20,24},{24,20},{28,16},{1,13},{... | collective-permute-start | bytes 442376 | tf_op jit(solution)/shard_map/ppermute | solution.py:416
  56.5 5.1 %collective-permute-start.24 = (bf16[2,2,256,128]{3,2,1,0:T(8,128)(2,1)S(1)}, bf16[2,2,256,128]{3,2,1,0:T(8,128)(2,1)S(1)}, u32[]{:S(2)}, u32[]{:S(2)}) collective-permute-start(bf16[2,2,256,128]{3,2,1,0:T(8,128)(2,1)S(1)} %get-tuple-element.90), channel_id=1, source_target_pairs={{0,1},{1,0},{2,3},{3,2},{4,5},{5,4},{6,7},{7,6},{8,9},{9,8},{10,11... | collective-permute-start | bytes 786440 | tf_op jit(solution)/shard_map/ppermute | solution.py:416
  61.7 6.0 %collective-permute-start.25 = (bf16[1,2,256,128]{3,2,1,0:T(8,128)(2,1)S(1)}, bf16[1,2,256,128]{3,2,1,0:T(8,128)(2,1)S(1)}, u32[]{:S(2)}, u32[]{:S(2)}) collective-permute-start(bf16[1,2,256,128]{3,2,1,0:T(8,128)(2,1)S(1)} %get-tuple-element.92), channel_id=1, source_target_pairs={{0,2},{1,3},{2,0},{3,1},{4,6},{5,7},{6,4},{7,5},{8,10},{9,11},{10,... | collective-permute-start | bytes 393224 | tf_op jit(solution)/shard_map/ppermute | solution.py:421
  63.3 7.5 %collective-permute-start.18 = (bf16[1,1,304,128]{3,2,1,0:T(8,128)(2,1)S(1)}, bf16[1,1,304,128]{3,2,1,0:T(8,128)(2,1)S(1)}, u32[]{:S(2)}, u32[]{:S(2)}) collective-permute-start(bf16[1,1,304,128]{3,2,1,0:T(8,128)(2,1)S(1)} %get-tuple-element.82), channel_id=1, source_target_pairs={{0,16},{1,17},{2,18},{3,19},{4,20},{5,21},{6,22},{7,23},{8,24},{9,... | collective-permute-start | bytes 233480 | tf_op jit(solution)/shard_map/ppermute | solution.py:421
  65.9 4.8 %collective-permute-start.19 = (bf16[1,1,304,128]{3,2,1,0:T(8,128)(2,1)S(1)}, bf16[1,1,304,128]{3,2,1,0:T(8,128)(2,1)S(1)}, u32[]{:S(2)}, u32[]{:S(2)}) collective-permute-start(bf16[1,1,304,128]{3,2,1,0:T(8,128)(2,1)S(1)} %get-tuple-element.83), channel_id=1, source_target_pairs={{0,2},{1,3},{2,0},{3,1},{4,6},{5,7},{6,4},{7,5},{8,10},{9,11},{10,... | collective-permute-start | bytes 233480 | tf_op jit(solution)/shard_map/ppermute | solution.py:421
  66.5 9.5 %collective-permute-start.20 = (bf16[1,1,304,128]{3,2,1,0:T(8,128)(2,1)S(1)}, bf16[1,1,304,128]{3,2,1,0:T(8,128)(2,1)S(1)}, u32[]{:S(2)}, u32[]{:S(2)}) collective-permute-start(bf16[1,1,304,128]{3,2,1,0:T(8,128)(2,1)S(1)} %get-tuple-element.84), channel_id=1, source_target_pairs={{0,18},{1,19},{2,16},{3,17},{4,22},{5,23},{6,20},{7,21},{8,26},{9,... | collective-permute-start | bytes 233480 | tf_op jit(solution)/shard_map/ppermute | solution.py:421
  67.8 8.8 %collective-permute-start.26 = (bf16[1,1,256,128]{3,2,1,0:T(8,128)(2,1)S(1)}, bf16[1,1,256,128]{3,2,1,0:T(8,128)(2,1)S(1)}, u32[]{:S(2)}, u32[]{:S(2)}) collective-permute-start(bf16[1,1,256,128]{3,2,1,0:T(8,128)(2,1)S(1)} %get-tuple-element.94), channel_id=1, source_target_pairs={{0,16},{1,17},{2,18},{3,19},{4,20},{5,21},{6,22},{7,23},{8,24},{9,... | collective-permute-start | bytes 196616 | tf_op jit(solution)/shard_map/ppermute | solution.py:421
  (6 other events, 45.3 us)

commit v16 on v15

--- a/solution.py
+++ b/solution.py
@@ -150,7 +150,7 @@
     late_refs, hidden_ref, grad_refs = refs[:n_late], refs[n_late], refs[n_late + 1 : -4]
     joined_ref, square_ref, acc_ref, slope_ref = refs[-4:]
     rows, dout = joined_ref.shape
-    step = acc_ref.shape[0]
+    step = slope_ref.shape[0]
     me, group, length, votes = info_ref[0], info_ref[1], info_ref[2], info_ref[3]
     near, far = group % NEAR, group // NEAR
     square_ref[...] = early_ref[...]
@@ -185,7 +185,7 @@
             misfit = predicted - next_ref[at, cs].astype(F32)
             grad = scaled * misfit
             slope = grad * gain
-            acc_ref[:, cs] += grad * normed
+            acc_ref[:, cs] += jnp.sum((grad * normed).reshape(step // 8, 8, 512), axis=0)
             slope_ref[:, cs] = slope
             sq = misfit * misfit
             ln = slope * normed
@@ -251,7 +251,7 @@
         scratch_shapes=[
             pltpu.VMEM((rows, dout), F32),
             pltpu.VMEM((rows, 128), F32),
-            pltpu.VMEM((step, dout), F32),
+            pltpu.VMEM((8, dout), F32),
             pltpu.VMEM((step, dout), F32),
         ],
         compiler_params=params(),

time: 77.6 us -> 77.6 us (level)
  no operation moved by 1% of the time
where the time goes in v16:
time: 77.6 us; the launch traced here: 77.4 us
  waiting for transfers between devices  33.4 us (43%)
  starting transfers between devices  26.7 us (34%)
  Pallas kernels  13.1 us (17%)
  between operations  2.07 us (3%)
  local copies, waits for them, and re-layouts  1.05 us (1%)
  other arithmetic  1.05 us (1%)
    ppermute x22, waiting for transfers between devices, swap(): return lax.ppermute(x, axis, [(i, i ^ mask) for i in range(n)])  27.5 us
    ppermute x22, starting transfers between devices, swap(): return lax.ppermute(x, axis, [(i, i ^ mask) for i in range(n)])  18.7 us
    ppermute x5, starting transfers between devices, swap_far(): lax.ppermute(x, ('dp', 'tensor'), [(i, i ^ mask) for i in range(n_dp * n_...  8 us
    ppermute x5, waiting for transfers between devices, swap_far(): lax.ppermute(x, ('dp', 'tensor'), [(i, i ^ mask) for i in range(n_dp * n_...  5.86 us
    pallas_call x1, Pallas kernels, attend(): pl.pallas_call(attend_body, in_specs=[SM, SM, VM, VM, VM], out_specs=[VM]...  4.74 us
    pallas_call x1, Pallas kernels, join(): pl.pallas_call(functools.partial(join_body, plan, len(late)), in_specs=[S...  3.39 us
    pallas_call x2, Pallas kernels, gradient(): pl.pallas_call(functools.partial(grad_body, plan, dout, [len(c) for c in...  2.5 us
    pallas_call x1, Pallas kernels, mix(): pl.pallas_call(functools.partial(mix_body, n_tensor, counts, split), in_s...  1.56 us
  transfers between devices with their start and end apart: 27, of which 16 were waited for; matrix products, arithmetic and copies ran while one was open for 3% of the time, Pallas kernels for 16%

profile of v16, /device:TPU:0, one launch (start us, length us, event | category | flops | bytes accessed | tf_op | source)
XLA Modules:
  0.0 77.4 jit_solution(6806517230461892579)
XLA Ops:
  2.1 2.6 %collective-permute-start = (bf16[256,512]{1,0:T(8,128)(2,1)S(1)}, bf16[256,512]{1,0:T(8,128)(2,1)S(1)}, u32[]{:S(2)}, u32[]{:S(2)}) collective-permute-start(bf16[256,512]{1,0:T(8,128)(2,1)S(1)} %dynamic-slice_bitcast_fusion), channel_id=1, source_target_pairs={{0,2},{1,3},{2,0},{3,1},{4,6},{5,7},{6,4},{7,5},{8,10},{9,11},{10,... | collective-permute-start | bytes 786440 | tf_op jit(solution)/shard_map/ppermute | solution.py:416
  5.4 4.7 %attend.1 = (bf16[256,256]{1,0:T(8,128)(2,1)}, bf16[256,256]{1,0:T(8,128)(2,1)}, bf16[256,256]{1,0:T(8,128)(2,1)}, bf16[256,256]{1,0:T(8,128)(2,1)}) custom-call(s32[1]{0:T(128)S(6)} %copy.12.len_ref, s32[1]{0:T(128)} %bitcast.me_ref, bf16[1024,256]{1,0:T(8,128)(2,1)} %bitcast.24, bf16[1024,256]{1,0:T(8,128)(2,1)} %bitcast.25, bf16[1024,256]{1,0:T(8,128)(2,1)} %bitcast.26), custom_call_target="tpu_custom_call" | custom-call | flops 1073741824 | bytes 2097152 | tf_op jit(solution)/shard_map/attend/pallas_call | solution.py:82
  10.1 1.6 %collective-permute-done.refs_2_ = bf16[256,512]{1,0:T(8,128)(2,1)S(1)} collective-permute-done((bf16[256,512]{1,0:T(8,128)(2,1)S(1)}, bf16[256,512]{1,0:T(8,128)(2,1)S(1)}, u32[]{:S(2)}, u32[]{:S(2)}) %collective-permute-start) | collective-permute-done | bytes 262176 | tf_op jit(solution)/shard_map/ppermute | solution.py:416
  11.7 1.7 %collective-permute-start.2 = (bf16[256,512]{1,0:T(8,128)(2,1)S(1)}, bf16[256,512]{1,0:T(8,128)(2,1)S(1)}, u32[]{:S(2)}, u32[]{:S(2)}) collective-permute-start(bf16[256,512]{1,0:T(8,128)(2,1)S(1)} %collective-permute-done.refs_2_), channel_id=1, source_target_pairs={{0,4},{4,0},{8,12},{12,8},{16,20},{20,16},{24,28},{28,24},{1,5},{5... | collective-permute-start | bytes 786440 | tf_op jit(solution)/shard_map/ppermute | solution.py:416
  13.4 1.6 %collective-permute-start.6 = (bf16[256,256]{1,0:T(8,128)(2,1)}, bf16[256,256]{1,0:T(8,128)(2,1)S(1)}, u32[]{:S(2)}, u32[]{:S(2)}) collective-permute-start(bf16[256,256]{1,0:T(8,128)(2,1)} %get-tuple-element.59), channel_id=1, source_target_pairs={{0,3},{1,2},{2,1},{3,0},{4,7},{5,6},{6,5},{7,4},{8,11},{9,10},{10,... | collective-permute-start | bytes 393224 | tf_op jit(solution)/shard_map/ppermute | solution.py:416
  15.6 3.6 %collective-permute-done.6 = bf16[256,256]{1,0:T(8,128)(2,1)S(1)} collective-permute-done((bf16[256,256]{1,0:T(8,128)(2,1)}, bf16[256,256]{1,0:T(8,128)(2,1)S(1)}, u32[]{:S(2)}, u32[]{:S(2)}) %collective-permute-start.6) | collective-permute-done | bytes 131104 | tf_op jit(solution)/shard_map/ppermute | solution.py:416
  19.2 3.0 %collective-permute-done.5 = bf16[256,256]{1,0:T(8,128)(2,1)S(1)} collective-permute-done((bf16[256,256]{1,0:T(8,128)(2,1)}, bf16[256,256]{1,0:T(8,128)(2,1)S(1)}, u32[]{:S(2)}, u32[]{:S(2)}) %collective-permute-start.5) | collective-permute-done | bytes 131104 | tf_op jit(solution)/shard_map/ppermute | solution.py:416
  23.2 1.6 %collective-permute-start.10 = (bf16[4,256,256]{2,1,0:T(8,128)(2,1)S(1)}, bf16[4,256,256]{2,1,0:T(8,128)(2,1)S(1)}, u32[]{:S(2)}, u32[]{:S(2)}) collective-permute-start(bf16[4,256,256]{2,1,0:T(8,128)(2,1)S(1)} %pad_maximum_fusion.ctx_ref.refs_0_), channel_id=1, source_target_pairs={{0,8},{4,12},{8,0},{12,4},{16,24},{20,28},{24,16},{28,20},{1,9},{5... | collective-permute-start | bytes 1572872 | tf_op jit(solution)/shard_map/ppermute | solution.py:416
  24.9 1.5 %collective-permute-start.7 = (bf16[256,1024]{1,0:T(8,128)(2,1)S(1)}, bf16[256,1024]{1,0:T(8,128)(2,1)S(1)}, u32[]{:S(2)}, u32[]{:S(2)}) collective-permute-start(bf16[256,1024]{1,0:T(8,128)(2,1)S(1)} %slice.12), channel_id=1, source_target_pairs={{0,2},{1,3},{2,0},{3,1},{4,6},{5,7},{6,4},{7,5},{8,10},{9,11},{10,... | collective-permute-start | bytes 1572872 | tf_op jit(solution)/shard_map/ppermute | solution.py:416
  28.5 1.6 %mix.1 = (f32[256,2048]{1,0:T(8,128)S(1)}, f32[256,128]{1,0:T(8,128)S(1)}, bf16[4,256,256]{2,1,0:T(8,128)(2,1)S(1)}) custom-call(s32[4]{0:T(128)S(1)} %pad_add_fusion.info_ref, bf16[4,256,256]{2,1,0:T(8,128)(2,1)S(1)} %pad_maximum_fusion.ctx_ref.refs_0_, bf16[256,2048]{1,0:T(8,128)(2,1)S(1)} %bitcast.18, ...), custom_call_target="tpu_custom_call" | custom-call | flops 1073741824 | bytes 6291456 | tf_op jit(solution)/shard_map/mix/pallas_call | solution.py:133
  30.0 6.6 %collective-permute-done.10.refs_2_ = bf16[4,256,256]{2,1,0:T(8,128)(2,1)S(1)} collective-permute-done((bf16[4,256,256]{2,1,0:T(8,128)(2,1)S(1)}, bf16[4,256,256]{2,1,0:T(8,128)(2,1)S(1)}, u32[]{:S(2)}, u32[]{:S(2)}) %collective-permute-start.10) | collective-permute-done | bytes 524320 | tf_op jit(solution)/shard_map/ppermute | solution.py:416
  36.6 1.3 %collective-permute-done.7.refs_0_ = bf16[256,1024]{1,0:T(8,128)(2,1)S(1)} collective-permute-done((bf16[256,1024]{1,0:T(8,128)(2,1)S(1)}, bf16[256,1024]{1,0:T(8,128)(2,1)S(1)}, u32[]{:S(2)}, u32[]{:S(2)}) %collective-permute-start.7) | collective-permute-done | bytes 524320 | tf_op jit(solution)/shard_map/ppermute | solution.py:416
  41.0 3.4 %join.1 = (bf16[256,2048]{1,0:T(8,128)(2,1)}, bf16[288,256]{1,0:T(8,128)(2,1)S(1)}, bf16[288,256]{1,0:T(8,128)(2,1)S(1)}, bf16[288,256]{1,0:T(8,128)(2,1)S(1)}, ...) custom-call(s32[4]{0:T(128)S(1)} %pad_add_fusion.info_ref, ...), custom_call_target="tpu_custom_call" | custom-call | flops 134217728 | bytes 6291456 | tf_op jit(solution)/shard_map/join/pallas_call | solution.py:246
  45.2 1.6 %collective-permute-start.22 = (bf16[256,256]{1,0:T(8,128)(2,1)S(1)}, bf16[256,256]{1,0:T(8,128)(2,1)S(1)}, u32[]{:S(2)}, u32[]{:S(2)}) collective-permute-start(bf16[256,256]{1,0:T(8,128)(2,1)S(1)} %get-tuple-element.87), channel_id=1, source_target_pairs={{0,8},{4,12},{8,0},{12,4},{16,24},{20,28},{24,16},{28,20},{1,9},{5... | collective-permute-start | bytes 393224 | tf_op jit(solution)/shard_map/ppermute | solution.py:416
  48.9 1.6 %collective-permute-start.15 = (bf16[288,256]{1,0:T(8,128)(2,1)S(1)}, bf16[288,256]{1,0:T(8,128)(2,1)S(1)}, u32[]{:S(2)}, u32[]{:S(2)}) collective-permute-start(bf16[288,256]{1,0:T(8,128)(2,1)S(1)} %get-tuple-element.77), channel_id=1, source_target_pairs={{0,8},{4,12},{8,0},{12,4},{16,24},{20,28},{24,16},{28,20},{1,9},{5... | collective-permute-start | bytes 442376 | tf_op jit(solution)/shard_map/ppermute | solution.py:416
  50.5 3.5 %collective-permute-done.21.refs_6_ = bf16[256,256]{1,0:T(8,128)(2,1)S(1)} collective-permute-done((bf16[256,256]{1,0:T(8,128)(2,1)S(1)}, bf16[256,256]{1,0:T(8,128)(2,1)S(1)}, u32[]{:S(2)}, u32[]{:S(2)}) %collective-permute-start.21) | collective-permute-done | bytes 131104 | tf_op jit(solution)/shard_map/ppermute | solution.py:416
  53.9 1.3 %collective-permute-start.16 = (bf16[288,256]{1,0:T(8,128)(2,1)S(1)}, bf16[288,256]{1,0:T(8,128)(2,1)S(1)}, u32[]{:S(2)}, u32[]{:S(2)}) collective-permute-start(bf16[288,256]{1,0:T(8,128)(2,1)S(1)} %get-tuple-element.78), channel_id=1, source_target_pairs={{0,12},{4,8},{8,4},{12,0},{16,28},{20,24},{24,20},{28,16},{1,13},{... | collective-permute-start | bytes 442376 | tf_op jit(solution)/shard_map/ppermute | solution.py:416
  55.2 1.3 %gradient.3 = (bf16[2,2,256,128]{3,2,1,0:T(8,128)(2,1)S(1)}, bf16[2,2,256,128]{3,2,1,0:T(8,128)(2,1)S(1)}) custom-call(s32[4]{0:T(128)S(1)} %pad_add_fusion.info_ref, bf16[4,256,256]{2,1,0:T(8,128)(2,1)S(1)} %pad_maximum_fusion.ctx_ref.refs_0_, bf16[4,256,256]{2,1,0:T(8,128)(2,1)S(1)} %collective-permute-done.9.refs_1_, ...), custom_call_target="tpu_custom_call" | custom-call | flops 536870912 | bytes 3145728 | tf_op jit(solution)/shard_map/gradient/pallas_call | solution.py:329
  56.6 1.4 %collective-permute-done.14.refs_6_ = bf16[288,256]{1,0:T(8,128)(2,1)S(1)} collective-permute-done((bf16[288,256]{1,0:T(8,128)(2,1)S(1)}, bf16[288,256]{1,0:T(8,128)(2,1)S(1)}, u32[]{:S(2)}, u32[]{:S(2)}) %collective-permute-start.14) | collective-permute-done | bytes 147488 | tf_op jit(solution)/shard_map/ppermute | solution.py:416
  57.9 2.3 %collective-permute-done.16.refs_8_ = bf16[288,256]{1,0:T(8,128)(2,1)S(1)} collective-permute-done((bf16[288,256]{1,0:T(8,128)(2,1)S(1)}, bf16[288,256]{1,0:T(8,128)(2,1)S(1)}, u32[]{:S(2)}, u32[]{:S(2)}) %collective-permute-start.16) | collective-permute-done | bytes 147488 | tf_op jit(solution)/shard_map/ppermute | solution.py:416
  60.3 1.2 %gradient.2 = (bf16[2,2,304,128]{3,2,1,0:T(8,128)(2,1)S(1)}, bf16[2,2,304,128]{3,2,1,0:T(8,128)(2,1)S(1)}) custom-call(s32[4]{0:T(128)S(1)} %pad_add_fusion.info_ref, bf16[4,256,256]{2,1,0:T(8,128)(2,1)S(1)} %pad_maximum_fusion.ctx_ref.refs_0_, bf16[4,256,256]{2,1,0:T(8,128)(2,1)S(1)} %collective-permute-done.9.refs_1_, ...), custom_call_target="tpu_custom_call" | custom-call | flops 536870912 | bytes 3145728 | tf_op jit(solution)/shard_map/gradient/pallas_call | solution.py:329
  63.3 2.7 %collective-permute-start.18 = (bf16[1,1,304,128]{3,2,1,0:T(8,128)(2,1)S(1)}, bf16[1,1,304,128]{3,2,1,0:T(8,128)(2,1)S(1)}, u32[]{:S(2)}, u32[]{:S(2)}) collective-permute-start(bf16[1,1,304,128]{3,2,1,0:T(8,128)(2,1)S(1)} %get-tuple-element.82), channel_id=1, source_target_pairs={{0,16},{1,17},{2,18},{3,19},{4,20},{5,21},{6,22},{7,23},{8,24},{9,... | collective-permute-start | bytes 233480 | tf_op jit(solution)/shard_map/ppermute | solution.py:421
  67.8 3.0 %collective-permute-start.26 = (bf16[1,1,256,128]{3,2,1,0:T(8,128)(2,1)S(1)}, bf16[1,1,256,128]{3,2,1,0:T(8,128)(2,1)S(1)}, u32[]{:S(2)}, u32[]{:S(2)}) collective-permute-start(bf16[1,1,256,128]{3,2,1,0:T(8,128)(2,1)S(1)} %get-tuple-element.94), channel_id=1, source_target_pairs={{0,16},{1,17},{2,18},{3,19},{4,20},{5,21},{6,22},{7,23},{8,24},{9,... | collective-permute-start | bytes 196616 | tf_op jit(solution)/shard_map/ppermute | solution.py:421
  70.8 5.2 %collective-permute-done.20.refs_3_ = bf16[1,1,304,128]{3,2,1,0:T(8,128)(2,1)S(1)} collective-permute-done((bf16[1,1,304,128]{3,2,1,0:T(8,128)(2,1)S(1)}, bf16[1,1,304,128]{3,2,1,0:T(8,128)(2,1)S(1)}, u32[]{:S(2)}, u32[]{:S(2)}) %collective-permute-start.20) | collective-permute-done | bytes 77856 | tf_op jit(solution)/shard_map/ppermute | solution.py:421
  (51 shorter events, 15.5 us)
Async XLA Ops:
  0.6 11.1 %collective-permute-start.1 = (bf16[256,2048]{1,0:T(8,128)(2,1)}, bf16[256,2048]{1,0:T(8,128)(2,1)S(1)}, u32[]{:S(2)}, u32[]{:S(2)}) collective-permute-start(bf16[256,2048]{1,0:T(8,128)(2,1)} %bitcast.16), channel_id=1, source_target_pairs={{0,1},{1,0},{2,3},{3,2},{4,5},{5,4},{6,7},{7,6},{8,9},{9,8},{10,11... | collective-permute-start | bytes 3145736 | tf_op jit(solution)/shard_map/ppermute | solution.py:416
  2.1 9.6 %collective-permute-start = (bf16[256,512]{1,0:T(8,128)(2,1)S(1)}, bf16[256,512]{1,0:T(8,128)(2,1)S(1)}, u32[]{:S(2)}, u32[]{:S(2)}) collective-permute-start(bf16[256,512]{1,0:T(8,128)(2,1)S(1)} %dynamic-slice_bitcast_fusion), channel_id=1, source_target_pairs={{0,2},{1,3},{2,0},{3,1},{4,6},{5,7},{6,4},{7,5},{8,10},{9,11},{10,... | collective-permute-start | bytes 786440 | tf_op jit(solution)/shard_map/ppermute | solution.py:416
  11.7 11.5 %collective-permute-start.2 = (bf16[256,512]{1,0:T(8,128)(2,1)S(1)}, bf16[256,512]{1,0:T(8,128)(2,1)S(1)}, u32[]{:S(2)}, u32[]{:S(2)}) collective-permute-start(bf16[256,512]{1,0:T(8,128)(2,1)S(1)} %collective-permute-done.refs_2_), channel_id=1, source_target_pairs={{0,4},{4,0},{8,12},{12,8},{16,20},{20,16},{24,28},{28,24},{1,5},{5... | collective-permute-start | bytes 786440 | tf_op jit(solution)/shard_map/ppermute | solution.py:416
  13.4 9.8 %collective-permute-start.3 = (bf16[256,512]{1,0:T(8,128)(2,1)S(1)}, bf16[256,512]{1,0:T(8,128)(2,1)S(1)}, u32[]{:S(2)}, u32[]{:S(2)}) collective-permute-start(bf16[256,512]{1,0:T(8,128)(2,1)S(1)} %collective-permute-done.refs_2_), channel_id=1, source_target_pairs={{0,1},{1,0},{2,3},{3,2},{4,5},{5,4},{6,7},{7,6},{8,9},{9,8},{10,11... | collective-permute-start | bytes 786440 | tf_op jit(solution)/shard_map/ppermute | solution.py:416
  13.4 5.8 %collective-permute-start.6 = (bf16[256,256]{1,0:T(8,128)(2,1)}, bf16[256,256]{1,0:T(8,128)(2,1)S(1)}, u32[]{:S(2)}, u32[]{:S(2)}) collective-permute-start(bf16[256,256]{1,0:T(8,128)(2,1)} %get-tuple-element.59), channel_id=1, source_target_pairs={{0,3},{1,2},{2,1},{3,0},{4,7},{5,6},{6,5},{7,4},{8,11},{9,10},{10,... | collective-permute-start | bytes 393224 | tf_op jit(solution)/shard_map/ppermute | solution.py:416
  15.0 4.2 %collective-permute-start.4 = (bf16[256,256]{1,0:T(8,128)(2,1)}, bf16[256,256]{1,0:T(8,128)(2,1)S(1)}, u32[]{:S(2)}, u32[]{:S(2)}) collective-permute-start(bf16[256,256]{1,0:T(8,128)(2,1)} %get-tuple-element.57), channel_id=1, source_target_pairs={{0,1},{1,0},{2,3},{3,2},{4,5},{5,4},{6,7},{7,6},{8,9},{9,8},{10,11... | collective-permute-start | bytes 393224 | tf_op jit(solution)/shard_map/ppermute | solution.py:416
  15.0 7.2 %collective-permute-start.5 = (bf16[256,256]{1,0:T(8,128)(2,1)}, bf16[256,256]{1,0:T(8,128)(2,1)S(1)}, u32[]{:S(2)}, u32[]{:S(2)}) collective-permute-start(bf16[256,256]{1,0:T(8,128)(2,1)} %get-tuple-element.58), channel_id=1, source_target_pairs={{0,2},{1,3},{2,0},{3,1},{4,6},{5,7},{6,4},{7,5},{8,10},{9,11},{10,... | collective-permute-start | bytes 393224 | tf_op jit(solution)/shard_map/ppermute | solution.py:416
  23.2 13.4 %collective-permute-start.10 = (bf16[4,256,256]{2,1,0:T(8,128)(2,1)S(1)}, bf16[4,256,256]{2,1,0:T(8,128)(2,1)S(1)}, u32[]{:S(2)}, u32[]{:S(2)}) collective-permute-start(bf16[4,256,256]{2,1,0:T(8,128)(2,1)S(1)} %pad_maximum_fusion.ctx_ref.refs_0_), channel_id=1, source_target_pairs={{0,8},{4,12},{8,0},{12,4},{16,24},{20,28},{24,16},{28,20},{1,9},{5... | collective-permute-start | bytes 1572872 | tf_op jit(solution)/shard_map/ppermute | solution.py:416
  24.9 13.0 %collective-permute-start.7 = (bf16[256,1024]{1,0:T(8,128)(2,1)S(1)}, bf16[256,1024]{1,0:T(8,128)(2,1)S(1)}, u32[]{:S(2)}, u32[]{:S(2)}) collective-permute-start(bf16[256,1024]{1,0:T(8,128)(2,1)S(1)} %slice.12), channel_id=1, source_target_pairs={{0,2},{1,3},{2,0},{3,1},{4,6},{5,7},{6,4},{7,5},{8,10},{9,11},{10,... | collective-permute-start | bytes 1572872 | tf_op jit(solution)/shard_map/ppermute | solution.py:416
  26.4 12.7 %collective-permute-start.9 = (bf16[4,256,256]{2,1,0:T(8,128)(2,1)S(1)}, bf16[4,256,256]{2,1,0:T(8,128)(2,1)S(1)}, u32[]{:S(2)}, u32[]{:S(2)}) collective-permute-start(bf16[4,256,256]{2,1,0:T(8,128)(2,1)S(1)} %pad_maximum_fusion.ctx_ref.refs_0_), channel_id=1, source_target_pairs={{0,4},{4,0},{8,12},{12,8},{16,20},{20,16},{24,28},{28,24},{1,5},{5... | collective-permute-start | bytes 1572872 | tf_op jit(solution)/shard_map/ppermute | solution.py:416
  39.1 9.2 %collective-permute-start.12 = (bf16[4,128,256]{2,1,0:T(8,128)(2,1)S(1)}, bf16[4,128,256]{2,1,0:T(8,128)(2,1)S(1)}, u32[]{:S(2)}, u32[]{:S(2)}) collective-permute-start(bf16[4,128,256]{2,1,0:T(8,128)(2,1)S(1)} %slice.10), channel_id=1, source_target_pairs={{0,8},{4,12},{8,0},{12,4},{16,24},{20,28},{24,16},{28,20},{1,9},{5... | collective-permute-start | bytes 786440 | tf_op jit(solution)/shard_map/ppermute | solution.py:416
  39.7 9.2 %collective-permute-start.13 = (bf16[4,128,256]{2,1,0:T(8,128)(2,1)S(1)}, bf16[4,128,256]{2,1,0:T(8,128)(2,1)S(1)}, u32[]{:S(2)}, u32[]{:S(2)}) collective-permute-start(bf16[4,128,256]{2,1,0:T(8,128)(2,1)S(1)} %slice.11), channel_id=1, source_target_pairs={{0,4},{4,0},{8,12},{12,8},{16,20},{20,16},{24,28},{28,24},{1,5},{5... | collective-permute-start | bytes 786440 | tf_op jit(solution)/shard_map/ppermute | solution.py:416
  44.4 9.5 %collective-permute-start.21 = (bf16[256,256]{1,0:T(8,128)(2,1)S(1)}, bf16[256,256]{1,0:T(8,128)(2,1)S(1)}, u32[]{:S(2)}, u32[]{:S(2)}) collective-permute-start(bf16[256,256]{1,0:T(8,128)(2,1)S(1)} %get-tuple-element.86), channel_id=1, source_target_pairs={{0,4},{4,0},{8,12},{12,8},{16,20},{20,16},{24,28},{28,24},{1,5},{5... | collective-permute-start | bytes 393224 | tf_op jit(solution)/shard_map/ppermute | solution.py:416
  45.2 10.0 %collective-permute-start.22 = (bf16[256,256]{1,0:T(8,128)(2,1)S(1)}, bf16[256,256]{1,0:T(8,128)(2,1)S(1)}, u32[]{:S(2)}, u32[]{:S(2)}) collective-permute-start(bf16[256,256]{1,0:T(8,128)(2,1)S(1)} %get-tuple-element.87), channel_id=1, source_target_pairs={{0,8},{4,12},{8,0},{12,4},{16,24},{20,28},{24,16},{28,20},{1,9},{5... | collective-permute-start | bytes 393224 | tf_op jit(solution)/shard_map/ppermute | solution.py:416
  46.8 8.4 %collective-permute-start.23 = (bf16[256,256]{1,0:T(8,128)(2,1)S(1)}, bf16[256,256]{1,0:T(8,128)(2,1)S(1)}, u32[]{:S(2)}, u32[]{:S(2)}) collective-permute-start(bf16[256,256]{1,0:T(8,128)(2,1)S(1)} %get-tuple-element.88), channel_id=1, source_target_pairs={{0,12},{4,8},{8,4},{12,0},{16,28},{20,24},{24,20},{28,16},{1,13},{... | collective-permute-start | bytes 393224 | tf_op jit(solution)/shard_map/ppermute | solution.py:416
  48.3 9.6 %collective-permute-start.14 = (bf16[288,256]{1,0:T(8,128)(2,1)S(1)}, bf16[288,256]{1,0:T(8,128)(2,1)S(1)}, u32[]{:S(2)}, u32[]{:S(2)}) collective-permute-start(bf16[288,256]{1,0:T(8,128)(2,1)S(1)} %get-tuple-element.76), channel_id=1, source_target_pairs={{0,4},{4,0},{8,12},{12,8},{16,20},{20,16},{24,28},{28,24},{1,5},{5... | collective-permute-start | bytes 442376 | tf_op jit(solution)/shard_map/ppermute | solution.py:416
  48.9 9.0 %collective-permute-start.15 = (bf16[288,256]{1,0:T(8,128)(2,1)S(1)}, bf16[288,256]{1,0:T(8,128)(2,1)S(1)}, u32[]{:S(2)}, u32[]{:S(2)}) collective-permute-start(bf16[288,256]{1,0:T(8,128)(2,1)S(1)} %get-tuple-element.77), channel_id=1, source_target_pairs={{0,8},{4,12},{8,0},{12,4},{16,24},{20,28},{24,16},{28,20},{1,9},{5... | collective-permute-start | bytes 442376 | tf_op jit(solution)/shard_map/ppermute | solution.py:416
  53.9 6.4 %collective-permute-start.16 = (bf16[288,256]{1,0:T(8,128)(2,1)S(1)}, bf16[288,256]{1,0:T(8,128)(2,1)S(1)}, u32[]{:S(2)}, u32[]{:S(2)}) collective-permute-start(bf16[288,256]{1,0:T(8,128)(2,1)S(1)} %get-tuple-element.78), channel_id=1, source_target_pairs={{0,12},{4,8},{8,4},{12,0},{16,28},{20,24},{24,20},{28,16},{1,13},{... | collective-permute-start | bytes 442376 | tf_op jit(solution)/shard_map/ppermute | solution.py:416
  56.5 5.1 %collective-permute-start.24 = (bf16[2,2,256,128]{3,2,1,0:T(8,128)(2,1)S(1)}, bf16[2,2,256,128]{3,2,1,0:T(8,128)(2,1)S(1)}, u32[]{:S(2)}, u32[]{:S(2)}) collective-permute-start(bf16[2,2,256,128]{3,2,1,0:T(8,128)(2,1)S(1)} %get-tuple-element.90), channel_id=1, source_target_pairs={{0,1},{1,0},{2,3},{3,2},{4,5},{5,4},{6,7},{7,6},{8,9},{9,8},{10,11... | collective-permute-start | bytes 786440 | tf_op jit(solution)/shard_map/ppermute | solution.py:416
  61.7 6.0 %collective-permute-start.25 = (bf16[1,2,256,128]{3,2,1,0:T(8,128)(2,1)S(1)}, bf16[1,2,256,128]{3,2,1,0:T(8,128)(2,1)S(1)}, u32[]{:S(2)}, u32[]{:S(2)}) collective-permute-start(bf16[1,2,256,128]{3,2,1,0:T(8,128)(2,1)S(1)} %get-tuple-element.92), channel_id=1, source_target_pairs={{0,2},{1,3},{2,0},{3,1},{4,6},{5,7},{6,4},{7,5},{8,10},{9,11},{10,... | collective-permute-start | bytes 393224 | tf_op jit(solution)/shard_map/ppermute | solution.py:421
  63.3 7.5 %collective-permute-start.18 = (bf16[1,1,304,128]{3,2,1,0:T(8,128)(2,1)S(1)}, bf16[1,1,304,128]{3,2,1,0:T(8,128)(2,1)S(1)}, u32[]{:S(2)}, u32[]{:S(2)}) collective-permute-start(bf16[1,1,304,128]{3,2,1,0:T(8,128)(2,1)S(1)} %get-tuple-element.82), channel_id=1, source_target_pairs={{0,16},{1,17},{2,18},{3,19},{4,20},{5,21},{6,22},{7,23},{8,24},{9,... | collective-permute-start | bytes 233480 | tf_op jit(solution)/shard_map/ppermute | solution.py:421
  65.9 4.8 %collective-permute-start.19 = (bf16[1,1,304,128]{3,2,1,0:T(8,128)(2,1)S(1)}, bf16[1,1,304,128]{3,2,1,0:T(8,128)(2,1)S(1)}, u32[]{:S(2)}, u32[]{:S(2)}) collective-permute-start(bf16[1,1,304,128]{3,2,1,0:T(8,128)(2,1)S(1)} %get-tuple-element.83), channel_id=1, source_target_pairs={{0,2},{1,3},{2,0},{3,1},{4,6},{5,7},{6,4},{7,5},{8,10},{9,11},{10,... | collective-permute-start | bytes 233480 | tf_op jit(solution)/shard_map/ppermute | solution.py:421
  66.5 9.5 %collective-permute-start.20 = (bf16[1,1,304,128]{3,2,1,0:T(8,128)(2,1)S(1)}, bf16[1,1,304,128]{3,2,1,0:T(8,128)(2,1)S(1)}, u32[]{:S(2)}, u32[]{:S(2)}) collective-permute-start(bf16[1,1,304,128]{3,2,1,0:T(8,128)(2,1)S(1)} %get-tuple-element.84), channel_id=1, source_target_pairs={{0,18},{1,19},{2,16},{3,17},{4,22},{5,23},{6,20},{7,21},{8,26},{9,... | collective-permute-start | bytes 233480 | tf_op jit(solution)/shard_map/ppermute | solution.py:421
  67.8 8.8 %collective-permute-start.26 = (bf16[1,1,256,128]{3,2,1,0:T(8,128)(2,1)S(1)}, bf16[1,1,256,128]{3,2,1,0:T(8,128)(2,1)S(1)}, u32[]{:S(2)}, u32[]{:S(2)}) collective-permute-start(bf16[1,1,256,128]{3,2,1,0:T(8,128)(2,1)S(1)} %get-tuple-element.94), channel_id=1, source_target_pairs={{0,16},{1,17},{2,18},{3,19},{4,20},{5,21},{6,22},{7,23},{8,24},{9,... | collective-permute-start | bytes 196616 | tf_op jit(solution)/shard_map/ppermute | solution.py:421
  (6 other events, 45.3 us)
